TPU v7x, 32 devices: a whole 2x2x4 slice. The times are simulated.
32 devices in a mesh: cond: 4 (over y, core), seq: 8 (over z, x).
Axes of the slice: x: 2, y: 2, z: 4, core: 2. Of those that a mesh axis runs over, the one named last changes fastest.
Arguments:
- inputs: bfloat16 [4, 4096, 1024], P(None, 'seq', 'cond'), may hold values from -100 to 100
- coarse_ids: int32 [4, 1024], P(None, 'seq'), may hold values from 0 to 2047
- segment_ids: int32 [4, 4096], P(None, 'seq'), may hold values from 0 to 31, never falling along the last dimension, each value on 1 to 256 neighbouring positions
- cotangent: bfloat16 [4, 4096, 1024], P(None, 'seq', 'cond'), may hold values from -6 to 6
- embed_table: bfloat16 [2048, 1024], P('seq', 'cond'), may hold values from -6 to 6
- conv_weight: bfloat16 [3, 1024, 1024], P(None, 'cond', 'seq'), may hold values from -0.109375 to 0.109375
- res_weight: bfloat16 [1024, 1024], P('seq', 'cond'), may hold values from -0.1875 to 0.1875
- up_weight: bfloat16 [1024, 4096], P('cond', 'seq'), may hold values from -0.1875 to 0.1875
- gain_one: bfloat16 [1024], P(('cond', 'seq')), may hold values from 0.5 to 1.5
- shift_one: bfloat16 [1024], P(('cond', 'seq')), may hold values from -2 to 2
- qkv_weight: bfloat16 [1024, 3, 1024], P('seq', None, 'cond'), may hold values from -0.1875 to 0.1875
- out_weight: bfloat16 [1024, 1024], P('cond', 'seq'), may hold values from -0.5 to 0.5
- gain_two: bfloat16 [1024], P(('cond', 'seq')), may hold values from 0.5 to 1.5
- shift_two: bfloat16 [1024], P(('cond', 'seq')), may hold values from -2 to 2
- in_weight: bfloat16 [1024, 4096], P('seq', 'cond'), may hold values from -0.1875 to 0.1875
- down_weight: bfloat16 [4096, 1024], P('cond', 'seq'), may hold values from -0.09375 to 0.09375
Outputs:
- activation: bfloat16 [4, 4096, 1024], P(None, 'seq', 'cond')
- input_grad: bfloat16 [4, 4096, 1024], P(None, 'seq', 'cond')
- grad_table: float32 [2048, 1024], P('seq', 'cond')
- grad_conv: float32 [3, 1024, 1024], P(None, 'cond', 'seq')
- grad_res: float32 [1024, 1024], P('seq', 'cond')
- grad_up: float32 [1024, 4096], P('cond', 'seq')
- grad_gain_one: float32 [1024], P(('cond', 'seq'))
- grad_shift_one: float32 [1024], P(('cond', 'seq'))
- grad_qkv: float32 [1024, 3, 1024], P('seq', None, 'cond')
- grad_out: float32 [1024, 1024], P('cond', 'seq')
- grad_gain_two: float32 [1024], P(('cond', 'seq'))
- grad_shift_two: float32 [1024], P(('cond', 'seq'))
- grad_in: float32 [1024, 4096], P('seq', 'cond')
- grad_down: float32 [4096, 1024], P('cond', 'seq')
All inputs are finite; a program needn't handle non-finite values.
Results may differ from a plain program's by a relative error of at most 0.02.
Values may be sent and summed in bfloat16 or wider, within the bound.
No kernel may reach another device: no remote copies, remote signals or barrier semaphores. Data moves between devices by JAX's collectives and lax.ppermute only.
A program may use at most 112 MiB of HBM per device.

v0:
```python
import math

import jax
import jax.numpy as jnp
from jax import lax
from jax.sharding import PartitionSpec as P

HEAD = 64
ROW = 64
CONV_DILATION = 27


EPSILON = 1e-05
NEG_FILL = -1e30


def extended(cells, sides, width):
    for axis, dim in sides:
        count = lax.axis_size(axis)
        ends = count - 1
        head = lax.slice_in_dim(cells, 0, width, axis=dim)
        tail = lax.slice_in_dim(cells, cells.shape[dim] - width, cells.shape[dim], axis=dim)
        cells = jnp.concatenate(
            [
                lax.ppermute(tail, axis, [(i, (i + 1) % count) for i in range(ends)]),
                cells,
                lax.ppermute(head, axis, [((i + 1) % count, i) for i in range(ends)]),
            ],
            axis=dim,
        )
    return cells


def gelu_exact(value):
    return jax.nn.gelu(value, approximate=False)


def gelu_back(value, grad_value):
    _, pull = jax.vjp(gelu_exact, value)
    return pull(grad_value)[0]


def gram_dot(left, right):
    return lax.dot_general(
        left, right, (((0,), (0,)), ((), ())), preferred_element_type=jnp.float32
    )


def times_t(left, right):
    return lax.dot_general(
        left, right, (((1,), (1,)), ((), ())), preferred_element_type=jnp.float32
    )


def fetch_weights(shards):
    return (
        lax.all_gather(shards[0], "seq", axis=0, tiled=True),
        lax.all_gather(shards[1], "seq", axis=2, tiled=True),
        lax.all_gather(shards[2], "seq", axis=0, tiled=True),
        lax.all_gather(shards[3], "seq", axis=1, tiled=True),
        lax.all_gather(shards[4], "seq", axis=0, tiled=True),
        lax.all_gather(shards[5], "seq", axis=0, tiled=True),
        lax.all_gather(shards[6], "seq", axis=0, tiled=True),
        lax.all_gather(shards[7], "seq", axis=1, tiled=True),
        lax.all_gather(shards[8], "seq", axis=0, tiled=True),
        lax.all_gather(shards[9], "seq", axis=0, tiled=True),
        lax.all_gather(shards[10], "seq", axis=0, tiled=True),
        lax.all_gather(shards[11], "seq", axis=1, tiled=True),
    )


def spread_grads(gradients):
    return (
        lax.psum_scatter(
            gradients[0].astype(jnp.bfloat16), "seq", scatter_dimension=0, tiled=True
        ).astype(jnp.float32),
        lax.psum_scatter(
            gradients[1].astype(jnp.bfloat16), "seq", scatter_dimension=2, tiled=True
        ).astype(jnp.float32),
        lax.psum_scatter(
            gradients[2].astype(jnp.bfloat16), "seq", scatter_dimension=0, tiled=True
        ).astype(jnp.float32),
        lax.psum_scatter(
            gradients[3].astype(jnp.bfloat16), "seq", scatter_dimension=1, tiled=True
        ).astype(jnp.float32),
        lax.psum_scatter(
            gradients[4].astype(jnp.bfloat16), "seq", scatter_dimension=0, tiled=True
        ).astype(jnp.float32),
        lax.psum_scatter(
            gradients[5].astype(jnp.bfloat16), "seq", scatter_dimension=0, tiled=True
        ).astype(jnp.float32),
        lax.psum_scatter(
            gradients[6].astype(jnp.bfloat16), "seq", scatter_dimension=0, tiled=True
        ).astype(jnp.float32),
        lax.psum_scatter(
            gradients[7].astype(jnp.bfloat16), "seq", scatter_dimension=1, tiled=True
        ).astype(jnp.float32),
        lax.psum_scatter(
            gradients[8].astype(jnp.bfloat16), "seq", scatter_dimension=0, tiled=True
        ).astype(jnp.float32),
        lax.psum_scatter(
            gradients[9].astype(jnp.bfloat16), "seq", scatter_dimension=0, tiled=True
        ).astype(jnp.float32),
        lax.psum_scatter(
            gradients[10].astype(jnp.bfloat16), "seq", scatter_dimension=0, tiled=True
        ).astype(jnp.float32),
        lax.psum_scatter(
            gradients[11].astype(jnp.bfloat16), "seq", scatter_dimension=1, tiled=True
        ).astype(jnp.float32),
    )


def gather_rows(value):
    return lax.all_gather(value, "cond", axis=1, tiled=True)


def share_rows(value):
    return lax.psum_scatter(value, "cond", scatter_dimension=1, tiled=True)


def moments(first_part, second_part):
    return lax.psum((first_part, second_part), "cond")


def norm_forward(stream, full_width):
    tot_sum, tot_sq = moments(jnp.sum(stream, axis=1), jnp.sum(stream * stream, axis=1))
    mean_row = tot_sum / full_width
    var_row = tot_sq / full_width - mean_row * mean_row
    rstd_row = lax.rsqrt(var_row + EPSILON)
    return ((stream - mean_row[:, None]) * rstd_row[:, None], rstd_row)


def norm_backward(normed, rstd_row, gain, grad_norm, full_width):
    scaled = grad_norm * gain
    tot_first, tot_second = moments(jnp.sum(scaled, axis=1), jnp.sum(scaled * normed, axis=1))
    grad_stream = rstd_row[:, None] * (
        scaled - tot_first[:, None] / full_width - normed * tot_second[:, None] / full_width
    )
    return (grad_stream, jnp.sum(grad_norm * normed, axis=0), jnp.sum(grad_norm, axis=0))


def attend_scores(query_part, key_part, allowed, score_scale):
    scores = (
        jnp.einsum("bqhd,bkhd->bhqk", query_part, key_part, preferred_element_type=jnp.float32)
        * score_scale
    )
    return jnp.where(allowed, scores, NEG_FILL)


def one_micro(inputs, coarse, segments, cotangent, full):
    (
        embed_table,
        conv_weight,
        res_weight,
        up_weight,
        gain_one,
        shift_one,
        qkv_weight,
        out_weight,
        gain_two,
        shift_two,
        in_weight,
        down_weight,
    ) = full
    tokens, quarter = inputs.shape
    model_width = quarter * lax.axis_size("cond")
    coarse_length = coarse.shape[0]
    dilation_step = CONV_DILATION
    table_rows = embed_table.shape[0]
    onehot = (coarse[:, None] == jnp.arange(table_rows, dtype=jnp.int32)[None, :]).astype(
        jnp.bfloat16
    )
    embed = jnp.dot(onehot, embed_table, preferred_element_type=jnp.float32)
    coarse_activation_rows = gelu_exact(embed).astype(jnp.bfloat16)
    padded_input = extended(coarse_activation_rows, (("seq", 0),), dilation_step)
    kernel_tap_rows = jnp.concatenate(
        [
            padded_input[kernel_tap * dilation_step : kernel_tap * dilation_step + coarse_length]
            for kernel_tap in range(3)
        ],
        axis=1,
    )
    conv_flat = conv_weight.reshape(3 * quarter, model_width)
    conv_out = lax.psum(
        jnp.dot(kernel_tap_rows, conv_flat, preferred_element_type=jnp.float32), "cond"
    )
    mixed_act = gelu_exact(conv_out).astype(jnp.bfloat16)
    res_out = jnp.dot(mixed_act, res_weight, preferred_element_type=jnp.float32)
    hidden_cond = (embed + res_out).astype(jnp.bfloat16)
    up_terms = jnp.dot(hidden_cond, up_weight, preferred_element_type=jnp.float32).reshape(
        tokens, model_width
    )
    stream_zero = inputs.astype(jnp.float32) + share_rows(up_terms)
    gain_first = gain_one.astype(jnp.float32)
    gain_second = gain_two.astype(jnp.float32)
    normed_one, rstd_one = norm_forward(stream_zero, model_width)
    norm_one = gather_rows(
        (normed_one * gain_first + shift_one.astype(jnp.float32)).astype(jnp.bfloat16)
    )
    qkv_all = jnp.einsum(
        "td,dje->tje", norm_one, qkv_weight, preferred_element_type=jnp.float32
    ).astype(jnp.bfloat16)
    local_width = qkv_all.shape[2]
    head_count = local_width // HEAD
    row_count = tokens // ROW
    block_shape = (row_count, ROW, head_count, HEAD)
    query_part = qkv_all[:, 0].reshape(block_shape)
    key_part = qkv_all[:, 1].reshape(block_shape)
    value_part = qkv_all[:, 2].reshape(block_shape)
    seg_rows = segments.reshape(row_count, ROW)
    places = jnp.arange(ROW)
    allowed = (
        (seg_rows[:, :, None] == seg_rows[:, None, :]) & (places[:, None] >= places[None, :])[None]
    )[:, None]
    score_scale = 1.0 / math.sqrt(HEAD)
    scores = attend_scores(query_part, key_part, allowed, score_scale)
    row_max = jnp.max(scores, axis=-1, keepdims=True)
    row_exp = jnp.exp(scores - row_max)
    row_total = jnp.sum(row_exp, axis=-1, keepdims=True)
    log_total = row_max + jnp.log(row_total)
    probs_low = (row_exp / row_total).astype(jnp.bfloat16)
    context = jnp.einsum(
        "bhqk,bkhd->bqhd", probs_low, value_part, preferred_element_type=jnp.float32
    )
    context = context.astype(jnp.bfloat16).reshape(tokens, local_width)
    stream_one = stream_zero + share_rows(
        jnp.dot(context, out_weight, preferred_element_type=jnp.float32)
    )
    normed_two, rstd_two = norm_forward(stream_one, model_width)
    norm_two = gather_rows(
        (normed_two * gain_second + shift_two.astype(jnp.float32)).astype(jnp.bfloat16)
    )
    mlp_pre = jnp.dot(norm_two, in_weight, preferred_element_type=jnp.float32)
    mlp_act = gelu_exact(mlp_pre).astype(jnp.bfloat16)
    stream_two = stream_one + share_rows(
        jnp.dot(mlp_act, down_weight, preferred_element_type=jnp.float32)
    )
    result = stream_two.astype(jnp.bfloat16)
    cot_whole = gather_rows(cotangent)
    grad_down = gram_dot(mlp_act, cot_whole)
    grad_pre = gelu_back(mlp_pre, times_t(cot_whole, down_weight)).astype(jnp.bfloat16)
    grad_in = gram_dot(norm_two, grad_pre)
    grad_norm_two = share_rows(times_t(grad_pre, in_weight))
    back_two, grad_gain_two, grad_shift_two = norm_backward(
        normed_two, rstd_two, gain_second, grad_norm_two, model_width
    )
    grad_stream_one = cotangent.astype(jnp.float32) + back_two
    grad_att = gather_rows(grad_stream_one.astype(jnp.bfloat16))
    grad_out = gram_dot(context, grad_att)
    grad_context = times_t(grad_att, out_weight).astype(jnp.bfloat16).reshape(block_shape)
    attn_probs = jnp.exp(attend_scores(query_part, key_part, allowed, score_scale) - log_total)
    probs_low = attn_probs.astype(jnp.bfloat16)
    grad_probs = jnp.einsum(
        "bqhd,bkhd->bhqk", grad_context, value_part, preferred_element_type=jnp.float32
    )
    inner_row = jnp.sum(attn_probs * grad_probs, axis=-1, keepdims=True)
    grad_scores = (attn_probs * (grad_probs - inner_row)).astype(jnp.bfloat16)
    grad_query = (
        jnp.einsum("bhqk,bkhd->bqhd", grad_scores, key_part, preferred_element_type=jnp.float32)
        * score_scale
    ).astype(jnp.bfloat16)
    grad_keys = (
        jnp.einsum("bhqk,bqhd->bkhd", grad_scores, query_part, preferred_element_type=jnp.float32)
        * score_scale
    ).astype(jnp.bfloat16)
    grad_values = jnp.einsum(
        "bhqk,bqhd->bkhd", probs_low, grad_context, preferred_element_type=jnp.float32
    ).astype(jnp.bfloat16)
    grad_rows = jnp.stack(
        [
            grad_query.reshape(tokens, local_width),
            grad_keys.reshape(tokens, local_width),
            grad_values.reshape(tokens, local_width),
        ],
        axis=1,
    )
    grad_qkv = jnp.einsum("td,tje->dje", norm_one, grad_rows, preferred_element_type=jnp.float32)
    grad_norm_one = share_rows(
        jnp.einsum("tje,dje->td", grad_rows, qkv_weight, preferred_element_type=jnp.float32)
    )
    back_one, grad_gain_one, grad_shift_one = norm_backward(
        normed_one, rstd_one, gain_first, grad_norm_one, model_width
    )
    input_grad = (grad_stream_one + back_one).astype(jnp.bfloat16)
    grad_up_rows = gather_rows(input_grad).reshape(coarse_length, 4 * model_width)
    grad_up = gram_dot(hidden_cond, grad_up_rows)
    grad_hidden = times_t(grad_up_rows, up_weight)
    grad_res_low = grad_hidden.astype(jnp.bfloat16)
    grad_res = gram_dot(mixed_act, grad_res_low)
    grad_mixed = lax.psum(times_t(grad_res_low, res_weight).astype(jnp.bfloat16), "cond").astype(
        jnp.float32
    )
    grad_conv_low = gelu_back(conv_out, grad_mixed).astype(jnp.bfloat16)
    grad_conv = gram_dot(kernel_tap_rows, grad_conv_low).reshape(3, quarter, model_width)
    grad_taps = times_t(grad_conv_low, conv_flat)
    grad_padded = jnp.pad(grad_taps[:, 0:quarter], ((0, 2 * dilation_step), (0, 0)))
    grad_padded = grad_padded + jnp.pad(
        grad_taps[:, quarter : 2 * quarter], ((dilation_step, dilation_step), (0, 0))
    )
    grad_padded = grad_padded + jnp.pad(
        grad_taps[:, 2 * quarter :], ((2 * dilation_step, 0), (0, 0))
    )
    rim_grads = jnp.concatenate(
        [grad_padded[:dilation_step], grad_padded[coarse_length + dilation_step :]], axis=0
    )
    rim_values = extended(rim_grads.astype(jnp.bfloat16), (("seq", 0),), dilation_step).astype(
        rim_grads.dtype
    )
    grad_act = grad_padded[dilation_step : dilation_step + coarse_length]
    grad_act = grad_act + jnp.pad(
        rim_values[:dilation_step], ((0, coarse_length - dilation_step), (0, 0))
    )
    grad_act = grad_act + jnp.pad(
        rim_values[3 * dilation_step :], ((coarse_length - dilation_step, 0), (0, 0))
    )
    grad_embed = (grad_hidden + gelu_back(embed, grad_act)).astype(jnp.bfloat16)
    grad_table = gram_dot(onehot, grad_embed)
    gradients = (
        grad_table,
        grad_conv,
        grad_res,
        grad_up,
        grad_gain_one,
        grad_shift_one,
        grad_qkv,
        grad_out,
        grad_gain_two,
        grad_shift_two,
        grad_in,
        grad_down,
    )
    return (result, input_grad, gradients)


def on_device(
    inputs,
    coarse_ids,
    segment_ids,
    cotangent,
    embed_table,
    conv_weight,
    res_weight,
    up_weight,
    gain_one,
    shift_one,
    qkv_weight,
    out_weight,
    gain_two,
    shift_two,
    in_weight,
    down_weight,
):
    shards = (
        embed_table,
        conv_weight,
        res_weight,
        up_weight,
        gain_one,
        shift_one,
        qkv_weight,
        out_weight,
        gain_two,
        shift_two,
        in_weight,
        down_weight,
    )
    outputs = []
    in_grads = []
    summed = None
    for index in range(inputs.shape[0]):
        full = fetch_weights(shards)
        result, input_grad, gradients = one_micro(
            inputs[index], coarse_ids[index], segment_ids[index], cotangent[index], full
        )
        outputs.append(result)
        in_grads.append(input_grad)
        shares = spread_grads(gradients)
        summed = shares if summed is None else jax.tree.map(jnp.add, summed, shares)
    return (jnp.stack(outputs), jnp.stack(in_grads)) + tuple(summed)


def solution(mesh):
    return jax.shard_map(
        on_device,
        mesh=mesh,
        in_specs=(
            P(None, "seq", "cond"),
            P(None, "seq"),
            P(None, "seq"),
            P(None, "seq", "cond"),
            P("seq", "cond"),
            P(None, "cond", "seq"),
            P("seq", "cond"),
            P("cond", "seq"),
            P(("cond", "seq")),
            P(("cond", "seq")),
            P("seq", None, "cond"),
            P("cond", "seq"),
            P(("cond", "seq")),
            P(("cond", "seq")),
            P("seq", "cond"),
            P("cond", "seq"),
        ),
        out_specs=(
            P(None, "seq", "cond"),
            P(None, "seq", "cond"),
            P("seq", "cond"),
            P(None, "cond", "seq"),
            P("seq", "cond"),
            P("cond", "seq"),
            P(("cond", "seq")),
            P(("cond", "seq")),
            P("seq", None, "cond"),
            P("cond", "seq"),
            P(("cond", "seq")),
            P(("cond", "seq")),
            P("seq", "cond"),
            P("cond", "seq"),
        ),
        check_vma=False,
    )
```

profile of v0, /device:TPU:0, one launch (start us, length us, event | category | flops | bytes accessed | tf_op | source)
XLA Modules:
  0.0 3656.3 jit_solution(12000477826808269472)
XLA Ops:
  9.6 43.4 %all-gather.31.cloned.1.call-done = bf16[2048,256]{1,0:T(8,128)(2,1)} async-done(((bf16[256,256]{1,0:T(8,128)(2,1)}), bf16[2048,256]{1,0:T(8,128)(2,1)}) %all-gather.31.cloned.1.call-update) | async-done | bytes 1048592 | tf_op jit(solution)/shard_map/all_gather | solution.py:57
  77.3 22.3 all-gather.33.cloned.1.call-done
  111.0 31.5 all_gather.66
  142.5 19.0 all-reduce.51.cloned.1.call-done
  166.6 48.3 %all-gather.35.cloned.1.call-done = bf16[256,4096]{1,0:T(8,128)(2,1)} async-done(((bf16[256,512]{1,0:T(8,128)(2,1)}), bf16[256,4096]{1,0:T(8,128)(2,1)}) %all-gather.35.cloned.1.call-update) | async-done | bytes 2097168 | tf_op jit(solution)/shard_map/all_gather | solution.py:60
  246.0 18.9 all-reduce.46
  265.0 17.2 reduce-scatter.83.cloned.1.call-done
  282.2 34.2 reduce-scatter.89.cloned.1.call-done
  316.4 34.0 reduce-scatter.95.cloned.1.call-done
  366.3 29.8 all_gather.140
  402.3 17.5 all-gather.55.cloned.1.call-done
  491.8 19.1 reduce-scatter.97.cloned.1.call-done
  512.8 31.9 reduce-scatter.91.cloned.1.call-done
  546.0 32.8 reduce-scatter.85.cloned.1.call-done
  580.0 32.6 reduce-scatter.79.cloned.1.call-done
  633.8 30.3 all-gather.43.cloned.1.call-done
  664.1 17.6 all-gather.57.cloned.1.call-done
  700.0 53.4 %all-gather.45.cloned.1.call-done = bf16[1024,1024]{1,0:T(8,128)(2,1)} async-done(((bf16[1024,128]{1,0:T(8,128)(2,1)}), bf16[1024,1024]{1,0:T(8,128)(2,1)}) %all-gather.45.cloned.1.call-update) | async-done | bytes 2097168 | tf_op jit(solution)/shard_map/all_gather | solution.py:68
  898.1 34.0 reduce-scatter.109.cloned.1.call-done
  932.1 34.0 reduce-scatter.105.cloned.1.call-done
  966.1 34.0 reduce-scatter.101.cloned.1.call-done
  1013.4 20.9 reduce-scatter.99.cloned.1.call-done
  1034.3 33.8 reduce-scatter.81.cloned.1.call-done
  1071.9 30.4 reduce-scatter.93.cloned.1.call-done
  1102.3 34.0 reduce-scatter.87.cloned.1.call-done
  1140.2 15.0 all-gather.65.cloned.1.call-done
  1222.2 23.0 reduce-scatter.115.cloned.1.call-done
  1245.2 34.0 reduce-scatter.103.cloned.1.call-done
  1279.2 34.2 reduce-scatter.111.cloned.1.call-done
  1313.4 33.8 reduce-scatter.107.cloned.1.call-done
  1384.0 15.9 all-gather.71.cloned.1.call-done
  1402.4 16.4 all-gather.67.cloned.1.call-done
  1601.5 19.8 reduce-scatter.177.cloned.1.call-done
  1622.4 69.0 %reduce-scatter.175.cloned.1.call-done = bf16[128,1024]{1,0:T(8,128)(2,1)} async-done(((bf16[1024,1024]{1,0:T(8,128)(2,1)}), bf16[128,1024]{1,0:T(8,128)(2,1)}) %reduce-scatter.175.cloned.1.call-update) | async-done | bytes 262160
  1692.5 69.1 %reduce-scatter.173.cloned.1.call-done = bf16[128,1024]{1,0:T(8,128)(2,1)} async-done(((bf16[1024,1024]{1,0:T(8,128)(2,1)}), bf16[128,1024]{1,0:T(8,128)(2,1)}) %reduce-scatter.173.cloned.1.call-update) | async-done | bytes 262160
  1764.9 66.7 %reduce-scatter.155.cloned.1.call-done = bf16[128,1024]{1,0:T(8,128)(2,1)} async-done(((bf16[1024,1024]{1,0:T(8,128)(2,1)}), bf16[128,1024]{1,0:T(8,128)(2,1)}) %reduce-scatter.155.cloned.1.call-update) | async-done | bytes 262160 | tf_op jit(solution)/shard_map/reduce_scatter | solution.py:104
  1831.7 70.3 %reduce-scatter.153.cloned.1.call-done = bf16[128,1024]{1,0:T(8,128)(2,1)} async-done(((bf16[1024,1024]{1,0:T(8,128)(2,1)}), bf16[128,1024]{1,0:T(8,128)(2,1)}) %reduce-scatter.153.cloned.1.call-update) | async-done | bytes 262160 | tf_op jit(solution)/shard_map/reduce_scatter | solution.py:104
  1902.0 70.2 %reduce-scatter.151.cloned.1.call-done = bf16[128,1024]{1,0:T(8,128)(2,1)} async-done(((bf16[1024,1024]{1,0:T(8,128)(2,1)}), bf16[128,1024]{1,0:T(8,128)(2,1)}) %reduce-scatter.151.cloned.1.call-update) | async-done | bytes 262160 | tf_op jit(solution)/shard_map/reduce_scatter | solution.py:104
  1972.2 70.2 %reduce-scatter.149.cloned.1.call-done = bf16[128,1024]{1,0:T(8,128)(2,1)} async-done(((bf16[1024,1024]{1,0:T(8,128)(2,1)}), bf16[128,1024]{1,0:T(8,128)(2,1)}) %reduce-scatter.149.cloned.1.call-update) | async-done | bytes 262160 | tf_op jit(solution)/shard_map/reduce_scatter | solution.py:104
  2044.6 62.7 %reduce-scatter.171.cloned.1.call-done = bf16[128,256]{1,0:T(8,128)(2,1)} async-done(((bf16[1024,256]{1,0:T(8,128)(2,1)}), bf16[128,256]{1,0:T(8,128)(2,1)}) %reduce-scatter.171.cloned.1.call-update) | async-done | bytes 65552
  2108.2 63.6 %reduce-scatter.165.cloned.1.call-done = bf16[128,256]{1,0:T(8,128)(2,1)} async-done(((bf16[1024,256]{1,0:T(8,128)(2,1)}), bf16[128,256]{1,0:T(8,128)(2,1)}) %reduce-scatter.165.cloned.1.call-update) | async-done | bytes 65552
  2172.8 63.1 %reduce-scatter.169.cloned.1.call-done = bf16[128,256]{1,0:T(8,128)(2,1)} async-done(((bf16[1024,256]{1,0:T(8,128)(2,1)}), bf16[128,256]{1,0:T(8,128)(2,1)}) %reduce-scatter.169.cloned.1.call-update) | async-done | bytes 65552
  2236.8 63.8 %reduce-scatter.167.cloned.1.call-done = bf16[128,256]{1,0:T(8,128)(2,1)} async-done(((bf16[1024,256]{1,0:T(8,128)(2,1)}), bf16[128,256]{1,0:T(8,128)(2,1)}) %reduce-scatter.167.cloned.1.call-update) | async-done | bytes 65552
  2302.3 66.3 %reduce-scatter.145.cloned.1.call-done = bf16[128,3,256]{2,0,1:T(8,128)(2,1)} async-done(((bf16[1024,3,256]{2,0,1:T(8,128)(2,1)}), bf16[128,3,256]{2,0,1:T(8,128)(2,1)}) %reduce-scatter.145.cloned.1.call-update) | async-done | bytes 196624 | tf_op jit(solution)/shard_map/reduce_scatter | solution.py:92
  2368.6 68.4 %reduce-scatter.143.cloned.1.call-done = bf16[128,3,256]{2,0,1:T(8,128)(2,1)} async-done(((bf16[1024,3,256]{2,0,1:T(8,128)(2,1)}), bf16[128,3,256]{2,0,1:T(8,128)(2,1)}) %reduce-scatter.143.cloned.1.call-update) | async-done | bytes 196624 | tf_op jit(solution)/shard_map/reduce_scatter | solution.py:92
  2437.0 67.8 %reduce-scatter.141.cloned.1.call-done = bf16[128,3,256]{2,0,1:T(8,128)(2,1)} async-done(((bf16[1024,3,256]{2,0,1:T(8,128)(2,1)}), bf16[128,3,256]{2,0,1:T(8,128)(2,1)}) %reduce-scatter.141.cloned.1.call-update) | async-done | bytes 196624 | tf_op jit(solution)/shard_map/reduce_scatter | solution.py:92
  2504.8 68.2 %reduce-scatter.147.cloned.1.call-done = bf16[128,3,256]{2,0,1:T(8,128)(2,1)} async-done(((bf16[1024,3,256]{2,0,1:T(8,128)(2,1)}), bf16[128,3,256]{2,0,1:T(8,128)(2,1)}) %reduce-scatter.147.cloned.1.call-update) | async-done | bytes 196624 | tf_op jit(solution)/shard_map/reduce_scatter | solution.py:92
  2575.2 19.8 all-reduce.45
  2598.5 38.8 %reduce-scatter.127.cloned.1.call-done = bf16[128,256]{1,0:T(8,128)(2,1)} async-done(((bf16[1024,256]{1,0:T(8,128)(2,1)}), bf16[128,256]{1,0:T(8,128)(2,1)}) %reduce-scatter.127.cloned.1.call-update) | async-done | bytes 65552 | tf_op jit(solution)/shard_map/reduce_scatter | solution.py:80
  2637.3 64.5 %reduce-scatter.129.cloned.1.call-done = bf16[128,256]{1,0:T(8,128)(2,1)} async-done(((bf16[1024,256]{1,0:T(8,128)(2,1)}), bf16[128,256]{1,0:T(8,128)(2,1)}) %reduce-scatter.129.cloned.1.call-update) | async-done | bytes 65552 | tf_op jit(solution)/shard_map/reduce_scatter | solution.py:80
  2701.8 64.2 %reduce-scatter.125.cloned.1.call-done = bf16[128,256]{1,0:T(8,128)(2,1)} async-done(((bf16[1024,256]{1,0:T(8,128)(2,1)}), bf16[128,256]{1,0:T(8,128)(2,1)}) %reduce-scatter.125.cloned.1.call-update) | async-done | bytes 65552 | tf_op jit(solution)/shard_map/reduce_scatter | solution.py:80
  2765.9 64.7 %reduce-scatter.131.cloned.1.call-done = bf16[128,256]{1,0:T(8,128)(2,1)} async-done(((bf16[1024,256]{1,0:T(8,128)(2,1)}), bf16[128,256]{1,0:T(8,128)(2,1)}) %reduce-scatter.131.cloned.1.call-update) | async-done | bytes 65552 | tf_op jit(solution)/shard_map/reduce_scatter | solution.py:80
  2832.3 64.2 %reduce-scatter.117.cloned.1.call-done = bf16[256,256]{1,0:T(8,128)(2,1)} async-done(((bf16[2048,256]{1,0:T(8,128)(2,1)}), bf16[256,256]{1,0:T(8,128)(2,1)}) %reduce-scatter.117.cloned.1.call-update) | async-done | bytes 131088 | tf_op jit(solution)/shard_map/reduce_scatter | solution.py:74
  2896.5 66.2 %reduce-scatter.119.cloned.1.call-done = bf16[256,256]{1,0:T(8,128)(2,1)} async-done(((bf16[2048,256]{1,0:T(8,128)(2,1)}), bf16[256,256]{1,0:T(8,128)(2,1)}) %reduce-scatter.119.cloned.1.call-update) | async-done | bytes 131088 | tf_op jit(solution)/shard_map/reduce_scatter | solution.py:74
  2962.6 65.8 %reduce-scatter.121.cloned.1.call-done = bf16[256,256]{1,0:T(8,128)(2,1)} async-done(((bf16[2048,256]{1,0:T(8,128)(2,1)}), bf16[256,256]{1,0:T(8,128)(2,1)}) %reduce-scatter.121.cloned.1.call-update) | async-done | bytes 131088 | tf_op jit(solution)/shard_map/reduce_scatter | solution.py:74
  3028.4 66.0 %reduce-scatter.123.cloned.1.call-done = bf16[256,256]{1,0:T(8,128)(2,1)} async-done(((bf16[2048,256]{1,0:T(8,128)(2,1)}), bf16[256,256]{1,0:T(8,128)(2,1)}) %reduce-scatter.123.cloned.1.call-update) | async-done | bytes 131088 | tf_op jit(solution)/shard_map/reduce_scatter | solution.py:74
  3096.3 65.2 %reduce-scatter.157.cloned.1.call-done = bf16[128,768]{1,0:T(8,128)(2,1)} async-done(((bf16[1024,768]{1,0:T(8,128)(2,1)}), bf16[128,768]{1,0:T(8,128)(2,1)}) %reduce-scatter.157.cloned.1.call-update) | async-done | bytes 196624
  3162.7 66.2 %reduce-scatter.159.cloned.1.call-done = bf16[128,768]{1,0:T(8,128)(2,1)} async-done(((bf16[1024,768]{1,0:T(8,128)(2,1)}), bf16[128,768]{1,0:T(8,128)(2,1)}) %reduce-scatter.159.cloned.1.call-update) | async-done | bytes 196624
  3230.2 65.9 %reduce-scatter.161.cloned.1.call-done = bf16[128,768]{1,0:T(8,128)(2,1)} async-done(((bf16[1024,768]{1,0:T(8,128)(2,1)}), bf16[128,768]{1,0:T(8,128)(2,1)}) %reduce-scatter.161.cloned.1.call-update) | async-done | bytes 196624
  3297.3 66.3 %reduce-scatter.163.cloned.1.call-done = bf16[128,768]{1,0:T(8,128)(2,1)} async-done(((bf16[1024,768]{1,0:T(8,128)(2,1)}), bf16[128,768]{1,0:T(8,128)(2,1)}) %reduce-scatter.163.cloned.1.call-update) | async-done | bytes 196624
  3365.7 68.7 %reduce-scatter.135.cloned.1.call-done = bf16[256,512]{1,0:T(8,128)(2,1)} async-done(((bf16[256,4096]{1,0:T(8,128)(2,1)}), bf16[256,512]{1,0:T(8,128)(2,1)}) %reduce-scatter.135.cloned.1.call-update) | async-done | bytes 262160 | tf_op jit(solution)/shard_map/reduce_scatter | solution.py:83
  3434.4 70.8 %reduce-scatter.137.cloned.1.call-done = bf16[256,512]{1,0:T(8,128)(2,1)} async-done(((bf16[256,4096]{1,0:T(8,128)(2,1)}), bf16[256,512]{1,0:T(8,128)(2,1)}) %reduce-scatter.137.cloned.1.call-update) | async-done | bytes 262160 | tf_op jit(solution)/shard_map/reduce_scatter | solution.py:83
  3505.2 71.0 %reduce-scatter.133.cloned.1.call-done = bf16[256,512]{1,0:T(8,128)(2,1)} async-done(((bf16[256,4096]{1,0:T(8,128)(2,1)}), bf16[256,512]{1,0:T(8,128)(2,1)}) %reduce-scatter.133.cloned.1.call-update) | async-done | bytes 262160 | tf_op jit(solution)/shard_map/reduce_scatter | solution.py:83
  3576.2 70.8 %reduce-scatter.139.cloned.1.call-done = bf16[256,512]{1,0:T(8,128)(2,1)} async-done(((bf16[256,4096]{1,0:T(8,128)(2,1)}), bf16[256,512]{1,0:T(8,128)(2,1)}) %reduce-scatter.139.cloned.1.call-update) | async-done | bytes 262160 | tf_op jit(solution)/shard_map/reduce_scatter | solution.py:83
  (987 shorter events, 690.2 us)
Async XLA Ops:
  8.7 152.9 %all-reduce.51.cloned.1.call-start = ((), (), s32[]{:S(2)}) async-start(), calls=%async_computation.130 | async-start | bytes 4194304 | tf_op jit(solution)/shard_map/psum | solution.py:184
  111.0 154.0 %reduce-scatter.77.cloned.1.call-start = ((), (), s32[]{:S(2)}) async-start(), calls=%async_computation.55 | async-start | bytes 2621440 | tf_op jit(solution)/shard_map/reduce_scatter | solution.py:118
  237.2 113.1 %reduce-scatter.95.cloned.1.call-start = ((), (), s32[]{:S(2)}) async-start(), calls=%async_computation.73 | async-start | bytes 2621440 | tf_op jit(solution)/shard_map/reduce_scatter | solution.py:118
  242.9 159.4 %all-gather.39.cloned.1.call-start = ((), (), s32[]{:S(2)}) async-start(), calls=%async_computation.57 | async-start | bytes 1769472 | tf_op jit(solution)/shard_map/all_gather | solution.py:63
  243.7 176.1 %all-gather.55.cloned.1.call-start = ((), (), s32[]{:S(2)}) async-start(), calls=%async_computation.74 | async-start | bytes 1310720 | tf_op jit(solution)/shard_map/all_gather | solution.py:114
  365.9 111.0 %all-gather.37.cloned.1.call-start = ((), (), s32[]{:S(2)}) async-start(), calls=%async_computation.56 | async-start | bytes 1310720 | tf_op jit(solution)/shard_map/all_gather | solution.py:114
  397.2 113.7 %reduce-scatter.97.cloned.1.call-start = ((), (), s32[]{:S(2)}) async-start(), calls=%async_computation.75 | async-start | bytes 2621440 | tf_op jit(solution)/shard_map/reduce_scatter | solution.py:118
  455.1 123.7 %reduce-scatter.85.cloned.1.call-start = ((), (), s32[]{:S(2)}) async-start(), calls=%async_computation.65 | async-start | bytes 2621440 | tf_op jit(solution)/shard_map/reduce_scatter | solution.py:118
  474.1 138.5 %reduce-scatter.79.cloned.1.call-start = ((), (), s32[]{:S(2)}) async-start(), calls=%async_computation.58 | async-start | bytes 2621440 | tf_op jit(solution)/shard_map/reduce_scatter | solution.py:118
  491.2 172.9 %all-gather.43.cloned.1.call-start = ((), (), s32[]{:S(2)}) async-start(), calls=%async_computation.60 | async-start | bytes 2359296 | tf_op jit(solution)/shard_map/all_gather | solution.py:67
  491.8 189.9 %all-gather.57.cloned.1.call-start = ((), (), s32[]{:S(2)}) async-start(), calls=%async_computation.76 | async-start | bytes 1310720 | tf_op jit(solution)/shard_map/all_gather | solution.py:114
  628.9 124.5 %all-gather.45.cloned.1.call-start = ((), (), s32[]{:S(2)}) async-start(), calls=%async_computation.61 | async-start | bytes 2359296 | tf_op jit(solution)/shard_map/all_gather | solution.py:68
  629.6 141.0 %all-gather.53.cloned.1.call-start = ((), (), s32[]{:S(2)}) async-start(), calls=%async_computation.71 | async-start | bytes 1310720 | tf_op jit(solution)/shard_map/all_gather | solution.py:114
  630.4 158.8 %all-gather.79.cloned.1.call-start = ((), (), s32[]{:S(2)}) async-start(), calls=%async_computation.116 | async-start | bytes 1310720 | tf_op jit(solution)/shard_map/all_gather | solution.py:114
  631.1 177.0 %all-gather.49.cloned.1.call-start = ((), (), s32[]{:S(2)}) async-start(), calls=%async_computation.66 | async-start | bytes 1310720 | tf_op jit(solution)/shard_map/all_gather | solution.py:114
  631.7 194.9 %all-gather.77.cloned.1.call-start = ((), (), s32[]{:S(2)}) async-start(), calls=%async_computation.115 | async-start | bytes 1310720 | tf_op jit(solution)/shard_map/all_gather | solution.py:114
  632.4 213.1 %all-gather.41.cloned.1.call-start = ((), (), s32[]{:S(2)}) async-start(), calls=%async_computation.59 | async-start | bytes 1310720 | tf_op jit(solution)/shard_map/all_gather | solution.py:114
  633.0 230.9 %all-gather.75.cloned.1.call-start = ((), (), s32[]{:S(2)}) async-start(), calls=%async_computation.114 | async-start | bytes 1310720 | tf_op jit(solution)/shard_map/all_gather | solution.py:114
  633.6 264.5 %reduce-scatter.113.cloned.1.call-start = ((), (), s32[]{:S(2)}) async-start(), calls=%async_computation.87 | async-start | bytes 2621440 | tf_op jit(solution)/shard_map/reduce_scatter | solution.py:118
  762.1 170.0 %reduce-scatter.109.cloned.1.call-start = ((), (), s32[]{:S(2)}) async-start(), calls=%async_computation.84 | async-start | bytes 2621440 | tf_op jit(solution)/shard_map/reduce_scatter | solution.py:118
  798.0 168.1 %reduce-scatter.105.cloned.1.call-start = ((), (), s32[]{:S(2)}) async-start(), calls=%async_computation.81 | async-start | bytes 2621440 | tf_op jit(solution)/shard_map/reduce_scatter | solution.py:118
  835.4 164.7 %reduce-scatter.101.cloned.1.call-start = ((), (), s32[]{:S(2)}) async-start(), calls=%async_computation.78 | async-start | bytes 2621440 | tf_op jit(solution)/shard_map/reduce_scatter | solution.py:118
  872.6 161.7 %reduce-scatter.99.cloned.1.call-start = ((), (), s32[]{:S(2)}) async-start(), calls=%async_computation.77 | async-start | bytes 2621440 | tf_op jit(solution)/shard_map/reduce_scatter | solution.py:118
  877.5 190.6 %reduce-scatter.81.cloned.1.call-start = ((), (), s32[]{:S(2)}) async-start(), calls=%async_computation.62 | async-start | bytes 2621440 | tf_op jit(solution)/shard_map/reduce_scatter | solution.py:118
  882.5 219.8 %reduce-scatter.93.cloned.1.call-start = ((), (), s32[]{:S(2)}) async-start(), calls=%async_computation.72 | async-start | bytes 2621440 | tf_op jit(solution)/shard_map/reduce_scatter | solution.py:118
  887.5 248.8 %reduce-scatter.87.cloned.1.call-start = ((), (), s32[]{:S(2)}) async-start(), calls=%async_computation.67 | async-start | bytes 2621440 | tf_op jit(solution)/shard_map/reduce_scatter | solution.py:118
  892.0 263.2 %all-gather.65.cloned.1.call-start = ((), (), s32[]{:S(2)}) async-start(), calls=%async_computation.88 | async-start | bytes 1310720 | tf_op jit(solution)/shard_map/all_gather | solution.py:114
  1071.8 120.8 %all-gather.63.cloned.1.call-start = ((), (), s32[]{:S(2)}) async-start(), calls=%async_computation.85 | async-start | bytes 1310720 | tf_op jit(solution)/shard_map/all_gather | solution.py:114
  1191.4 121.9 %reduce-scatter.111.cloned.1.call-start = ((), (), s32[]{:S(2)}) async-start(), calls=%async_computation.86 | async-start | bytes 2621440 | tf_op jit(solution)/shard_map/reduce_scatter | solution.py:118
  1206.4 140.8 %reduce-scatter.107.cloned.1.call-start = ((), (), s32[]{:S(2)}) async-start(), calls=%async_computation.83 | async-start | bytes 2621440 | tf_op jit(solution)/shard_map/reduce_scatter | solution.py:118
  1222.2 159.4 %all-gather.69.cloned.1.call-start = ((), (), s32[]{:S(2)}) async-start(), calls=%async_computation.92 | async-start | bytes 1310720 | tf_op jit(solution)/shard_map/all_gather | solution.py:114
  1367.3 143.5 %all-reduce.53.cloned.1.call-start = ((), (), s32[]{:S(2)}) async-start(), calls=%async_computation.131 | async-start | bytes 2097152 | tf_op jit(solution)/shard_map/psum | solution.py:290
  1442.8 157.6 %reduce-scatter.179.cloned.1.call-start = ((), (), s32[]{:S(2)}) async-start(), calls=%async_computation.129 | async-start | bytes 2359296
  1448.2 173.0 %reduce-scatter.177.cloned.1.call-start = ((), (), s32[]{:S(2)}) async-start(), calls=%async_computation.128 | async-start | bytes 2359296
  1454.6 236.8 %reduce-scatter.175.cloned.1.call-start = ((), (), s32[]{:S(2)}) async-start(), calls=%async_computation.127 | async-start | bytes 2359296
  1460.9 300.7 %reduce-scatter.173.cloned.1.call-start = ((), (), s32[]{:S(2)}) async-start(), calls=%async_computation.126 | async-start | bytes 2359296
  1467.2 364.4 %reduce-scatter.155.cloned.1.call-start = ((), (), s32[]{:S(2)}) async-start(), calls=%async_computation.113 | async-start | bytes 2359296 | tf_op jit(solution)/shard_map/reduce_scatter | solution.py:104
  1471.5 430.4 %reduce-scatter.153.cloned.1.call-start = ((), (), s32[]{:S(2)}) async-start(), calls=%async_computation.112 | async-start | bytes 2359296 | tf_op jit(solution)/shard_map/reduce_scatter | solution.py:104
  1475.7 496.5 %reduce-scatter.151.cloned.1.call-start = ((), (), s32[]{:S(2)}) async-start(), calls=%async_computation.111 | async-start | bytes 2359296 | tf_op jit(solution)/shard_map/reduce_scatter | solution.py:104
  1479.8 562.6 %reduce-scatter.149.cloned.1.call-start = ((), (), s32[]{:S(2)}) async-start(), calls=%async_computation.110 | async-start | bytes 2359296 | tf_op jit(solution)/shard_map/reduce_scatter | solution.py:104
  1484.0 623.3 %reduce-scatter.171.cloned.1.call-start = ((), (), s32[]{:S(2)}) async-start(), calls=%async_computation.125 | async-start | bytes 589824
  1486.8 685.0 %reduce-scatter.165.cloned.1.call-start = ((), (), s32[]{:S(2)}) async-start(), calls=%async_computation.122 | async-start | bytes 589824
  1488.3 747.6 %reduce-scatter.169.cloned.1.call-start = ((), (), s32[]{:S(2)}) async-start(), calls=%async_computation.124 | async-start | bytes 589824
  1489.9 810.7 %reduce-scatter.167.cloned.1.call-start = ((), (), s32[]{:S(2)}) async-start(), calls=%async_computation.123 | async-start | bytes 589824
  1491.5 877.1 %reduce-scatter.145.cloned.1.call-start = ((), (), s32[]{:S(2)}) async-start(), calls=%async_computation.108 | async-start | bytes 1769472 | tf_op jit(solution)/shard_map/reduce_scatter | solution.py:92
  1495.0 941.9 %reduce-scatter.143.cloned.1.call-start = ((), (), s32[]{:S(2)}) async-start(), calls=%async_computation.107 | async-start | bytes 1769472 | tf_op jit(solution)/shard_map/reduce_scatter | solution.py:92
  1498.6 1006.1 %reduce-scatter.141.cloned.1.call-start = ((), (), s32[]{:S(2)}) async-start(), calls=%async_computation.106 | async-start | bytes 1769472 | tf_op jit(solution)/shard_map/reduce_scatter | solution.py:92
  1502.3 1070.8 %reduce-scatter.147.cloned.1.call-start = ((), (), s32[]{:S(2)}) async-start(), calls=%async_computation.109 | async-start | bytes 1769472 | tf_op jit(solution)/shard_map/reduce_scatter | solution.py:92
  1504.6 1132.7 %reduce-scatter.127.cloned.1.call-start = ((), (), s32[]{:S(2)}) async-start(), calls=%async_computation.99 | async-start | bytes 589824 | tf_op jit(solution)/shard_map/reduce_scatter | solution.py:80
  1505.8 1196.0 %reduce-scatter.129.cloned.1.call-start = ((), (), s32[]{:S(2)}) async-start(), calls=%async_computation.100 | async-start | bytes 589824 | tf_op jit(solution)/shard_map/reduce_scatter | solution.py:80
  1507.0 1258.9 %reduce-scatter.125.cloned.1.call-start = ((), (), s32[]{:S(2)}) async-start(), calls=%async_computation.98 | async-start | bytes 589824 | tf_op jit(solution)/shard_map/reduce_scatter | solution.py:80
  1509.3 1321.4 %reduce-scatter.131.cloned.1.call-start = ((), (), s32[]{:S(2)}) async-start(), calls=%async_computation.101 | async-start | bytes 589824 | tf_op jit(solution)/shard_map/reduce_scatter | solution.py:80
  1510.7 1385.8 %reduce-scatter.117.cloned.1.call-start = ((), (), s32[]{:S(2)}) async-start(), calls=%async_computation.91 | async-start | bytes 1179648 | tf_op jit(solution)/shard_map/reduce_scatter | solution.py:74
  1523.7 1438.9 %reduce-scatter.119.cloned.1.call-start = ((), (), s32[]{:S(2)}) async-start(), calls=%async_computation.93 | async-start | bytes 1179648 | tf_op jit(solution)/shard_map/reduce_scatter | solution.py:74
  1537.6 1490.9 %reduce-scatter.121.cloned.1.call-start = ((), (), s32[]{:S(2)}) async-start(), calls=%async_computation.95 | async-start | bytes 1179648 | tf_op jit(solution)/shard_map/reduce_scatter | solution.py:74
  1550.6 1543.8 %reduce-scatter.123.cloned.1.call-start = ((), (), s32[]{:S(2)}) async-start(), calls=%async_computation.97 | async-start | bytes 1179648 | tf_op jit(solution)/shard_map/reduce_scatter | solution.py:74
  1564.9 1596.6 %reduce-scatter.157.cloned.1.call-start = ((), (), s32[]{:S(2)}) async-start(), calls=%async_computation.118 | async-start | bytes 1769472
  1571.3 1657.6 %reduce-scatter.159.cloned.1.call-start = ((), (), s32[]{:S(2)}) async-start(), calls=%async_computation.119 | async-start | bytes 1769472
  1577.7 1718.4 %reduce-scatter.161.cloned.1.call-start = ((), (), s32[]{:S(2)}) async-start(), calls=%async_computation.120 | async-start | bytes 1769472
  1584.1 1779.5 %reduce-scatter.163.cloned.1.call-start = ((), (), s32[]{:S(2)}) async-start(), calls=%async_computation.121 | async-start | bytes 1769472
  1590.6 1843.8 %reduce-scatter.135.cloned.1.call-start = ((), (), s32[]{:S(2)}) async-start(), calls=%async_computation.103 | async-start | bytes 2359296 | tf_op jit(solution)/shard_map/reduce_scatter | solution.py:83
  1593.0 1912.2 %reduce-scatter.137.cloned.1.call-start = ((), (), s32[]{:S(2)}) async-start(), calls=%async_computation.104 | async-start | bytes 2359296 | tf_op jit(solution)/shard_map/reduce_scatter | solution.py:83
  1595.2 1980.9 %reduce-scatter.133.cloned.1.call-start = ((), (), s32[]{:S(2)}) async-start(), calls=%async_computation.102 | async-start | bytes 2359296 | tf_op jit(solution)/shard_map/reduce_scatter | solution.py:83
  1597.4 2049.5 %reduce-scatter.139.cloned.1.call-start = ((), (), s32[]{:S(2)}) async-start(), calls=%async_computation.105 | async-start | bytes 2359296 | tf_op jit(solution)/shard_map/reduce_scatter | solution.py:83
  (250 other events, 20175.1 us)
Sparse Core Ops, SparseCore 0:
  10.1 42.8 all-gather.30
  55.1 44.4 all-gather.32
  110.5 51.0 all-reduce.50
  163.7 51.1 all-gather.34
  218.7 29.6 reduce-scatter.76
  250.7 31.4 reduce-scatter.82
  284.9 31.4 reduce-scatter.88
  318.9 31.4 reduce-scatter.94
  352.8 49.4 all-gather.38
  479.4 31.4 reduce-scatter.96
  513.3 31.4 reduce-scatter.90
  547.3 31.4 reduce-scatter.84
  581.1 31.4 reduce-scatter.78
  614.8 49.2 all-gather.42
  702.3 51.0 all-gather.44
  809.7 16.8 all-gather.76
  866.6 31.4 reduce-scatter.112
  900.6 31.4 reduce-scatter.108
  934.6 31.4 reduce-scatter.104
  968.6 31.4 reduce-scatter.100
  1002.8 31.4 reduce-scatter.98
  1036.6 31.4 reduce-scatter.80
  1070.8 31.4 reduce-scatter.92
  1104.8 31.4 reduce-scatter.86
  1138.3 16.8 all-gather.64
  1213.7 31.4 reduce-scatter.114
  1247.7 31.4 reduce-scatter.102
  1281.9 31.4 reduce-scatter.110
  1315.7 31.4 reduce-scatter.106
  1363.6 17.8 all-gather.68
  1420.3 16.8 all-gather.72
  1442.9 36.5 all-reduce.52
  1482.8 68.3 reduce-scatter.178
  1554.7 66.5 reduce-scatter.176
  1624.7 66.6 reduce-scatter.174
  1694.9 66.6 reduce-scatter.172
  1765.0 66.6 reduce-scatter.154
  1835.2 66.7 reduce-scatter.152
  1905.5 66.6 reduce-scatter.150
  1975.7 66.6 reduce-scatter.148
  2046.3 60.8 reduce-scatter.170
  2110.8 60.9 reduce-scatter.164
  2175.0 60.8 reduce-scatter.168
  2239.6 61.0 reduce-scatter.166
  2304.1 64.4 reduce-scatter.144
  2372.5 64.4 reduce-scatter.142
  2440.3 64.4 reduce-scatter.140
  2508.5 64.5 reduce-scatter.146
  2576.4 60.8 reduce-scatter.126
  2640.8 60.9 reduce-scatter.128
  2705.0 60.9 reduce-scatter.124
  2769.6 60.9 reduce-scatter.130
  2834.1 62.3 reduce-scatter.116
  2900.1 62.4 reduce-scatter.118
  2966.1 62.3 reduce-scatter.120
  3032.1 62.3 reduce-scatter.122
  3097.7 63.7 reduce-scatter.156
  3165.2 63.7 reduce-scatter.158
  3232.4 63.7 reduce-scatter.160
  3299.8 63.7 reduce-scatter.162
  3367.1 67.2 reduce-scatter.134
  3438.0 67.1 reduce-scatter.136
  3508.7 67.3 reduce-scatter.132
  3579.7 67.1 reduce-scatter.138
  (16 shorter events, 263.8 us)
where the time goes:
time: 3670 us; the launch traced here: 3660 us
  waiting for transfers between devices  2990 us (81%)
  matrix products  239 us (7%)
  local copies, waits for them, and re-layouts  152 us (4%)
  blocking collectives  141 us (4%)
  other arithmetic  64.4 us (2%)
  starting transfers between devices  47.6 us (1%)
    unnamed x92, waiting for transfers between devices  686 us
    reduce_scatter x20, waiting for transfers between devices, share_rows(): return lax.psum_scatter(value, 'cond', scatter_dimension=1, tiled=True)  554 us
    reduce_scatter x4, waiting for transfers between devices, spread_grads(): lax.psum_scatter(gradients[3].astype(jnp.bfloat16), 'seq', scatter_dimens...  281 us
    reduce_scatter x4, waiting for transfers between devices, spread_grads(): lax.psum_scatter(gradients[10].astype(jnp.bfloat16), 'seq', scatter_dimen...  278 us
    reduce_scatter x4, waiting for transfers between devices, spread_grads(): lax.psum_scatter(gradients[6].astype(jnp.bfloat16), 'seq', scatter_dimens...  271 us
    reduce_scatter x4, waiting for transfers between devices, spread_grads(): lax.psum_scatter(gradients[0].astype(jnp.bfloat16), 'seq', scatter_dimens...  262 us
    reduce_scatter x4, waiting for transfers between devices, spread_grads(): lax.psum_scatter(gradients[2].astype(jnp.bfloat16), 'seq', scatter_dimens...  232 us
    all_gather x20, waiting for transfers between devices, gather_rows(): return lax.all_gather(value, 'cond', axis=1, tiled=True)  185 us
  transfers between devices with their start and end apart: 96, of which 85 were waited for; matrix products, arithmetic and copies ran while one was open for 11% of the time, Pallas kernels for 0%

commit v1 on v0

v1 whole, which is shorter than its diff:
```python
import math

import jax
import jax.numpy as jnp
from jax import lax
from jax.experimental import pallas as pl
from jax.experimental.pallas import tpu as pltpu
from jax.sharding import PartitionSpec as P

HEAD = 64
ROW = 64
CONV_DILATION = 27
EPSILON = 1e-05
NEG_FILL = -1e30
LANES = 128
BF16 = jnp.bfloat16
F32 = jnp.float32


def tuned():
    return lax.axis_size("seq") == 8


def swap(x, j):
    return lax.ppermute(x, "cond", [(i, i ^ j) for i in range(4)])


def hop(x, k):
    return lax.ppermute(x, "seq", [(i, i ^ k) for i in range(8)])


def place():
    c = lax.axis_index("cond")
    if tuned():
        s = lax.axis_index("seq")
        return c, s >> 1, s & 1
    zero = jnp.zeros((), jnp.int32)
    return c, zero, zero


def dot(a, b, dims=((1,), (0,))):
    return lax.dot_general(a, b, (dims, ((), ())), preferred_element_type=F32)


def gram(a, b):
    return dot(a, b, ((0,), (0,)))


def dot_t(a, b):
    return dot(a, b, ((1,), (1,)))


def gelu(v):
    return 0.5 * v * (1.0 + lax.erf(v * math.sqrt(0.5)))


def gelu_grad(v):
    return 0.5 * (1.0 + lax.erf(v * math.sqrt(0.5))) + v * (
        math.sqrt(0.5 / math.pi) * jnp.exp(-0.5 * v * v)
    )


def pick(items, t):
    low, high = (t & 1) == 1, (t & 2) == 2
    items = [jnp.where(low, items[i ^ 1], items[i]) for i in range(4)]
    return [jnp.where(high, items[i ^ 2], items[i]) for i in range(4)]


def regroup(x, dim, outer, inner):
    n = x.shape[dim] // 8
    shape = x.shape
    x = x.reshape(shape[:dim] + (outer, inner, n) + shape[dim + 1 :])
    return jnp.swapaxes(x, dim, dim + 1).reshape(shape)


def gather(shard, dim):
    if tuned():
        near = jnp.concatenate([shard] + [hop(shard, 2 * k) for k in (1, 2, 3)], axis=dim)
        return jnp.concatenate([near, hop(near, 1)], axis=dim)
    return regroup(lax.all_gather(shard, "seq", axis=dim, tiled=True), dim, 4, 2)


def scatter(full, dim):
    full = full.astype(BF16)
    if tuned():
        near, far = jnp.split(full, 2, axis=dim)
        near = near.astype(F32) + hop(far, 1).astype(F32)
        parts = jnp.split(near, 4, axis=dim)
        total = parts[0]
        for k in (1, 2, 3):
            total = total + hop(parts[k].astype(BF16), 2 * k).astype(F32)
        return total
    return lax.psum_scatter(
        regroup(full, dim, 2, 4), "seq", scatter_dimension=dim, tiled=True
    ).astype(F32)


def spread(x):
    y = swap(x, 2)
    return [x, swap(x, 1), y, swap(y, 1)]


def exchange(items):
    return [items[0]] + [swap(items[j], j) for j in (1, 2, 3)]


def fold(items, wire=BF16, place_rows=None):
    fix = place_rows or (lambda x, j: x)
    one = fix(swap(items[1].astype(wire), 1), 1).astype(F32)
    three = fix(swap(items[3].astype(wire), 1), 1).astype(F32)
    zero = items[0].astype(F32) + one
    two = (items[2].astype(F32) + three).astype(BF16)
    return zero + fix(swap(two, 2), 2).astype(F32)


def copy_block(index_ref, in_ref, out_ref):
    out_ref[...] = in_ref[...]


def move_blocks(x, index):
    rows = x.shape[0]
    count = index.shape[0]
    return pl.pallas_call(
        copy_block,
        out_shape=jax.ShapeDtypeStruct((rows, count * LANES), x.dtype),
        grid_spec=pltpu.PrefetchScalarGridSpec(
            num_scalar_prefetch=1,
            grid=(count,),
            in_specs=[pl.BlockSpec((rows, LANES), lambda i, index: (0, index[i]))],
            out_specs=pl.BlockSpec((rows, LANES), lambda i, index: (0, i)),
        ),
        name="move_blocks",
    )(index, x)


def normalize(stream):
    mean = jnp.mean(stream, axis=1, keepdims=True)
    centred = stream - mean
    rstd = lax.rsqrt(jnp.mean(centred * centred, axis=1, keepdims=True) + EPSILON)
    return centred * rstd, rstd


def normalize_back(normed, rstd, gain, grad):
    scaled = grad * gain
    back = rstd * (
        scaled
        - jnp.mean(scaled, axis=1, keepdims=True)
        - normed * jnp.mean(scaled * normed, axis=1, keepdims=True)
    )
    return back, jnp.sum(grad * normed, axis=0), jnp.sum(grad, axis=0)


def vector_owner(c, z, x):
    i = jnp.arange(32)
    kx, kz, part = i >> 4, (i >> 2) & 3, i & 3
    j = kz ^ z ^ c
    source = ((kx ^ x) << 2) | part
    if tuned():
        piece = j * 8 + ((((source & 1) ^ x) << 2) | ((source >> 1) ^ z))
    else:
        piece = j * 8 + source
    return piece[:, None] == jnp.arange(32)[None, :]


def gather_vectors(vectors, c, z, x):
    pieces = lax.all_gather(vectors, "seq", axis=1, tiled=True) if not tuned() else gather(vectors, 1)
    pieces = jnp.stack(spread(pieces), axis=1)
    count, _, width = pieces.shape
    pieces = pieces.reshape(count, 32, width // 8)
    owner = vector_owner(c, z, x).astype(BF16)
    full = jnp.einsum("dp,vpn->vdn", owner, pieces, preferred_element_type=F32)
    return full.reshape(count, 4 * width)


def scatter_vectors(full, c, z, x):
    count, width = full.shape
    owner = vector_owner(c, z, x).astype(F32)
    pieces = jnp.einsum(
        "dp,vdn->vpn",
        owner,
        full.reshape(count, 32, width // 32),
        precision=lax.Precision.HIGHEST,
        preferred_element_type=F32,
    ).reshape(count, 4, width // 4)
    mine = fold([pieces[:, j] for j in range(4)], F32)
    if tuned():
        return scatter(mine, 1)
    return lax.psum_scatter(mine, "seq", scatter_dimension=1, tiled=True)


def attend(qkv, allowed):
    rows = qkv.shape[0] // ROW
    width = qkv.shape[1] // 3
    shape = (rows, ROW, width // HEAD, HEAD)
    query, key, value = (qkv[:, i * width : (i + 1) * width].reshape(shape) for i in range(3))
    scores = jnp.einsum("bqhd,bkhd->bhqk", query, key, preferred_element_type=F32) * (
        1.0 / math.sqrt(HEAD)
    )
    scores = jnp.where(allowed, scores, NEG_FILL)
    exps = jnp.exp(scores - jnp.max(scores, axis=-1, keepdims=True))
    probs = exps / jnp.sum(exps, axis=-1, keepdims=True)
    context = jnp.einsum("bhqk,bkhd->bqhd", probs.astype(BF16), value, preferred_element_type=F32)
    return context.astype(BF16).reshape(qkv.shape[0], width), probs


def attend_back(qkv, probs, grad_context):
    rows = qkv.shape[0] // ROW
    width = qkv.shape[1] // 3
    shape = (rows, ROW, width // HEAD, HEAD)
    query, key, value = (qkv[:, i * width : (i + 1) * width].reshape(shape) for i in range(3))
    scale = 1.0 / math.sqrt(HEAD)
    grad_context = grad_context.reshape(shape)
    grad_probs = jnp.einsum("bqhd,bkhd->bhqk", grad_context, value, preferred_element_type=F32)
    inner = jnp.sum(probs * grad_probs, axis=-1, keepdims=True)
    grad_scores = (probs * (grad_probs - inner)).astype(BF16)
    grads = (
        jnp.einsum("bhqk,bkhd->bqhd", grad_scores, key, preferred_element_type=F32) * scale,
        jnp.einsum("bhqk,bqhd->bkhd", grad_scores, query, preferred_element_type=F32) * scale,
        jnp.einsum("bhqk,bqhd->bkhd", probs.astype(BF16), grad_context, preferred_element_type=F32),
    )
    return jnp.concatenate(
        [g.astype(BF16).reshape(qkv.shape[0], width) for g in grads], axis=1
    )


def edges(cells):
    count = lax.axis_size("seq")
    head, tail = cells
    return (
        lax.ppermute(tail, "seq", [(i, i + 1) for i in range(count - 1)]),
        lax.ppermute(head, "seq", [(i + 1, i) for i in range(count - 1)]),
    )


def on_device(
    inputs,
    coarse_ids,
    segment_ids,
    cotangent,
    embed_table,
    conv_weight,
    res_weight,
    up_weight,
    gain_one,
    shift_one,
    qkv_weight,
    out_weight,
    gain_two,
    shift_two,
    in_weight,
    down_weight,
):
    c, z, x = place()
    turn = c ^ z
    micros, tokens, quarter = inputs.shape
    width = 4 * quarter
    coarse = coarse_ids.shape[1]
    half = width // 2
    step = CONV_DILATION
    slot = jnp.arange(8, dtype=jnp.int32)
    to_layer = (((slot & 3) ^ turn) << 1) | ((slot >> 2) ^ x)
    to_quarters = (((slot & 1) ^ x) << 2) | ((slot >> 1) ^ turn)

    table = gather(embed_table, 0)
    conv = gather(conv_weight.reshape(3 * quarter, -1), 1)
    res = spread(gather(res_weight, 0))
    up = spread(gather(up_weight, 1))
    vectors = gather_vectors(jnp.stack([gain_one, shift_one, gain_two, shift_two]), c, z, x)
    qkv_w = spread(gather(qkv_weight.reshape(-1, 3 * quarter), 0))
    out_w = spread(gather(out_weight, 1))
    in_w = gather(in_weight, 0)
    down_w = move_blocks(gather(down_weight, 1), to_quarters)
    gain1, shift1, gain2, shift2 = (vectors[i][None, :] for i in range(4))

    mine = pick([inputs[i] for i in range(4)], c)
    stream_in = move_blocks(jnp.concatenate(exchange(mine), axis=1), to_layer)
    cot = jnp.concatenate(pick([cotangent[i] for i in range(4)], c), axis=0)
    cots = [item.reshape(micros, tokens, quarter) for item in spread(cot)]
    cot_all = jnp.concatenate(
        [jnp.concatenate([cots[j][m ^ j] for m in range(4)], axis=0) for j in range(4)], axis=1
    )
    cot_mine = move_blocks(cot_all[:tokens], to_layer)

    ids = jnp.concatenate(pick([coarse_ids[i] for i in range(4)], c))
    vocab = table.shape[0]
    code = jnp.arange(vocab, dtype=jnp.int32)
    block = vocab // 8
    slot_of = code // block
    code = ((((slot_of & 3) ^ z) << 1) | ((slot_of >> 2) ^ x)) * block + code % block
    onehot = (ids[:, None] == code[None, :]).astype(BF16)
    embed = dot(onehot, table)
    act = gelu(embed).astype(BF16).reshape(micros, coarse, quarter)
    before, after = edges((act[:, :step], act[:, coarse - step :]))
    padded = jnp.concatenate([before, act, after], axis=1)
    taps = jnp.concatenate(
        [padded[:, k * step : k * step + coarse] for k in range(3)], axis=2
    ).reshape(micros * coarse, 3 * quarter)
    conv_terms = dot(taps, conv).reshape(micros, coarse, width)
    conv_out = fold([conv_terms[j] for j in range(4)])
    embeds = exchange([e for e in embed.astype(BF16).reshape(micros, coarse, quarter)])

    mixed = gelu(conv_out).astype(BF16)
    hidden = [(embeds[j].astype(F32) + dot(mixed, res[j])).astype(BF16) for j in range(4)]
    up_terms = dot(hidden[0], up[0])
    for j in (1, 2, 3):
        up_terms = up_terms + dot(hidden[j], up[j])
    phase_index = jnp.arange(32, dtype=jnp.int32)
    r, p = phase_index >> 3, phase_index & 7
    bz, bx = (p & 3) ^ z, (p >> 2) ^ x
    from_up = ((bz >> 1) ^ x) * 16 + (r ^ z) * 4 + ((bz & 1) << 1 | bx)
    i = phase_index
    kx, kz, w = i >> 4, (i >> 2) & 3, i & 3
    h = kx ^ x
    bz2, bx2 = (h << 1) | (w >> 1), w & 1
    to_up = (kz ^ z) * 8 + ((bx2 ^ x) << 2 | (bz2 ^ z))
    up_terms = move_blocks(up_terms, from_up).reshape(tokens, width)
    stream_zero = stream_in.astype(F32) + up_terms
    normed_one, rstd_one = normalize(stream_zero)
    norm_one = (normed_one * gain1 + shift1).astype(BF16)
    segments = lax.dynamic_index_in_dim(segment_ids, c, 0, keepdims=False)
    rows = segments.reshape(tokens // ROW, ROW)
    spots = jnp.arange(ROW)
    allowed = (
        (rows[:, :, None] == rows[:, None, :]) & (spots[:, None] >= spots[None, :])[None]
    )[:, None]
    qkv = [dot(norm_one, qkv_w[j]).astype(BF16) for j in range(4)]
    context, probs = zip(*[attend(qkv[j], allowed) for j in range(4)])
    stream_one = stream_zero
    for j in range(4):
        stream_one = stream_one + dot(context[j], out_w[j])
    normed_two, rstd_two = normalize(stream_one)
    norm_two = (normed_two * gain2 + shift2).astype(BF16)

    norm_all = jnp.concatenate(spread(norm_two), axis=0)
    mlp_pre = dot(norm_all, in_w)
    mlp_act = gelu(mlp_pre).astype(BF16)
    grad_down = gram(mlp_act, cot_all).astype(BF16)
    grad_down = scatter(move_blocks(grad_down, to_layer), 1)
    mlp_out = dot(mlp_act, down_w)
    stream_q = move_blocks(stream_one, to_quarters)
    mlp_out = mlp_out.reshape(micros, tokens, width)
    mlp_out = jnp.concatenate([(mlp_out[0] + stream_q)[None], mlp_out[1:]], axis=0)
    result = fold(
        [mlp_out[:, :, j * quarter : (j + 1) * quarter] for j in range(4)],
        place_rows=lambda v, j: jnp.stack([v[m ^ j] for m in range(4)]),
    ).astype(BF16)
    result = jnp.stack(pick([result[m] for m in range(4)], c))

    grad_pre = (gelu_grad(mlp_pre) * dot_t(cot_all, down_w)).astype(BF16)
    grad_in = scatter(gram(norm_all, grad_pre), 0)
    grad_norm_two = dot_t(grad_pre, in_w).reshape(micros, tokens, width)
    grad_norm_two = fold([grad_norm_two[j] for j in range(4)])

    back_two, grad_gain2, grad_shift2 = normalize_back(normed_two, rstd_two, gain2, grad_norm_two)
    grad_stream_one = cot_mine.astype(F32) + back_two
    grad_att = grad_stream_one.astype(BF16)
    grad_out = scatter(fold([gram(context[j], grad_att) for j in range(4)]), 1)
    grad_rows = [
        attend_back(qkv[j], probs[j], dot_t(grad_att, out_w[j]).astype(BF16)) for j in range(4)
    ]
    grad_qkv = scatter(fold([gram(norm_one, grad_rows[j]) for j in range(4)]), 0)
    grad_norm_one = dot_t(grad_rows[0], qkv_w[0])
    for j in (1, 2, 3):
        grad_norm_one = grad_norm_one + dot_t(grad_rows[j], qkv_w[j])
    back_one, grad_gain1, grad_shift1 = normalize_back(normed_one, rstd_one, gain1, grad_norm_one)
    input_grad = (grad_stream_one + back_one).astype(BF16)
    grad_vectors = scatter_vectors(
        jnp.stack([grad_gain1, grad_shift1, grad_gain2, grad_shift2]), c, z, x
    )
    grad_in_q = move_blocks(input_grad, to_quarters)
    grad_in_q = exchange([grad_in_q[:, j * quarter : (j + 1) * quarter] for j in range(4)])
    input_grads = jnp.stack(pick(grad_in_q, c))

    grad_up_rows = move_blocks(input_grad.reshape(coarse, 4 * width), to_up)
    grad_up = scatter(fold([gram(hidden[j], grad_up_rows) for j in range(4)]), 1)
    grad_hidden = [dot_t(grad_up_rows, up[j]).astype(BF16) for j in range(4)]
    grad_res = scatter(fold([gram(mixed, grad_hidden[j]) for j in range(4)]), 0)
    grad_mixed = dot_t(grad_hidden[0], res[0])
    for j in (1, 2, 3):
        grad_mixed = grad_mixed + dot_t(grad_hidden[j], res[j])
    grad_conv_low = (gelu_grad(conv_out) * grad_mixed).astype(BF16)

    grad_conv_all = jnp.concatenate(spread(grad_conv_low), axis=0)
    grad_conv = scatter(gram(taps, grad_conv_all), 1).reshape(conv_weight.shape)
    grad_taps = dot_t(grad_conv_all, conv).reshape(micros, coarse, 3 * quarter)
    tap = [grad_taps[:, :, k * quarter : (k + 1) * quarter] for k in range(3)]
    before, after = edges((tap[0][:, :step].astype(BF16), tap[2][:, coarse - step :].astype(BF16)))
    blank = jnp.zeros((micros, coarse - step, quarter), F32)
    grad_act = (
        tap[1]
        + jnp.concatenate([tap[0][:, step:], after.astype(F32)], axis=1)
        + jnp.concatenate([before.astype(F32), tap[2][:, : coarse - step]], axis=1)
    ).reshape(micros * coarse, quarter)
    grad_hidden_q = jnp.concatenate(exchange(grad_hidden), axis=0)
    grad_embed = (grad_hidden_q.astype(F32) + gelu_grad(embed) * grad_act).astype(BF16)
    grad_table = scatter(gram(onehot, grad_embed), 0)
    return (
        result,
        input_grads,
        grad_table,
        grad_conv,
        grad_res,
        grad_up,
        grad_vectors[0],
        grad_vectors[1],
        grad_qkv.reshape(qkv_weight.shape),
        grad_out,
        grad_vectors[2],
        grad_vectors[3],
        grad_in,
        grad_down,
    )


def solution(mesh):
    wide = P(("cond", "seq"))
    acts = P(None, "seq", "cond")
    weights = (
        P("seq", "cond"),
        P(None, "cond", "seq"),
        P("seq", "cond"),
        P("cond", "seq"),
        wide,
        wide,
        P("seq", None, "cond"),
        P("cond", "seq"),
        wide,
        wide,
        P("seq", "cond"),
        P("cond", "seq"),
    )
    return jax.shard_map(
        on_device,
        mesh=mesh,
        in_specs=(acts, P(None, "seq"), P(None, "seq"), acts) + weights,
        out_specs=(acts, acts) + weights,
        check_vma=False,
    )
```

time: 3670 us -> 1090 us (0.30)
  waiting for transfers between devices: 2990 us -> 384 us
  blocking collectives: 141 us -> 0 us
  starting transfers between devices: 47.6 us -> 144 us
  Pallas kernels: 0 us -> 70.8 us
  matrix products: 239 us -> 179 us
  other arithmetic: 64.4 us -> 119 us
    reduce_scatter x40 -> x0, waiting for transfers between devices: 1880 us -> none  [the longest x20 554 us: share_rows(): return lax.psum_scatter(value, 'cond', scatter_dimension=1, tiled=True)]
    unnamed x92 -> x0, waiting for transfers between devices: 686 us -> none
    all_gather x26 -> x0, waiting for transfers between devices: 388 us -> none  [the longest x20 185 us: gather_rows(): return lax.all_gather(value, 'cond', axis=1, tiled=True)]
    ppermute x16 -> x136, waiting for transfers between devices: 20.6 us -> 384 us  [the longest x72 199 us: hop(): return lax.ppermute(x, 'seq', [(i, i ^ k) for i in range(8)])]
    ppermute x16 -> x136, starting transfers between devices: 41.7 us -> 144 us  [the longest x72 104 us: hop(): return lax.ppermute(x, 'seq', [(i, i ^ k) for i in range(8)])]
    pallas_call x0 -> x8, Pallas kernels: none -> 70.8 us  [move_blocks(): pl.pallas_call(copy_block, out_shape=jax.ShapeDtypeStruct((rows, count *...]
    concatenate x0 -> x14, other arithmetic: none -> 63.4 us  [the longest x1 49.2 us: on_device(): jnp.concatenate([jnp.concatenate([cots[j][m ^ j] for m in range(4)], axis...]
    all_gather x2 -> x0, blocking collectives: 61.3 us -> none  [the longest x1 31.5 us: fetch_weights(): lax.all_gather(shards[2], 'seq', axis=0, tiled=True)]
  transfers between devices with their start and end apart: 96 -> 136, of which waited for: 85 -> 42; matrix products, arithmetic and copies ran while one was open for 11% -> 39% of each run, Pallas kernels for 0% -> 6%
where the time goes in v1:
time: 1090 us; the launch traced here: 1070 us
  waiting for transfers between devices  384 us (35%)
  matrix products  179 us (16%)
  local copies, waits for them, and re-layouts  172 us (16%)
  starting transfers between devices  144 us (13%)
  other arithmetic  119 us (11%)
  Pallas kernels  70.8 us (6%)
    ppermute x72, waiting for transfers between devices, hop(): return lax.ppermute(x, 'seq', [(i, i ^ k) for i in range(8)])  199 us
    ppermute x60, waiting for transfers between devices, swap(): return lax.ppermute(x, 'cond', [(i, i ^ j) for i in range(4)])  149 us
    dot_general x59, matrix products, dot(): return lax.dot_general(a, b, (dims, ((), ())), preferred_element_type=F32)  141 us
    ppermute x72, starting transfers between devices, hop(): return lax.ppermute(x, 'seq', [(i, i ^ k) for i in range(8)])  104 us
    pallas_call x8, Pallas kernels, move_blocks(): pl.pallas_call(copy_block, out_shape=jax.ShapeDtypeStruct((rows, count *...  70.8 us
    concatenate x1, other arithmetic, on_device(): jnp.concatenate([jnp.concatenate([cots[j][m ^ j] for m in range(4)], axis...  49.2 us
    unnamed x420, local copies, waits for them, and re-layouts  40.6 us
    reshape x20, local copies, waits for them, and re-layouts, attend(): qkv[:, i * width:(i + 1) * width].reshape(shape)  32.7 us
  transfers between devices with their start and end apart: 136, of which 42 were waited for; matrix products, arithmetic and copies ran while one was open for 39% of the time, Pallas kernels for 6%

profile of v1, /device:TPU:0, one launch (start us, length us, event | category | flops | bytes accessed | tf_op | source)
XLA Modules:
  0.0 1072.8 jit_solution(168932139278075985)
XLA Ops:
  2.0 5.0 collective-permute-start.35
  7.7 3.8 collective-permute-start.18
  36.8 3.8 collective-permute-start.46
  44.1 3.2 collective-permute-start.5
  53.7 3.2 collective-permute-start.42
  63.4 3.2 collective-permute-start.11
  74.0 10.6 collective-permute-done.41
  89.5 9.9 collective-permute-start.20
  99.4 4.9 collective-permute-done.10
  104.3 3.0 collective-permute-start.57
  111.9 14.8 %collective-permute-done.21 = bf16[256,512]{1,0:T(8,128)(2,1)S(1)} collective-permute-done((bf16[256,512]{1,0:T(8,128)(2,1)S(1)}, bf16[256,512]{1,0:T(8,128)(2,1)S(1)}, u32[]{:S(2)}, u32[]{:S(2)}) %collective-permute-start.21) | collective-permute-done | bytes 262176 | tf_op jit(solution)/shard_map/ppermute | solution.py:29
  126.8 3.1 collective-permute-start.61
  131.1 17.3 %collective-permute-done.62 = bf16[1024,128]{1,0:T(8,128)(2,1)S(1)} collective-permute-done((bf16[1024,128]{1,0:T(8,128)(2,1)S(1)}, bf16[1024,128]{1,0:T(8,128)(2,1)S(1)}, u32[]{:S(2)}, u32[]{:S(2)}) %collective-permute-start.62) | collective-permute-done | bytes 262176 | tf_op jit(solution)/shard_map/ppermute | solution.py:29
  159.1 3.2 collective-permute-done.2
  168.4 5.9 move_blocks.8
  179.9 3.4 collective-permute-done.6
  186.0 3.4 collective-permute-start.7
  191.8 32.5 %collective-permute-done.7 = bf16[4,27,256]{2,1,0:T(8,128)(2,1)S(1)} collective-permute-done((bf16[4,27,256]{2,1,0:T(8,128)(2,1)S(1)}, bf16[4,27,256]{2,1,0:T(8,128)(2,1)S(1)}, u32[]{:S(2)}, u32[]{:S(2)}) %collective-permute-start.7) | collective-permute-done | bytes 55328 | tf_op jit(solution)/shard_map/ppermute | solution.py:230
  229.9 15.4 %collective-permute-done.43 = bf16[512,768]{0,1:T(8,128)(2,1)S(1)} collective-permute-done((bf16[512,768]{0,1:T(8,128)(2,1)S(1)}, bf16[512,768]{0,1:T(8,128)(2,1)S(1)}, u32[]{:S(2)}, u32[]{:S(2)}) %collective-permute-start.43) | collective-permute-done | bytes 786464 | tf_op jit(solution)/shard_map/ppermute | solution.py:29
  253.0 24.0 %collective-permute-done.30 = bf16[128,256]{1,0:T(8,128)(2,1)S(1)} collective-permute-done((bf16[128,256]{1,0:T(8,128)(2,1)S(1)}, bf16[128,256]{1,0:T(8,128)(2,1)S(1)}, u32[]{:S(2)}, u32[]{:S(2)}) %collective-permute-start.30) | collective-permute-done | bytes 65568 | tf_op jit(solution)/shard_map/ppermute | solution.py:25
  279.6 10.4 collective-permute-done.64
  291.0 6.4 move_blocks.10
  309.7 41.7 %collective-permute-done.27 = bf16[128,256]{1,0:T(8,128)(2,1)S(1)} collective-permute-done((bf16[128,256]{1,0:T(8,128)(2,1)S(1)}, bf16[128,256]{1,0:T(8,128)(2,1)S(1)}, u32[]{:S(2)}, u32[]{:S(2)}) %collective-permute-start.27) | collective-permute-done | bytes 65568 | tf_op jit(solution)/shard_map/ppermute | solution.py:25
  361.3 17.3 %move_blocks.9 = f32[128,4096]{1,0:T(8,128)} custom-call(s32[32]{0:T(128)} %or_add_fusion.2.index_ref, f32[128,4096]{1,0:T(8,128)} %convolution_add_fusion.1.in_ref), custom_call_target="tpu_custom_call" | custom-call | tf_op jit(solution)/shard_map/move_blocks/pallas_call | solution.py:123
  403.1 3.8 convolution_convert_fusion.10
  464.4 49.2 %maximum_maximum_fusion = bf16[2048,1024]{1,0:T(8,128)(2,1)} fusion(bf16[512,256]{1,0:T(8,128)(2,1)S(1)} %copy-done.74, bf16[512,256]{1,0:T(8,128)(2,1)S(1)} %copy-done.75, bf16[512,256]{1,0:T(8,128)(2,1)S(1)} %copy-done.76, bf16[512,256]{1,0:T(8,128)(2,1)S(1)} %copy-done.73, bf16[1024,256]{1,0:T(8,128)(2,1)S(1)} %get-tuple-element.96, ...), kind=kLoop, calls=%fused_computation.31 | loop fusion | flops 58720256 | bytes 8388608 | tf_op jit(solution)/shard_map/concatenate | solution.py:279
  514.1 9.8 maximum_maximum_fusion.1.in_ref
  523.9 6.0 move_blocks.12
  529.9 9.0 fusion.228
  538.9 6.4 move_blocks.11
  545.4 13.9 %fusion.9 = (bf16[2048,1024]{1,0:T(8,128)(2,1)}, bf16[2048,1024]{1,0:T(8,128)(2,1)S(1)}) fusion(f32[2048,1024]{1,0:T(8,128)} %fusion.228, bf16[1024,1024]{1,0:T(8,128)(2,1)} %constant_dynamic-update-slice_fusion.30, bf16[512,1024]{1,0:T(8,128)(2,1)} %collective-permute-done.56, bf16[512,1024]{1,0:T(8,128)(2,1)} %collective-permute-done.55, ...), kind=kOutput, calls=%fused_computation.15 | convolution fusion | flops 4339007488 | bytes 23068672 | tf_op jit(solution)/shard_map/dot_general | solution.py:42
  559.2 6.0 convolution_convert_fusion.2.in_ref
  565.3 6.7 fusion.227
  572.0 6.4 move_blocks.15
  581.5 3.4 slice.452
  584.9 3.4 fusion.29
  590.2 7.4 fusion.220
  599.1 8.0 convolution_convert_fusion.3
  612.2 20.3 %collective-permute-done.128 = bf16[512,1024]{1,0:T(8,128)(2,1)S(1)} collective-permute-done((bf16[512,1024]{1,0:T(8,128)(2,1)S(1)}, bf16[512,1024]{1,0:T(8,128)(2,1)S(1)}, u32[]{:S(2)}, u32[]{:S(2)}) %collective-permute-start.128) | collective-permute-done | bytes 1048608 | tf_op jit(solution)/shard_map/ppermute | solution.py:29
  637.5 3.4 collective-permute-start.131
  640.9 7.3 collective-permute-done.134
  649.1 5.6 collective-permute-done.129
  655.9 12.8 %collective-permute-done.130 = bf16[128,1024]{1,0:T(8,128)(2,1)S(1)} collective-permute-done((bf16[128,1024]{1,0:T(8,128)(2,1)S(1)}, bf16[128,1024]{1,0:T(8,128)(2,1)S(1)}, u32[]{:S(2)}, u32[]{:S(2)}) %collective-permute-start.130) | collective-permute-done | bytes 262176 | tf_op jit(solution)/shard_map/ppermute | solution.py:29
  678.2 3.0 fusion.66
  715.9 3.0 fusion.69
  778.2 3.5 multiply_reduce_fusion.1
  783.9 16.1 %move_blocks.14 = bf16[128,4096]{1,0:T(8,128)(2,1)} custom-call(s32[32]{0:T(128)} %or_add_fusion.index_ref, bf16[128,4096]{1,0:T(8,128)(2,1)} %reshape.465.in_ref), custom_call_target="tpu_custom_call" | custom-call | tf_op jit(solution)/shard_map/move_blocks/pallas_call | solution.py:123
  806.2 6.2 move_blocks.13
  812.4 3.7 convolution_convert_fusion.5
  816.2 4.2 fusion.236
  820.4 3.6 fusion.172
  849.3 4.8 collective-permute-done.109
  868.9 4.6 collective-permute-done.75
  873.6 3.2 collective-permute-done.74
  896.1 8.5 collective-permute-done.123
  921.1 4.6 collective-permute-done.87
  928.8 10.1 collective-permute-done.89
  941.1 5.2 collective-permute-done.96
  949.6 13.4 %collective-permute-done.116 = bf16[1024,768]{0,1:T(8,128)(2,1)S(1)} collective-permute-done((bf16[1024,768]{0,1:T(8,128)(2,1)S(1)}, bf16[1024,768]{0,1:T(8,128)(2,1)S(1)}, u32[]{:S(2)}, u32[]{:S(2)}) %collective-permute-start.116) | collective-permute-done | bytes 1572896 | tf_op jit(solution)/shard_map/ppermute | solution.py:25
  965.1 40.7 %collective-permute-done.102 = bf16[256,4096]{1,0:T(8,128)(2,1)S(1)} collective-permute-done((bf16[256,4096]{1,0:T(8,128)(2,1)S(1)}, bf16[256,4096]{1,0:T(8,128)(2,1)S(1)}, u32[]{:S(2)}, u32[]{:S(2)}) %collective-permute-start.102) | collective-permute-done | bytes 2097184 | tf_op jit(solution)/shard_map/ppermute | solution.py:25
  1021.8 8.1 collective-permute-done.103
  1035.7 5.2 collective-permute-done.91
  1043.5 18.5 %collective-permute-done.119 = bf16[128,768]{0,1:T(8,128)(2,1)S(1)} collective-permute-done((bf16[128,768]{0,1:T(8,128)(2,1)S(1)}, bf16[128,768]{0,1:T(8,128)(2,1)S(1)}, u32[]{:S(2)}, u32[]{:S(2)}) %collective-permute-start.119) | collective-permute-done | bytes 196640 | tf_op jit(solution)/shard_map/ppermute | solution.py:29
  1063.0 8.7 collective-permute-done.105
  (950 shorter events, 451.4 us)
Async XLA Ops:
  2.0 24.9 %collective-permute-start.35 = (bf16[4,32]{1,0:T(4,128)(2,1)}, bf16[4,32]{1,0:T(4,128)(2,1)}, u32[]{:S(2)}, u32[]{:S(2)}) collective-permute-start(bf16[4,32]{1,0:T(4,128)(2,1)} %pad_maximum_fusion.25), channel_id=1, source_target_pairs={{0,6},{1,7},{2,4},{3,5},{4,2},{5,3},{6,0},{7,1},{8,14},{9,15},{10,... | collective-permute-start | bytes 776 | tf_op jit(solution)/shard_map/ppermute | solution.py:29
  7.7 36.5 %collective-permute-start.18 = (bf16[128,256]{1,0:T(8,128)(2,1)}, bf16[128,256]{1,0:T(8,128)(2,1)}, u32[]{:S(2)}, u32[]{:S(2)}) collective-permute-start(bf16[128,256]{1,0:T(8,128)(2,1)} %param.22), channel_id=1, source_target_pairs={{0,6},{1,7},{2,4},{3,5},{4,2},{5,3},{6,0},{7,1},{8,14},{9,15},{10,... | collective-permute-start | bytes 196616 | tf_op jit(solution)/shard_map/ppermute | solution.py:29
  11.5 35.9 %collective-permute-start.17 = (bf16[128,256]{1,0:T(8,128)(2,1)}, bf16[128,256]{1,0:T(8,128)(2,1)}, u32[]{:S(2)}, u32[]{:S(2)}) collective-permute-start(bf16[128,256]{1,0:T(8,128)(2,1)} %param.22), channel_id=1, source_target_pairs={{0,4},{1,5},{2,6},{3,7},{4,0},{5,1},{6,2},{7,3},{8,12},{9,13},{10,... | collective-permute-start | bytes 196616 | tf_op jit(solution)/shard_map/ppermute | solution.py:29
  53.7 34.1 %collective-permute-start.42 = (bf16[128,768]{0,1:T(8,128)(2,1)S(1)}, bf16[128,768]{0,1:T(8,128)(2,1)S(1)}, u32[]{:S(2)}, u32[]{:S(2)}) collective-permute-start(bf16[128,768]{0,1:T(8,128)(2,1)S(1)} %bitcast.343), channel_id=1, source_target_pairs={{0,6},{1,7},{2,4},{3,5},{4,2},{5,3},{6,0},{7,1},{8,14},{9,15},{10,... | collective-permute-start | bytes 589832 | tf_op jit(solution)/shard_map/ppermute | solution.py:29
  57.0 27.7 %collective-permute-start.41 = (bf16[128,768]{0,1:T(8,128)(2,1)S(1)}, bf16[128,768]{0,1:T(8,128)(2,1)S(1)}, u32[]{:S(2)}, u32[]{:S(2)}) collective-permute-start(bf16[128,768]{0,1:T(8,128)(2,1)S(1)} %bitcast.344), channel_id=1, source_target_pairs={{0,4},{1,5},{2,6},{3,7},{4,0},{5,1},{6,2},{7,3},{8,12},{9,13},{10,... | collective-permute-start | bytes 589832 | tf_op jit(solution)/shard_map/ppermute | solution.py:29
  63.4 26.1 %collective-permute-start.11 = (bf16[768,128]{1,0:T(8,128)(2,1)}, bf16[768,128]{1,0:T(8,128)(2,1)S(1)}, u32[]{:S(2)}, u32[]{:S(2)}) collective-permute-start(bf16[768,128]{1,0:T(8,128)(2,1)} %bitcast.348), channel_id=1, source_target_pairs={{0,6},{1,7},{2,4},{3,5},{4,2},{5,3},{6,0},{7,1},{8,14},{9,15},{10,... | collective-permute-start | bytes 589832 | tf_op jit(solution)/shard_map/ppermute | solution.py:29
  66.7 37.6 %collective-permute-start.10 = (bf16[768,128]{1,0:T(8,128)(2,1)}, bf16[768,128]{1,0:T(8,128)(2,1)S(1)}, u32[]{:S(2)}, u32[]{:S(2)}) collective-permute-start(bf16[768,128]{1,0:T(8,128)(2,1)} %bitcast.349), channel_id=1, source_target_pairs={{0,4},{1,5},{2,6},{3,7},{4,0},{5,1},{6,2},{7,3},{8,12},{9,13},{10,... | collective-permute-start | bytes 589832 | tf_op jit(solution)/shard_map/ppermute | solution.py:29
  70.8 33.5 %collective-permute-start.9 = (bf16[768,128]{1,0:T(8,128)(2,1)S(1)}, bf16[768,128]{1,0:T(8,128)(2,1)S(1)}, u32[]{:S(2)}, u32[]{:S(2)}) collective-permute-start(bf16[768,128]{1,0:T(8,128)(2,1)S(1)} %bitcast.351), channel_id=1, source_target_pairs={{0,2},{1,3},{2,0},{3,1},{4,6},{5,7},{6,4},{7,5},{8,10},{9,11},{10,... | collective-permute-start | bytes 589832 | tf_op jit(solution)/shard_map/ppermute | solution.py:29
  84.6 42.2 %collective-permute-start.22 = (bf16[256,512]{1,0:T(8,128)(2,1)S(1)}, bf16[256,512]{1,0:T(8,128)(2,1)S(1)}, u32[]{:S(2)}, u32[]{:S(2)}) collective-permute-start(bf16[256,512]{1,0:T(8,128)(2,1)S(1)} %copy-done.112), channel_id=1, source_target_pairs={{0,6},{1,7},{2,4},{3,5},{4,2},{5,3},{6,0},{7,1},{8,14},{9,15},{10,... | collective-permute-start | bytes 786440 | tf_op jit(solution)/shard_map/ppermute | solution.py:29
  87.8 38.9 %collective-permute-start.21 = (bf16[256,512]{1,0:T(8,128)(2,1)S(1)}, bf16[256,512]{1,0:T(8,128)(2,1)S(1)}, u32[]{:S(2)}, u32[]{:S(2)}) collective-permute-start(bf16[256,512]{1,0:T(8,128)(2,1)S(1)} %copy-done.112), channel_id=1, source_target_pairs={{0,4},{1,5},{2,6},{3,7},{4,0},{5,1},{6,2},{7,3},{8,12},{9,13},{10,... | collective-permute-start | bytes 786440 | tf_op jit(solution)/shard_map/ppermute | solution.py:29
  104.3 60.6 %collective-permute-start.58 = (bf16[128,1024]{1,0:T(8,128)(2,1)S(1)}, bf16[128,1024]{1,0:T(8,128)(2,1)S(1)}, u32[]{:S(2)}, u32[]{:S(2)}) collective-permute-start(bf16[128,1024]{1,0:T(8,128)(2,1)S(1)} %copy-done.116), channel_id=1, source_target_pairs={{0,4},{1,5},{2,6},{3,7},{4,0},{5,1},{6,2},{7,3},{8,12},{9,13},{10,... | collective-permute-start | bytes 786440 | tf_op jit(solution)/shard_map/ppermute | solution.py:29
  104.3 49.0 %collective-permute-start.57 = (bf16[128,1024]{1,0:T(8,128)(2,1)S(1)}, bf16[128,1024]{1,0:T(8,128)(2,1)S(1)}, u32[]{:S(2)}, u32[]{:S(2)}) collective-permute-start(bf16[128,1024]{1,0:T(8,128)(2,1)S(1)} %copy-done.116), channel_id=1, source_target_pairs={{0,2},{1,3},{2,0},{3,1},{4,6},{5,7},{6,4},{7,5},{8,10},{9,11},{10,... | collective-permute-start | bytes 786440 | tf_op jit(solution)/shard_map/ppermute | solution.py:29
  126.8 23.1 %collective-permute-start.61 = (bf16[1024,128]{1,0:T(8,128)(2,1)S(1)}, bf16[1024,128]{1,0:T(8,128)(2,1)S(1)}, u32[]{:S(2)}, u32[]{:S(2)}) collective-permute-start(bf16[1024,128]{1,0:T(8,128)(2,1)S(1)} %copy-done.114), channel_id=1, source_target_pairs={{0,2},{1,3},{2,0},{3,1},{4,6},{5,7},{6,4},{7,5},{8,10},{9,11},{10,... | collective-permute-start | bytes 786440 | tf_op jit(solution)/shard_map/ppermute | solution.py:29
  131.1 25.3 %collective-permute-start = (bf16[512,256]{1,0:T(8,128)(2,1)S(1)}, bf16[512,256]{1,0:T(8,128)(2,1)S(1)}, u32[]{:S(2)}, u32[]{:S(2)}) collective-permute-start(bf16[512,256]{1,0:T(8,128)(2,1)S(1)} %copy-done.159), channel_id=1, source_target_pairs={{0,8},{8,0},{16,24},{24,16},{1,9},{9,1},{17,25},{25,17},{2,10},{10... | collective-permute-start | bytes 786440 | tf_op jit(solution)/shard_map/ppermute | solution.py:25
  156.3 92.0 %collective-permute-start.69 = (bf16[2048,256]{1,0:T(8,128)(2,1)}, bf16[2048,256]{1,0:T(8,128)(2,1)S(1)}, u32[]{:S(2)}, u32[]{:S(2)}) collective-permute-start(bf16[2048,256]{1,0:T(8,128)(2,1)} %pad_maximum_fusion.7), channel_id=1, source_target_pairs={{0,16},{8,24},{16,0},{24,8},{1,17},{9,25},{17,1},{25,9},{2,18},{10... | collective-permute-start | bytes 3145736 | tf_op jit(solution)/shard_map/ppermute | solution.py:25
  166.1 60.9 %collective-permute-start.12 = (bf16[768,512]{1,0:T(8,128)(2,1)}, bf16[768,512]{1,0:T(8,128)(2,1)}, u32[]{:S(2)}, u32[]{:S(2)}) collective-permute-start(bf16[768,512]{1,0:T(8,128)(2,1)} %pad_maximum_fusion.11), channel_id=1, source_target_pairs={{0,1},{1,0},{2,3},{3,2},{4,5},{5,4},{6,7},{7,6},{8,9},{9,8},{10,11... | collective-permute-start | bytes 2359304 | tf_op jit(solution)/shard_map/ppermute | solution.py:29
  175.9 52.6 %collective-permute-start.23 = (bf16[256,2048]{1,0:T(8,128)(2,1)S(1)}, bf16[256,2048]{1,0:T(8,128)(2,1)S(1)}, u32[]{:S(2)}, u32[]{:S(2)}) collective-permute-start(bf16[256,2048]{1,0:T(8,128)(2,1)S(1)} %copy-done.104), channel_id=1, source_target_pairs={{0,1},{1,0},{2,3},{3,2},{4,5},{5,4},{6,7},{7,6},{8,9},{9,8},{10,11... | collective-permute-start | bytes 3145736 | tf_op jit(solution)/shard_map/ppermute | solution.py:29
  186.0 38.3 %collective-permute-start.7 = (bf16[4,27,256]{2,1,0:T(8,128)(2,1)S(1)}, bf16[4,27,256]{2,1,0:T(8,128)(2,1)S(1)}, u32[]{:S(2)}, u32[]{:S(2)}) collective-permute-start(bf16[4,27,256]{2,1,0:T(8,128)(2,1)S(1)} %get-tuple-element.165), channel_id=1, source_target_pairs={{0,1},{1,2},{2,3},{3,4},{4,5},{5,6},{6,7},{8,9},{9,10},{10,11},{11... | collective-permute-start | bytes 165896 | tf_op jit(solution)/shard_map/ppermute | solution.py:230
  189.4 35.0 %collective-permute-start.8 = (bf16[4,27,256]{2,1,0:T(8,128)(2,1)S(1)}, bf16[4,27,256]{2,1,0:T(8,128)(2,1)S(1)}, u32[]{:S(2)}, u32[]{:S(2)}) collective-permute-start(bf16[4,27,256]{2,1,0:T(8,128)(2,1)S(1)} %get-tuple-element.166), channel_id=1, source_target_pairs={{1,0},{2,1},{3,2},{4,3},{5,4},{6,5},{7,6},{9,8},{10,9},{11,10},{12... | collective-permute-start | bytes 165896 | tf_op jit(solution)/shard_map/ppermute | solution.py:231
  224.3 26.2 %collective-permute-start.68 = (bf16[2048,256]{1,0:T(8,128)(2,1)}, bf16[2048,256]{1,0:T(8,128)(2,1)S(1)}, u32[]{:S(2)}, u32[]{:S(2)}) collective-permute-start(bf16[2048,256]{1,0:T(8,128)(2,1)} %pad_maximum_fusion.7), channel_id=1, source_target_pairs={{0,8},{8,0},{16,24},{24,16},{1,9},{9,1},{17,25},{25,17},{2,10},{10... | collective-permute-start | bytes 3145736 | tf_op jit(solution)/shard_map/ppermute | solution.py:25
  227.1 50.9 %collective-permute-start.60 = (bf16[512,1024]{1,0:T(8,128)(2,1)S(1)}, bf16[512,1024]{1,0:T(8,128)(2,1)S(1)}, u32[]{:S(2)}, u32[]{:S(2)}) collective-permute-start(bf16[512,1024]{1,0:T(8,128)(2,1)S(1)} %pad_maximum_fusion.4), channel_id=1, source_target_pairs={{0,1},{1,0},{2,3},{3,2},{4,5},{5,4},{6,7},{7,6},{8,9},{9,8},{10,11... | collective-permute-start | bytes 3145736 | tf_op jit(solution)/shard_map/ppermute | solution.py:29
  228.6 74.5 %collective-permute-start.29 = (bf16[256,4096]{1,0:T(8,128)(2,1)S(1)}, bf16[256,4096]{1,0:T(8,128)(2,1)}, u32[]{:S(2)}, u32[]{:S(2)}) collective-permute-start(bf16[256,4096]{1,0:T(8,128)(2,1)S(1)} %constant_dynamic-update-slice_fusion.15), channel_id=1, source_target_pairs={{0,16},{8,24},{16,0},{24,8},{1,17},{9,25},{17,1},{25,9},{2,18},{10... | collective-permute-start | bytes 6291464 | tf_op jit(solution)/shard_map/ppermute | solution.py:25
  245.3 44.7 %collective-permute-start.64 = (bf16[1024,512]{1,0:T(8,128)(2,1)S(1)}, bf16[1024,512]{1,0:T(8,128)(2,1)S(1)}, u32[]{:S(2)}, u32[]{:S(2)}) collective-permute-start(bf16[1024,512]{1,0:T(8,128)(2,1)S(1)} %copy-done.103), channel_id=1, source_target_pairs={{0,1},{1,0},{2,3},{3,2},{4,5},{5,4},{6,7},{7,6},{8,9},{9,8},{10,11... | collective-permute-start | bytes 3145736 | tf_op jit(solution)/shard_map/ppermute | solution.py:29
  250.6 26.7 %collective-permute-start.13 = (bf16[128,1024]{1,0:T(8,128)(2,1)S(1)}, bf16[128,1024]{1,0:T(8,128)(2,1)S(1)}, u32[]{:S(2)}, u32[]{:S(2)}) collective-permute-start(bf16[128,1024]{1,0:T(8,128)(2,1)S(1)} %get-tuple-element.123), channel_id=1, source_target_pairs={{0,8},{8,0},{16,24},{24,16},{1,9},{9,1},{17,25},{25,17},{2,10},{10... | collective-permute-start | bytes 786440 | tf_op jit(solution)/shard_map/ppermute | solution.py:25
  252.1 24.8 %collective-permute-start.30 = (bf16[128,256]{1,0:T(8,128)(2,1)S(1)}, bf16[128,256]{1,0:T(8,128)(2,1)S(1)}, u32[]{:S(2)}, u32[]{:S(2)}) collective-permute-start(bf16[128,256]{1,0:T(8,128)(2,1)S(1)} %get-tuple-element.160), channel_id=1, source_target_pairs={{0,24},{8,16},{16,8},{24,0},{1,25},{9,17},{17,9},{25,1},{2,26},{10... | collective-permute-start | bytes 196616 | tf_op jit(solution)/shard_map/ppermute | solution.py:25
  276.9 24.7 %collective-permute-start.28 = (bf16[1024,256]{1,0:T(8,128)(2,1)}, bf16[1024,256]{1,0:T(8,128)(2,1)}, u32[]{:S(2)}, u32[]{:S(2)}) collective-permute-start(bf16[1024,256]{1,0:T(8,128)(2,1)} %constant_dynamic-update-slice_fusion.10), channel_id=1, source_target_pairs={{0,16},{8,24},{16,0},{24,8},{1,17},{9,25},{17,1},{25,9},{2,18},{10... | collective-permute-start | bytes 1572872 | tf_op jit(solution)/shard_map/ppermute | solution.py:25
  277.3 24.4 %collective-permute-start.25 = (bf16[1024,256]{1,0:T(8,128)(2,1)}, bf16[1024,256]{1,0:T(8,128)(2,1)}, u32[]{:S(2)}, u32[]{:S(2)}) collective-permute-start(bf16[1024,256]{1,0:T(8,128)(2,1)} %constant_dynamic-update-slice_fusion.10), channel_id=1, source_target_pairs={{0,8},{8,0},{16,24},{24,16},{1,9},{9,1},{17,25},{25,17},{2,10},{10... | collective-permute-start | bytes 1572872 | tf_op jit(solution)/shard_map/ppermute | solution.py:25
  290.0 64.7 %collective-permute-start.26 = (bf16[256,4096]{1,0:T(8,128)(2,1)S(1)}, bf16[256,4096]{1,0:T(8,128)(2,1)}, u32[]{:S(2)}, u32[]{:S(2)}) collective-permute-start(bf16[256,4096]{1,0:T(8,128)(2,1)S(1)} %constant_dynamic-update-slice_fusion.15), channel_id=1, source_target_pairs={{0,8},{8,0},{16,24},{24,16},{1,9},{9,1},{17,25},{25,17},{2,10},{10... | collective-permute-start | bytes 6291464 | tf_op jit(solution)/shard_map/ppermute | solution.py:25
  301.7 52.5 %collective-permute-start.50 = (bf16[1024,768]{0,1:T(8,128)(2,1)}, bf16[1024,768]{0,1:T(8,128)(2,1)}, u32[]{:S(2)}, u32[]{:S(2)}) collective-permute-start(bf16[1024,768]{0,1:T(8,128)(2,1)} %constant_dynamic-update-slice_fusion.20), channel_id=1, source_target_pairs={{0,16},{8,24},{16,0},{24,8},{1,17},{9,25},{17,1},{25,9},{2,18},{10... | collective-permute-start | bytes 4718600 | tf_op jit(solution)/shard_map/ppermute | solution.py:25
  303.1 55.1 %collective-permute-start.32 = (bf16[256,4096]{1,0:T(8,128)(2,1)}, bf16[256,4096]{1,0:T(8,128)(2,1)S(1)}, u32[]{:S(2)}, u32[]{:S(2)}) collective-permute-start(bf16[256,4096]{1,0:T(8,128)(2,1)} %collective-permute-done.29), channel_id=1, source_target_pairs={{0,8},{8,0},{16,24},{24,16},{1,9},{9,1},{17,25},{25,17},{2,10},{10... | collective-permute-start | bytes 6291464 | tf_op jit(solution)/shard_map/ppermute | solution.py:25
  306.3 47.8 %collective-permute-start.51 = (bf16[256,1024]{1,0:T(8,128)(2,1)}, bf16[256,1024]{1,0:T(8,128)(2,1)}, u32[]{:S(2)}, u32[]{:S(2)}) collective-permute-start(bf16[256,1024]{1,0:T(8,128)(2,1)} %constant_dynamic-update-slice_fusion.25), channel_id=1, source_target_pairs={{0,16},{8,24},{16,0},{24,8},{1,17},{9,25},{17,1},{25,9},{2,18},{10... | collective-permute-start | bytes 1572872 | tf_op jit(solution)/shard_map/ppermute | solution.py:25
  308.4 43.0 %collective-permute-start.27 = (bf16[128,256]{1,0:T(8,128)(2,1)S(1)}, bf16[128,256]{1,0:T(8,128)(2,1)S(1)}, u32[]{:S(2)}, u32[]{:S(2)}) collective-permute-start(bf16[128,256]{1,0:T(8,128)(2,1)S(1)} %copy-done.166), channel_id=1, source_target_pairs={{0,16},{8,24},{16,0},{24,8},{1,17},{9,25},{17,1},{25,9},{2,18},{10... | collective-permute-start | bytes 196616 | tf_op jit(solution)/shard_map/ppermute | solution.py:25
  353.6 104.6 %collective-permute-start.49 = (bf16[256,1024]{1,0:T(8,128)(2,1)}, bf16[256,1024]{1,0:T(8,128)(2,1)}, u32[]{:S(2)}, u32[]{:S(2)}) collective-permute-start(bf16[256,1024]{1,0:T(8,128)(2,1)} %constant_dynamic-update-slice_fusion.25), channel_id=1, source_target_pairs={{0,8},{8,0},{16,24},{24,16},{1,9},{9,1},{17,25},{25,17},{2,10},{10... | collective-permute-start | bytes 1572872 | tf_op jit(solution)/shard_map/ppermute | solution.py:25
  354.1 105.7 %collective-permute-start.53 = (bf16[256,1024]{1,0:T(8,128)(2,1)}, bf16[256,1024]{1,0:T(8,128)(2,1)}, u32[]{:S(2)}, u32[]{:S(2)}) collective-permute-start(bf16[256,1024]{1,0:T(8,128)(2,1)} %collective-permute-done.51), channel_id=1, source_target_pairs={{0,8},{8,0},{16,24},{24,16},{1,9},{9,1},{17,25},{25,17},{2,10},{10... | collective-permute-start | bytes 1572872 | tf_op jit(solution)/shard_map/ppermute | solution.py:25
  354.2 52.7 %collective-permute-start.48 = (bf16[1024,768]{0,1:T(8,128)(2,1)}, bf16[1024,768]{0,1:T(8,128)(2,1)}, u32[]{:S(2)}, u32[]{:S(2)}) collective-permute-start(bf16[1024,768]{0,1:T(8,128)(2,1)} %constant_dynamic-update-slice_fusion.20), channel_id=1, source_target_pairs={{0,8},{8,0},{16,24},{24,16},{1,9},{9,1},{17,25},{25,17},{2,10},{10... | collective-permute-start | bytes 4718600 | tf_op jit(solution)/shard_map/ppermute | solution.py:25
  354.6 28.9 %collective-permute-start.52 = (bf16[1024,768]{0,1:T(8,128)(2,1)}, bf16[1024,768]{0,1:T(8,128)(2,1)}, u32[]{:S(2)}, u32[]{:S(2)}) collective-permute-start(bf16[1024,768]{0,1:T(8,128)(2,1)} %collective-permute-done.50), channel_id=1, source_target_pairs={{0,8},{8,0},{16,24},{24,16},{1,9},{9,1},{17,25},{25,17},{2,10},{10... | collective-permute-start | bytes 4718600 | tf_op jit(solution)/shard_map/ppermute | solution.py:25
  463.5 50.6 %collective-permute-start.55 = (bf16[512,1024]{1,0:T(8,128)(2,1)}, bf16[512,1024]{1,0:T(8,128)(2,1)}, u32[]{:S(2)}, u32[]{:S(2)}) collective-permute-start(bf16[512,1024]{1,0:T(8,128)(2,1)} %add_convert_fusion.4), channel_id=1, source_target_pairs={{0,16},{8,24},{16,0},{24,8},{1,17},{9,25},{17,1},{25,9},{2,18},{10... | collective-permute-start | bytes 3145736 | tf_op jit(solution)/shard_map/ppermute | solution.py:25
  513.6 31.8 %collective-permute-start.54 = (bf16[512,1024]{1,0:T(8,128)(2,1)}, bf16[512,1024]{1,0:T(8,128)(2,1)}, u32[]{:S(2)}, u32[]{:S(2)}) collective-permute-start(bf16[512,1024]{1,0:T(8,128)(2,1)} %add_convert_fusion.4), channel_id=1, source_target_pairs={{0,8},{8,0},{16,24},{24,16},{1,9},{9,1},{17,25},{25,17},{2,10},{10... | collective-permute-start | bytes 3145736 | tf_op jit(solution)/shard_map/ppermute | solution.py:25
  514.0 31.3 %collective-permute-start.56 = (bf16[512,1024]{1,0:T(8,128)(2,1)}, bf16[512,1024]{1,0:T(8,128)(2,1)}, u32[]{:S(2)}, u32[]{:S(2)}) collective-permute-start(bf16[512,1024]{1,0:T(8,128)(2,1)} %collective-permute-done.55), channel_id=1, source_target_pairs={{0,8},{8,0},{16,24},{24,16},{1,9},{9,1},{17,25},{25,17},{2,10},{10... | collective-permute-start | bytes 3145736 | tf_op jit(solution)/shard_map/ppermute | solution.py:25
  579.7 28.0 %collective-permute-start.132 = (bf16[1024,512]{1,0:T(8,128)(2,1)S(1)}, bf16[1024,512]{1,0:T(8,128)(2,1)S(1)}, u32[]{:S(2)}, u32[]{:S(2)}) collective-permute-start(bf16[1024,512]{1,0:T(8,128)(2,1)S(1)} %split.288), channel_id=1, source_target_pairs={{0,1},{1,0},{2,3},{3,2},{4,5},{5,4},{6,7},{7,6},{8,9},{9,8},{10,11... | collective-permute-start | bytes 3145736 | tf_op jit(solution)/shard_map/ppermute | solution.py:29
  607.2 25.3 %collective-permute-start.128 = (bf16[512,1024]{1,0:T(8,128)(2,1)S(1)}, bf16[512,1024]{1,0:T(8,128)(2,1)S(1)}, u32[]{:S(2)}, u32[]{:S(2)}) collective-permute-start(bf16[512,1024]{1,0:T(8,128)(2,1)S(1)} %split.282), channel_id=1, source_target_pairs={{0,1},{1,0},{2,3},{3,2},{4,5},{5,4},{6,7},{7,6},{8,9},{9,8},{10,11... | collective-permute-start | bytes 3145736 | tf_op jit(solution)/shard_map/ppermute | solution.py:29
  607.7 26.4 %collective-permute-start.65 = (bf16[4,512,256]{2,1,0:T(8,128)(2,1)S(1)}, bf16[4,512,256]{2,1,0:T(8,128)(2,1)S(1)}, u32[]{:S(2)}, u32[]{:S(2)}) collective-permute-start(bf16[4,512,256]{2,1,0:T(8,128)(2,1)S(1)} %get-tuple-element.60), channel_id=1, source_target_pairs={{0,8},{8,0},{16,24},{24,16},{1,9},{9,1},{17,25},{25,17},{2,10},{10... | collective-permute-start | bytes 3145736 | tf_op jit(solution)/shard_map/ppermute | solution.py:25
  607.7 61.9 %collective-permute-start.71 = (bf16[512,1024]{1,0:T(8,128)(2,1)S(1)}, bf16[512,1024]{1,0:T(8,128)(2,1)S(1)}, u32[]{:S(2)}, u32[]{:S(2)}) collective-permute-start(bf16[512,1024]{1,0:T(8,128)(2,1)S(1)} %get-tuple-element.57), channel_id=1, source_target_pairs={{0,8},{8,0},{16,24},{24,16},{1,9},{9,1},{17,25},{25,17},{2,10},{10... | collective-permute-start | bytes 3145736 | tf_op jit(solution)/shard_map/ppermute | solution.py:25
  609.3 27.2 %collective-permute-start.133 = (bf16[1024,128]{1,0:T(8,128)(2,1)S(1)}, bf16[1024,128]{1,0:T(8,128)(2,1)S(1)}, u32[]{:S(2)}, u32[]{:S(2)}) collective-permute-start(bf16[1024,128]{1,0:T(8,128)(2,1)S(1)} %get-tuple-element.79), channel_id=1, source_target_pairs={{0,2},{1,3},{2,0},{3,1},{4,6},{5,7},{6,4},{7,5},{8,10},{9,11},{10,... | collective-permute-start | bytes 786440 | tf_op jit(solution)/shard_map/ppermute | solution.py:29
  609.5 28.0 %collective-permute-start.135 = (bf16[1024,128]{1,0:T(8,128)(2,1)S(1)}, bf16[1024,128]{1,0:T(8,128)(2,1)S(1)}, u32[]{:S(2)}, u32[]{:S(2)}) collective-permute-start(bf16[1024,128]{1,0:T(8,128)(2,1)S(1)} %get-tuple-element.80), channel_id=1, source_target_pairs={{0,6},{1,7},{2,4},{3,5},{4,2},{5,3},{6,0},{7,1},{8,14},{9,15},{10,... | collective-permute-start | bytes 786440 | tf_op jit(solution)/shard_map/ppermute | solution.py:29
  632.5 37.1 %collective-permute-start.73 = (bf16[512,1024]{1,0:T(8,128)(2,1)S(1)}, bf16[512,1024]{1,0:T(8,128)(2,1)S(1)}, u32[]{:S(2)}, u32[]{:S(2)}) collective-permute-start(bf16[512,1024]{1,0:T(8,128)(2,1)S(1)} %fusion.27), channel_id=1, source_target_pairs={{0,16},{8,24},{16,0},{24,8},{1,17},{9,25},{17,1},{25,9},{2,18},{10... | collective-permute-start | bytes 3145736 | tf_op jit(solution)/shard_map/ppermute | solution.py:25
  654.8 169.3 %collective-permute-start.67 = (bf16[4,512,256]{2,1,0:T(8,128)(2,1)}, bf16[4,512,256]{2,1,0:T(8,128)(2,1)}, u32[]{:S(2)}, u32[]{:S(2)}) collective-permute-start(bf16[4,512,256]{2,1,0:T(8,128)(2,1)} %fusion.26), channel_id=1, source_target_pairs={{0,16},{8,24},{16,0},{24,8},{1,17},{9,25},{17,1},{25,9},{2,18},{10... | collective-permute-start | bytes 3145736 | tf_op jit(solution)/shard_map/ppermute | solution.py:25
  835.4 54.4 %collective-permute-start.77 = (bf16[128,256]{1,0:T(8,128)(2,1)S(1)}, bf16[128,256]{1,0:T(8,128)(2,1)S(1)}, u32[]{:S(2)}, u32[]{:S(2)}) collective-permute-start(bf16[128,256]{1,0:T(8,128)(2,1)S(1)} %convolution_convert_fusion.29), channel_id=1, source_target_pairs={{0,8},{8,0},{16,24},{24,16},{1,9},{9,1},{17,25},{25,17},{2,10},{10... | collective-permute-start | bytes 196616 | tf_op jit(solution)/shard_map/ppermute | solution.py:25
  866.0 24.3 %collective-permute-start.78 = (bf16[128,256]{1,0:T(8,128)(2,1)S(1)}, bf16[128,256]{1,0:T(8,128)(2,1)S(1)}, u32[]{:S(2)}, u32[]{:S(2)}) collective-permute-start(bf16[128,256]{1,0:T(8,128)(2,1)S(1)} %convolution_convert_fusion.28), channel_id=1, source_target_pairs={{0,16},{8,24},{16,0},{24,8},{1,17},{9,25},{17,1},{25,9},{2,18},{10... | collective-permute-start | bytes 196616 | tf_op jit(solution)/shard_map/ppermute | solution.py:25
  867.5 22.9 %collective-permute-start.79 = (bf16[128,256]{1,0:T(8,128)(2,1)S(1)}, bf16[128,256]{1,0:T(8,128)(2,1)S(1)}, u32[]{:S(2)}, u32[]{:S(2)}) collective-permute-start(bf16[128,256]{1,0:T(8,128)(2,1)S(1)} %convolution_convert_fusion.27), channel_id=1, source_target_pairs={{0,24},{8,16},{16,8},{24,0},{1,25},{9,17},{17,9},{25,1},{2,26},{10... | collective-permute-start | bytes 196616 | tf_op jit(solution)/shard_map/ppermute | solution.py:25
  889.6 24.9 %collective-permute-start.101 = (bf16[256,4096]{1,0:T(8,128)(2,1)S(1)}, bf16[256,4096]{1,0:T(8,128)(2,1)S(1)}, u32[]{:S(2)}, u32[]{:S(2)}) collective-permute-start(bf16[256,4096]{1,0:T(8,128)(2,1)S(1)} %copy-done.85), channel_id=1, source_target_pairs={{0,8},{8,0},{16,24},{24,16},{1,9},{9,1},{17,25},{25,17},{2,10},{10... | collective-permute-start | bytes 6291464 | tf_op jit(solution)/shard_map/ppermute | solution.py:25
  918.2 29.2 %collective-permute-start.114 = (bf16[1024,768]{0,1:T(8,128)(2,1)S(1)}, bf16[1024,768]{0,1:T(8,128)(2,1)S(1)}, u32[]{:S(2)}, u32[]{:S(2)}) collective-permute-start(bf16[1024,768]{0,1:T(8,128)(2,1)S(1)} %copy-done.184), channel_id=1, source_target_pairs={{0,8},{8,0},{16,24},{24,16},{1,9},{9,1},{17,25},{25,17},{2,10},{10... | collective-permute-start | bytes 4718600 | tf_op jit(solution)/shard_map/ppermute | solution.py:25
  918.2 45.9 %collective-permute-start.100 = (bf16[256,4096]{1,0:T(8,128)(2,1)S(1)}, bf16[256,4096]{1,0:T(8,128)(2,1)S(1)}, u32[]{:S(2)}, u32[]{:S(2)}) collective-permute-start(bf16[256,4096]{1,0:T(8,128)(2,1)S(1)} %convolution_convert_fusion.1), channel_id=1, source_target_pairs={{0,8},{8,0},{16,24},{24,16},{1,9},{9,1},{17,25},{25,17},{2,10},{10... | collective-permute-start | bytes 6291464 | tf_op jit(solution)/shard_map/ppermute | solution.py:25
  925.7 37.3 %collective-permute-start.116 = (bf16[1024,768]{0,1:T(8,128)(2,1)S(1)}, bf16[1024,768]{0,1:T(8,128)(2,1)S(1)}, u32[]{:S(2)}, u32[]{:S(2)}) collective-permute-start(bf16[1024,768]{0,1:T(8,128)(2,1)S(1)} %add_convert_fusion.2), channel_id=1, source_target_pairs={{0,16},{8,24},{16,0},{24,8},{1,17},{9,25},{17,1},{25,9},{2,18},{10... | collective-permute-start | bytes 4718600 | tf_op jit(solution)/shard_map/ppermute | solution.py:25
  926.5 79.3 %collective-permute-start.102 = (bf16[256,4096]{1,0:T(8,128)(2,1)S(1)}, bf16[256,4096]{1,0:T(8,128)(2,1)S(1)}, u32[]{:S(2)}, u32[]{:S(2)}) collective-permute-start(bf16[256,4096]{1,0:T(8,128)(2,1)S(1)} %fusion.15), channel_id=1, source_target_pairs={{0,16},{8,24},{16,0},{24,8},{1,17},{9,25},{17,1},{25,9},{2,18},{10... | collective-permute-start | bytes 6291464 | tf_op jit(solution)/shard_map/ppermute | solution.py:25
  946.3 61.3 %collective-permute-start.125 = (bf16[256,128]{1,0:T(8,128)(2,1)S(1)}, bf16[256,128]{1,0:T(8,128)(2,1)S(1)}, u32[]{:S(2)}, u32[]{:S(2)}) collective-permute-start(bf16[256,128]{1,0:T(8,128)(2,1)S(1)} %get-tuple-element.154), channel_id=1, source_target_pairs={{0,2},{1,3},{2,0},{3,1},{4,6},{5,7},{6,4},{7,5},{8,10},{9,11},{10,... | collective-permute-start | bytes 196616 | tf_op jit(solution)/shard_map/ppermute | solution.py:29
  947.4 60.3 %collective-permute-start.127 = (bf16[256,128]{1,0:T(8,128)(2,1)S(1)}, bf16[256,128]{1,0:T(8,128)(2,1)S(1)}, u32[]{:S(2)}, u32[]{:S(2)}) collective-permute-start(bf16[256,128]{1,0:T(8,128)(2,1)S(1)} %get-tuple-element.155), channel_id=1, source_target_pairs={{0,6},{1,7},{2,4},{3,5},{4,2},{5,3},{6,0},{7,1},{8,14},{9,15},{10,... | collective-permute-start | bytes 196616 | tf_op jit(solution)/shard_map/ppermute | solution.py:29
  963.0 46.7 %collective-permute-start.126 = (bf16[256,128]{1,0:T(8,128)(2,1)S(1)}, bf16[256,128]{1,0:T(8,128)(2,1)S(1)}, u32[]{:S(2)}, u32[]{:S(2)}) collective-permute-start(bf16[256,128]{1,0:T(8,128)(2,1)S(1)} %get-tuple-element.156), channel_id=1, source_target_pairs={{0,4},{1,5},{2,6},{3,7},{4,0},{5,1},{6,2},{7,3},{8,12},{9,13},{10,... | collective-permute-start | bytes 196616 | tf_op jit(solution)/shard_map/ppermute | solution.py:29
  964.1 55.0 %collective-permute-start.117 = (bf16[512,768]{0,1:T(8,128)(2,1)S(1)}, bf16[512,768]{0,1:T(8,128)(2,1)S(1)}, u32[]{:S(2)}, u32[]{:S(2)}) collective-permute-start(bf16[512,768]{0,1:T(8,128)(2,1)S(1)} %split.270), channel_id=1, source_target_pairs={{0,1},{1,0},{2,3},{3,2},{4,5},{5,4},{6,7},{7,6},{8,9},{9,8},{10,11... | collective-permute-start | bytes 2359304 | tf_op jit(solution)/shard_map/ppermute | solution.py:29
  1006.9 23.1 %collective-permute-start.103 = (bf16[256,2048]{1,0:T(8,128)(2,1)S(1)}, bf16[256,2048]{1,0:T(8,128)(2,1)S(1)}, u32[]{:S(2)}, u32[]{:S(2)}) collective-permute-start(bf16[256,2048]{1,0:T(8,128)(2,1)S(1)} %split.262), channel_id=1, source_target_pairs={{0,1},{1,0},{2,3},{3,2},{4,5},{5,4},{6,7},{7,6},{8,9},{9,8},{10,11... | collective-permute-start | bytes 3145736 | tf_op jit(solution)/shard_map/ppermute | solution.py:29
  1019.5 23.2 %collective-permute-start.118 = (bf16[128,768]{0,1:T(8,128)(2,1)S(1)}, bf16[128,768]{0,1:T(8,128)(2,1)S(1)}, u32[]{:S(2)}, u32[]{:S(2)}) collective-permute-start(bf16[128,768]{0,1:T(8,128)(2,1)S(1)} %get-tuple-element.127), channel_id=1, source_target_pairs={{0,2},{1,3},{2,0},{3,1},{4,6},{5,7},{6,4},{7,5},{8,10},{9,11},{10,... | collective-permute-start | bytes 589832 | tf_op jit(solution)/shard_map/ppermute | solution.py:29
  1033.4 28.6 %collective-permute-start.119 = (bf16[128,768]{0,1:T(8,128)(2,1)S(1)}, bf16[128,768]{0,1:T(8,128)(2,1)S(1)}, u32[]{:S(2)}, u32[]{:S(2)}) collective-permute-start(bf16[128,768]{0,1:T(8,128)(2,1)S(1)} %get-tuple-element.129), channel_id=1, source_target_pairs={{0,4},{1,5},{2,6},{3,7},{4,0},{5,1},{6,2},{7,3},{8,12},{9,13},{10,... | collective-permute-start | bytes 589832 | tf_op jit(solution)/shard_map/ppermute | solution.py:29
  1033.4 29.6 %collective-permute-start.104 = (bf16[256,512]{1,0:T(8,128)(2,1)}, bf16[256,512]{1,0:T(8,128)(2,1)S(1)}, u32[]{:S(2)}, u32[]{:S(2)}) collective-permute-start(bf16[256,512]{1,0:T(8,128)(2,1)} %get-tuple-element.85), channel_id=1, source_target_pairs={{0,2},{1,3},{2,0},{3,1},{4,6},{5,7},{6,4},{7,5},{8,10},{9,11},{10,... | collective-permute-start | bytes 786440 | tf_op jit(solution)/shard_map/ppermute | solution.py:29
  1042.7 29.0 %collective-permute-start.105 = (bf16[256,512]{1,0:T(8,128)(2,1)S(1)}, bf16[256,512]{1,0:T(8,128)(2,1)S(1)}, u32[]{:S(2)}, u32[]{:S(2)}) collective-permute-start(bf16[256,512]{1,0:T(8,128)(2,1)S(1)} %get-tuple-element.87), channel_id=1, source_target_pairs={{0,4},{1,5},{2,6},{3,7},{4,0},{5,1},{6,2},{7,3},{8,12},{9,13},{10,... | collective-permute-start | bytes 786440 | tf_op jit(solution)/shard_map/ppermute | solution.py:29
  (260 other events, 3189.9 us)

commit v2 on v1

--- a/solution.py
+++ b/solution.py
@@ -113,24 +113,241 @@
     return zero + fix(swap(two, 2), 2).astype(F32)
 
 
-def copy_block(index_ref, in_ref, out_ref):
-    out_ref[...] = in_ref[...]
-
-
-def move_blocks(x, index):
-    rows = x.shape[0]
-    count = index.shape[0]
+def lane_block(i):
+    return pl.ds(pl.multiple_of(i * LANES, LANES), LANES)
+
+
+def reorder_tile(index_ref, in_ref, out_ref):
+    for i in range(in_ref.shape[1] // LANES):
+        out_ref[:, i * LANES : (i + 1) * LANES] = in_ref[:, lane_block(index_ref[i])]
+
+
+def reorder(x, index):
+    rows, width = x.shape
+    tile = rows // 4
+    block = pl.BlockSpec((tile, width), lambda i, index: (i, 0))
     return pl.pallas_call(
-        copy_block,
-        out_shape=jax.ShapeDtypeStruct((rows, count * LANES), x.dtype),
+        reorder_tile,
+        out_shape=jax.ShapeDtypeStruct(x.shape, x.dtype),
         grid_spec=pltpu.PrefetchScalarGridSpec(
-            num_scalar_prefetch=1,
-            grid=(count,),
-            in_specs=[pl.BlockSpec((rows, LANES), lambda i, index: (0, index[i]))],
-            out_specs=pl.BlockSpec((rows, LANES), lambda i, index: (0, i)),
+            num_scalar_prefetch=1, grid=(4,), in_specs=[block], out_specs=block
         ),
-        name="move_blocks",
+        name="reorder",
     )(index, x)
+
+
+def copy_two(index_a, index_b, a_ref, b_ref, out_a, out_b):
+    out_a[...] = a_ref[...].reshape(out_a.shape)
+    out_b[...] = b_ref[...].reshape(out_b.shape)
+
+
+def unpack_rows(packed, index_a, index_b):
+    _, _, n, w = packed.shape
+    shape = jax.ShapeDtypeStruct((8 * n, w), packed.dtype)
+    out = pl.BlockSpec((n, w), lambda i, a, b: (i, 0))
+    return pl.pallas_call(
+        copy_two,
+        out_shape=(shape, shape),
+        grid_spec=pltpu.PrefetchScalarGridSpec(
+            num_scalar_prefetch=2,
+            grid=(8,),
+            in_specs=[
+                pl.BlockSpec((1, 1, n, w), lambda i, a, b: (a[i], 0, 0, 0)),
+                pl.BlockSpec((1, 1, n, w), lambda i, a, b: (b[i], 1, 0, 0)),
+            ],
+            out_specs=(out, out),
+        ),
+        name="unpack_rows",
+    )(index_a, index_b, packed, packed)
+
+
+def copy_pair(index_a, index_b, a_ref, b_ref, out_ref):
+    out_ref[0, 0] = a_ref[...]
+    out_ref[0, 1] = b_ref[...]
+
+
+def pack_rows(a, b, index_a, index_b):
+    n, w = a.shape[0] // 8, a.shape[1]
+    return pl.pallas_call(
+        copy_pair,
+        out_shape=jax.ShapeDtypeStruct((8, 2, n, w), a.dtype),
+        grid_spec=pltpu.PrefetchScalarGridSpec(
+            num_scalar_prefetch=2,
+            grid=(8,),
+            in_specs=[
+                pl.BlockSpec((n, w), lambda i, a, b: (a[i], 0)),
+                pl.BlockSpec((n, w), lambda i, a, b: (b[i], 0)),
+            ],
+            out_specs=pl.BlockSpec((1, 2, n, w), lambda i, a, b: (i, 0, 0, 0)),
+        ),
+        name="pack_rows",
+    )(index_a, index_b, a, b)
+
+
+VMEM_ROOM = 48 * 1024 * 1024
+
+
+def enter_body(from_up, to_layer, up_ref, q0, q1, q2, q3, out_ref, held, spaced):
+    coarse = up_ref.shape[0]
+    quarter = q0.shape[1]
+    for j, ref in enumerate((q0, q1, q2, q3)):
+        held[:, j * quarter : (j + 1) * quarter] = ref[...]
+    for r in range(4):
+        for p in range(8):
+            spaced[p, pl.ds(r, coarse, stride=4), :] = up_ref[:, lane_block(from_up[r * 8 + p])]
+    for p in range(8):
+        out_ref[:, p * LANES : (p + 1) * LANES] = spaced[p] + held[
+            :, lane_block(to_layer[p])
+        ].astype(F32)
+
+
+def enter(up_terms, quarters, from_up, to_layer):
+    coarse, wide = up_terms.shape
+    whole = lambda shape: pl.BlockSpec(shape, lambda i, a, b: (0, 0))
+    tokens, quarter = quarters[0].shape
+    return pl.pallas_call(
+        enter_body,
+        out_shape=jax.ShapeDtypeStruct((tokens, wide // 4), F32),
+        grid_spec=pltpu.PrefetchScalarGridSpec(
+            num_scalar_prefetch=2,
+            grid=(1,),
+            in_specs=[whole((coarse, wide))] + [whole((tokens, quarter))] * 4,
+            out_specs=whole((tokens, wide // 4)),
+            scratch_shapes=[
+                pltpu.VMEM((tokens, wide // 4), BF16),
+                pltpu.VMEM((8, tokens, LANES), F32),
+            ],
+        ),
+        compiler_params=pltpu.CompilerParams(vmem_limit_bytes=VMEM_ROOM),
+        name="enter",
+    )(from_up, to_layer, up_terms, *quarters)
+
+
+def leave_body(to_up, to_quarters, in_ref, rows_ref, q0, q1, q2, q3, spaced):
+    coarse = rows_ref.shape[0]
+    for p in range(8):
+        spaced[p] = in_ref[:, p * LANES : (p + 1) * LANES]
+    for i in range(32):
+        source = to_up[i]
+        rows_ref[:, i * LANES : (i + 1) * LANES] = spaced[
+            source & 7, pl.ds(source >> 3, coarse, stride=4), :
+        ].astype(BF16)
+    for j, ref in enumerate((q0, q1, q2, q3)):
+        for half in range(2):
+            ref[:, half * LANES : (half + 1) * LANES] = in_ref[
+                :, lane_block(to_quarters[2 * j + half])
+            ].astype(BF16)
+
+
+def leave(grad, to_up, to_quarters):
+    tokens, width = grad.shape
+    whole = lambda shape: pl.BlockSpec(shape, lambda i, a, b: (0, 0))
+    shapes = [(tokens // 4, 4 * width)] + [(tokens, width // 4)] * 4
+    return pl.pallas_call(
+        leave_body,
+        out_shape=[jax.ShapeDtypeStruct(shape, BF16) for shape in shapes],
+        grid_spec=pltpu.PrefetchScalarGridSpec(
+            num_scalar_prefetch=2,
+            grid=(1,),
+            in_specs=[whole((tokens, width))],
+            out_specs=[whole(shape) for shape in shapes],
+            scratch_shapes=[pltpu.VMEM((8, tokens, LANES), F32)],
+        ),
+        compiler_params=pltpu.CompilerParams(vmem_limit_bytes=VMEM_ROOM),
+        name="leave",
+    )(to_up, to_quarters, grad)
+
+
+TILE = 128
+SCALE = 1.0 / math.sqrt(HEAD)
+
+
+def by_head(x):
+    heads = x.shape[1] // HEAD
+    feature = lax.broadcasted_iota(jnp.int32, x.shape, 1) // HEAD
+    return jnp.concatenate(
+        [jnp.where(feature == h, x, jnp.zeros_like(x)) for h in range(heads)], axis=0
+    )
+
+
+def of_heads(x):
+    heads = x.shape[1] // HEAD
+    feature = lax.broadcasted_iota(jnp.int32, (TILE, x.shape[1]), 1) // HEAD
+    out = x[:TILE]
+    for h in range(1, heads):
+        out = jnp.where(feature == h, x[h * TILE : (h + 1) * TILE], out)
+    return out
+
+
+def visible(column, row):
+    i = lax.broadcasted_iota(jnp.int32, (TILE, TILE), 0)
+    j = lax.broadcasted_iota(jnp.int32, (TILE, TILE), 1)
+    return (column == row) & (i >= j) & (i // ROW == j // ROW)
+
+
+def soft(query, keys, allowed):
+    scores = dot_t(query, keys) * SCALE
+    probs = []
+    for h in range(scores.shape[1] // TILE):
+        part = jnp.where(allowed, scores[:, h * TILE : (h + 1) * TILE], NEG_FILL)
+        exps = jnp.exp(part - jnp.max(part, axis=1, keepdims=True))
+        probs.append(exps * (1.0 / jnp.sum(exps, axis=1, keepdims=True)))
+    return probs
+
+
+def attend_body(column_ref, row_ref, *refs):
+    allowed = visible(column_ref[...], row_ref[0])
+    for qkv_ref, out_ref in zip(refs[:4], refs[4:]):
+        n = out_ref.shape[1]
+        probs = soft(qkv_ref[:, :n], by_head(qkv_ref[:, n : 2 * n]), allowed)
+        low = jnp.concatenate([p.astype(BF16) for p in probs], axis=1)
+        out_ref[...] = dot(low, by_head(qkv_ref[:, 2 * n :])).astype(BF16)
+
+
+def attend_back_body(column_ref, row_ref, *refs):
+    allowed = visible(column_ref[...], row_ref[0])
+    for qkv_ref, grad_ref, out_ref in zip(refs[:4], refs[4:8], refs[8:]):
+        n = grad_ref.shape[1]
+        query, grad = qkv_ref[:, :n], grad_ref[...]
+        keys = by_head(qkv_ref[:, n : 2 * n])
+        probs = soft(query, keys, allowed)
+        grad_probs = dot_t(grad, by_head(qkv_ref[:, 2 * n :]))
+        grads = []
+        for h, p in enumerate(probs):
+            part = grad_probs[:, h * TILE : (h + 1) * TILE]
+            inner = jnp.sum(p * part, axis=1, keepdims=True)
+            grads.append((p * (part - inner)).astype(BF16))
+        grads = jnp.concatenate(grads, axis=1)
+        low = jnp.concatenate([p.astype(BF16) for p in probs], axis=1)
+        out_ref[:, :n] = (dot(grads, keys) * SCALE).astype(BF16)
+        out_ref[:, n : 2 * n] = (of_heads(gram(grads, query)) * SCALE).astype(BF16)
+        out_ref[:, 2 * n :] = of_heads(gram(low, grad)).astype(BF16)
+
+
+def tiled_call(body, segments, arrays, widths, name):
+    tokens = arrays[0].shape[0]
+    tiles = tokens // TILE
+    wide = lambda w: pl.BlockSpec((TILE, w), lambda i: (i, 0))
+    return pl.pallas_call(
+        body,
+        out_shape=[jax.ShapeDtypeStruct((tokens, w), BF16) for w in widths],
+        grid=(tiles,),
+        in_specs=[wide(1), pl.BlockSpec((1, 1, TILE), lambda i: (i, 0, 0))]
+        + [wide(a.shape[1]) for a in arrays],
+        out_specs=[wide(w) for w in widths],
+        compiler_params=pltpu.CompilerParams(vmem_limit_bytes=VMEM_ROOM),
+        name=name,
+    )(segments.reshape(tokens, 1), segments.reshape(tiles, 1, TILE), *arrays)
+
+
+def attend(qkv, segments):
+    return tiled_call(attend_body, segments, qkv, [q.shape[1] // 3 for q in qkv], "attend")
+
+
+def attend_back(qkv, grads, segments):
+    return tiled_call(
+        attend_back_body, segments, (*qkv, *grads), [q.shape[1] for q in qkv], "attend_back"
+    )
 
 
 def normalize(stream):
@@ -188,38 +405,18 @@
     return lax.psum_scatter(mine, "seq", scatter_dimension=1, tiled=True)
 
 
-def attend(qkv, allowed):
-    rows = qkv.shape[0] // ROW
-    width = qkv.shape[1] // 3
-    shape = (rows, ROW, width // HEAD, HEAD)
-    query, key, value = (qkv[:, i * width : (i + 1) * width].reshape(shape) for i in range(3))
-    scores = jnp.einsum("bqhd,bkhd->bhqk", query, key, preferred_element_type=F32) * (
-        1.0 / math.sqrt(HEAD)
-    )
-    scores = jnp.where(allowed, scores, NEG_FILL)
-    exps = jnp.exp(scores - jnp.max(scores, axis=-1, keepdims=True))
-    probs = exps / jnp.sum(exps, axis=-1, keepdims=True)
-    context = jnp.einsum("bhqk,bkhd->bqhd", probs.astype(BF16), value, preferred_element_type=F32)
-    return context.astype(BF16).reshape(qkv.shape[0], width), probs
-
-
-def attend_back(qkv, probs, grad_context):
-    rows = qkv.shape[0] // ROW
-    width = qkv.shape[1] // 3
-    shape = (rows, ROW, width // HEAD, HEAD)
-    query, key, value = (qkv[:, i * width : (i + 1) * width].reshape(shape) for i in range(3))
-    scale = 1.0 / math.sqrt(HEAD)
-    grad_context = grad_context.reshape(shape)
-    grad_probs = jnp.einsum("bqhd,bkhd->bhqk", grad_context, value, preferred_element_type=F32)
-    inner = jnp.sum(probs * grad_probs, axis=-1, keepdims=True)
-    grad_scores = (probs * (grad_probs - inner)).astype(BF16)
-    grads = (
-        jnp.einsum("bhqk,bkhd->bqhd", grad_scores, key, preferred_element_type=F32) * scale,
-        jnp.einsum("bhqk,bqhd->bkhd", grad_scores, query, preferred_element_type=F32) * scale,
-        jnp.einsum("bhqk,bqhd->bkhd", probs.astype(BF16), grad_context, preferred_element_type=F32),
-    )
-    return jnp.concatenate(
-        [g.astype(BF16).reshape(qkv.shape[0], width) for g in grads], axis=1
+def join_rows(packed):
+    pieces, _, n, w = packed.shape
+    return (
+        packed.reshape(8, pieces // 8, 2, n, w).swapaxes(1, 2).reshape(8, 2, n * pieces // 8, w)
+    )
+
+
+def split_rows(packed):
+    _, _, n, w = packed.shape
+    share = lax.axis_size("seq") // 8
+    return (
+        packed.reshape(8, 2, share, n // share, w).swapaxes(1, 2).reshape(8 * share, 2, n // share, w)
     )
 
 
@@ -260,6 +457,10 @@
     slot = jnp.arange(8, dtype=jnp.int32)
     to_layer = (((slot & 3) ^ turn) << 1) | ((slot >> 2) ^ x)
     to_quarters = (((slot & 1) ^ x) << 2) | ((slot >> 1) ^ turn)
+    natural_of_layer = (((slot & 3) ^ z) << 1) | ((slot >> 2) ^ x)
+    natural_of_quarters = (((slot >> 1) ^ c) << 1) | (slot & 1)
+    layer_of_natural = (((slot & 1) ^ x) << 2) | ((slot >> 1) ^ z)
+    quarters_of_natural = natural_of_quarters
 
     table = gather(embed_table, 0)
     conv = gather(conv_weight.reshape(3 * quarter, -1), 1)
@@ -268,18 +469,19 @@
     vectors = gather_vectors(jnp.stack([gain_one, shift_one, gain_two, shift_two]), c, z, x)
     qkv_w = spread(gather(qkv_weight.reshape(-1, 3 * quarter), 0))
     out_w = spread(gather(out_weight, 1))
-    in_w = gather(in_weight, 0)
-    down_w = move_blocks(gather(down_weight, 1), to_quarters)
+    mlp_w = lax.all_gather(jnp.stack([in_weight, down_weight.T]), "seq", axis=0)
+    mlp_w = join_rows(mlp_w)
+    in_w, down_t = unpack_rows(mlp_w, natural_of_layer, natural_of_quarters)
     gain1, shift1, gain2, shift2 = (vectors[i][None, :] for i in range(4))
 
     mine = pick([inputs[i] for i in range(4)], c)
-    stream_in = move_blocks(jnp.concatenate(exchange(mine), axis=1), to_layer)
+    stream_in = exchange(mine)
     cot = jnp.concatenate(pick([cotangent[i] for i in range(4)], c), axis=0)
     cots = [item.reshape(micros, tokens, quarter) for item in spread(cot)]
     cot_all = jnp.concatenate(
         [jnp.concatenate([cots[j][m ^ j] for m in range(4)], axis=0) for j in range(4)], axis=1
     )
-    cot_mine = move_blocks(cot_all[:tokens], to_layer)
+    cot_mine = reorder(cot_all[:tokens], to_layer)
 
     ids = jnp.concatenate(pick([coarse_ids[i] for i in range(4)], c))
     vocab = table.shape[0]
@@ -313,18 +515,12 @@
     h = kx ^ x
     bz2, bx2 = (h << 1) | (w >> 1), w & 1
     to_up = (kz ^ z) * 8 + ((bx2 ^ x) << 2 | (bz2 ^ z))
-    up_terms = move_blocks(up_terms, from_up).reshape(tokens, width)
-    stream_zero = stream_in.astype(F32) + up_terms
+    stream_zero = enter(up_terms, stream_in, from_up, to_layer)
     normed_one, rstd_one = normalize(stream_zero)
     norm_one = (normed_one * gain1 + shift1).astype(BF16)
     segments = lax.dynamic_index_in_dim(segment_ids, c, 0, keepdims=False)
-    rows = segments.reshape(tokens // ROW, ROW)
-    spots = jnp.arange(ROW)
-    allowed = (
-        (rows[:, :, None] == rows[:, None, :]) & (spots[:, None] >= spots[None, :])[None]
-    )[:, None]
     qkv = [dot(norm_one, qkv_w[j]).astype(BF16) for j in range(4)]
-    context, probs = zip(*[attend(qkv[j], allowed) for j in range(4)])
+    context = attend(qkv, segments)
     stream_one = stream_zero
     for j in range(4):
         stream_one = stream_one + dot(context[j], out_w[j])
@@ -334,10 +530,9 @@
     norm_all = jnp.concatenate(spread(norm_two), axis=0)
     mlp_pre = dot(norm_all, in_w)
     mlp_act = gelu(mlp_pre).astype(BF16)
-    grad_down = gram(mlp_act, cot_all).astype(BF16)
-    grad_down = scatter(move_blocks(grad_down, to_layer), 1)
-    mlp_out = dot(mlp_act, down_w)
-    stream_q = move_blocks(stream_one, to_quarters)
+    grad_down = gram(cot_all, mlp_act).astype(BF16)
+    mlp_out = dot_t(mlp_act, down_t)
+    stream_q = reorder(stream_one, to_quarters)
     mlp_out = mlp_out.reshape(micros, tokens, width)
     mlp_out = jnp.concatenate([(mlp_out[0] + stream_q)[None], mlp_out[1:]], axis=0)
     result = fold(
@@ -346,8 +541,11 @@
     ).astype(BF16)
     result = jnp.stack(pick([result[m] for m in range(4)], c))
 
-    grad_pre = (gelu_grad(mlp_pre) * dot_t(cot_all, down_w)).astype(BF16)
-    grad_in = scatter(gram(norm_all, grad_pre), 0)
+    grad_pre = (gelu_grad(mlp_pre) * dot(cot_all, down_t)).astype(BF16)
+    grad_in = gram(norm_all, grad_pre).astype(BF16)
+    grad_mlp = pack_rows(grad_in, grad_down, layer_of_natural, quarters_of_natural)
+    grad_mlp = lax.psum_scatter(split_rows(grad_mlp), "seq", scatter_dimension=0, tiled=False)
+    grad_in, grad_down = grad_mlp[0].astype(F32), grad_mlp[1].astype(F32).T
     grad_norm_two = dot_t(grad_pre, in_w).reshape(micros, tokens, width)
     grad_norm_two = fold([grad_norm_two[j] for j in range(4)])
 
@@ -355,23 +553,19 @@
     grad_stream_one = cot_mine.astype(F32) + back_two
     grad_att = grad_stream_one.astype(BF16)
     grad_out = scatter(fold([gram(context[j], grad_att) for j in range(4)]), 1)
-    grad_rows = [
-        attend_back(qkv[j], probs[j], dot_t(grad_att, out_w[j]).astype(BF16)) for j in range(4)
-    ]
+    grad_context = [dot_t(grad_att, out_w[j]).astype(BF16) for j in range(4)]
+    grad_rows = attend_back(qkv, grad_context, segments)
     grad_qkv = scatter(fold([gram(norm_one, grad_rows[j]) for j in range(4)]), 0)
     grad_norm_one = dot_t(grad_rows[0], qkv_w[0])
     for j in (1, 2, 3):
         grad_norm_one = grad_norm_one + dot_t(grad_rows[j], qkv_w[j])
     back_one, grad_gain1, grad_shift1 = normalize_back(normed_one, rstd_one, gain1, grad_norm_one)
-    input_grad = (grad_stream_one + back_one).astype(BF16)
+    input_grad = grad_stream_one + back_one
     grad_vectors = scatter_vectors(
         jnp.stack([grad_gain1, grad_shift1, grad_gain2, grad_shift2]), c, z, x
     )
-    grad_in_q = move_blocks(input_grad, to_quarters)
-    grad_in_q = exchange([grad_in_q[:, j * quarter : (j + 1) * quarter] for j in range(4)])
-    input_grads = jnp.stack(pick(grad_in_q, c))
-
-    grad_up_rows = move_blocks(input_grad.reshape(coarse, 4 * width), to_up)
+    grad_up_rows, *grad_in_q = leave(input_grad, to_up, to_quarters)
+    input_grads = jnp.stack(pick(exchange(grad_in_q), c))
     grad_up = scatter(fold([gram(hidden[j], grad_up_rows) for j in range(4)]), 1)
     grad_hidden = [dot_t(grad_up_rows, up[j]).astype(BF16) for j in range(4)]
     grad_res = scatter(fold([gram(mixed, grad_hidden[j]) for j in range(4)]), 0)

time: 1090 us -> 800 us (0.73)
  local copies, waits for them, and re-layouts: 172 us -> 58 us
  matrix products: 179 us -> 107 us
  other arithmetic: 119 us -> 62.1 us
  Pallas kernels: 70.8 us -> 46.2 us
  starting transfers between devices: 144 us -> 120 us
  between operations: 4.03 us -> 17 us
    reshape x46 -> x2, local copies, waits for them, and re-layouts: 75.3 us -> 0.85 us  [the longest x1 0.71 us: tiled_call(): segments.reshape(tiles, 1, TILE)]
    concatenate x1, other arithmetic: 49.2 us -> 11.5 us  [on_device(): jnp.concatenate([jnp.concatenate([cots[j][m ^ j] for m in range(4)], axis...]
    dot_general x24 -> x0, matrix products: 36.2 us -> none  [the longest x4 11.9 us: attend_back(): jnp.einsum('bhqk,bqhd->bkhd', probs.astype(BF16), grad_context, preferred...]
    dot_general x59, matrix products: 141 us -> 106 us  [dot(): return lax.dot_general(a, b, (dims, ((), ())), preferred_element_type=F32)]
    ppermute x60, waiting for transfers between devices: 149 us -> 183 us  [swap(): return lax.ppermute(x, 'cond', [(i, i ^ j) for i in range(4)])]
    ppermute x2, waiting for transfers between devices: 32.5 us -> 0.01 us  [edges(): lax.ppermute(tail, 'seq', [(i, i + 1) for i in range(count - 1)])]
    ppermute x72 -> x56, starting transfers between devices: 104 us -> 76.7 us  [hop(): return lax.ppermute(x, 'seq', [(i, i ^ k) for i in range(8)])]
    pallas_call x8, Pallas kernels: 70.8 us -> 46.2 us  [the longest x2 20.2 us: tiled_call(): pl.pallas_call(body, out_shape=[jax.ShapeDtypeStruct((tokens, w), BF16) f...]
  transfers between devices with their start and end apart: 136 -> 122, of which waited for: 42 -> 42; matrix products, arithmetic and copies ran while one was open for 39% -> 23% of each run, Pallas kernels for 6% -> 6%
where the time goes in v2:
time: 800 us; the launch traced here: 794 us
  waiting for transfers between devices  382 us (48%)
  starting transfers between devices  120 us (15%)
  matrix products  107 us (13%)
  other arithmetic  62.1 us (8%)
  local copies, waits for them, and re-layouts  58 us (7%)
  Pallas kernels  46.2 us (6%)
  between operations  17 us (2%)
    ppermute x56, waiting for transfers between devices, hop(): return lax.ppermute(x, 'seq', [(i, i ^ k) for i in range(8)])  195 us
    ppermute x60, waiting for transfers between devices, swap(): return lax.ppermute(x, 'cond', [(i, i ^ j) for i in range(4)])  183 us
    dot_general x59, matrix products, dot(): return lax.dot_general(a, b, (dims, ((), ())), preferred_element_type=F32)  106 us
    ppermute x56, starting transfers between devices, hop(): return lax.ppermute(x, 'seq', [(i, i ^ k) for i in range(8)])  76.7 us
    unnamed x332, local copies, waits for them, and re-layouts  35.6 us
    ppermute x60, starting transfers between devices, swap(): return lax.ppermute(x, 'cond', [(i, i ^ j) for i in range(4)])  33.7 us
    pallas_call x2, Pallas kernels, tiled_call(): pl.pallas_call(body, out_shape=[jax.ShapeDtypeStruct((tokens, w), BF16) f...  20.2 us
  transfers between devices with their start and end apart: 122, of which 42 were waited for; matrix products, arithmetic and copies ran while one was open for 23% of the time, Pallas kernels for 6%

profile of v2, /device:TPU:0, one launch (start us, length us, event | category | flops | bytes accessed | tf_op | source)
XLA Modules:
  0.0 793.5 jit_solution(8685909125486951871)
XLA Ops:
  8.1 5.1 collective-permute-start.35
  13.9 3.7 collective-permute-start.15
  43.0 3.9 collective-permute-start.49
  55.3 2.9 collective-permute-start.2
  64.2 2.9 collective-permute-start.42
  71.0 9.0 %collective-permute-done = bf16[256,256]{1,0:T(8,128)(2,1)S(1)} collective-permute-done((bf16[256,256]{1,0:T(8,128)(2,1)S(1)}, bf16[256,256]{1,0:T(8,128)(2,1)S(1)}, u32[]{:S(2)}, u32[]{:S(2)}) %collective-permute-start) | collective-permute-done | bytes 131104 | tf_op jit(solution)/shard_map/ppermute | solution.py:29
  80.7 9.8 %collective-permute-done.1 = bf16[256,256]{1,0:T(8,128)(2,1)S(1)} collective-permute-done((bf16[256,256]{1,0:T(8,128)(2,1)S(1)}, bf16[256,256]{1,0:T(8,128)(2,1)S(1)}, u32[]{:S(2)}, u32[]{:S(2)}) %collective-permute-start.1) | collective-permute-done | bytes 131104 | tf_op jit(solution)/shard_map/ppermute | solution.py:29
  91.9 8.8 %collective-permute-done.40 = bf16[128,768]{0,1:T(8,128)(2,1)S(1)} collective-permute-done((bf16[128,768]{0,1:T(8,128)(2,1)S(1)}, bf16[128,768]{0,1:T(8,128)(2,1)S(1)}, u32[]{:S(2)}, u32[]{:S(2)}) %collective-permute-start.40) | collective-permute-done | bytes 196640 | tf_op jit(solution)/shard_map/ppermute | solution.py:29
  104.0 22.8 %collective-permute-done.41 = bf16[128,768]{0,1:T(8,128)(2,1)S(1)} collective-permute-done((bf16[128,768]{0,1:T(8,128)(2,1)}, bf16[128,768]{0,1:T(8,128)(2,1)S(1)}, u32[]{:S(2)}, u32[]{:S(2)}) %collective-permute-start.41) | collective-permute-done | bytes 196640 | tf_op jit(solution)/shard_map/ppermute | solution.py:29
  127.6 4.4 collective-permute-start.17
  133.7 15.0 %collective-permute-done.7 = bf16[768,128]{1,0:T(8,128)(2,1)S(1)} collective-permute-done((bf16[768,128]{1,0:T(8,128)(2,1)}, bf16[768,128]{1,0:T(8,128)(2,1)S(1)}, u32[]{:S(2)}, u32[]{:S(2)}) %collective-permute-start.7) | collective-permute-done | bytes 196640 | tf_op jit(solution)/shard_map/ppermute | solution.py:29
  150.9 8.0 %collective-permute-done.18 = bf16[256,512]{1,0:T(8,128)(2,1)S(1)} collective-permute-done((bf16[256,512]{1,0:T(8,128)(2,1)S(1)}, bf16[256,512]{1,0:T(8,128)(2,1)S(1)}, u32[]{:S(2)}, u32[]{:S(2)}) %collective-permute-start.18) | collective-permute-done | bytes 262176 | tf_op jit(solution)/shard_map/ppermute | solution.py:29
  160.8 2.8 collective-permute-done.3
  165.2 3.4 collective-permute-start.4
  170.4 30.6 %collective-permute-done.20 = bf16[256,2048]{1,0:T(8,128)(2,1)S(1)} collective-permute-done((bf16[256,2048]{1,0:T(8,128)(2,1)S(1)}, bf16[256,2048]{1,0:T(8,128)(2,1)S(1)}, u32[]{:S(2)}, u32[]{:S(2)}) %collective-permute-start.20) | collective-permute-done | bytes 1048608 | tf_op jit(solution)/shard_map/ppermute | solution.py:29
  208.6 4.0 collective-permute-done.50
  213.9 11.0 %collective-permute-done.43 = bf16[512,768]{0,1:T(8,128)(2,1)S(1)} collective-permute-done((bf16[512,768]{0,1:T(8,128)(2,1)S(1)}, bf16[512,768]{0,1:T(8,128)(2,1)S(1)}, u32[]{:S(2)}, u32[]{:S(2)}) %collective-permute-start.43) | collective-permute-done | bytes 786464 | tf_op jit(solution)/shard_map/ppermute | solution.py:29
  227.2 32.0 %collective-permute-done.25 = bf16[1024,256]{1,0:T(8,128)(2,1)S(1)} collective-permute-done((bf16[1024,256]{1,0:T(8,128)(2,1)S(1)}, bf16[1024,256]{1,0:T(8,128)(2,1)S(1)}, u32[]{:S(2)}, u32[]{:S(2)}) %collective-permute-start.25) | collective-permute-done | bytes 524320 | tf_op jit(solution)/shard_map/ppermute | solution.py:25
  264.8 4.3 collective-permute-done.27
  281.2 32.5 %collective-permute-done.31.q2 = bf16[512,256]{1,0:T(8,128)(2,1)S(1)} collective-permute-done((bf16[512,256]{1,0:T(8,128)(2,1)S(1)}, bf16[512,256]{1,0:T(8,128)(2,1)S(1)}, u32[]{:S(2)}, u32[]{:S(2)}) %collective-permute-start.31) | collective-permute-done | bytes 262176 | tf_op jit(solution)/shard_map/ppermute | solution.py:25
  316.9 2.8 convolution_convert_fusion.10.refs_0_
  322.2 24.4 %collective-permute-done.52 = bf16[256,1024]{1,0:T(8,128)(2,1)} collective-permute-done((bf16[256,1024]{1,0:T(8,128)(2,1)}, bf16[256,1024]{1,0:T(8,128)(2,1)}, u32[]{:S(2)}, u32[]{:S(2)}) %collective-permute-start.52) | collective-permute-done | bytes 524320 | tf_op jit(solution)/shard_map/ppermute | solution.py:25
  349.6 2.7 convolution_convert_fusion.9.refs_1_
  352.4 7.2 attend.1
  371.9 9.6 %maximum_maximum_fusion.1.in_ref = bf16[512,1024]{1,0:T(8,128)(2,1)} fusion(bf16[512,256]{1,0:T(8,128)(2,1)S(1)} %get-tuple-element.127, bf16[512,256]{1,0:T(8,128)(2,1)S(1)} %get-tuple-element.128, bf16[1024,256]{1,0:T(8,128)(2,1)S(1)} %get-tuple-element.125, bf16[1024,256]{1,0:T(8,128)(2,1)S(1)} %get-tuple-element.124, ...), kind=kLoop, calls=%fused_computation.98 | loop fusion | flops 14680064 | bytes 5242880 | tf_op jit(solution)/shard_map/slice | solution.py:484
  381.5 4.1 reorder.3
  385.8 6.5 collective-permute-done.55
  392.3 11.5 %maximum_maximum_fusion = bf16[2048,1024]{1,0:T(8,128)(2,1)} fusion(bf16[512,256]{1,0:T(8,128)(2,1)} %copy-done.61, bf16[512,256]{1,0:T(8,128)(2,1)} %copy-done.62, bf16[512,256]{1,0:T(8,128)(2,1)} %copy-done.63, bf16[512,256]{1,0:T(8,128)(2,1)} %copy-done.60, bf16[1024,256]{1,0:T(8,128)(2,1)} %copy-done.40, bf16[1024,256]{1,0:T(8,128)(2,1)} %copy-done.39, ...), kind=kLoop, calls=%fused_computation.27 | loop fusion | flops 58720256 | bytes 8388608 | tf_op jit(solution)/shard_map/concatenate | solution.py:481
  403.8 4.5 reorder.2
  408.3 7.3 unpack_rows.1
  415.6 8.2 %fusion.34 = f32[2048,1024]{1,0:T(8,128)S(1)} fusion(bf16[1024,1024]{1,0:T(8,128)(2,1)} %get-tuple-element.33, bf16[512,1024]{1,0:T(8,128)(2,1)} %collective-permute-done.56, bf16[512,1024]{1,0:T(8,128)(2,1)} %collective-permute-done.55, bf16[512,1024]{1,0:T(8,128)(2,1)} %collective-permute-done.54, bf16[512,1024]{1,0:T(8,128)(2,1)} %add_convert_fusion.3), kind=kOutput, calls=%fused_computation.114 | convolution fusion | flops 4311744512 | bytes 14680064 | tf_op jit(solution)/shard_map/dot_general | solution.py:42
  423.9 9.5 %fusion.5 = (bf16[2048,1024]{1,0:T(8,128)(2,1)}, bf16[2048,1024]{1,0:T(8,128)(2,1)S(1)}) fusion(f32[2048,1024]{1,0:T(8,128)S(1)} %fusion.34, bf16[2048,1024]{1,0:T(8,128)(2,1)S(1)} %copy-done.42, bf16[1024,1024]{1,0:T(8,128)(2,1)S(1)} %copy-done.144), kind=kOutput, calls=%fused_computation.11 | convolution fusion | flops 4322230272 | bytes 23068672 | tf_op jit(solution)/shard_map/dot_general | solution.py:42
  435.4 4.7 fusion.151
  447.3 6.6 fusion.144
  455.6 3.6 copy-done.148
  459.2 8.3 %convolution_convert_fusion.3.a_ref = bf16[1024,1024]{1,0:T(8,128)(2,1)} fusion(bf16[2048,1024]{1,0:T(8,128)(2,1)S(1)} %copy-done.148, bf16[512,1024]{1,0:T(8,128)(2,1)} %collective-permute-done.56, bf16[512,1024]{1,0:T(8,128)(2,1)} %collective-permute-done.55, bf16[512,1024]{1,0:T(8,128)(2,1)} %collective-permute-done.54, ...), kind=kOutput, calls=%fused_computation.65 | convolution fusion | flops 4312793088 | bytes 10485760 | tf_op jit(solution)/shard_map/dot_general | solution.py:42
  470.1 5.9 convolution_convert_fusion.2.b_ref
  476.0 7.3 pack_rows.1
  485.2 2.8 fusion.22
  491.2 4.0 collective-permute-done.65
  495.2 3.9 multiply_reduce_fusion
  508.5 13.0 %attend_back.1 = (bf16[512,768]{1,0:T(8,128)(2,1)S(1)}, bf16[512,768]{1,0:T(8,128)(2,1)S(1)}, bf16[512,768]{1,0:T(8,128)(2,1)S(1)}, bf16[512,768]{1,0:T(8,128)(2,1)S(1)}) custom-call(s32[512,1]{1,0:T(8,128)S(1)} %copy.66.column_ref, s32[4,1,128]{2,1,0:T(1,128)S(1)} %get-tuple-element.194.row_ref, bf16[512,768]{1,0:T(8,128)(2,1)S(1)} %convolution_convert_fusion.10.refs_0_, ...), custom_call_target="tpu_custom_call" | custom-call | tf_op jit(solution)/shard_map/attend_back/pallas_call | solution.py:331
  521.6 3.3 fusion.152
  531.9 3.2 multiply_reduce_fusion.1
  563.4 2.6 collective-permute-start.102
  567.6 3.3 collective-permute-start.103
  574.3 3.1 collective-permute-done.105
  581.0 5.5 collective-permute-done.73
  589.7 3.5 collective-permute-start.76
  596.6 4.3 collective-permute-done.75
  604.2 2.7 collective-permute-start.77
  607.4 8.6 %collective-permute-done.115 = bf16[256,1024]{1,0:T(8,128)(2,1)S(1)} collective-permute-done((bf16[256,1024]{1,0:T(8,128)(2,1)S(1)}, bf16[256,1024]{1,0:T(8,128)(2,1)S(1)}, u32[]{:S(2)}, u32[]{:S(2)}) %collective-permute-start.115) | collective-permute-done | bytes 524320 | tf_op jit(solution)/shard_map/ppermute | solution.py:25
  626.6 2.8 collective-permute-done.87
  632.7 3.8 collective-permute-done.79
  639.6 10.8 %collective-permute-done.81 = bf16[768,512]{1,0:T(8,128)(2,1)S(1)} collective-permute-done((bf16[768,512]{1,0:T(8,128)(2,1)S(1)}, bf16[768,512]{1,0:T(8,128)(2,1)S(1)}, u32[]{:S(2)}, u32[]{:S(2)}) %collective-permute-start.81) | collective-permute-done | bytes 786464 | tf_op jit(solution)/shard_map/ppermute | solution.py:29
  652.7 5.5 collective-permute-done.88
  661.0 12.8 %collective-permute-done.108 = bf16[1024,768]{0,1:T(8,128)(2,1)S(1)} collective-permute-done((bf16[1024,768]{0,1:T(8,128)(2,1)S(1)}, bf16[1024,768]{0,1:T(8,128)(2,1)S(1)}, u32[]{:S(2)}, u32[]{:S(2)}) %collective-permute-start.108) | collective-permute-done | bytes 1572896 | tf_op jit(solution)/shard_map/ppermute | solution.py:25
  675.7 41.3 %collective-permute-done.94 = bf16[256,4096]{1,0:T(8,128)(2,1)S(1)} collective-permute-done((bf16[256,4096]{1,0:T(8,128)(2,1)S(1)}, bf16[256,4096]{1,0:T(8,128)(2,1)S(1)}, u32[]{:S(2)}, u32[]{:S(2)}) %collective-permute-start.94) | collective-permute-done | bytes 2097184 | tf_op jit(solution)/shard_map/ppermute | solution.py:25
  731.6 10.0 %collective-permute-done.95 = bf16[256,2048]{1,0:T(8,128)(2,1)S(1)} collective-permute-done((bf16[256,2048]{1,0:T(8,128)(2,1)S(1)}, bf16[256,2048]{1,0:T(8,128)(2,1)S(1)}, u32[]{:S(2)}, u32[]{:S(2)}) %collective-permute-start.95) | collective-permute-done | bytes 1048608 | tf_op jit(solution)/shard_map/ppermute | solution.py:29
  743.1 4.3 collective-permute-start.96
  747.3 3.8 collective-permute-done.83
  751.1 3.0 collective-permute-start.98
  755.0 18.0 %collective-permute-done.111 = bf16[128,768]{0,1:T(8,128)(2,1)S(1)} collective-permute-done((bf16[128,768]{0,1:T(8,128)(2,1)S(1)}, bf16[128,768]{0,1:T(8,128)(2,1)S(1)}, u32[]{:S(2)}, u32[]{:S(2)}) %collective-permute-start.111) | collective-permute-done | bytes 196640 | tf_op jit(solution)/shard_map/ppermute | solution.py:29
  774.0 8.7 %collective-permute-done.97 = bf16[256,512]{1,0:T(8,128)(2,1)S(1)} collective-permute-done((bf16[256,512]{1,0:T(8,128)(2,1)S(1)}, bf16[256,512]{1,0:T(8,128)(2,1)S(1)}, u32[]{:S(2)}, u32[]{:S(2)}) %collective-permute-start.97) | collective-permute-done | bytes 262176 | tf_op jit(solution)/shard_map/ppermute | solution.py:29
  (723 shorter events, 236.1 us)
Async XLA Ops:
  7.2 401.1 %all-gather.3.cloned.1.call-start = ((), (), s32[]{:S(2)}) async-start(), calls=%async_computation.2 | async-start | bytes 4718592 | tf_op jit(solution)/shard_map/all_gather | solution.py:472
  8.1 25.3 %collective-permute-start.35 = (bf16[4,32]{1,0:T(4,128)(2,1)S(1)}, bf16[4,32]{1,0:T(4,128)(2,1)}, u32[]{:S(2)}, u32[]{:S(2)}) collective-permute-start(bf16[4,32]{1,0:T(4,128)(2,1)S(1)} %pad_maximum_fusion.23), channel_id=1, source_target_pairs={{0,6},{1,7},{2,4},{3,5},{4,2},{5,3},{6,0},{7,1},{8,14},{9,15},{10,... | collective-permute-start | bytes 776 | tf_op jit(solution)/shard_map/ppermute | solution.py:29
  13.2 20.8 %collective-permute-start.34 = (bf16[4,32]{1,0:T(4,128)(2,1)S(1)}, bf16[4,32]{1,0:T(4,128)(2,1)}, u32[]{:S(2)}, u32[]{:S(2)}) collective-permute-start(bf16[4,32]{1,0:T(4,128)(2,1)S(1)} %pad_maximum_fusion.23), channel_id=1, source_target_pairs={{0,4},{1,5},{2,6},{3,7},{4,0},{5,1},{6,2},{7,3},{8,12},{9,13},{10,... | collective-permute-start | bytes 776 | tf_op jit(solution)/shard_map/ppermute | solution.py:29
  13.9 41.4 %collective-permute-start.15 = (bf16[128,256]{1,0:T(8,128)(2,1)}, bf16[128,256]{1,0:T(8,128)(2,1)}, u32[]{:S(2)}, u32[]{:S(2)}) collective-permute-start(bf16[128,256]{1,0:T(8,128)(2,1)} %param.22), channel_id=1, source_target_pairs={{0,6},{1,7},{2,4},{3,5},{4,2},{5,3},{6,0},{7,1},{8,14},{9,15},{10,... | collective-permute-start | bytes 196616 | tf_op jit(solution)/shard_map/ppermute | solution.py:29
  17.6 40.5 %collective-permute-start.14 = (bf16[128,256]{1,0:T(8,128)(2,1)}, bf16[128,256]{1,0:T(8,128)(2,1)}, u32[]{:S(2)}, u32[]{:S(2)}) collective-permute-start(bf16[128,256]{1,0:T(8,128)(2,1)} %param.22), channel_id=1, source_target_pairs={{0,4},{1,5},{2,6},{3,7},{4,0},{5,1},{6,2},{7,3},{8,12},{9,13},{10,... | collective-permute-start | bytes 196616 | tf_op jit(solution)/shard_map/ppermute | solution.py:29
  20.6 763.0 %reduce-scatter.2.cloned.1.call-start = ((), (), s32[]{:S(2)}) async-start(), calls=%async_computation.1 | async-start | bytes 4718592 | tf_op jit(solution)/shard_map/reduce_scatter | solution.py:547
  43.0 21.2 %collective-permute-start.49 = (bf16[256,128]{1,0:T(8,128)(2,1)}, bf16[256,128]{1,0:T(8,128)(2,1)}, u32[]{:S(2)}, u32[]{:S(2)}) collective-permute-start(bf16[256,128]{1,0:T(8,128)(2,1)} %param.27), channel_id=1, source_target_pairs={{0,6},{1,7},{2,4},{3,5},{4,2},{5,3},{6,0},{7,1},{8,14},{9,15},{10,... | collective-permute-start | bytes 196616 | tf_op jit(solution)/shard_map/ppermute | solution.py:29
  55.3 25.4 %collective-permute-start.2 = (bf16[256,256]{1,0:T(8,128)(2,1)S(1)}, bf16[256,256]{1,0:T(8,128)(2,1)S(1)}, u32[]{:S(2)}, u32[]{:S(2)}) collective-permute-start(bf16[256,256]{1,0:T(8,128)(2,1)S(1)} %copy-done.101), channel_id=1, source_target_pairs={{0,6},{1,7},{2,4},{3,5},{4,2},{5,3},{6,0},{7,1},{8,14},{9,15},{10,... | collective-permute-start | bytes 393224 | tf_op jit(solution)/shard_map/ppermute | solution.py:29
  58.2 32.4 %collective-permute-start.1 = (bf16[256,256]{1,0:T(8,128)(2,1)S(1)}, bf16[256,256]{1,0:T(8,128)(2,1)S(1)}, u32[]{:S(2)}, u32[]{:S(2)}) collective-permute-start(bf16[256,256]{1,0:T(8,128)(2,1)S(1)} %copy-done.101), channel_id=1, source_target_pairs={{0,4},{1,5},{2,6},{3,7},{4,0},{5,1},{6,2},{7,3},{8,12},{9,13},{10,... | collective-permute-start | bytes 393224 | tf_op jit(solution)/shard_map/ppermute | solution.py:29
  64.2 63.3 %collective-permute-start.42 = (bf16[128,768]{0,1:T(8,128)(2,1)}, bf16[128,768]{0,1:T(8,128)(2,1)S(1)}, u32[]{:S(2)}, u32[]{:S(2)}) collective-permute-start(bf16[128,768]{0,1:T(8,128)(2,1)} %bitcast.226), channel_id=1, source_target_pairs={{0,6},{1,7},{2,4},{3,5},{4,2},{5,3},{6,0},{7,1},{8,14},{9,15},{10,... | collective-permute-start | bytes 589832 | tf_op jit(solution)/shard_map/ppermute | solution.py:29
  67.1 59.6 %collective-permute-start.41 = (bf16[128,768]{0,1:T(8,128)(2,1)}, bf16[128,768]{0,1:T(8,128)(2,1)S(1)}, u32[]{:S(2)}, u32[]{:S(2)}) collective-permute-start(bf16[128,768]{0,1:T(8,128)(2,1)} %bitcast.227), channel_id=1, source_target_pairs={{0,4},{1,5},{2,6},{3,7},{4,0},{5,1},{6,2},{7,3},{8,12},{9,13},{10,... | collective-permute-start | bytes 589832 | tf_op jit(solution)/shard_map/ppermute | solution.py:29
  80.7 51.4 %collective-permute-start.8 = (bf16[768,128]{1,0:T(8,128)(2,1)}, bf16[768,128]{1,0:T(8,128)(2,1)S(1)}, u32[]{:S(2)}, u32[]{:S(2)}) collective-permute-start(bf16[768,128]{1,0:T(8,128)(2,1)} %bitcast.232), channel_id=1, source_target_pairs={{0,6},{1,7},{2,4},{3,5},{4,2},{5,3},{6,0},{7,1},{8,14},{9,15},{10,... | collective-permute-start | bytes 589832 | tf_op jit(solution)/shard_map/ppermute | solution.py:29
  90.5 58.1 %collective-permute-start.7 = (bf16[768,128]{1,0:T(8,128)(2,1)}, bf16[768,128]{1,0:T(8,128)(2,1)S(1)}, u32[]{:S(2)}, u32[]{:S(2)}) collective-permute-start(bf16[768,128]{1,0:T(8,128)(2,1)} %bitcast.233), channel_id=1, source_target_pairs={{0,4},{1,5},{2,6},{3,7},{4,0},{5,1},{6,2},{7,3},{8,12},{9,13},{10,... | collective-permute-start | bytes 589832 | tf_op jit(solution)/shard_map/ppermute | solution.py:29
  100.8 26.7 %collective-permute-start.6 = (bf16[768,128]{1,0:T(8,128)(2,1)}, bf16[768,128]{1,0:T(8,128)(2,1)S(1)}, u32[]{:S(2)}, u32[]{:S(2)}) collective-permute-start(bf16[768,128]{1,0:T(8,128)(2,1)} %bitcast.234), channel_id=1, source_target_pairs={{0,2},{1,3},{2,0},{3,1},{4,6},{5,7},{6,4},{7,5},{8,10},{9,11},{10,... | collective-permute-start | bytes 589832 | tf_op jit(solution)/shard_map/ppermute | solution.py:29
  126.8 23.5 %collective-permute-start.19 = (bf16[256,512]{1,0:T(8,128)(2,1)S(1)}, bf16[256,512]{1,0:T(8,128)(2,1)S(1)}, u32[]{:S(2)}, u32[]{:S(2)}) collective-permute-start(bf16[256,512]{1,0:T(8,128)(2,1)S(1)} %copy-done.84), channel_id=1, source_target_pairs={{0,6},{1,7},{2,4},{3,5},{4,2},{5,3},{6,0},{7,1},{8,14},{9,15},{10,... | collective-permute-start | bytes 786440 | tf_op jit(solution)/shard_map/ppermute | solution.py:29
  127.5 31.4 %collective-permute-start.18 = (bf16[256,512]{1,0:T(8,128)(2,1)S(1)}, bf16[256,512]{1,0:T(8,128)(2,1)S(1)}, u32[]{:S(2)}, u32[]{:S(2)}) collective-permute-start(bf16[256,512]{1,0:T(8,128)(2,1)S(1)} %copy-done.84), channel_id=1, source_target_pairs={{0,4},{1,5},{2,6},{3,7},{4,0},{5,1},{6,2},{7,3},{8,12},{9,13},{10,... | collective-permute-start | bytes 786440 | tf_op jit(solution)/shard_map/ppermute | solution.py:29
  127.6 31.3 %collective-permute-start.17 = (bf16[256,512]{1,0:T(8,128)(2,1)S(1)}, bf16[256,512]{1,0:T(8,128)(2,1)S(1)}, u32[]{:S(2)}, u32[]{:S(2)}) collective-permute-start(bf16[256,512]{1,0:T(8,128)(2,1)S(1)} %copy-done.84), channel_id=1, source_target_pairs={{0,2},{1,3},{2,0},{3,1},{4,6},{5,7},{6,4},{7,5},{8,10},{9,11},{10,... | collective-permute-start | bytes 786440 | tf_op jit(solution)/shard_map/ppermute | solution.py:29
  132.1 75.8 %collective-permute-start.16 = (bf16[512,256]{1,0:T(8,128)(2,1)S(1)}, bf16[512,256]{1,0:T(8,128)(2,1)S(1)}, u32[]{:S(2)}, u32[]{:S(2)}) collective-permute-start(bf16[512,256]{1,0:T(8,128)(2,1)S(1)} %pad_maximum_fusion.18), channel_id=1, source_target_pairs={{0,1},{1,0},{2,3},{3,2},{4,5},{5,4},{6,7},{7,6},{8,9},{9,8},{10,11... | collective-permute-start | bytes 786440 | tf_op jit(solution)/shard_map/ppermute | solution.py:29
  150.3 55.3 %collective-permute-start.9 = (bf16[768,512]{1,0:T(8,128)(2,1)S(1)}, bf16[768,512]{1,0:T(8,128)(2,1)S(1)}, u32[]{:S(2)}, u32[]{:S(2)}) collective-permute-start(bf16[768,512]{1,0:T(8,128)(2,1)S(1)} %pad_maximum_fusion.8), channel_id=1, source_target_pairs={{0,1},{1,0},{2,3},{3,2},{4,5},{5,4},{6,7},{7,6},{8,9},{9,8},{10,11... | collective-permute-start | bytes 2359304 | tf_op jit(solution)/shard_map/ppermute | solution.py:29
  159.0 42.0 %collective-permute-start.20 = (bf16[256,2048]{1,0:T(8,128)(2,1)S(1)}, bf16[256,2048]{1,0:T(8,128)(2,1)S(1)}, u32[]{:S(2)}, u32[]{:S(2)}) collective-permute-start(bf16[256,2048]{1,0:T(8,128)(2,1)S(1)} %pad_maximum_fusion.2), channel_id=1, source_target_pairs={{0,1},{1,0},{2,3},{3,2},{4,5},{5,4},{6,7},{7,6},{8,9},{9,8},{10,11... | collective-permute-start | bytes 3145736 | tf_op jit(solution)/shard_map/ppermute | solution.py:29
  165.2 37.6 %collective-permute-start.4 = (bf16[4,27,256]{2,1,0:T(8,128)(2,1)S(1)}, bf16[4,27,256]{2,1,0:T(8,128)(2,1)S(1)}, u32[]{:S(2)}, u32[]{:S(2)}) collective-permute-start(bf16[4,27,256]{2,1,0:T(8,128)(2,1)S(1)} %get-tuple-element.184), channel_id=1, source_target_pairs={{0,1},{1,2},{2,3},{3,4},{4,5},{5,6},{6,7},{8,9},{9,10},{10,11},{11... | collective-permute-start | bytes 165896 | tf_op jit(solution)/shard_map/ppermute | solution.py:427
  168.6 36.7 %collective-permute-start.5 = (bf16[4,27,256]{2,1,0:T(8,128)(2,1)S(1)}, bf16[4,27,256]{2,1,0:T(8,128)(2,1)S(1)}, u32[]{:S(2)}, u32[]{:S(2)}) collective-permute-start(bf16[4,27,256]{2,1,0:T(8,128)(2,1)S(1)} %get-tuple-element.185), channel_id=1, source_target_pairs={{1,0},{2,1},{3,2},{4,3},{5,4},{6,5},{7,6},{9,8},{10,9},{11,10},{12... | collective-permute-start | bytes 165896 | tf_op jit(solution)/shard_map/ppermute | solution.py:428
  201.1 61.1 %collective-permute-start.26 = (bf16[256,4096]{1,0:T(8,128)(2,1)S(1)}, bf16[256,4096]{1,0:T(8,128)(2,1)S(1)}, u32[]{:S(2)}, u32[]{:S(2)}) collective-permute-start(bf16[256,4096]{1,0:T(8,128)(2,1)S(1)} %constant_dynamic-update-slice_fusion.15), channel_id=1, source_target_pairs={{0,16},{8,24},{16,0},{24,8},{1,17},{9,25},{17,1},{25,9},{2,18},{10... | collective-permute-start | bytes 6291464 | tf_op jit(solution)/shard_map/ppermute | solution.py:25
  208.0 51.3 %collective-permute-start.25 = (bf16[1024,256]{1,0:T(8,128)(2,1)S(1)}, bf16[1024,256]{1,0:T(8,128)(2,1)S(1)}, u32[]{:S(2)}, u32[]{:S(2)}) collective-permute-start(bf16[1024,256]{1,0:T(8,128)(2,1)S(1)} %constant_dynamic-update-slice_fusion.10), channel_id=1, source_target_pairs={{0,16},{8,24},{16,0},{24,8},{1,17},{9,25},{17,1},{25,9},{2,18},{10... | collective-permute-start | bytes 1572872 | tf_op jit(solution)/shard_map/ppermute | solution.py:25
  213.3 45.9 %collective-permute-start.10 = (bf16[128,1024]{1,0:T(8,128)(2,1)S(1)}, bf16[128,1024]{1,0:T(8,128)(2,1)S(1)}, u32[]{:S(2)}, u32[]{:S(2)}) collective-permute-start(bf16[128,1024]{1,0:T(8,128)(2,1)S(1)} %get-tuple-element.152), channel_id=1, source_target_pairs={{0,8},{8,0},{16,24},{24,16},{1,9},{9,1},{17,25},{25,17},{2,10},{10... | collective-permute-start | bytes 786440 | tf_op jit(solution)/shard_map/ppermute | solution.py:25
  213.3 62.1 %collective-permute-start.23 = (bf16[256,4096]{1,0:T(8,128)(2,1)S(1)}, bf16[256,4096]{1,0:T(8,128)(2,1)S(1)}, u32[]{:S(2)}, u32[]{:S(2)}) collective-permute-start(bf16[256,4096]{1,0:T(8,128)(2,1)S(1)} %constant_dynamic-update-slice_fusion.15), channel_id=1, source_target_pairs={{0,8},{8,0},{16,24},{24,16},{1,9},{9,1},{17,25},{25,17},{2,10},{10... | collective-permute-start | bytes 6291464 | tf_op jit(solution)/shard_map/ppermute | solution.py:25
  224.8 37.2 %collective-permute-start.12 = (bf16[128,1024]{1,0:T(8,128)(2,1)S(1)}, bf16[128,1024]{1,0:T(8,128)(2,1)S(1)}, u32[]{:S(2)}, u32[]{:S(2)}) collective-permute-start(bf16[128,1024]{1,0:T(8,128)(2,1)S(1)} %fusion.49), channel_id=1, source_target_pairs={{0,16},{8,24},{16,0},{24,8},{1,17},{9,25},{17,1},{25,9},{2,18},{10... | collective-permute-start | bytes 786440 | tf_op jit(solution)/shard_map/ppermute | solution.py:25
  259.2 20.9 %collective-permute-start.32 = (bf16[512,256]{1,0:T(8,128)(2,1)S(1)}, bf16[512,256]{1,0:T(8,128)(2,1)S(1)}, u32[]{:S(2)}, u32[]{:S(2)}) collective-permute-start(bf16[512,256]{1,0:T(8,128)(2,1)S(1)} %copy-done.118), channel_id=1, source_target_pairs={{0,24},{8,16},{16,8},{24,0},{1,25},{9,17},{17,9},{25,1},{2,26},{10... | collective-permute-start | bytes 786440 | tf_op jit(solution)/shard_map/ppermute | solution.py:25
  270.6 43.2 %collective-permute-start.45 = (bf16[1024,768]{0,1:T(8,128)(2,1)}, bf16[1024,768]{0,1:T(8,128)(2,1)}, u32[]{:S(2)}, u32[]{:S(2)}) collective-permute-start(bf16[1024,768]{0,1:T(8,128)(2,1)} %constant_dynamic-update-slice_fusion.20), channel_id=1, source_target_pairs={{0,16},{8,24},{16,0},{24,8},{1,17},{9,25},{17,1},{25,9},{2,18},{10... | collective-permute-start | bytes 4718600 | tf_op jit(solution)/shard_map/ppermute | solution.py:25
  275.4 38.3 %collective-permute-start.31 = (bf16[512,256]{1,0:T(8,128)(2,1)S(1)}, bf16[512,256]{1,0:T(8,128)(2,1)S(1)}, u32[]{:S(2)}, u32[]{:S(2)}) collective-permute-start(bf16[512,256]{1,0:T(8,128)(2,1)S(1)} %copy-done.116), channel_id=1, source_target_pairs={{0,16},{8,24},{16,0},{24,8},{1,17},{9,25},{17,1},{25,9},{2,18},{10... | collective-permute-start | bytes 786440 | tf_op jit(solution)/shard_map/ppermute | solution.py:25
  278.2 68.3 %collective-permute-start.61 = (bf16[2048,256]{1,0:T(8,128)(2,1)}, bf16[2048,256]{1,0:T(8,128)(2,1)}, u32[]{:S(2)}, u32[]{:S(2)}) collective-permute-start(bf16[2048,256]{1,0:T(8,128)(2,1)} %pad_maximum_fusion.4), channel_id=1, source_target_pairs={{0,16},{8,24},{16,0},{24,8},{1,17},{9,25},{17,1},{25,9},{2,18},{10... | collective-permute-start | bytes 3145736 | tf_op jit(solution)/shard_map/ppermute | solution.py:25
  280.1 87.5 %collective-permute-start.60 = (bf16[2048,256]{1,0:T(8,128)(2,1)}, bf16[2048,256]{1,0:T(8,128)(2,1)}, u32[]{:S(2)}, u32[]{:S(2)}) collective-permute-start(bf16[2048,256]{1,0:T(8,128)(2,1)} %pad_maximum_fusion.4), channel_id=1, source_target_pairs={{0,8},{8,0},{16,24},{24,16},{1,9},{9,1},{17,25},{25,17},{2,10},{10... | collective-permute-start | bytes 3145736 | tf_op jit(solution)/shard_map/ppermute | solution.py:25
  280.2 66.3 %collective-permute-start.52 = (bf16[256,1024]{1,0:T(8,128)(2,1)}, bf16[256,1024]{1,0:T(8,128)(2,1)}, u32[]{:S(2)}, u32[]{:S(2)}) collective-permute-start(bf16[256,1024]{1,0:T(8,128)(2,1)} %constant_dynamic-update-slice_fusion.25), channel_id=1, source_target_pairs={{0,16},{8,24},{16,0},{24,8},{1,17},{9,25},{17,1},{25,9},{2,18},{10... | collective-permute-start | bytes 1572872 | tf_op jit(solution)/shard_map/ppermute | solution.py:25
  313.7 35.9 %collective-permute-start.44 = (bf16[1024,768]{0,1:T(8,128)(2,1)}, bf16[1024,768]{0,1:T(8,128)(2,1)}, u32[]{:S(2)}, u32[]{:S(2)}) collective-permute-start(bf16[1024,768]{0,1:T(8,128)(2,1)} %constant_dynamic-update-slice_fusion.20), channel_id=1, source_target_pairs={{0,8},{8,0},{16,24},{24,16},{1,9},{9,1},{17,25},{25,17},{2,10},{10... | collective-permute-start | bytes 4718600 | tf_op jit(solution)/shard_map/ppermute | solution.py:25
  313.7 33.3 %collective-permute-start.46 = (bf16[1024,768]{0,1:T(8,128)(2,1)}, bf16[1024,768]{0,1:T(8,128)(2,1)}, u32[]{:S(2)}, u32[]{:S(2)}) collective-permute-start(bf16[1024,768]{0,1:T(8,128)(2,1)} %collective-permute-done.45), channel_id=1, source_target_pairs={{0,8},{8,0},{16,24},{24,16},{1,9},{9,1},{17,25},{25,17},{2,10},{10... | collective-permute-start | bytes 4718600 | tf_op jit(solution)/shard_map/ppermute | solution.py:25
  347.1 23.5 %collective-permute-start.62 = (bf16[2048,256]{1,0:T(8,128)(2,1)}, bf16[2048,256]{1,0:T(8,128)(2,1)S(1)}, u32[]{:S(2)}, u32[]{:S(2)}) collective-permute-start(bf16[2048,256]{1,0:T(8,128)(2,1)} %collective-permute-done.61), channel_id=1, source_target_pairs={{0,8},{8,0},{16,24},{24,16},{1,9},{9,1},{17,25},{25,17},{2,10},{10... | collective-permute-start | bytes 3145736 | tf_op jit(solution)/shard_map/ppermute | solution.py:25
  366.4 25.8 %collective-permute-start.55 = (bf16[512,1024]{1,0:T(8,128)(2,1)}, bf16[512,1024]{1,0:T(8,128)(2,1)}, u32[]{:S(2)}, u32[]{:S(2)}) collective-permute-start(bf16[512,1024]{1,0:T(8,128)(2,1)} %add_convert_fusion.3), channel_id=1, source_target_pairs={{0,16},{8,24},{16,0},{24,8},{1,17},{9,25},{17,1},{25,9},{2,18},{10... | collective-permute-start | bytes 3145736 | tf_op jit(solution)/shard_map/ppermute | solution.py:25
  385.6 29.9 %collective-permute-start.54 = (bf16[512,1024]{1,0:T(8,128)(2,1)}, bf16[512,1024]{1,0:T(8,128)(2,1)}, u32[]{:S(2)}, u32[]{:S(2)}) collective-permute-start(bf16[512,1024]{1,0:T(8,128)(2,1)} %add_convert_fusion.3), channel_id=1, source_target_pairs={{0,8},{8,0},{16,24},{24,16},{1,9},{9,1},{17,25},{25,17},{2,10},{10... | collective-permute-start | bytes 3145736 | tf_op jit(solution)/shard_map/ppermute | solution.py:25
  392.3 23.3 %collective-permute-start.56 = (bf16[512,1024]{1,0:T(8,128)(2,1)}, bf16[512,1024]{1,0:T(8,128)(2,1)}, u32[]{:S(2)}, u32[]{:S(2)}) collective-permute-start(bf16[512,1024]{1,0:T(8,128)(2,1)} %collective-permute-done.55), channel_id=1, source_target_pairs={{0,8},{8,0},{16,24},{24,16},{1,9},{9,1},{17,25},{25,17},{2,10},{10... | collective-permute-start | bytes 3145736 | tf_op jit(solution)/shard_map/ppermute | solution.py:25
  446.5 36.8 %collective-permute-start.58 = (bf16[4,512,256]{2,1,0:T(8,128)(2,1)}, bf16[4,512,256]{2,1,0:T(8,128)(2,1)}, u32[]{:S(2)}, u32[]{:S(2)}) collective-permute-start(bf16[4,512,256]{2,1,0:T(8,128)(2,1)} %get-tuple-element.101), channel_id=1, source_target_pairs={{0,8},{8,0},{16,24},{24,16},{1,9},{9,1},{17,25},{25,17},{2,10},{10... | collective-permute-start | bytes 3145736 | tf_op jit(solution)/shard_map/ppermute | solution.py:25
  447.0 42.0 %collective-permute-start.57 = (bf16[4,512,256]{2,1,0:T(8,128)(2,1)}, bf16[4,512,256]{2,1,0:T(8,128)(2,1)}, u32[]{:S(2)}, u32[]{:S(2)}) collective-permute-start(bf16[4,512,256]{2,1,0:T(8,128)(2,1)} %get-tuple-element.102), channel_id=1, source_target_pairs={{0,8},{8,0},{16,24},{24,16},{1,9},{9,1},{17,25},{25,17},{2,10},{10... | collective-permute-start | bytes 3145736 | tf_op jit(solution)/shard_map/ppermute | solution.py:25
  455.1 36.1 %collective-permute-start.63 = (bf16[512,1024]{1,0:T(8,128)(2,1)}, bf16[512,1024]{1,0:T(8,128)(2,1)}, u32[]{:S(2)}, u32[]{:S(2)}) collective-permute-start(bf16[512,1024]{1,0:T(8,128)(2,1)} %get-tuple-element.99), channel_id=1, source_target_pairs={{0,8},{8,0},{16,24},{24,16},{1,9},{9,1},{17,25},{25,17},{2,10},{10... | collective-permute-start | bytes 3145736 | tf_op jit(solution)/shard_map/ppermute | solution.py:25
  468.9 26.3 %collective-permute-start.65 = (bf16[512,1024]{1,0:T(8,128)(2,1)}, bf16[512,1024]{1,0:T(8,128)(2,1)}, u32[]{:S(2)}, u32[]{:S(2)}) collective-permute-start(bf16[512,1024]{1,0:T(8,128)(2,1)} %fusion.23), channel_id=1, source_target_pairs={{0,16},{8,24},{16,0},{24,8},{1,17},{9,25},{17,1},{25,9},{2,18},{10... | collective-permute-start | bytes 3145736 | tf_op jit(solution)/shard_map/ppermute | solution.py:25
  487.9 64.2 %collective-permute-start.59 = (bf16[4,512,256]{2,1,0:T(8,128)(2,1)}, bf16[4,512,256]{2,1,0:T(8,128)(2,1)}, u32[]{:S(2)}, u32[]{:S(2)}) collective-permute-start(bf16[4,512,256]{2,1,0:T(8,128)(2,1)} %fusion.22), channel_id=1, source_target_pairs={{0,16},{8,24},{16,0},{24,8},{1,17},{9,25},{17,1},{25,9},{2,18},{10... | collective-permute-start | bytes 3145736 | tf_op jit(solution)/shard_map/ppermute | solution.py:25
  544.2 56.9 %collective-permute-start.69 = (bf16[128,256]{1,0:T(8,128)(2,1)S(1)}, bf16[128,256]{1,0:T(8,128)(2,1)S(1)}, u32[]{:S(2)}, u32[]{:S(2)}) collective-permute-start(bf16[128,256]{1,0:T(8,128)(2,1)S(1)} %convolution_convert_fusion.21), channel_id=1, source_target_pairs={{0,8},{8,0},{16,24},{24,16},{1,9},{9,1},{17,25},{25,17},{2,10},{10... | collective-permute-start | bytes 196616 | tf_op jit(solution)/shard_map/ppermute | solution.py:25
  544.6 34.2 %collective-permute-start.66 = (bf16[512,256]{1,0:T(8,128)(2,1)S(1)}, bf16[512,256]{1,0:T(8,128)(2,1)S(1)}, u32[]{:S(2)}, u32[]{:S(2)}) collective-permute-start(bf16[512,256]{1,0:T(8,128)(2,1)S(1)} %get-tuple-element.39), channel_id=1, source_target_pairs={{0,24},{8,16},{16,8},{24,0},{1,25},{9,17},{17,9},{25,1},{2,26},{10... | collective-permute-start | bytes 786440 | tf_op jit(solution)/shard_map/ppermute | solution.py:25
  578.9 22.8 %collective-permute-start.70 = (bf16[128,256]{1,0:T(8,128)(2,1)S(1)}, bf16[128,256]{1,0:T(8,128)(2,1)S(1)}, u32[]{:S(2)}, u32[]{:S(2)}) collective-permute-start(bf16[128,256]{1,0:T(8,128)(2,1)S(1)} %convolution_convert_fusion.20), channel_id=1, source_target_pairs={{0,16},{8,24},{16,0},{24,8},{1,17},{9,25},{17,1},{25,9},{2,18},{10... | collective-permute-start | bytes 196616 | tf_op jit(solution)/shard_map/ppermute | solution.py:25
  580.0 21.8 %collective-permute-start.71 = (bf16[128,256]{1,0:T(8,128)(2,1)S(1)}, bf16[128,256]{1,0:T(8,128)(2,1)S(1)}, u32[]{:S(2)}, u32[]{:S(2)}) collective-permute-start(bf16[128,256]{1,0:T(8,128)(2,1)S(1)} %convolution_convert_fusion.19), channel_id=1, source_target_pairs={{0,24},{8,16},{16,8},{24,0},{1,25},{9,17},{17,9},{25,1},{2,26},{10... | collective-permute-start | bytes 196616 | tf_op jit(solution)/shard_map/ppermute | solution.py:25
  600.9 22.9 %collective-permute-start.93 = (bf16[256,4096]{1,0:T(8,128)(2,1)S(1)}, bf16[256,4096]{1,0:T(8,128)(2,1)S(1)}, u32[]{:S(2)}, u32[]{:S(2)}) collective-permute-start(bf16[256,4096]{1,0:T(8,128)(2,1)S(1)} %copy-done.68), channel_id=1, source_target_pairs={{0,8},{8,0},{16,24},{24,16},{1,9},{9,1},{17,25},{25,17},{2,10},{10... | collective-permute-start | bytes 6291464 | tf_op jit(solution)/shard_map/ppermute | solution.py:25
  629.5 29.9 %collective-permute-start.106 = (bf16[1024,768]{0,1:T(8,128)(2,1)S(1)}, bf16[1024,768]{0,1:T(8,128)(2,1)S(1)}, u32[]{:S(2)}, u32[]{:S(2)}) collective-permute-start(bf16[1024,768]{0,1:T(8,128)(2,1)S(1)} %convolution_convert_fusion.5), channel_id=1, source_target_pairs={{0,8},{8,0},{16,24},{24,16},{1,9},{9,1},{17,25},{25,17},{2,10},{10... | collective-permute-start | bytes 4718600 | tf_op jit(solution)/shard_map/ppermute | solution.py:25
  629.5 45.3 %collective-permute-start.92 = (bf16[256,4096]{1,0:T(8,128)(2,1)S(1)}, bf16[256,4096]{1,0:T(8,128)(2,1)S(1)}, u32[]{:S(2)}, u32[]{:S(2)}) collective-permute-start(bf16[256,4096]{1,0:T(8,128)(2,1)S(1)} %convolution_convert_fusion.1), channel_id=1, source_target_pairs={{0,8},{8,0},{16,24},{24,16},{1,9},{9,1},{17,25},{25,17},{2,10},{10... | collective-permute-start | bytes 6291464 | tf_op jit(solution)/shard_map/ppermute | solution.py:25
  636.5 37.3 %collective-permute-start.108 = (bf16[1024,768]{0,1:T(8,128)(2,1)S(1)}, bf16[1024,768]{0,1:T(8,128)(2,1)S(1)}, u32[]{:S(2)}, u32[]{:S(2)}) collective-permute-start(bf16[1024,768]{0,1:T(8,128)(2,1)S(1)} %add_convert_fusion.2), channel_id=1, source_target_pairs={{0,16},{8,24},{16,0},{24,8},{1,17},{9,25},{17,1},{25,9},{2,18},{10... | collective-permute-start | bytes 4718600 | tf_op jit(solution)/shard_map/ppermute | solution.py:25
  637.7 79.3 %collective-permute-start.94 = (bf16[256,4096]{1,0:T(8,128)(2,1)S(1)}, bf16[256,4096]{1,0:T(8,128)(2,1)S(1)}, u32[]{:S(2)}, u32[]{:S(2)}) collective-permute-start(bf16[256,4096]{1,0:T(8,128)(2,1)S(1)} %fusion.11), channel_id=1, source_target_pairs={{0,16},{8,24},{16,0},{24,8},{1,17},{9,25},{17,1},{25,9},{2,18},{10... | collective-permute-start | bytes 6291464 | tf_op jit(solution)/shard_map/ppermute | solution.py:25
  658.2 60.3 %collective-permute-start.117 = (bf16[256,128]{1,0:T(8,128)(2,1)S(1)}, bf16[256,128]{1,0:T(8,128)(2,1)S(1)}, u32[]{:S(2)}, u32[]{:S(2)}) collective-permute-start(bf16[256,128]{1,0:T(8,128)(2,1)S(1)} %get-tuple-element.173), channel_id=1, source_target_pairs={{0,2},{1,3},{2,0},{3,1},{4,6},{5,7},{6,4},{7,5},{8,10},{9,11},{10,... | collective-permute-start | bytes 196616 | tf_op jit(solution)/shard_map/ppermute | solution.py:29
  659.4 59.2 %collective-permute-start.119 = (bf16[256,128]{1,0:T(8,128)(2,1)S(1)}, bf16[256,128]{1,0:T(8,128)(2,1)S(1)}, u32[]{:S(2)}, u32[]{:S(2)}) collective-permute-start(bf16[256,128]{1,0:T(8,128)(2,1)S(1)} %get-tuple-element.174), channel_id=1, source_target_pairs={{0,6},{1,7},{2,4},{3,5},{4,2},{5,3},{6,0},{7,1},{8,14},{9,15},{10,... | collective-permute-start | bytes 196616 | tf_op jit(solution)/shard_map/ppermute | solution.py:29
  673.8 46.0 %collective-permute-start.118 = (bf16[256,128]{1,0:T(8,128)(2,1)S(1)}, bf16[256,128]{1,0:T(8,128)(2,1)S(1)}, u32[]{:S(2)}, u32[]{:S(2)}) collective-permute-start(bf16[256,128]{1,0:T(8,128)(2,1)S(1)} %get-tuple-element.175), channel_id=1, source_target_pairs={{0,4},{1,5},{2,6},{3,7},{4,0},{5,1},{6,2},{7,3},{8,12},{9,13},{10,... | collective-permute-start | bytes 196616 | tf_op jit(solution)/shard_map/ppermute | solution.py:29
  674.8 54.3 %collective-permute-start.109 = (bf16[512,768]{0,1:T(8,128)(2,1)S(1)}, bf16[512,768]{0,1:T(8,128)(2,1)S(1)}, u32[]{:S(2)}, u32[]{:S(2)}) collective-permute-start(bf16[512,768]{0,1:T(8,128)(2,1)S(1)} %split.216), channel_id=1, source_target_pairs={{0,1},{1,0},{2,3},{3,2},{4,5},{5,4},{6,7},{7,6},{8,9},{9,8},{10,11... | collective-permute-start | bytes 2359304 | tf_op jit(solution)/shard_map/ppermute | solution.py:29
  718.1 23.5 %collective-permute-start.95 = (bf16[256,2048]{1,0:T(8,128)(2,1)S(1)}, bf16[256,2048]{1,0:T(8,128)(2,1)S(1)}, u32[]{:S(2)}, u32[]{:S(2)}) collective-permute-start(bf16[256,2048]{1,0:T(8,128)(2,1)S(1)} %split.208), channel_id=1, source_target_pairs={{0,1},{1,0},{2,3},{3,2},{4,5},{5,4},{6,7},{7,6},{8,9},{9,8},{10,11... | collective-permute-start | bytes 3145736 | tf_op jit(solution)/shard_map/ppermute | solution.py:29
  728.4 22.7 %collective-permute-start.83 = (bf16[768,128]{1,0:T(8,128)(2,1)S(1)}, bf16[768,128]{1,0:T(8,128)(2,1)S(1)}, u32[]{:S(2)}, u32[]{:S(2)}) collective-permute-start(bf16[768,128]{1,0:T(8,128)(2,1)S(1)} %get-tuple-element.163), channel_id=1, source_target_pairs={{0,4},{1,5},{2,6},{3,7},{4,0},{5,1},{6,2},{7,3},{8,12},{9,13},{10,... | collective-permute-start | bytes 589832 | tf_op jit(solution)/shard_map/ppermute | solution.py:29
  729.6 24.6 %collective-permute-start.110 = (bf16[128,768]{0,1:T(8,128)(2,1)S(1)}, bf16[128,768]{0,1:T(8,128)(2,1)S(1)}, u32[]{:S(2)}, u32[]{:S(2)}) collective-permute-start(bf16[128,768]{0,1:T(8,128)(2,1)S(1)} %get-tuple-element.156), channel_id=1, source_target_pairs={{0,2},{1,3},{2,0},{3,1},{4,6},{5,7},{6,4},{7,5},{8,10},{9,11},{10,... | collective-permute-start | bytes 589832 | tf_op jit(solution)/shard_map/ppermute | solution.py:29
  743.1 29.9 %collective-permute-start.111 = (bf16[128,768]{0,1:T(8,128)(2,1)S(1)}, bf16[128,768]{0,1:T(8,128)(2,1)S(1)}, u32[]{:S(2)}, u32[]{:S(2)}) collective-permute-start(bf16[128,768]{0,1:T(8,128)(2,1)S(1)} %get-tuple-element.158), channel_id=1, source_target_pairs={{0,4},{1,5},{2,6},{3,7},{4,0},{5,1},{6,2},{7,3},{8,12},{9,13},{10,... | collective-permute-start | bytes 589832 | tf_op jit(solution)/shard_map/ppermute | solution.py:29
  743.1 30.9 %collective-permute-start.96 = (bf16[256,512]{1,0:T(8,128)(2,1)}, bf16[256,512]{1,0:T(8,128)(2,1)S(1)}, u32[]{:S(2)}, u32[]{:S(2)}) collective-permute-start(bf16[256,512]{1,0:T(8,128)(2,1)} %get-tuple-element.113), channel_id=1, source_target_pairs={{0,2},{1,3},{2,0},{3,1},{4,6},{5,7},{6,4},{7,5},{8,10},{9,11},{10,... | collective-permute-start | bytes 786440 | tf_op jit(solution)/shard_map/ppermute | solution.py:29
  751.1 22.9 %collective-permute-start.98 = (bf16[256,512]{1,0:T(8,128)(2,1)}, bf16[256,512]{1,0:T(8,128)(2,1)S(1)}, u32[]{:S(2)}, u32[]{:S(2)}) collective-permute-start(bf16[256,512]{1,0:T(8,128)(2,1)} %get-tuple-element.114), channel_id=1, source_target_pairs={{0,6},{1,7},{2,4},{3,5},{4,2},{5,3},{6,0},{7,1},{8,14},{9,15},{10,... | collective-permute-start | bytes 786440 | tf_op jit(solution)/shard_map/ppermute | solution.py:29
  754.1 28.5 %collective-permute-start.97 = (bf16[256,512]{1,0:T(8,128)(2,1)S(1)}, bf16[256,512]{1,0:T(8,128)(2,1)S(1)}, u32[]{:S(2)}, u32[]{:S(2)}) collective-permute-start(bf16[256,512]{1,0:T(8,128)(2,1)S(1)} %get-tuple-element.115), channel_id=1, source_target_pairs={{0,4},{1,5},{2,6},{3,7},{4,0},{5,1},{6,2},{7,3},{8,12},{9,13},{10,... | collective-permute-start | bytes 786440 | tf_op jit(solution)/shard_map/ppermute | solution.py:29
  (209 other events, 2291.6 us)
Sparse Core Ops, SparseCore 0:
  20.7 123.3 all-gather.2
  483.4 88.9 reduce-scatter.1

commit v3 on v2

--- a/solution.py
+++ b/solution.py
@@ -31,11 +31,11 @@
 
 def place():
     c = lax.axis_index("cond")
-    if tuned():
-        s = lax.axis_index("seq")
-        return c, s >> 1, s & 1
-    zero = jnp.zeros((), jnp.int32)
-    return c, zero, zero
+    return c, (lax.axis_index("seq") & 1 if tuned() else jnp.zeros((), jnp.int32))
+
+
+def after(value, *before):
+    return lax.optimization_barrier((value, *before))[0]
 
 
 def dot(a, b, dims=((1,), (0,))):
@@ -73,26 +73,110 @@
     return jnp.swapaxes(x, dim, dim + 1).reshape(shape)
 
 
-def gather(shard, dim):
+CELL = 256
+ALONG_Z = [[0, 2, 4, 6], [1, 3, 5, 7]]
+VMEM_ROOM = 48 * 1024 * 1024
+
+
+def bundle(shards):
+    return jnp.concatenate(
+        [s[:, i : i + CELL] for s in shards for i in range(0, s.shape[1], CELL)], axis=0
+    )
+
+
+def along_z(x):
+    return lax.all_to_all(x, "seq", 0, 0, axis_index_groups=ALONG_Z, tiled=True)
+
+
+def unpack_body(shapes, near_ref, far_ref, *outs):
+    p = pl.program_id(0)
+
+    def copy(ref):
+        at = 0
+        for (r, w), out in zip(shapes, outs):
+            for i in range(0, w, CELL):
+                out[:, i : i + CELL] = ref[0, at : at + r]
+                at += r
+
+    pl.when(p < 4)(lambda: copy(near_ref))
+    pl.when(p >= 4)(lambda: copy(far_ref))
+
+
+def unpack(near, far, shapes):
+    block = (1,) + near.shape[1:]
+    return pl.pallas_call(
+        lambda *refs: unpack_body(shapes, *refs),
+        out_shape=[jax.ShapeDtypeStruct((8 * r, w), near.dtype) for r, w in shapes],
+        grid=(8,),
+        in_specs=[
+            pl.BlockSpec(block, lambda p: (jnp.minimum(p, 3), 0, 0)),
+            pl.BlockSpec(block, lambda p: (jnp.maximum(p - 4, 0), 0, 0)),
+        ],
+        out_specs=[pl.BlockSpec((r, w), lambda p: (p, 0)) for r, w in shapes],
+        compiler_params=pltpu.CompilerParams(vmem_limit_bytes=VMEM_ROOM),
+        name="unpack",
+    )(near, far)
+
+
+def gather_plain(shards):
+    return [regroup(lax.all_gather(s, "seq", axis=0, tiled=True), 0, 4, 2) for s in shards]
+
+
+def pack_body(shapes, *refs):
+    out = refs[-1]
+    at = 0
+    for (r, w), near, far in zip(shapes, refs[0::2], refs[1::2]):
+        total = (near[...].astype(F32) + far[...].astype(F32)).astype(BF16)
+        for i in range(0, w, CELL):
+            out[0, at : at + r] = total[:, i : i + CELL]
+            at += r
+
+
+def pack(nears, fars):
+    shapes = [(f.shape[0] // 4, f.shape[1]) for f in fars]
+    rows = sum(r * w for r, w in shapes) // CELL
+    specs = [pl.BlockSpec((r, w), lambda p: (p, 0)) for r, w in shapes for _ in range(2)]
+    return pl.pallas_call(
+        lambda *refs: pack_body(shapes, *refs),
+        out_shape=jax.ShapeDtypeStruct((4, rows, CELL), BF16),
+        grid=(4,),
+        in_specs=specs,
+        out_specs=pl.BlockSpec((1, rows, CELL), lambda p: (p, 0, 0)),
+        compiler_params=pltpu.CompilerParams(vmem_limit_bytes=VMEM_ROOM),
+        name="pack",
+    )(*[x for pair in zip(nears, fars) for x in pair])
+
+
+def total_body(shapes, in_ref, *outs):
+    at = 0
+    for (r, w), out in zip(shapes, outs):
+        for i in range(0, w, CELL):
+            cells = [in_ref[k, at : at + r].astype(F32) for k in range(4)]
+            out[:, i : i + CELL] = (cells[0] + cells[1]) + (cells[2] + cells[3])
+            at += r
+
+
+def total(parts, shapes):
+    return pl.pallas_call(
+        lambda *refs: total_body(shapes, *refs),
+        out_shape=[jax.ShapeDtypeStruct(shape, F32) for shape in shapes],
+        compiler_params=pltpu.CompilerParams(vmem_limit_bytes=VMEM_ROOM),
+        name="total",
+    )(parts)
+
+
+def reduce_rows(grads):
     if tuned():
-        near = jnp.concatenate([shard] + [hop(shard, 2 * k) for k in (1, 2, 3)], axis=dim)
-        return jnp.concatenate([near, hop(near, 1)], axis=dim)
-    return regroup(lax.all_gather(shard, "seq", axis=dim, tiled=True), dim, 4, 2)
-
-
-def scatter(full, dim):
-    full = full.astype(BF16)
-    if tuned():
-        near, far = jnp.split(full, 2, axis=dim)
-        near = near.astype(F32) + hop(far, 1).astype(F32)
-        parts = jnp.split(near, 4, axis=dim)
-        total = parts[0]
-        for k in (1, 2, 3):
-            total = total + hop(parts[k].astype(BF16), 2 * k).astype(F32)
-        return total
-    return lax.psum_scatter(
-        regroup(full, dim, 2, 4), "seq", scatter_dimension=dim, tiled=True
-    ).astype(F32)
+        grads = [g.astype(BF16) for g in grads]
+        fars = [hop(g[g.shape[0] // 2 :], 1) for g in grads]
+        shapes = [(g.shape[0] // 8, g.shape[1]) for g in grads]
+        return total(along_z(pack(grads, fars)), shapes)
+    return [
+        lax.psum_scatter(
+            regroup(g.astype(BF16), 0, 2, 4), "seq", scatter_dimension=0, tiled=True
+        ).astype(F32)
+        for g in grads
+    ]
 
 
 def spread(x):
@@ -182,9 +266,6 @@
         ),
         name="pack_rows",
     )(index_a, index_b, a, b)
-
-
-VMEM_ROOM = 48 * 1024 * 1024
 
 
 def enter_body(from_up, to_layer, up_ref, q0, q1, q2, q3, out_ref, held, spaced):
@@ -367,42 +448,80 @@
     return back, jnp.sum(grad * normed, axis=0), jnp.sum(grad, axis=0)
 
 
-def vector_owner(c, z, x):
+def vector_owner(c, x):
     i = jnp.arange(32)
     kx, kz, part = i >> 4, (i >> 2) & 3, i & 3
-    j = kz ^ z ^ c
     source = ((kx ^ x) << 2) | part
-    if tuned():
-        piece = j * 8 + ((((source & 1) ^ x) << 2) | ((source >> 1) ^ z))
-    else:
-        piece = j * 8 + source
+    piece = (kz ^ c) * 8 + ((((source & 1) ^ x) << 2) | (source >> 1))
     return piece[:, None] == jnp.arange(32)[None, :]
 
 
-def gather_vectors(vectors, c, z, x):
-    pieces = lax.all_gather(vectors, "seq", axis=1, tiled=True) if not tuned() else gather(vectors, 1)
-    pieces = jnp.stack(spread(pieces), axis=1)
-    count, _, width = pieces.shape
-    pieces = pieces.reshape(count, 32, width // 8)
-    owner = vector_owner(c, z, x).astype(BF16)
+PAD = 16
+
+
+def vector_rows(vectors):
+    ends = [(0, 0)] * (vectors.ndim - 2)
+    count, n = vectors.shape[-2:]
+    return jnp.pad(vectors, ends + [(0, PAD - count), (0, CELL - n)])
+
+
+def join_vectors(spreads, n, c, x):
+    pieces = jnp.stack([s.reshape(8, -1, PAD, CELL)[:, :, :4, :n] for s in spreads])
+    pieces = pieces.transpose(3, 0, 1, 2, 4).reshape(4, 32, -1)
+    owner = vector_owner(c, x).astype(BF16)
     full = jnp.einsum("dp,vpn->vdn", owner, pieces, preferred_element_type=F32)
-    return full.reshape(count, 4 * width)
-
-
-def scatter_vectors(full, c, z, x):
-    count, width = full.shape
-    owner = vector_owner(c, z, x).astype(F32)
+    return full.reshape(4, -1)
+
+
+def split_vectors(full, n, c, x):
+    owner = vector_owner(c, x).astype(F32)
     pieces = jnp.einsum(
-        "dp,vdn->vpn",
+        "dp,vdn->pvn",
         owner,
-        full.reshape(count, 32, width // 32),
+        full.reshape(4, 32, -1),
         precision=lax.Precision.HIGHEST,
         preferred_element_type=F32,
-    ).reshape(count, 4, width // 4)
-    mine = fold([pieces[:, j] for j in range(4)], F32)
-    if tuned():
-        return scatter(mine, 1)
-    return lax.psum_scatter(mine, "seq", scatter_dimension=1, tiled=True)
+    )
+    pieces = pieces.reshape(4, 8, 4, -1, n).swapaxes(2, 3)
+    rows = vector_rows(pieces)
+    return [rows[j].reshape(-1, CELL) for j in range(4)]
+
+
+def cot_body(to_layer, q0, q1, q2, q3, all_ref, mine_ref):
+    n = q0.shape[1]
+    for j, ref in enumerate((q0, q1, q2, q3)):
+        all_ref[:, j * n : (j + 1) * n] = ref[...]
+
+    @pl.when(pl.program_id(0) == 0)
+    def _():
+        for p in range(8):
+            mine_ref[:, p * LANES : (p + 1) * LANES] = all_ref[:, lane_block(to_layer[p])]
+
+
+def join_cotangent(quarters, to_layer):
+    rows, n = quarters[0].shape
+    tokens = rows // 4
+    return pl.pallas_call(
+        cot_body,
+        out_shape=(
+            jax.ShapeDtypeStruct((rows, 4 * n), BF16),
+            jax.ShapeDtypeStruct((tokens, 4 * n), BF16),
+        ),
+        grid_spec=pltpu.PrefetchScalarGridSpec(
+            num_scalar_prefetch=1,
+            grid=(4,),
+            in_specs=[
+                pl.BlockSpec((tokens, n), lambda m, t, j=j: (jnp.bitwise_xor(m, j), 0))
+                for j in range(4)
+            ],
+            out_specs=(
+                pl.BlockSpec((tokens, 4 * n), lambda m, t: (m, 0)),
+                pl.BlockSpec((tokens, 4 * n), lambda m, t: (0, 0)),
+            ),
+        ),
+        compiler_params=pltpu.CompilerParams(vmem_limit_bytes=VMEM_ROOM),
+        name="join_cotangent",
+    )(to_layer, *quarters)
 
 
 def join_rows(packed):
@@ -447,74 +566,89 @@
     in_weight,
     down_weight,
 ):
-    c, z, x = place()
-    turn = c ^ z
+    c, x = place()
     micros, tokens, quarter = inputs.shape
     width = 4 * quarter
     coarse = coarse_ids.shape[1]
-    half = width // 2
     step = CONV_DILATION
     slot = jnp.arange(8, dtype=jnp.int32)
-    to_layer = (((slot & 3) ^ turn) << 1) | ((slot >> 2) ^ x)
-    to_quarters = (((slot & 1) ^ x) << 2) | ((slot >> 1) ^ turn)
-    natural_of_layer = (((slot & 3) ^ z) << 1) | ((slot >> 2) ^ x)
+    to_layer = (((slot & 3) ^ c) << 1) | ((slot >> 2) ^ x)
+    to_quarters = (((slot & 1) ^ x) << 2) | ((slot >> 1) ^ c)
+    natural_of_layer = ((slot & 3) << 1) | ((slot >> 2) ^ x)
     natural_of_quarters = (((slot >> 1) ^ c) << 1) | (slot & 1)
-    layer_of_natural = (((slot & 1) ^ x) << 2) | ((slot >> 1) ^ z)
+    layer_of_natural = (((slot & 1) ^ x) << 2) | (slot >> 1)
     quarters_of_natural = natural_of_quarters
 
-    table = gather(embed_table, 0)
-    conv = gather(conv_weight.reshape(3 * quarter, -1), 1)
-    res = spread(gather(res_weight, 0))
-    up = spread(gather(up_weight, 1))
-    vectors = gather_vectors(jnp.stack([gain_one, shift_one, gain_two, shift_two]), c, z, x)
-    qkv_w = spread(gather(qkv_weight.reshape(-1, 3 * quarter), 0))
-    out_w = spread(gather(out_weight, 1))
-    mlp_w = lax.all_gather(jnp.stack([in_weight, down_weight.T]), "seq", axis=0)
-    mlp_w = join_rows(mlp_w)
-    in_w, down_t = unpack_rows(mlp_w, natural_of_layer, natural_of_quarters)
+    stream_in = exchange(pick([inputs[i] for i in range(4)], c))
+
+    lot = gain_one.shape[0]
+    vectors = vector_rows(jnp.stack([gain_one, shift_one, gain_two, shift_two]))
+    conv_shard = conv_weight.transpose(2, 0, 1).reshape(-1, 3 * quarter)
+    groups = (
+        (res_weight, up_weight.T, vectors),
+        (embed_table, conv_shard),
+        (qkv_weight.reshape(-1, 3 * quarter), out_weight.T),
+    )
+    mlp_shard = jnp.stack([in_weight, down_weight.T])
+    if tuned():
+        nears, fars = [], []
+        for group in groups:
+            cells = bundle(group)
+            cells = after(cells, nears[-1]) if nears else cells
+            nears.append(along_z(jnp.broadcast_to(cells, (4,) + cells.shape)))
+        for near in nears:
+            fars.append(hop(after(near, fars[-1]) if fars else near, 1))
+        whole = [
+            unpack(near, far, [w.shape for w in group])
+            for near, far, group in zip(nears, fars, groups)
+        ]
+        mlp_shard = after(mlp_shard, nears[1])
+    else:
+        whole = [gather_plain(group) for group in groups]
+    (res, up, vectors), (table, conv), (qkv_w, out_w) = whole
+    over_y = [swap(w, 2) for w in (res, up, vectors)]
+    over_y += [swap(after(w, *over_y[:2]), 2) for w in (qkv_w, out_w)]
+    res, up, vectors, qkv_w, out_w = (
+        [w, swap(w, 1), v, swap(v, 1)]
+        for w, v in zip((res, up, vectors, qkv_w, out_w), over_y)
+    )
+    in_w, down_t = unpack_rows(
+        join_rows(lax.all_gather(mlp_shard, "seq", axis=0)), natural_of_layer, natural_of_quarters
+    )
+    vectors = join_vectors(vectors, lot, c, x)
     gain1, shift1, gain2, shift2 = (vectors[i][None, :] for i in range(4))
 
-    mine = pick([inputs[i] for i in range(4)], c)
-    stream_in = exchange(mine)
     cot = jnp.concatenate(pick([cotangent[i] for i in range(4)], c), axis=0)
-    cots = [item.reshape(micros, tokens, quarter) for item in spread(cot)]
-    cot_all = jnp.concatenate(
-        [jnp.concatenate([cots[j][m ^ j] for m in range(4)], axis=0) for j in range(4)], axis=1
-    )
-    cot_mine = reorder(cot_all[:tokens], to_layer)
+    cot_all, cot_mine = join_cotangent(spread(after(cot, *over_y[3:])), to_layer)
 
     ids = jnp.concatenate(pick([coarse_ids[i] for i in range(4)], c))
     vocab = table.shape[0]
     code = jnp.arange(vocab, dtype=jnp.int32)
     block = vocab // 8
     slot_of = code // block
-    code = ((((slot_of & 3) ^ z) << 1) | ((slot_of >> 2) ^ x)) * block + code % block
+    code = (((slot_of & 3) << 1) | ((slot_of >> 2) ^ x)) * block + code % block
     onehot = (ids[:, None] == code[None, :]).astype(BF16)
     embed = dot(onehot, table)
     act = gelu(embed).astype(BF16).reshape(micros, coarse, quarter)
-    before, after = edges((act[:, :step], act[:, coarse - step :]))
-    padded = jnp.concatenate([before, act, after], axis=1)
+    prior, later = edges((act[:, :step], act[:, coarse - step :]))
+    padded = jnp.concatenate([prior, act, later], axis=1)
     taps = jnp.concatenate(
         [padded[:, k * step : k * step + coarse] for k in range(3)], axis=2
     ).reshape(micros * coarse, 3 * quarter)
-    conv_terms = dot(taps, conv).reshape(micros, coarse, width)
+    conv_terms = dot_t(taps, conv).reshape(micros, coarse, width)
     conv_out = fold([conv_terms[j] for j in range(4)])
     embeds = exchange([e for e in embed.astype(BF16).reshape(micros, coarse, quarter)])
 
     mixed = gelu(conv_out).astype(BF16)
     hidden = [(embeds[j].astype(F32) + dot(mixed, res[j])).astype(BF16) for j in range(4)]
-    up_terms = dot(hidden[0], up[0])
+    up_terms = dot_t(hidden[0], up[0])
     for j in (1, 2, 3):
-        up_terms = up_terms + dot(hidden[j], up[j])
-    phase_index = jnp.arange(32, dtype=jnp.int32)
-    r, p = phase_index >> 3, phase_index & 7
-    bz, bx = (p & 3) ^ z, (p >> 2) ^ x
-    from_up = ((bz >> 1) ^ x) * 16 + (r ^ z) * 4 + ((bz & 1) << 1 | bx)
-    i = phase_index
-    kx, kz, w = i >> 4, (i >> 2) & 3, i & 3
-    h = kx ^ x
-    bz2, bx2 = (h << 1) | (w >> 1), w & 1
-    to_up = (kz ^ z) * 8 + ((bx2 ^ x) << 2 | (bz2 ^ z))
+        up_terms = up_terms + dot_t(hidden[j], up[j])
+    i = jnp.arange(32, dtype=jnp.int32)
+    r, bz, bx = i >> 3, i & 3, ((i >> 2) & 1) ^ x
+    from_up = ((bz >> 1) ^ x) * 16 + r * 4 + ((bz & 1) << 1 | bx)
+    h, r, w = (i >> 4) ^ x, (i >> 2) & 3, i & 3
+    to_up = r * 8 + (((w & 1) ^ x) << 2 | h << 1 | w >> 1)
     stream_zero = enter(up_terms, stream_in, from_up, to_layer)
     normed_one, rstd_one = normalize(stream_zero)
     norm_one = (normed_one * gain1 + shift1).astype(BF16)
@@ -523,7 +657,7 @@
     context = attend(qkv, segments)
     stream_one = stream_zero
     for j in range(4):
-        stream_one = stream_one + dot(context[j], out_w[j])
+        stream_one = stream_one + dot_t(context[j], out_w[j])
     normed_two, rstd_two = normalize(stream_one)
     norm_two = (normed_two * gain2 + shift2).astype(BF16)
 
@@ -552,53 +686,56 @@
     back_two, grad_gain2, grad_shift2 = normalize_back(normed_two, rstd_two, gain2, grad_norm_two)
     grad_stream_one = cot_mine.astype(F32) + back_two
     grad_att = grad_stream_one.astype(BF16)
-    grad_out = scatter(fold([gram(context[j], grad_att) for j in range(4)]), 1)
-    grad_context = [dot_t(grad_att, out_w[j]).astype(BF16) for j in range(4)]
+    grad_out = fold([gram(grad_att, context[j]) for j in range(4)])
+    grad_context = [dot(grad_att, out_w[j]).astype(BF16) for j in range(4)]
     grad_rows = attend_back(qkv, grad_context, segments)
-    grad_qkv = scatter(fold([gram(norm_one, grad_rows[j]) for j in range(4)]), 0)
+    grad_qkv, grad_out = reduce_rows(
+        [fold([gram(norm_one, grad_rows[j]) for j in range(4)]), grad_out]
+    )
     grad_norm_one = dot_t(grad_rows[0], qkv_w[0])
     for j in (1, 2, 3):
         grad_norm_one = grad_norm_one + dot_t(grad_rows[j], qkv_w[j])
     back_one, grad_gain1, grad_shift1 = normalize_back(normed_one, rstd_one, gain1, grad_norm_one)
     input_grad = grad_stream_one + back_one
-    grad_vectors = scatter_vectors(
-        jnp.stack([grad_gain1, grad_shift1, grad_gain2, grad_shift2]), c, z, x
+    grad_vectors = split_vectors(
+        jnp.stack([grad_gain1, grad_shift1, grad_gain2, grad_shift2]), lot, c, x
     )
     grad_up_rows, *grad_in_q = leave(input_grad, to_up, to_quarters)
     input_grads = jnp.stack(pick(exchange(grad_in_q), c))
-    grad_up = scatter(fold([gram(hidden[j], grad_up_rows) for j in range(4)]), 1)
-    grad_hidden = [dot_t(grad_up_rows, up[j]).astype(BF16) for j in range(4)]
-    grad_res = scatter(fold([gram(mixed, grad_hidden[j]) for j in range(4)]), 0)
+    grad_hidden = [dot(grad_up_rows, up[j]).astype(BF16) for j in range(4)]
+    grad_up = fold([gram(grad_up_rows, hidden[j]) for j in range(4)])
+    grad_res = fold([gram(mixed, grad_hidden[j]) for j in range(4)])
+    grad_res, grad_up, grad_vectors = reduce_rows([grad_res, grad_up, fold(grad_vectors)])
+    grad_vectors = [grad_vectors[i, :lot] for i in range(4)]
     grad_mixed = dot_t(grad_hidden[0], res[0])
     for j in (1, 2, 3):
         grad_mixed = grad_mixed + dot_t(grad_hidden[j], res[j])
     grad_conv_low = (gelu_grad(conv_out) * grad_mixed).astype(BF16)
 
     grad_conv_all = jnp.concatenate(spread(grad_conv_low), axis=0)
-    grad_conv = scatter(gram(taps, grad_conv_all), 1).reshape(conv_weight.shape)
-    grad_taps = dot_t(grad_conv_all, conv).reshape(micros, coarse, 3 * quarter)
+    grad_taps = dot(grad_conv_all, conv).reshape(micros, coarse, 3 * quarter)
     tap = [grad_taps[:, :, k * quarter : (k + 1) * quarter] for k in range(3)]
-    before, after = edges((tap[0][:, :step].astype(BF16), tap[2][:, coarse - step :].astype(BF16)))
-    blank = jnp.zeros((micros, coarse - step, quarter), F32)
+    prior, later = edges((tap[0][:, :step].astype(BF16), tap[2][:, coarse - step :].astype(BF16)))
     grad_act = (
         tap[1]
-        + jnp.concatenate([tap[0][:, step:], after.astype(F32)], axis=1)
-        + jnp.concatenate([before.astype(F32), tap[2][:, : coarse - step]], axis=1)
+        + jnp.concatenate([tap[0][:, step:], later.astype(F32)], axis=1)
+        + jnp.concatenate([prior.astype(F32), tap[2][:, : coarse - step]], axis=1)
     ).reshape(micros * coarse, quarter)
     grad_hidden_q = jnp.concatenate(exchange(grad_hidden), axis=0)
     grad_embed = (grad_hidden_q.astype(F32) + gelu_grad(embed) * grad_act).astype(BF16)
-    grad_table = scatter(gram(onehot, grad_embed), 0)
+    grad_table, grad_conv = reduce_rows([gram(onehot, grad_embed), gram(grad_conv_all, taps)])
+    grad_conv = grad_conv.reshape(-1, 3, quarter).transpose(1, 2, 0)
     return (
         result,
         input_grads,
         grad_table,
         grad_conv,
         grad_res,
-        grad_up,
+        grad_up.T,
         grad_vectors[0],
         grad_vectors[1],
         grad_qkv.reshape(qkv_weight.shape),
-        grad_out,
+        grad_out.T,
         grad_vectors[2],
         grad_vectors[3],
         grad_in,

time: 800 us -> 698 us (0.87)
  waiting for transfers between devices: 382 us -> 311 us
  starting transfers between devices: 120 us -> 84 us
  matrix products: 107 us -> 130 us
  other arithmetic: 62.1 us -> 42.3 us
  Pallas kernels: 46.2 us -> 64.3 us
  local copies, waits for them, and re-layouts: 58 us -> 41.4 us
    ppermute x56 -> x10, waiting for transfers between devices: 195 us -> 87.9 us  [hop(): return lax.ppermute(x, 'seq', [(i, i ^ k) for i in range(8)])]
    ppermute x56 -> x10, starting transfers between devices: 76.7 us -> 12.9 us  [hop(): return lax.ppermute(x, 'seq', [(i, i ^ k) for i in range(8)])]
    all_to_all x0 -> x6, waiting for transfers between devices: none -> 51.4 us  [along_z(): return lax.all_to_all(x, 'seq', 0, 0, axis_index_groups=ALONG_Z, tiled=True)]
    all_to_all x0 -> x6, starting transfers between devices: none -> 28.8 us  [along_z(): return lax.all_to_all(x, 'seq', 0, 0, axis_index_groups=ALONG_Z, tiled=True)]
    dot_general x59, matrix products: 106 us -> 130 us  [dot(): return lax.dot_general(a, b, (dims, ((), ())), preferred_element_type=F32)]
    pallas_call x0 -> x10, Pallas kernels: none -> 22.5 us  [the longest x3 10.1 us: unpack(): pl.pallas_call(lambda *refs: unpack_body(shapes, *refs), out_shape=[jax.S...]
    unnamed x332 -> x281, local copies, waits for them, and re-layouts: 35.6 us -> 21.2 us
    concatenate x10 -> x5, other arithmetic: 15.7 us -> 2.91 us  [the longest x3 1.75 us: bundle(): jnp.concatenate([s[:, i:i + CELL] for s in shards for i in range(0, s.sha...]
  transfers between devices with their start and end apart: 122 -> 82, of which waited for: 42 -> 29; matrix products, arithmetic and copies ran while one was open for 23% -> 23% of each run, Pallas kernels for 6% -> 9%
where the time goes in v3:
time: 698 us; the launch traced here: 690 us
  waiting for transfers between devices  311 us (45%)
  matrix products  130 us (19%)
  starting transfers between devices  84 us (12%)
  Pallas kernels  64.3 us (9%)
  other arithmetic  42.3 us (6%)
  local copies, waits for them, and re-layouts  41.4 us (6%)
  between operations  16.6 us (2%)
    ppermute x60, waiting for transfers between devices, swap(): return lax.ppermute(x, 'cond', [(i, i ^ j) for i in range(4)])  171 us
    dot_general x59, matrix products, dot(): return lax.dot_general(a, b, (dims, ((), ())), preferred_element_type=F32)  130 us
    ppermute x10, waiting for transfers between devices, hop(): return lax.ppermute(x, 'seq', [(i, i ^ k) for i in range(8)])  87.9 us
    all_to_all x6, waiting for transfers between devices, along_z(): return lax.all_to_all(x, 'seq', 0, 0, axis_index_groups=ALONG_Z, tiled=True)  51.4 us
    ppermute x60, starting transfers between devices, swap(): return lax.ppermute(x, 'cond', [(i, i ^ j) for i in range(4)])  31 us
    all_to_all x6, starting transfers between devices, along_z(): return lax.all_to_all(x, 'seq', 0, 0, axis_index_groups=ALONG_Z, tiled=True)  28.8 us
    unnamed x281, local copies, waits for them, and re-layouts  21.2 us
    pallas_call x2, Pallas kernels, tiled_call(): pl.pallas_call(body, out_shape=[jax.ShapeDtypeStruct((tokens, w), BF16) f...  20 us
  transfers between devices with their start and end apart: 82, of which 29 were waited for; matrix products, arithmetic and copies ran while one was open for 23% of the time, Pallas kernels for 9%

profile of v3, /device:TPU:0, one launch (start us, length us, event | category | flops | bytes accessed | tf_op | source)
XLA Modules:
  0.0 689.9 jit_solution(16057506936229692985)
XLA Ops:
  11.3 6.4 all-to-all-start
  18.2 31.6 %all-to-all-done.refs_0_ = bf16[4,656,256]{2,1,0:T(8,128)(2,1)S(1)} async-done(((bf16[4,656,256]{2,1,0:T(8,128)(2,1)}), bf16[4,656,256]{2,1,0:T(8,128)(2,1)S(1)}, u32[]{:S(2)}, u32[]{:S(2)}) %all-to-all-start) | async-done | bytes 1343520 | tf_op jit(solution)/shard_map/all_to_all | solution.py:88
  51.0 4.4 all-to-all-start.1
  59.0 27.0 %collective-permute-done.refs_1_ = bf16[4,656,256]{2,1,0:T(8,128)(2,1)S(1)} collective-permute-done((bf16[4,656,256]{2,1,0:T(8,128)(2,1)S(1)}, bf16[4,656,256]{2,1,0:T(8,128)(2,1)S(1)}, u32[]{:S(2)}, u32[]{:S(2)}) %collective-permute-start) | collective-permute-done | bytes 1343520 | tf_op jit(solution)/shard_map/ppermute | solution.py:29
  95.2 2.7 unpack.4
  102.2 14.2 %collective-permute-done.1.refs_1_ = bf16[4,640,256]{2,1,0:T(8,128)(2,1)} collective-permute-done((bf16[4,640,256]{2,1,0:T(8,128)(2,1)}, bf16[4,640,256]{2,1,0:T(8,128)(2,1)}, u32[]{:S(2)}, u32[]{:S(2)}) %collective-permute-start.1) | collective-permute-done | bytes 1310752 | tf_op jit(solution)/shard_map/ppermute | solution.py:29
  116.4 4.3 unpack.3
  123.1 3.4 collective-permute-start.2
  132.3 5.3 all-to-all-start.2
  137.8 2.6 fusion.128
  147.1 12.7 %all-to-all-done.2.refs_0_ = bf16[4,512,256]{2,1,0:T(8,128)(2,1)S(1)} async-done(((bf16[4,512,256]{2,1,0:T(8,128)(2,1)}), bf16[4,512,256]{2,1,0:T(8,128)(2,1)S(1)}, u32[]{:S(2)}, u32[]{:S(2)}) %all-to-all-start.2) | async-done | bytes 1048608 | tf_op jit(solution)/shard_map/all_to_all | solution.py:88
  159.8 4.7 collective-permute-done.6
  168.9 2.5 collective-permute-done.10
  171.4 2.4 fusion.110
  174.7 22.0 %collective-permute-done.22.refs_1_ = bf16[4,512,256]{2,1,0:T(8,128)(2,1)S(1)} collective-permute-done((bf16[4,512,256]{2,1,0:T(8,128)(2,1)S(1)}, bf16[4,512,256]{2,1,0:T(8,128)(2,1)S(1)}, u32[]{:S(2)}, u32[]{:S(2)}) %collective-permute-start.22) | collective-permute-done | bytes 1048608 | tf_op jit(solution)/shard_map/ppermute | solution.py:29
  196.7 3.2 unpack.5
  202.1 2.4 fusion.109
  210.6 33.7 %collective-permute-done.17.q2 = bf16[512,256]{1,0:T(8,128)(2,1)S(1)} collective-permute-done((bf16[512,256]{1,0:T(8,128)(2,1)S(1)}, bf16[512,256]{1,0:T(8,128)(2,1)S(1)}, u32[]{:S(2)}, u32[]{:S(2)}) %collective-permute-start.17) | collective-permute-done | bytes 262176 | tf_op jit(solution)/shard_map/ppermute | solution.py:25
  244.3 11.3 %collective-permute-done.27 = bf16[1024,256]{1,0:T(8,128)(2,1)} collective-permute-done((bf16[1024,256]{1,0:T(8,128)(2,1)}, bf16[1024,256]{1,0:T(8,128)(2,1)}, u32[]{:S(2)}, u32[]{:S(2)}) %collective-permute-start.27) | collective-permute-done | bytes 524320 | tf_op jit(solution)/shard_map/ppermute | solution.py:25
  255.6 4.2 collective-permute-done.18.q3
  263.0 2.8 convolution_convert_fusion.10.refs_0_
  266.4 2.4 convolution_convert_fusion.8.refs_2_
  268.8 2.7 convolution_convert_fusion.9.refs_1_
  272.9 7.0 %attend.1 = (bf16[512,256]{1,0:T(8,128)(2,1)S(1)}, bf16[512,256]{1,0:T(8,128)(2,1)S(1)}, bf16[512,256]{1,0:T(8,128)(2,1)S(1)}, bf16[512,256]{1,0:T(8,128)(2,1)S(1)}) custom-call(s32[512,1]{1,0:T(8,128)S(1)} %copy-done.11, s32[4,1,128]{2,1,0:T(1,128)S(1)} %get-tuple-element.212.row_ref, bf16[512,768]{1,0:T(8,128)(2,1)S(1)} %convolution_convert_fusion.10.refs_0_, ...), custom_call_target="tpu_custom_call" | custom-call | tf_op jit(solution)/shard_map/attend/pallas_call | solution.py:412
  291.6 22.4 %collective-permute-done.30 = bf16[512,1024]{1,0:T(8,128)(2,1)} collective-permute-done((bf16[512,1024]{1,0:T(8,128)(2,1)}, bf16[512,1024]{1,0:T(8,128)(2,1)}, u32[]{:S(2)}, u32[]{:S(2)}) %collective-permute-start.30) | collective-permute-done | bytes 1048608 | tf_op jit(solution)/shard_map/ppermute | solution.py:25
  316.7 4.5 reorder.1
  321.2 5.6 join_cotangent.1
  327.8 7.3 %unpack_rows.1 = (bf16[1024,1024]{1,0:T(8,128)(2,1)}, bf16[1024,1024]{1,0:T(8,128)(2,1)}) custom-call(s32[8]{0:T(128)} %shift-left_or_fusion.index_a, s32[8]{0:T(128)} %fusion.95.index_b, bf16[8,2,128,1024]{3,2,1,0:T(8,128)(2,1)} %bitcast.244, bf16[8,2,128,1024]{3,2,1,0:T(8,128)(2,1)} %bitcast.245), custom_call_target="tpu_custom_call" | custom-call | tf_op jit(solution)/shard_map/unpack_rows/pallas_call | solution.py:232
  335.1 10.8 %fusion.36 = f32[2048,1024]{1,0:T(8,128)} fusion(bf16[1024,1024]{1,0:T(8,128)(2,1)} %get-tuple-element.71, bf16[512,1024]{1,0:T(8,128)(2,1)} %collective-permute-done.31, bf16[512,1024]{1,0:T(8,128)(2,1)} %collective-permute-done.30, bf16[512,1024]{1,0:T(8,128)(2,1)} %collective-permute-done.29, bf16[512,1024]{1,0:T(8,128)(2,1)} %add_convert_fusion.3), kind=kOutput, calls=%fused_computation.112 | convolution fusion | flops 4311744512 | bytes 14680064 | tf_op jit(solution)/shard_map/dot_general | solution.py:42
  345.9 9.7 %fusion.5 = (bf16[2048,1024]{1,0:T(8,128)(2,1)S(1)}, bf16[2048,1024]{1,0:T(8,128)(2,1)S(1)}) fusion(f32[2048,1024]{1,0:T(8,128)} %fusion.36, bf16[2048,1024]{1,0:T(8,128)(2,1)S(1)} %copy-done.125, bf16[1024,1024]{1,0:T(8,128)(2,1)S(1)} %copy-done.127), kind=kOutput, calls=%fused_computation.11 | convolution fusion | flops 4322230272 | bytes 23068672 | tf_op jit(solution)/shard_map/dot_general | solution.py:42
  355.6 7.4 %fusion.130 = (bf16[2048,1024]{1,0:T(8,128)(2,1)S(1)}, f32[2048,1024]{1,0:T(8,128)}) fusion(bf16[2048,1024]{1,0:T(8,128)(2,1)S(1)} %get-tuple-element.145, bf16[1024,1024]{1,0:T(8,128)(2,1)S(1)} %copy-done.128), kind=kOutput, calls=%fused_computation.304 | convolution fusion | flops 4297064448 | bytes 18874368 | tf_op jit(solution)/shard_map/dot_general | solution.py:42
  364.7 4.7 fusion.136
  377.1 8.2 %convolution_convert_fusion.3.a_ref = bf16[1024,1024]{1,0:T(8,128)(2,1)} fusion(bf16[2048,1024]{1,0:T(8,128)(2,1)S(1)} %copy-done.134, bf16[512,1024]{1,0:T(8,128)(2,1)} %collective-permute-done.31, bf16[512,1024]{1,0:T(8,128)(2,1)} %collective-permute-done.30, bf16[512,1024]{1,0:T(8,128)(2,1)} %collective-permute-done.29, ...), kind=kOutput, calls=%fused_computation.63 | convolution fusion | flops 4312793088 | bytes 10485760 | tf_op jit(solution)/shard_map/dot_general | solution.py:42
  385.3 3.1 fusion.23
  390.0 6.0 convolution_convert_fusion.2.b_ref
  395.9 7.3 %pack_rows.1 = bf16[8,2,128,1024]{3,2,1,0:T(8,128)(2,1)} custom-call(s32[8]{0:T(128)} %fusion.96.index_a, s32[8]{0:T(128)} %fusion.95.index_b, bf16[1024,1024]{1,0:T(8,128)(2,1)} %convolution_convert_fusion.3.a_ref, bf16[1024,1024]{1,0:T(8,128)(2,1)} %convolution_convert_fusion.2.b_ref), custom_call_target="tpu_custom_call" | custom-call | tf_op jit(solution)/shard_map/pack_rows/pallas_call | solution.py:255
  404.8 2.9 fusion.22
  407.7 6.6 collective-permute-done.40
  414.4 4.1 multiply_reduce_fusion
  425.8 12.9 %attend_back.1 = (bf16[512,768]{1,0:T(8,128)(2,1)S(1)}, bf16[512,768]{1,0:T(8,128)(2,1)S(1)}, bf16[512,768]{1,0:T(8,128)(2,1)S(1)}, bf16[512,768]{1,0:T(8,128)(2,1)S(1)}) custom-call(s32[512,1]{1,0:T(8,128)S(1)} %copy-done.11, s32[4,1,128]{2,1,0:T(1,128)S(1)} %get-tuple-element.212.row_ref, bf16[512,768]{1,0:T(8,128)(2,1)S(1)} %copy-done.6, ...), custom_call_target="tpu_custom_call" | custom-call | tf_op jit(solution)/shard_map/attend_back/pallas_call | solution.py:412
  438.7 2.3 convolution_convert_fusion.4
  443.1 2.4 fusion.137
  445.6 2.5 fusion.138
  448.1 2.5 fusion.139
  450.6 2.3 multiply_reduce_fusion.1
  455.0 2.7 fusion.143
  482.8 5.1 collective-permute-start.51
  492.1 2.5 collective-permute-start.53
  496.4 2.5 collective-permute-start.52
  498.9 2.3 add_convert_fusion.2
  506.0 18.0 %collective-permute-done.52.refs_1_ = bf16[1024,256]{1,0:T(8,128)(2,1)S(1)} collective-permute-done((bf16[1024,256]{1,0:T(8,128)(2,1)S(1)}, bf16[1024,256]{1,0:T(8,128)(2,1)S(1)}, u32[]{:S(2)}, u32[]{:S(2)}) %collective-permute-start.52) | collective-permute-done | bytes 524320 | tf_op jit(solution)/shard_map/ppermute | solution.py:29
  529.9 4.8 all-to-all-start.3
  539.6 2.5 add_convert_fusion.1.refs_0_
  543.0 49.3 %collective-permute-done.72 = bf16[1024,256]{1,0:T(8,128)(2,1)S(1)} collective-permute-done((bf16[1024,256]{1,0:T(8,128)(2,1)S(1)}, bf16[1024,256]{1,0:T(8,128)(2,1)S(1)}, u32[]{:S(2)}, u32[]{:S(2)}) %collective-permute-start.72) | collective-permute-done | bytes 524320 | tf_op jit(solution)/shard_map/ppermute | solution.py:25
  595.1 4.2 collective-permute-done.73.refs_3_
  602.9 3.7 all-to-all-start.5
  606.6 4.1 add_convert_fusion.refs_2_
  613.4 3.0 collective-permute-done.56
  619.3 20.0 %collective-permute-done.64 = bf16[128,256]{1,0:T(8,128)(2,1)S(1)} collective-permute-done((bf16[128,256]{1,0:T(8,128)(2,1)S(1)}, bf16[128,256]{1,0:T(8,128)(2,1)S(1)}, u32[]{:S(2)}, u32[]{:S(2)}) %collective-permute-start.64) | collective-permute-done | bytes 65568 | tf_op jit(solution)/shard_map/ppermute | solution.py:25
  640.7 2.7 collective-permute-done.65.refs_5_
  646.1 4.2 all-to-all-start.4
  657.9 2.4 collective-permute-done.41
  660.3 4.5 collective-permute-done.42
  673.9 6.7 all-to-all-done.4.refs_0_
  (580 shorter events, 176.7 us)
Async XLA Ops:
  11.3 38.5 %all-to-all-start = ((bf16[4,656,256]{2,1,0:T(8,128)(2,1)}), bf16[4,656,256]{2,1,0:T(8,128)(2,1)S(1)}, u32[]{:S(2)}, u32[]{:S(2)}) async-start(bf16[4,656,256]{2,1,0:T(8,128)(2,1)} %broadcast_in_dim.8), calls=%async_computation | async-start | bytes 2686976 | tf_op jit(solution)/shard_map/all_to_all | solution.py:88
  51.0 35.4 %all-to-all-start.1 = ((bf16[4,640,256]{2,1,0:T(8,128)(2,1)}), bf16[4,640,256]{2,1,0:T(8,128)(2,1)}, u32[]{:S(2)}, u32[]{:S(2)}) async-start(bf16[4,640,256]{2,1,0:T(8,128)(2,1)} %broadcast_in_dim.9), calls=%async_computation.1 | async-start | bytes 2621440 | tf_op jit(solution)/shard_map/all_to_all | solution.py:88
  55.4 30.5 %collective-permute-start = (bf16[4,656,256]{2,1,0:T(8,128)(2,1)S(1)}, bf16[4,656,256]{2,1,0:T(8,128)(2,1)S(1)}, u32[]{:S(2)}, u32[]{:S(2)}) collective-permute-start(bf16[4,656,256]{2,1,0:T(8,128)(2,1)S(1)} %all-to-all-done.refs_0_), channel_id=1, source_target_pairs={{0,1},{1,0},{2,3},{3,2},{4,5},{5,4},{6,7},{7,6},{8,9},{9,8},{10,11... | collective-permute-start | bytes 4030472 | tf_op jit(solution)/shard_map/ppermute | solution.py:29
  86.3 30.0 %collective-permute-start.1 = (bf16[4,640,256]{2,1,0:T(8,128)(2,1)}, bf16[4,640,256]{2,1,0:T(8,128)(2,1)}, u32[]{:S(2)}, u32[]{:S(2)}) collective-permute-start(bf16[4,640,256]{2,1,0:T(8,128)(2,1)} %all-to-all-done.1.refs_0_), channel_id=1, source_target_pairs={{0,1},{1,0},{2,3},{3,2},{4,5},{5,4},{6,7},{7,6},{8,9},{9,8},{10,11... | collective-permute-start | bytes 3932168 | tf_op jit(solution)/shard_map/ppermute | solution.py:29
  99.4 68.1 %collective-permute-start.12 = (bf16[4096,256]{1,0:T(8,128)(2,1)S(1)}, bf16[4096,256]{1,0:T(8,128)(2,1)}, u32[]{:S(2)}, u32[]{:S(2)}) collective-permute-start(bf16[4096,256]{1,0:T(8,128)(2,1)S(1)} %get-tuple-element.58), channel_id=1, source_target_pairs={{0,16},{8,24},{16,0},{24,8},{1,17},{9,25},{17,1},{25,9},{2,18},{10... | collective-permute-start | bytes 6291464 | tf_op jit(solution)/shard_map/ppermute | solution.py:25
  100.0 100.4 %collective-permute-start.9 = (bf16[4096,256]{1,0:T(8,128)(2,1)S(1)}, bf16[4096,256]{1,0:T(8,128)(2,1)}, u32[]{:S(2)}, u32[]{:S(2)}) collective-permute-start(bf16[4096,256]{1,0:T(8,128)(2,1)S(1)} %get-tuple-element.58), channel_id=1, source_target_pairs={{0,8},{8,0},{16,24},{24,16},{1,9},{9,1},{17,25},{25,17},{2,10},{10... | collective-permute-start | bytes 6291464 | tf_op jit(solution)/shard_map/ppermute | solution.py:25
  102.2 26.8 %collective-permute-start.21 = (bf16[128,256]{1,0:T(8,128)(2,1)S(1)}, bf16[128,256]{1,0:T(8,128)(2,1)S(1)}, u32[]{:S(2)}, u32[]{:S(2)}) collective-permute-start(bf16[128,256]{1,0:T(8,128)(2,1)S(1)} %collective-permute-done.20), channel_id=1, source_target_pairs={{0,8},{8,0},{16,24},{24,16},{1,9},{9,1},{17,25},{25,17},{2,10},{10... | collective-permute-start | bytes 196616 | tf_op jit(solution)/shard_map/ppermute | solution.py:25
  123.1 14.5 %collective-permute-start.2 = (bf16[4,27,256]{2,1,0:T(8,128)(2,1)}, bf16[4,27,256]{2,1,0:T(8,128)(2,1)S(1)}, u32[]{:S(2)}, u32[]{:S(2)}) collective-permute-start(bf16[4,27,256]{2,1,0:T(8,128)(2,1)} %get-tuple-element.194), channel_id=1, source_target_pairs={{0,1},{1,2},{2,3},{3,4},{4,5},{5,6},{6,7},{8,9},{9,10},{10,11},{11... | collective-permute-start | bytes 165896 | tf_op jit(solution)/shard_map/ppermute | solution.py:546
  126.5 11.1 %collective-permute-start.3 = (bf16[4,27,256]{2,1,0:T(8,128)(2,1)}, bf16[4,27,256]{2,1,0:T(8,128)(2,1)S(1)}, u32[]{:S(2)}, u32[]{:S(2)}) collective-permute-start(bf16[4,27,256]{2,1,0:T(8,128)(2,1)} %get-tuple-element.195), channel_id=1, source_target_pairs={{1,0},{2,1},{3,2},{4,3},{5,4},{6,5},{7,6},{9,8},{10,9},{11,10},{12... | collective-permute-start | bytes 165896 | tf_op jit(solution)/shard_map/ppermute | solution.py:547
  129.0 38.1 %collective-permute-start.11 = (bf16[1024,256]{1,0:T(8,128)(2,1)}, bf16[1024,256]{1,0:T(8,128)(2,1)}, u32[]{:S(2)}, u32[]{:S(2)}) collective-permute-start(bf16[1024,256]{1,0:T(8,128)(2,1)} %get-tuple-element.57), channel_id=1, source_target_pairs={{0,16},{8,24},{16,0},{24,8},{1,17},{9,25},{17,1},{25,9},{2,18},{10... | collective-permute-start | bytes 1572872 | tf_op jit(solution)/shard_map/ppermute | solution.py:25
  132.3 27.5 %all-to-all-start.2 = ((bf16[4,512,256]{2,1,0:T(8,128)(2,1)}), bf16[4,512,256]{2,1,0:T(8,128)(2,1)S(1)}, u32[]{:S(2)}, u32[]{:S(2)}) async-start(bf16[4,512,256]{2,1,0:T(8,128)(2,1)} %broadcast_in_dim.10), calls=%async_computation.2 | async-start | bytes 2097152 | tf_op jit(solution)/shard_map/all_to_all | solution.py:88
  137.6 190.2 %all-gather.3.cloned.1.call-start = ((), (), s32[]{:S(2)}) async-start(), calls=%async_computation.8 | async-start | bytes 4718592 | tf_op jit(solution)/shard_map/all_gather | solution.py:616
  141.4 18.4 %collective-permute-start.4 = (bf16[128,1024]{1,0:T(8,128)(2,1)}, bf16[128,1024]{1,0:T(8,128)(2,1)}, u32[]{:S(2)}, u32[]{:S(2)}) collective-permute-start(bf16[128,1024]{1,0:T(8,128)(2,1)} %get-tuple-element.179), channel_id=1, source_target_pairs={{0,8},{8,0},{16,24},{24,16},{1,9},{9,1},{17,25},{25,17},{2,10},{10... | collective-permute-start | bytes 786440 | tf_op jit(solution)/shard_map/ppermute | solution.py:25
  143.5 21.0 %collective-permute-start.6 = (bf16[128,1024]{1,0:T(8,128)(2,1)}, bf16[128,1024]{1,0:T(8,128)(2,1)}, u32[]{:S(2)}, u32[]{:S(2)}) collective-permute-start(bf16[128,1024]{1,0:T(8,128)(2,1)} %fusion.49), channel_id=1, source_target_pairs={{0,16},{8,24},{16,0},{24,8},{1,17},{9,25},{17,1},{25,9},{2,18},{10... | collective-permute-start | bytes 786440 | tf_op jit(solution)/shard_map/ppermute | solution.py:25
  146.4 524.6 %reduce-scatter.2.cloned.1.call-start = ((), (), s32[]{:S(2)}) async-start(), calls=%async_computation.7 | async-start | bytes 4718592 | tf_op jit(solution)/shard_map/reduce_scatter | solution.py:681
  159.8 14.1 %collective-permute-start.8 = (bf16[1024,256]{1,0:T(8,128)(2,1)}, bf16[1024,256]{1,0:T(8,128)(2,1)S(1)}, u32[]{:S(2)}, u32[]{:S(2)}) collective-permute-start(bf16[1024,256]{1,0:T(8,128)(2,1)} %get-tuple-element.57), channel_id=1, source_target_pairs={{0,8},{8,0},{16,24},{24,16},{1,9},{9,1},{17,25},{25,17},{2,10},{10... | collective-permute-start | bytes 1572872 | tf_op jit(solution)/shard_map/ppermute | solution.py:25
  164.5 32.2 %collective-permute-start.22 = (bf16[4,512,256]{2,1,0:T(8,128)(2,1)S(1)}, bf16[4,512,256]{2,1,0:T(8,128)(2,1)S(1)}, u32[]{:S(2)}, u32[]{:S(2)}) collective-permute-start(bf16[4,512,256]{2,1,0:T(8,128)(2,1)S(1)} %all-to-all-done.2.refs_0_), channel_id=1, source_target_pairs={{0,1},{1,0},{2,3},{3,2},{4,5},{5,4},{6,7},{7,6},{8,9},{9,8},{10,11... | collective-permute-start | bytes 3145736 | tf_op jit(solution)/shard_map/ppermute | solution.py:29
  167.6 41.5 %collective-permute-start.15 = (bf16[4096,256]{1,0:T(8,128)(2,1)}, bf16[4096,256]{1,0:T(8,128)(2,1)S(1)}, u32[]{:S(2)}, u32[]{:S(2)}) collective-permute-start(bf16[4096,256]{1,0:T(8,128)(2,1)} %collective-permute-done.12), channel_id=1, source_target_pairs={{0,8},{8,0},{16,24},{24,16},{1,9},{9,1},{17,25},{25,17},{2,10},{10... | collective-permute-start | bytes 6291464 | tf_op jit(solution)/shard_map/ppermute | solution.py:25
  171.4 39.0 %collective-permute-start.16 = (bf16[512,256]{1,0:T(8,128)(2,1)}, bf16[512,256]{1,0:T(8,128)(2,1)S(1)}, u32[]{:S(2)}, u32[]{:S(2)}) collective-permute-start(bf16[512,256]{1,0:T(8,128)(2,1)} %get-tuple-element.176), channel_id=1, source_target_pairs={{0,8},{8,0},{16,24},{24,16},{1,9},{9,1},{17,25},{25,17},{2,10},{10... | collective-permute-start | bytes 786440 | tf_op jit(solution)/shard_map/ppermute | solution.py:25
  173.9 25.9 %collective-permute-start.7 = (bf16[128,256]{1,0:T(8,128)(2,1)}, bf16[128,256]{1,0:T(8,128)(2,1)S(1)}, u32[]{:S(2)}, u32[]{:S(2)}) collective-permute-start(bf16[128,256]{1,0:T(8,128)(2,1)} %get-tuple-element.191), channel_id=1, source_target_pairs={{0,8},{8,0},{16,24},{24,16},{1,9},{9,1},{17,25},{25,17},{2,10},{10... | collective-permute-start | bytes 196616 | tf_op jit(solution)/shard_map/ppermute | solution.py:25
  196.7 10.0 %collective-permute-start.14 = (bf16[1024,256]{1,0:T(8,128)(2,1)}, bf16[1024,256]{1,0:T(8,128)(2,1)S(1)}, u32[]{:S(2)}, u32[]{:S(2)}) collective-permute-start(bf16[1024,256]{1,0:T(8,128)(2,1)} %collective-permute-done.11), channel_id=1, source_target_pairs={{0,8},{8,0},{16,24},{24,16},{1,9},{9,1},{17,25},{25,17},{2,10},{10... | collective-permute-start | bytes 1572872 | tf_op jit(solution)/shard_map/ppermute | solution.py:25
  200.4 61.2 %collective-permute-start.24 = (bf16[1024,768]{1,0:T(8,128)(2,1)}, bf16[1024,768]{1,0:T(8,128)(2,1)}, u32[]{:S(2)}, u32[]{:S(2)}) collective-permute-start(bf16[1024,768]{1,0:T(8,128)(2,1)} %get-tuple-element.63), channel_id=1, source_target_pairs={{0,16},{8,24},{16,0},{24,8},{1,17},{9,25},{17,1},{25,9},{2,18},{10... | collective-permute-start | bytes 4718600 | tf_op jit(solution)/shard_map/ppermute | solution.py:25
  206.8 37.5 %collective-permute-start.17 = (bf16[512,256]{1,0:T(8,128)(2,1)S(1)}, bf16[512,256]{1,0:T(8,128)(2,1)S(1)}, u32[]{:S(2)}, u32[]{:S(2)}) collective-permute-start(bf16[512,256]{1,0:T(8,128)(2,1)S(1)} %copy-done.91), channel_id=1, source_target_pairs={{0,16},{8,24},{16,0},{24,8},{1,17},{9,25},{17,1},{25,9},{2,18},{10... | collective-permute-start | bytes 786440 | tf_op jit(solution)/shard_map/ppermute | solution.py:25
  207.1 48.5 %collective-permute-start.27 = (bf16[1024,256]{1,0:T(8,128)(2,1)}, bf16[1024,256]{1,0:T(8,128)(2,1)}, u32[]{:S(2)}, u32[]{:S(2)}) collective-permute-start(bf16[1024,256]{1,0:T(8,128)(2,1)} %get-tuple-element.68), channel_id=1, source_target_pairs={{0,16},{8,24},{16,0},{24,8},{1,17},{9,25},{17,1},{25,9},{2,18},{10... | collective-permute-start | bytes 1572872 | tf_op jit(solution)/shard_map/ppermute | solution.py:25
  209.1 50.8 %collective-permute-start.18 = (bf16[512,256]{1,0:T(8,128)(2,1)S(1)}, bf16[512,256]{1,0:T(8,128)(2,1)S(1)}, u32[]{:S(2)}, u32[]{:S(2)}) collective-permute-start(bf16[512,256]{1,0:T(8,128)(2,1)S(1)} %copy-done.90), channel_id=1, source_target_pairs={{0,24},{8,16},{16,8},{24,0},{1,25},{9,17},{17,9},{25,1},{2,26},{10... | collective-permute-start | bytes 786440 | tf_op jit(solution)/shard_map/ppermute | solution.py:25
  210.4 58.4 %collective-permute-start.23 = (bf16[1024,768]{1,0:T(8,128)(2,1)}, bf16[1024,768]{1,0:T(8,128)(2,1)}, u32[]{:S(2)}, u32[]{:S(2)}) collective-permute-start(bf16[1024,768]{1,0:T(8,128)(2,1)} %get-tuple-element.63), channel_id=1, source_target_pairs={{0,8},{8,0},{16,24},{24,16},{1,9},{9,1},{17,25},{25,17},{2,10},{10... | collective-permute-start | bytes 4718600 | tf_op jit(solution)/shard_map/ppermute | solution.py:25
  244.3 39.1 %collective-permute-start.26 = (bf16[1024,256]{1,0:T(8,128)(2,1)}, bf16[1024,256]{1,0:T(8,128)(2,1)}, u32[]{:S(2)}, u32[]{:S(2)}) collective-permute-start(bf16[1024,256]{1,0:T(8,128)(2,1)} %get-tuple-element.68), channel_id=1, source_target_pairs={{0,8},{8,0},{16,24},{24,16},{1,9},{9,1},{17,25},{25,17},{2,10},{10... | collective-permute-start | bytes 1572872 | tf_op jit(solution)/shard_map/ppermute | solution.py:25
  255.6 29.3 %collective-permute-start.28 = (bf16[1024,256]{1,0:T(8,128)(2,1)}, bf16[1024,256]{1,0:T(8,128)(2,1)}, u32[]{:S(2)}, u32[]{:S(2)}) collective-permute-start(bf16[1024,256]{1,0:T(8,128)(2,1)} %collective-permute-done.27), channel_id=1, source_target_pairs={{0,8},{8,0},{16,24},{24,16},{1,9},{9,1},{17,25},{25,17},{2,10},{10... | collective-permute-start | bytes 1572872 | tf_op jit(solution)/shard_map/ppermute | solution.py:25
  265.8 25.3 %collective-permute-start.36 = (bf16[2048,256]{1,0:T(8,128)(2,1)S(1)}, bf16[2048,256]{1,0:T(8,128)(2,1)}, u32[]{:S(2)}, u32[]{:S(2)}) collective-permute-start(bf16[2048,256]{1,0:T(8,128)(2,1)S(1)} %copy-done.2), channel_id=1, source_target_pairs={{0,16},{8,24},{16,0},{24,8},{1,17},{9,25},{17,1},{25,9},{2,18},{10... | collective-permute-start | bytes 3145736 | tf_op jit(solution)/shard_map/ppermute | solution.py:25
  288.8 25.1 %collective-permute-start.30 = (bf16[512,1024]{1,0:T(8,128)(2,1)}, bf16[512,1024]{1,0:T(8,128)(2,1)}, u32[]{:S(2)}, u32[]{:S(2)}) collective-permute-start(bf16[512,1024]{1,0:T(8,128)(2,1)} %add_convert_fusion.3), channel_id=1, source_target_pairs={{0,16},{8,24},{16,0},{24,8},{1,17},{9,25},{17,1},{25,9},{2,18},{10... | collective-permute-start | bytes 3145736 | tf_op jit(solution)/shard_map/ppermute | solution.py:25
  290.3 30.9 %collective-permute-start.35 = (bf16[2048,256]{1,0:T(8,128)(2,1)S(1)}, bf16[2048,256]{1,0:T(8,128)(2,1)}, u32[]{:S(2)}, u32[]{:S(2)}) collective-permute-start(bf16[2048,256]{1,0:T(8,128)(2,1)S(1)} %copy-done.2), channel_id=1, source_target_pairs={{0,8},{8,0},{16,24},{24,16},{1,9},{9,1},{17,25},{25,17},{2,10},{10... | collective-permute-start | bytes 3145736 | tf_op jit(solution)/shard_map/ppermute | solution.py:25
  291.1 30.1 %collective-permute-start.37 = (bf16[2048,256]{1,0:T(8,128)(2,1)}, bf16[2048,256]{1,0:T(8,128)(2,1)}, u32[]{:S(2)}, u32[]{:S(2)}) collective-permute-start(bf16[2048,256]{1,0:T(8,128)(2,1)} %collective-permute-done.36.q2), channel_id=1, source_target_pairs={{0,8},{8,0},{16,24},{24,16},{1,9},{9,1},{17,25},{25,17},{2,10},{10... | collective-permute-start | bytes 3145736 | tf_op jit(solution)/shard_map/ppermute | solution.py:25
  291.1 44.0 %collective-permute-start.29 = (bf16[512,1024]{1,0:T(8,128)(2,1)}, bf16[512,1024]{1,0:T(8,128)(2,1)}, u32[]{:S(2)}, u32[]{:S(2)}) collective-permute-start(bf16[512,1024]{1,0:T(8,128)(2,1)} %add_convert_fusion.3), channel_id=1, source_target_pairs={{0,8},{8,0},{16,24},{24,16},{1,9},{9,1},{17,25},{25,17},{2,10},{10... | collective-permute-start | bytes 3145736 | tf_op jit(solution)/shard_map/ppermute | solution.py:25
  314.0 21.1 %collective-permute-start.31 = (bf16[512,1024]{1,0:T(8,128)(2,1)}, bf16[512,1024]{1,0:T(8,128)(2,1)}, u32[]{:S(2)}, u32[]{:S(2)}) collective-permute-start(bf16[512,1024]{1,0:T(8,128)(2,1)} %collective-permute-done.30), channel_id=1, source_target_pairs={{0,8},{8,0},{16,24},{24,16},{1,9},{9,1},{17,25},{25,17},{2,10},{10... | collective-permute-start | bytes 3145736 | tf_op jit(solution)/shard_map/ppermute | solution.py:25
  364.2 21.2 %collective-permute-start.39 = (bf16[512,1024]{1,0:T(8,128)(2,1)S(1)}, bf16[512,1024]{1,0:T(8,128)(2,1)S(1)}, u32[]{:S(2)}, u32[]{:S(2)}) collective-permute-start(bf16[512,1024]{1,0:T(8,128)(2,1)S(1)} %get-tuple-element.148), channel_id=1, source_target_pairs={{0,8},{8,0},{16,24},{24,16},{1,9},{9,1},{17,25},{25,17},{2,10},{10... | collective-permute-start | bytes 3145736 | tf_op jit(solution)/shard_map/ppermute | solution.py:25
  364.7 43.0 %collective-permute-start.38 = (bf16[512,1024]{1,0:T(8,128)(2,1)}, bf16[512,1024]{1,0:T(8,128)(2,1)}, u32[]{:S(2)}, u32[]{:S(2)}) collective-permute-start(bf16[512,1024]{1,0:T(8,128)(2,1)} %get-tuple-element.147), channel_id=1, source_target_pairs={{0,8},{8,0},{16,24},{24,16},{1,9},{9,1},{17,25},{25,17},{2,10},{10... | collective-permute-start | bytes 3145736 | tf_op jit(solution)/shard_map/ppermute | solution.py:25
  375.6 27.6 %collective-permute-start.33 = (bf16[4,512,256]{2,1,0:T(8,128)(2,1)}, bf16[4,512,256]{2,1,0:T(8,128)(2,1)S(1)}, u32[]{:S(2)}, u32[]{:S(2)}) collective-permute-start(bf16[4,512,256]{2,1,0:T(8,128)(2,1)} %get-tuple-element.149), channel_id=1, source_target_pairs={{0,8},{8,0},{16,24},{24,16},{1,9},{9,1},{17,25},{25,17},{2,10},{10... | collective-permute-start | bytes 3145736 | tf_op jit(solution)/shard_map/ppermute | solution.py:25
  388.5 25.9 %collective-permute-start.40 = (bf16[512,1024]{1,0:T(8,128)(2,1)}, bf16[512,1024]{1,0:T(8,128)(2,1)}, u32[]{:S(2)}, u32[]{:S(2)}) collective-permute-start(bf16[512,1024]{1,0:T(8,128)(2,1)} %fusion.23), channel_id=1, source_target_pairs={{0,16},{8,24},{16,0},{24,8},{1,17},{9,25},{17,1},{25,9},{2,18},{10... | collective-permute-start | bytes 3145736 | tf_op jit(solution)/shard_map/ppermute | solution.py:25
  471.5 20.4 %collective-permute-start.46 = (bf16[128,256]{1,0:T(8,128)(2,1)S(1)}, bf16[128,256]{1,0:T(8,128)(2,1)S(1)}, u32[]{:S(2)}, u32[]{:S(2)}) collective-permute-start(bf16[128,256]{1,0:T(8,128)(2,1)S(1)} %convolution_convert_fusion.19), channel_id=1, source_target_pairs={{0,24},{8,16},{16,8},{24,0},{1,25},{9,17},{17,9},{25,1},{2,26},{10... | collective-permute-start | bytes 196616 | tf_op jit(solution)/shard_map/ppermute | solution.py:25
  472.2 26.7 %collective-permute-start.67 = (bf16[1024,768]{1,0:T(8,128)(2,1)S(1)}, bf16[1024,768]{1,0:T(8,128)(2,1)S(1)}, u32[]{:S(2)}, u32[]{:S(2)}) collective-permute-start(bf16[1024,768]{1,0:T(8,128)(2,1)S(1)} %copy-done.129), channel_id=1, source_target_pairs={{0,8},{8,0},{16,24},{24,16},{1,9},{9,1},{17,25},{25,17},{2,10},{10... | collective-permute-start | bytes 4718600 | tf_op jit(solution)/shard_map/ppermute | solution.py:25
  472.2 31.6 %collective-permute-start.59 = (bf16[4096,256]{1,0:T(8,128)(2,1)S(1)}, bf16[4096,256]{1,0:T(8,128)(2,1)S(1)}, u32[]{:S(2)}, u32[]{:S(2)}) collective-permute-start(bf16[4096,256]{1,0:T(8,128)(2,1)S(1)} %convolution_convert_fusion), channel_id=1, source_target_pairs={{0,8},{8,0},{16,24},{24,16},{1,9},{9,1},{17,25},{25,17},{2,10},{10... | collective-permute-start | bytes 6291464 | tf_op jit(solution)/shard_map/ppermute | solution.py:25
  492.0 46.1 %collective-permute-start.66 = (bf16[1024,768]{1,0:T(8,128)(2,1)}, bf16[1024,768]{1,0:T(8,128)(2,1)}, u32[]{:S(2)}, u32[]{:S(2)}) collective-permute-start(bf16[1024,768]{1,0:T(8,128)(2,1)} %convolution_convert_fusion.5), channel_id=1, source_target_pairs={{0,8},{8,0},{16,24},{24,16},{1,9},{9,1},{17,25},{25,17},{2,10},{10... | collective-permute-start | bytes 4718600 | tf_op jit(solution)/shard_map/ppermute | solution.py:25
  492.1 32.7 %collective-permute-start.53 = (bf16[512,768]{1,0:T(8,128)(2,1)S(1)}, bf16[512,768]{1,0:T(8,128)(2,1)S(1)}, u32[]{:S(2)}, u32[]{:S(2)}) collective-permute-start(bf16[512,768]{1,0:T(8,128)(2,1)S(1)} %slice.417), channel_id=1, source_target_pairs={{0,1},{1,0},{2,3},{3,2},{4,5},{5,4},{6,7},{7,6},{8,9},{9,8},{10,11... | collective-permute-start | bytes 2359304 | tf_op jit(solution)/shard_map/ppermute | solution.py:29
  496.4 27.6 %collective-permute-start.52 = (bf16[1024,256]{1,0:T(8,128)(2,1)S(1)}, bf16[1024,256]{1,0:T(8,128)(2,1)S(1)}, u32[]{:S(2)}, u32[]{:S(2)}) collective-permute-start(bf16[1024,256]{1,0:T(8,128)(2,1)S(1)} %slice.416), channel_id=1, source_target_pairs={{0,1},{1,0},{2,3},{3,2},{4,5},{5,4},{6,7},{7,6},{8,9},{9,8},{10,11... | collective-permute-start | bytes 1572872 | tf_op jit(solution)/shard_map/ppermute | solution.py:29
  501.2 38.4 %collective-permute-start.68 = (bf16[1024,768]{1,0:T(8,128)(2,1)}, bf16[1024,768]{1,0:T(8,128)(2,1)}, u32[]{:S(2)}, u32[]{:S(2)}) collective-permute-start(bf16[1024,768]{1,0:T(8,128)(2,1)} %add_convert_fusion.2), channel_id=1, source_target_pairs={{0,16},{8,24},{16,0},{24,8},{1,17},{9,25},{17,1},{25,9},{2,18},{10... | collective-permute-start | bytes 4718600 | tf_op jit(solution)/shard_map/ppermute | solution.py:25
  503.8 32.3 %collective-permute-start.71 = (bf16[1024,256]{1,0:T(8,128)(2,1)}, bf16[1024,256]{1,0:T(8,128)(2,1)}, u32[]{:S(2)}, u32[]{:S(2)}) collective-permute-start(bf16[1024,256]{1,0:T(8,128)(2,1)} %convolution_convert_fusion.11), channel_id=1, source_target_pairs={{0,8},{8,0},{16,24},{24,16},{1,9},{9,1},{17,25},{25,17},{2,10},{10... | collective-permute-start | bytes 1572872 | tf_op jit(solution)/shard_map/ppermute | solution.py:25
  524.8 76.6 %collective-permute-start.58 = (bf16[4096,256]{1,0:T(8,128)(2,1)}, bf16[4096,256]{1,0:T(8,128)(2,1)}, u32[]{:S(2)}, u32[]{:S(2)}) collective-permute-start(bf16[4096,256]{1,0:T(8,128)(2,1)} %convolution_convert_fusion.1), channel_id=1, source_target_pairs={{0,8},{8,0},{16,24},{24,16},{1,9},{9,1},{17,25},{25,17},{2,10},{10... | collective-permute-start | bytes 6291464 | tf_op jit(solution)/shard_map/ppermute | solution.py:25
  524.8 81.8 %collective-permute-start.60 = (bf16[4096,256]{1,0:T(8,128)(2,1)}, bf16[4096,256]{1,0:T(8,128)(2,1)}, u32[]{:S(2)}, u32[]{:S(2)}) collective-permute-start(bf16[4096,256]{1,0:T(8,128)(2,1)} %fusion.11), channel_id=1, source_target_pairs={{0,16},{8,24},{16,0},{24,8},{1,17},{9,25},{17,1},{25,9},{2,18},{10... | collective-permute-start | bytes 6291464 | tf_op jit(solution)/shard_map/ppermute | solution.py:25
  529.9 73.0 %all-to-all-start.3 = ((bf16[4,640,256]{2,1,0:T(8,128)(2,1)}), bf16[4,640,256]{2,1,0:T(8,128)(2,1)S(1)}, u32[]{:S(2)}, u32[]{:S(2)}) async-start(bf16[4,640,256]{2,1,0:T(8,128)(2,1)} %pack.3), calls=%async_computation.3 | async-start | bytes 2621440 | tf_op jit(solution)/shard_map/all_to_all | solution.py:88
  538.1 54.3 %collective-permute-start.72 = (bf16[1024,256]{1,0:T(8,128)(2,1)S(1)}, bf16[1024,256]{1,0:T(8,128)(2,1)S(1)}, u32[]{:S(2)}, u32[]{:S(2)}) collective-permute-start(bf16[1024,256]{1,0:T(8,128)(2,1)S(1)} %add_convert_fusion.6), channel_id=1, source_target_pairs={{0,16},{8,24},{16,0},{24,8},{1,17},{9,25},{17,1},{25,9},{2,18},{10... | collective-permute-start | bytes 1572872 | tf_op jit(solution)/shard_map/ppermute | solution.py:25
  542.2 57.1 %collective-permute-start.69 = (bf16[512,768]{1,0:T(8,128)(2,1)S(1)}, bf16[512,768]{1,0:T(8,128)(2,1)S(1)}, u32[]{:S(2)}, u32[]{:S(2)}) collective-permute-start(bf16[512,768]{1,0:T(8,128)(2,1)S(1)} %slice.423), channel_id=1, source_target_pairs={{0,1},{1,0},{2,3},{3,2},{4,5},{5,4},{6,7},{7,6},{8,9},{9,8},{10,11... | collective-permute-start | bytes 2359304 | tf_op jit(solution)/shard_map/ppermute | solution.py:29
  542.9 51.0 %collective-permute-start.55 = (bf16[1024,256]{1,0:T(8,128)(2,1)S(1)}, bf16[1024,256]{1,0:T(8,128)(2,1)S(1)}, u32[]{:S(2)}, u32[]{:S(2)}) collective-permute-start(bf16[1024,256]{1,0:T(8,128)(2,1)S(1)} %copy-done.79), channel_id=1, source_target_pairs={{0,8},{8,0},{16,24},{24,16},{1,9},{9,1},{17,25},{25,17},{2,10},{10... | collective-permute-start | bytes 1572872 | tf_op jit(solution)/shard_map/ppermute | solution.py:25
  593.9 56.4 %collective-permute-start.32 = (bf16[4,512,256]{2,1,0:T(8,128)(2,1)}, bf16[4,512,256]{2,1,0:T(8,128)(2,1)}, u32[]{:S(2)}, u32[]{:S(2)}) collective-permute-start(bf16[4,512,256]{2,1,0:T(8,128)(2,1)} %get-tuple-element.150), channel_id=1, source_target_pairs={{0,8},{8,0},{16,24},{24,16},{1,9},{9,1},{17,25},{25,17},{2,10},{10... | collective-permute-start | bytes 3145736 | tf_op jit(solution)/shard_map/ppermute | solution.py:25
  599.3 12.7 %collective-permute-start.63 = (bf16[128,256]{1,0:T(8,128)(2,1)S(1)}, bf16[128,256]{1,0:T(8,128)(2,1)S(1)}, u32[]{:S(2)}, u32[]{:S(2)}) collective-permute-start(bf16[128,256]{1,0:T(8,128)(2,1)S(1)} %bitcast.262), channel_id=1, source_target_pairs={{0,8},{8,0},{16,24},{24,16},{1,9},{9,1},{17,25},{25,17},{2,10},{10... | collective-permute-start | bytes 196616 | tf_op jit(solution)/shard_map/ppermute | solution.py:25
  599.3 14.0 %collective-permute-start.54 = (bf16[1024,256]{1,0:T(8,128)(2,1)}, bf16[1024,256]{1,0:T(8,128)(2,1)S(1)}, u32[]{:S(2)}, u32[]{:S(2)}) collective-permute-start(bf16[1024,256]{1,0:T(8,128)(2,1)} %convolution_convert_fusion.14), channel_id=1, source_target_pairs={{0,8},{8,0},{16,24},{24,16},{1,9},{9,1},{17,25},{25,17},{2,10},{10... | collective-permute-start | bytes 1572872 | tf_op jit(solution)/shard_map/ppermute | solution.py:25
  601.4 14.9 %collective-permute-start.56 = (bf16[1024,256]{1,0:T(8,128)(2,1)}, bf16[1024,256]{1,0:T(8,128)(2,1)}, u32[]{:S(2)}, u32[]{:S(2)}) collective-permute-start(bf16[1024,256]{1,0:T(8,128)(2,1)} %add_convert_fusion.8), channel_id=1, source_target_pairs={{0,16},{8,24},{16,0},{24,8},{1,17},{9,25},{17,1},{25,9},{2,18},{10... | collective-permute-start | bytes 1572872 | tf_op jit(solution)/shard_map/ppermute | solution.py:25
  602.9 42.3 %all-to-all-start.5 = ((bf16[4,512,256]{2,1,0:T(8,128)(2,1)}), bf16[4,512,256]{2,1,0:T(8,128)(2,1)S(1)}, u32[]{:S(2)}, u32[]{:S(2)}) async-start(bf16[4,512,256]{2,1,0:T(8,128)(2,1)} %pack.5), calls=%async_computation.5 | async-start | bytes 2097152 | tf_op jit(solution)/shard_map/all_to_all | solution.py:88
  610.8 32.6 %collective-permute-start.61 = (bf16[2048,256]{1,0:T(8,128)(2,1)S(1)}, bf16[2048,256]{1,0:T(8,128)(2,1)S(1)}, u32[]{:S(2)}, u32[]{:S(2)}) collective-permute-start(bf16[2048,256]{1,0:T(8,128)(2,1)S(1)} %slice.419), channel_id=1, source_target_pairs={{0,1},{1,0},{2,3},{3,2},{4,5},{5,4},{6,7},{7,6},{8,9},{9,8},{10,11... | collective-permute-start | bytes 3145736 | tf_op jit(solution)/shard_map/ppermute | solution.py:29
  612.0 41.7 %collective-permute-start.34 = (bf16[4,512,256]{2,1,0:T(8,128)(2,1)}, bf16[4,512,256]{2,1,0:T(8,128)(2,1)}, u32[]{:S(2)}, u32[]{:S(2)}) collective-permute-start(bf16[4,512,256]{2,1,0:T(8,128)(2,1)} %fusion.22), channel_id=1, source_target_pairs={{0,16},{8,24},{16,0},{24,8},{1,17},{9,25},{17,1},{25,9},{2,18},{10... | collective-permute-start | bytes 3145736 | tf_op jit(solution)/shard_map/ppermute | solution.py:25
  616.4 23.0 %collective-permute-start.64 = (bf16[128,256]{1,0:T(8,128)(2,1)S(1)}, bf16[128,256]{1,0:T(8,128)(2,1)S(1)}, u32[]{:S(2)}, u32[]{:S(2)}) collective-permute-start(bf16[128,256]{1,0:T(8,128)(2,1)S(1)} %fusion.55), channel_id=1, source_target_pairs={{0,16},{8,24},{16,0},{24,8},{1,17},{9,25},{17,1},{25,9},{2,18},{10... | collective-permute-start | bytes 196616 | tf_op jit(solution)/shard_map/ppermute | solution.py:25
  619.3 24.1 %collective-permute-start.57 = (bf16[512,256]{1,0:T(8,128)(2,1)S(1)}, bf16[512,256]{1,0:T(8,128)(2,1)S(1)}, u32[]{:S(2)}, u32[]{:S(2)}) collective-permute-start(bf16[512,256]{1,0:T(8,128)(2,1)S(1)} %slice.418), channel_id=1, source_target_pairs={{0,1},{1,0},{2,3},{3,2},{4,5},{5,4},{6,7},{7,6},{8,9},{9,8},{10,11... | collective-permute-start | bytes 786440 | tf_op jit(solution)/shard_map/ppermute | solution.py:29
  646.1 34.5 %all-to-all-start.4 = ((bf16[4,656,256]{2,1,0:T(8,128)(2,1)}), bf16[4,656,256]{2,1,0:T(8,128)(2,1)S(1)}, u32[]{:S(2)}, u32[]{:S(2)}) async-start(bf16[4,656,256]{2,1,0:T(8,128)(2,1)} %pack.4), calls=%async_computation.4 | async-start | bytes 2686976 | tf_op jit(solution)/shard_map/all_to_all | solution.py:88
  651.8 13.1 %collective-permute-start.42 = (bf16[512,256]{1,0:T(8,128)(2,1)S(1)}, bf16[512,256]{1,0:T(8,128)(2,1)S(1)}, u32[]{:S(2)}, u32[]{:S(2)}) collective-permute-start(bf16[512,256]{1,0:T(8,128)(2,1)S(1)} %copy-done.37), channel_id=1, source_target_pairs={{0,16},{8,24},{16,0},{24,8},{1,17},{9,25},{17,1},{25,9},{2,18},{10... | collective-permute-start | bytes 786440 | tf_op jit(solution)/shard_map/ppermute | solution.py:25
  652.7 12.2 %collective-permute-start.43 = (bf16[512,256]{1,0:T(8,128)(2,1)S(1)}, bf16[512,256]{1,0:T(8,128)(2,1)S(1)}, u32[]{:S(2)}, u32[]{:S(2)}) collective-permute-start(bf16[512,256]{1,0:T(8,128)(2,1)S(1)} %copy-done.35), channel_id=1, source_target_pairs={{0,8},{8,0},{16,24},{24,16},{1,9},{9,1},{17,25},{25,17},{2,10},{10... | collective-permute-start | bytes 786440 | tf_op jit(solution)/shard_map/ppermute | solution.py:25
  (153 other events, 1539.4 us)
Sparse Core Ops, SparseCore 0:
  146.5 80.4 all-gather.2
  403.4 88.1 reduce-scatter.1

commit v4 on v3

--- a/solution.py
+++ b/solution.py
@@ -179,93 +179,83 @@
     ]
 
 
-def spread(x):
-    y = swap(x, 2)
-    return [x, swap(x, 1), y, swap(y, 1)]
-
-
-def exchange(items):
-    return [items[0]] + [swap(items[j], j) for j in (1, 2, 3)]
-
-
-def fold(items, wire=BF16, place_rows=None):
-    fix = place_rows or (lambda x, j: x)
+class Line:
+    def __init__(self):
+        self.last = ()
+
+    def send(self, *items):
+        items = [(after(x, *self.last) if self.last else x, j) for x, j in items]
+        self.last = [swap(x, j) for x, j in items]
+        return self.last
+
+    def spread(self, x):
+        (y,) = self.send((x, 2))
+        return [x, swap(x, 1), y, swap(y, 1)]
+
+    def exchange(self, items):
+        two, three = self.send((items[2], 2), (items[3], 3))
+        return [items[0], swap(items[1], 1), two, three]
+
+
+def same(x, j):
+    return x
+
+
+def fold_core(items, wire=BF16, fix=same):
     one = fix(swap(items[1].astype(wire), 1), 1).astype(F32)
     three = fix(swap(items[3].astype(wire), 1), 1).astype(F32)
-    zero = items[0].astype(F32) + one
-    two = (items[2].astype(F32) + three).astype(BF16)
-    return zero + fix(swap(two, 2), 2).astype(F32)
+    return items[0].astype(F32) + one, (items[2].astype(F32) + three).astype(wire)
+
+
+def fold(line, items, wire=BF16, fix=same):
+    zero, two = fold_core(items, wire, fix)
+    return zero + fix(line.send((two, 2))[0], 2).astype(F32)
 
 
 def lane_block(i):
     return pl.ds(pl.multiple_of(i * LANES, LANES), LANES)
 
 
-def reorder_tile(index_ref, in_ref, out_ref):
-    for i in range(in_ref.shape[1] // LANES):
-        out_ref[:, i * LANES : (i + 1) * LANES] = in_ref[:, lane_block(index_ref[i])]
-
-
-def reorder(x, index):
-    rows, width = x.shape
-    tile = rows // 4
-    block = pl.BlockSpec((tile, width), lambda i, index: (i, 0))
-    return pl.pallas_call(
-        reorder_tile,
-        out_shape=jax.ShapeDtypeStruct(x.shape, x.dtype),
+def split_body(index_ref, in_ref, a_ref, b_ref):
+    a_ref[...] = in_ref[:, : a_ref.shape[1]]
+    b_ref[...] = in_ref[:, a_ref.shape[1] :]
+
+
+def join_body(index_ref, a_ref, b_ref, out_ref):
+    out_ref[:, : a_ref.shape[1]] = a_ref[...]
+    out_ref[:, a_ref.shape[1] :] = b_ref[...]
+
+
+def split_columns(x, index, first):
+    n, w = x.shape[0] // 8, x.shape[1]
+    widths = (first, w - first)
+    return pl.pallas_call(
+        split_body,
+        out_shape=[jax.ShapeDtypeStruct((8 * n, v), x.dtype) for v in widths],
         grid_spec=pltpu.PrefetchScalarGridSpec(
-            num_scalar_prefetch=1, grid=(4,), in_specs=[block], out_specs=block
+            num_scalar_prefetch=1,
+            grid=(8,),
+            in_specs=[pl.BlockSpec((n, w), lambda i, index: (index[i], 0))],
+            out_specs=[pl.BlockSpec((n, v), lambda i, index: (i, 0)) for v in widths],
         ),
-        name="reorder",
+        name="split_columns",
     )(index, x)
 
 
-def copy_two(index_a, index_b, a_ref, b_ref, out_a, out_b):
-    out_a[...] = a_ref[...].reshape(out_a.shape)
-    out_b[...] = b_ref[...].reshape(out_b.shape)
-
-
-def unpack_rows(packed, index_a, index_b):
-    _, _, n, w = packed.shape
-    shape = jax.ShapeDtypeStruct((8 * n, w), packed.dtype)
-    out = pl.BlockSpec((n, w), lambda i, a, b: (i, 0))
-    return pl.pallas_call(
-        copy_two,
-        out_shape=(shape, shape),
+def join_columns(a, b, index):
+    n = a.shape[0] // 8
+    widths = (a.shape[1], b.shape[1])
+    return pl.pallas_call(
+        join_body,
+        out_shape=jax.ShapeDtypeStruct((8 * n, sum(widths)), a.dtype),
         grid_spec=pltpu.PrefetchScalarGridSpec(
-            num_scalar_prefetch=2,
+            num_scalar_prefetch=1,
             grid=(8,),
-            in_specs=[
-                pl.BlockSpec((1, 1, n, w), lambda i, a, b: (a[i], 0, 0, 0)),
-                pl.BlockSpec((1, 1, n, w), lambda i, a, b: (b[i], 1, 0, 0)),
-            ],
-            out_specs=(out, out),
+            in_specs=[pl.BlockSpec((n, v), lambda i, index: (index[i], 0)) for v in widths],
+            out_specs=pl.BlockSpec((n, sum(widths)), lambda i, index: (i, 0)),
         ),
-        name="unpack_rows",
-    )(index_a, index_b, packed, packed)
-
-
-def copy_pair(index_a, index_b, a_ref, b_ref, out_ref):
-    out_ref[0, 0] = a_ref[...]
-    out_ref[0, 1] = b_ref[...]
-
-
-def pack_rows(a, b, index_a, index_b):
-    n, w = a.shape[0] // 8, a.shape[1]
-    return pl.pallas_call(
-        copy_pair,
-        out_shape=jax.ShapeDtypeStruct((8, 2, n, w), a.dtype),
-        grid_spec=pltpu.PrefetchScalarGridSpec(
-            num_scalar_prefetch=2,
-            grid=(8,),
-            in_specs=[
-                pl.BlockSpec((n, w), lambda i, a, b: (a[i], 0)),
-                pl.BlockSpec((n, w), lambda i, a, b: (b[i], 0)),
-            ],
-            out_specs=pl.BlockSpec((1, 2, n, w), lambda i, a, b: (i, 0, 0, 0)),
-        ),
-        name="pack_rows",
-    )(index_a, index_b, a, b)
+        name="join_columns",
+    )(index, a, b)
 
 
 def enter_body(from_up, to_layer, up_ref, q0, q1, q2, q3, out_ref, held, spaced):
@@ -487,41 +477,152 @@
     return [rows[j].reshape(-1, CELL) for j in range(4)]
 
 
-def cot_body(to_layer, q0, q1, q2, q3, all_ref, mine_ref):
-    n = q0.shape[1]
+MLP_TILE = 256
+TURNS = 8
+
+
+def order_of(k):
+    return ((k & 1) << 1) | (k >> 1)
+
+
+def mlp_body(index, *refs):
+    (n0, n1, n2, n3, q0, q1, q2, q3, in_ref, down_ref, stream_ref) = refs[:11]
+    (act_ref, grad_ref, norm_ref, cot_ref, d0, d1, d2, d3, keep_ref, send_ref, mine_ref) = refs[11:22]
+    wide, other = refs[22:]
+    tile = pl.program_id(0)
+    k = tile // 2
+    layer_of_natural, natural_of_layer, quarter_at = (
+        [index[row * 8 + i] for i in range(8)] for row in range(3)
+    )
+    for at, ref in enumerate((n0, n2, n1, n3)):
+
+        @pl.when(k == at)
+        def _(ref=ref):
+            for b in range(8):
+                norm_ref[:, b * LANES : (b + 1) * LANES] = ref[:, lane_block(layer_of_natural[b])]
+
+    quarters = [pl.ds(pl.multiple_of(quarter_at[j] * 256, 256), 256) for j in range(4)]
     for j, ref in enumerate((q0, q1, q2, q3)):
-        all_ref[:, j * n : (j + 1) * n] = ref[...]
-
-    @pl.when(pl.program_id(0) == 0)
+        cot_ref[:, quarters[j]] = ref[...]
+    weight_in = in_ref[...].reshape(-1, in_ref.shape[-1])
+    weight_down = down_ref[...].reshape(-1, down_ref.shape[-1])
+    pre = dot(norm_ref[...], weight_in)
+    half = 0.5 + 0.5 * lax.erf(pre * math.sqrt(0.5))
+    act = (pre * half).astype(BF16)
+    act_ref[...] = act
+    slope = half + pre * (math.sqrt(0.5 / math.pi) * jnp.exp(-0.5 * pre * pre))
+    grad = (slope * dot(cot_ref[...], weight_down)).astype(BF16)
+    grad_ref[...] = grad
+    wide[...] = dot_t(act, weight_down)
+
+    @pl.when(tile < 2)
+    def _():
+        for b in range(8):
+            at = slice(b * LANES, (b + 1) * LANES)
+            wide[:, at] = wide[:, at] + stream_ref[:, lane_block(layer_of_natural[b])]
+        for p in range(8):
+            mine_ref[:, p * LANES : (p + 1) * LANES] = cot_ref[:, lane_block(natural_of_layer[p])]
+
+    for j, ref in enumerate((d0, d1, d2, d3)):
+        ref[...] = wide[:, quarters[j]].astype(BF16)
+    other[...] = dot_t(grad, weight_in)
+
+    @pl.when(tile < 4)
     def _():
         for p in range(8):
-            mine_ref[:, p * LANES : (p + 1) * LANES] = all_ref[:, lane_block(to_layer[p])]
-
-
-def join_cotangent(quarters, to_layer):
-    rows, n = quarters[0].shape
-    tokens = rows // 4
-    return pl.pallas_call(
-        cot_body,
-        out_shape=(
-            jax.ShapeDtypeStruct((rows, 4 * n), BF16),
-            jax.ShapeDtypeStruct((tokens, 4 * n), BF16),
-        ),
+            keep_ref[:, p * LANES : (p + 1) * LANES] = other[:, lane_block(natural_of_layer[p])]
+
+    @pl.when(tile >= 4)
+    def _():
+        for p in range(8):
+            send_ref[:, p * LANES : (p + 1) * LANES] = other[
+                :, lane_block(natural_of_layer[p])
+            ].astype(BF16)
+
+
+def mlp(norms, cots, weights, stream, index):
+    tokens, width = norms[0].shape
+    rows, quarter = cots[0].shape
+    hidden = weights.shape[-1]
+    n = weights.shape[2]
+    tile = MLP_TILE
+    per = tokens // tile
+    assert per == 2
+    held = lambda start, count: lambda i, index: (jnp.clip(i - start, 0, count - 1), 0)
+    norm_specs = [
+        pl.BlockSpec((tile, width), held(2 * order_of(m), 2)) for m in range(4)
+    ]
+    cot_specs = [
+        pl.BlockSpec(
+            (tile, quarter),
+            lambda i, index, j=j: (
+                jnp.bitwise_xor(order_of(i // 2), j) * 2 + lax.rem(i, 2),
+                0,
+            ),
+        )
+        for j in range(4)
+    ]
+    weight_specs = [
+        pl.BlockSpec((8, 1, n, hidden), lambda i, index, k=k: (0, k, 0, 0)) for k in range(2)
+    ]
+    each = lambda w: pl.BlockSpec((tile, w), lambda i, index: (i, 0))
+    shape = jax.ShapeDtypeStruct
+    return pl.pallas_call(
+        mlp_body,
+        out_shape=[
+            shape((rows, hidden), BF16),
+            shape((rows, hidden), BF16),
+            shape((rows, width), BF16),
+            shape((rows, width), BF16),
+            *[shape((rows, quarter), BF16)] * 4,
+            shape((rows // 2, width), F32),
+            shape((rows // 2, width), BF16),
+            shape((tokens, width), BF16),
+        ],
         grid_spec=pltpu.PrefetchScalarGridSpec(
             num_scalar_prefetch=1,
-            grid=(4,),
-            in_specs=[
-                pl.BlockSpec((tokens, n), lambda m, t, j=j: (jnp.bitwise_xor(m, j), 0))
-                for j in range(4)
+            grid=(TURNS,),
+            in_specs=norm_specs
+            + cot_specs
+            + weight_specs
+            + [pl.BlockSpec((tile, width), held(0, 2))],
+            out_specs=[each(hidden), each(hidden), each(width), each(width)]
+            + [each(quarter)] * 4
+            + [
+                pl.BlockSpec((tile, width), held(0, 4)),
+                pl.BlockSpec((tile, width), held(4, 4)),
+                pl.BlockSpec((tile, width), held(0, 2)),
             ],
-            out_specs=(
-                pl.BlockSpec((tokens, 4 * n), lambda m, t: (m, 0)),
-                pl.BlockSpec((tokens, 4 * n), lambda m, t: (0, 0)),
-            ),
+            scratch_shapes=[pltpu.VMEM((tile, width), F32), pltpu.VMEM((tile, width), F32)],
         ),
         compiler_params=pltpu.CompilerParams(vmem_limit_bytes=VMEM_ROOM),
-        name="join_cotangent",
-    )(to_layer, *quarters)
+        name="mlp",
+    )(index, *norms, *cots, weights, weights, stream)
+
+
+def mlp_grads_body(norm_ref, cot_ref, act_ref, grad_ref, out_ref):
+    for k, (left, right) in enumerate(((norm_ref, grad_ref), (cot_ref, act_ref))):
+        block = gram(left[...], right[...]).astype(BF16)
+        n = out_ref.shape[2]
+        for i in range(out_ref.shape[0]):
+            out_ref[i, k] = block[i * n : (i + 1) * n]
+
+
+def mlp_grads(norm, cot, act, grad):
+    rows, width = norm.shape
+    hidden = act.shape[1]
+    n = width // 8
+    whole = pl.BlockSpec((rows, hidden), lambda i: (0, 0))
+    part = pl.BlockSpec((rows, 2 * n), lambda i: (0, i))
+    return pl.pallas_call(
+        mlp_grads_body,
+        out_shape=jax.ShapeDtypeStruct((8, 2, n, hidden), BF16),
+        grid=(4,),
+        in_specs=[part, part, whole, whole],
+        out_specs=pl.BlockSpec((2, 2, n, hidden), lambda i: (i, 0, 0, 0)),
+        compiler_params=pltpu.CompilerParams(vmem_limit_bytes=VMEM_ROOM),
+        name="mlp_grads",
+    )(norm, cot, act, grad)
 
 
 def join_rows(packed):
@@ -575,51 +676,34 @@
     to_layer = (((slot & 3) ^ c) << 1) | ((slot >> 2) ^ x)
     to_quarters = (((slot & 1) ^ x) << 2) | ((slot >> 1) ^ c)
     natural_of_layer = ((slot & 3) << 1) | ((slot >> 2) ^ x)
-    natural_of_quarters = (((slot >> 1) ^ c) << 1) | (slot & 1)
     layer_of_natural = (((slot & 1) ^ x) << 2) | (slot >> 1)
-    quarters_of_natural = natural_of_quarters
-
-    stream_in = exchange(pick([inputs[i] for i in range(4)], c))
+
+    line = Line()
+    stream_in = line.exchange(pick([inputs[i] for i in range(4)], c))
+    cots = line.spread(jnp.concatenate(pick([cotangent[i] for i in range(4)], c), axis=0))
 
     lot = gain_one.shape[0]
     vectors = vector_rows(jnp.stack([gain_one, shift_one, gain_two, shift_two]))
     conv_shard = conv_weight.transpose(2, 0, 1).reshape(-1, 3 * quarter)
-    groups = (
-        (res_weight, up_weight.T, vectors),
-        (embed_table, conv_shard),
-        (qkv_weight.reshape(-1, 3 * quarter), out_weight.T),
-    )
+    groups = ((embed_table, conv_shard, vectors), (res_weight, up_weight.T))
+    attn_shard = jnp.concatenate([qkv_weight.reshape(-1, 3 * quarter), out_weight.T], axis=1)
     mlp_shard = jnp.stack([in_weight, down_weight.T])
     if tuned():
-        nears, fars = [], []
-        for group in groups:
-            cells = bundle(group)
-            cells = after(cells, nears[-1]) if nears else cells
-            nears.append(along_z(jnp.broadcast_to(cells, (4,) + cells.shape)))
-        for near in nears:
-            fars.append(hop(after(near, fars[-1]) if fars else near, 1))
-        whole = [
-            unpack(near, far, [w.shape for w in group])
-            for near, far, group in zip(nears, fars, groups)
-        ]
-        mlp_shard = after(mlp_shard, nears[1])
+        first, second = (bundle(group) for group in groups)
+        first = along_z(jnp.broadcast_to(first, (4,) + first.shape))
+        second = after(second, first)
+        second = along_z(jnp.broadcast_to(second, (4,) + second.shape))
+        attn_shard = after(attn_shard, second)
+        first_far = hop(after(first, *stream_in), 1)
+        second_far = hop(after(second, first_far, *cots), 1)
+        table, conv, vectors = unpack(first, first_far, [w.shape for w in groups[0]])
+        res, up = unpack(second, second_far, [w.shape for w in groups[1]])
     else:
-        whole = [gather_plain(group) for group in groups]
-    (res, up, vectors), (table, conv), (qkv_w, out_w) = whole
-    over_y = [swap(w, 2) for w in (res, up, vectors)]
-    over_y += [swap(after(w, *over_y[:2]), 2) for w in (qkv_w, out_w)]
-    res, up, vectors, qkv_w, out_w = (
-        [w, swap(w, 1), v, swap(v, 1)]
-        for w, v in zip((res, up, vectors, qkv_w, out_w), over_y)
-    )
-    in_w, down_t = unpack_rows(
-        join_rows(lax.all_gather(mlp_shard, "seq", axis=0)), natural_of_layer, natural_of_quarters
-    )
-    vectors = join_vectors(vectors, lot, c, x)
+        (table, conv, vectors), (res, up) = (gather_plain(group) for group in groups)
+    attn_w = lax.all_gather(attn_shard, "seq", axis=0, tiled=True)
+    mlp_w = lax.all_gather(after(mlp_shard, attn_w), "seq", axis=0)
+    vectors = join_vectors(line.spread(vectors), lot, c, x)
     gain1, shift1, gain2, shift2 = (vectors[i][None, :] for i in range(4))
-
-    cot = jnp.concatenate(pick([cotangent[i] for i in range(4)], c), axis=0)
-    cot_all, cot_mine = join_cotangent(spread(after(cot, *over_y[3:])), to_layer)
 
     ids = jnp.concatenate(pick([coarse_ids[i] for i in range(4)], c))
     vocab = table.shape[0]
@@ -636,14 +720,16 @@
         [padded[:, k * step : k * step + coarse] for k in range(3)], axis=2
     ).reshape(micros * coarse, 3 * quarter)
     conv_terms = dot_t(taps, conv).reshape(micros, coarse, width)
-    conv_out = fold([conv_terms[j] for j in range(4)])
-    embeds = exchange([e for e in embed.astype(BF16).reshape(micros, coarse, quarter)])
-
+    conv_out = fold(line, [conv_terms[j] for j in range(4)])
     mixed = gelu(conv_out).astype(BF16)
-    hidden = [(embeds[j].astype(F32) + dot(mixed, res[j])).astype(BF16) for j in range(4)]
-    up_terms = dot_t(hidden[0], up[0])
-    for j in (1, 2, 3):
-        up_terms = up_terms + dot_t(hidden[j], up[j])
+    mixed_all = jnp.concatenate(line.spread(mixed), axis=0)
+    hidden = (embed + dot(mixed_all, res)).astype(BF16)
+    up_terms = dot_t(hidden, up).reshape(micros, coarse, 4 * width)
+    up_terms = fold(line, [up_terms[j] for j in range(4)])
+    qkv_w, out_w = split_columns(attn_w, natural_of_layer, 3 * quarter)
+    qkv_w = line.spread(qkv_w)
+    out_w = line.spread(out_w)
+
     i = jnp.arange(32, dtype=jnp.int32)
     r, bz, bx = i >> 3, i & 3, ((i >> 2) & 1) ^ x
     from_up = ((bz >> 1) ^ x) * 16 + r * 4 + ((bz & 1) << 1 | bx)
@@ -661,37 +747,48 @@
     normed_two, rstd_two = normalize(stream_one)
     norm_two = (normed_two * gain2 + shift2).astype(BF16)
 
-    norm_all = jnp.concatenate(spread(norm_two), axis=0)
-    mlp_pre = dot(norm_all, in_w)
-    mlp_act = gelu(mlp_pre).astype(BF16)
-    grad_down = gram(cot_all, mlp_act).astype(BF16)
-    mlp_out = dot_t(mlp_act, down_t)
-    stream_q = reorder(stream_one, to_quarters)
-    mlp_out = mlp_out.reshape(micros, tokens, width)
-    mlp_out = jnp.concatenate([(mlp_out[0] + stream_q)[None], mlp_out[1:]], axis=0)
-    result = fold(
-        [mlp_out[:, :, j * quarter : (j + 1) * quarter] for j in range(4)],
-        place_rows=lambda v, j: jnp.stack([v[m ^ j] for m in range(4)]),
-    ).astype(BF16)
-    result = jnp.stack(pick([result[m] for m in range(4)], c))
-
-    grad_pre = (gelu_grad(mlp_pre) * dot(cot_all, down_t)).astype(BF16)
-    grad_in = gram(norm_all, grad_pre).astype(BF16)
-    grad_mlp = pack_rows(grad_in, grad_down, layer_of_natural, quarters_of_natural)
+    norm_all = line.spread(norm_two)
+    index = jnp.concatenate([layer_of_natural, natural_of_layer, jnp.tile(jnp.arange(4) ^ c, 2)])
+    mlp_act, grad_pre, norm_rows, cot_rows, *outs, keep, send, cot_mine = mlp(
+        norm_all, cots, join_rows(mlp_w), stream_one, index.astype(jnp.int32)
+    )
+    from_core = swap(send, 1).astype(F32)
+    over_y = (keep[tokens:] + from_core[tokens:]).astype(BF16)
+    (from_y,) = line.send((over_y, 2))
+    grad_mlp = mlp_grads(after(norm_rows, over_y), cot_rows, mlp_act, grad_pre)
+    turned = lambda v, j: jnp.stack([v[m ^ order_of(j)] for m in range(4)])
+    result, over_y = fold_core(
+        [d.reshape(micros, tokens, quarter) for d in outs], fix=turned
+    )
+    from_y, _, over_y = lax.optimization_barrier((from_y, grad_mlp, over_y))
+    grad_norm_two = keep[:tokens] + from_core[:tokens] + from_y.astype(F32)
+    (from_y,) = line.send((over_y, 2))
+    result = (result + turned(from_y, 2).astype(F32)).astype(BF16)
+    result = jnp.stack(pick([result[order_of(m)] for m in range(4)], c))
     grad_mlp = lax.psum_scatter(split_rows(grad_mlp), "seq", scatter_dimension=0, tiled=False)
     grad_in, grad_down = grad_mlp[0].astype(F32), grad_mlp[1].astype(F32).T
-    grad_norm_two = dot_t(grad_pre, in_w).reshape(micros, tokens, width)
-    grad_norm_two = fold([grad_norm_two[j] for j in range(4)])
 
     back_two, grad_gain2, grad_shift2 = normalize_back(normed_two, rstd_two, gain2, grad_norm_two)
     grad_stream_one = cot_mine.astype(F32) + back_two
     grad_att = grad_stream_one.astype(BF16)
-    grad_out = fold([gram(grad_att, context[j]) for j in range(4)])
+    grad_out, over_y = fold_core([gram(grad_att, context[j]) for j in range(4)])
     grad_context = [dot(grad_att, out_w[j]).astype(BF16) for j in range(4)]
-    grad_rows = attend_back(qkv, grad_context, segments)
-    grad_qkv, grad_out = reduce_rows(
-        [fold([gram(norm_one, grad_rows[j]) for j in range(4)]), grad_out]
-    )
+    grad_context[0] = after(grad_context[0], over_y)
+    (from_y,) = line.send((over_y, 2))
+    grad_out = (grad_out + from_y.astype(F32)).astype(BF16)
+    grad_rows = list(attend_back(qkv, grad_context, segments))
+    grad_qkv = [
+        fold_core([gram(norm_one, g[:, k * quarter : (k + 1) * quarter]) for g in grad_rows])
+        for k in range(3)
+    ]
+    grad_rows[0] = after(grad_rows[0], grad_qkv[0][1])
+
+    def finish(part):
+        zero, two = grad_qkv[part]
+        (from_y,) = line.send((two, 2))
+        grad_qkv[part] = (zero + from_y.astype(F32)).astype(BF16)
+
+    finish(0)
     grad_norm_one = dot_t(grad_rows[0], qkv_w[0])
     for j in (1, 2, 3):
         grad_norm_one = grad_norm_one + dot_t(grad_rows[j], qkv_w[j])
@@ -701,18 +798,22 @@
         jnp.stack([grad_gain1, grad_shift1, grad_gain2, grad_shift2]), lot, c, x
     )
     grad_up_rows, *grad_in_q = leave(input_grad, to_up, to_quarters)
-    input_grads = jnp.stack(pick(exchange(grad_in_q), c))
-    grad_hidden = [dot(grad_up_rows, up[j]).astype(BF16) for j in range(4)]
-    grad_up = fold([gram(grad_up_rows, hidden[j]) for j in range(4)])
-    grad_res = fold([gram(mixed, grad_hidden[j]) for j in range(4)])
-    grad_res, grad_up, grad_vectors = reduce_rows([grad_res, grad_up, fold(grad_vectors)])
-    grad_vectors = [grad_vectors[i, :lot] for i in range(4)]
-    grad_mixed = dot_t(grad_hidden[0], res[0])
-    for j in (1, 2, 3):
-        grad_mixed = grad_mixed + dot_t(grad_hidden[j], res[j])
+    grad_up_rows = jnp.concatenate(line.spread(grad_up_rows), axis=0)
+    finish(1)
+    grad_hidden = dot(grad_up_rows, up)
+    grad_hidden_low = grad_hidden.astype(BF16)
+    grad_mixed = dot_t(grad_hidden_low, res).reshape(micros, coarse, width)
+    grad_mixed = fold(line, [grad_mixed[j] for j in range(4)])
+    finish(2)
     grad_conv_low = (gelu_grad(conv_out) * grad_mixed).astype(BF16)
-
-    grad_conv_all = jnp.concatenate(spread(grad_conv_low), axis=0)
+    grad_up = gram(grad_up_rows, hidden)
+    grad_res = gram(mixed_all, grad_hidden_low)
+    grad_attn = join_columns(jnp.concatenate(grad_qkv, axis=1), grad_out, layer_of_natural)
+    grad_attn = lax.psum_scatter(grad_attn, "seq", scatter_dimension=0, tiled=True).astype(F32)
+    grad_qkv, grad_out = grad_attn[:, : 3 * quarter], grad_attn[:, 3 * quarter :]
+
+    grad_conv_all = jnp.concatenate(line.spread(grad_conv_low), axis=0)
+    input_grads = jnp.stack(pick(line.exchange(grad_in_q), c))
     grad_taps = dot(grad_conv_all, conv).reshape(micros, coarse, 3 * quarter)
     tap = [grad_taps[:, :, k * quarter : (k + 1) * quarter] for k in range(3)]
     prior, later = edges((tap[0][:, :step].astype(BF16), tap[2][:, coarse - step :].astype(BF16)))
@@ -721,8 +822,11 @@
         + jnp.concatenate([tap[0][:, step:], later.astype(F32)], axis=1)
         + jnp.concatenate([prior.astype(F32), tap[2][:, : coarse - step]], axis=1)
     ).reshape(micros * coarse, quarter)
-    grad_hidden_q = jnp.concatenate(exchange(grad_hidden), axis=0)
-    grad_embed = (grad_hidden_q.astype(F32) + gelu_grad(embed) * grad_act).astype(BF16)
+    grad_res, grad_up, grad_vectors = reduce_rows(
+        [grad_res, grad_up, fold(line, grad_vectors)]
+    )
+    grad_vectors = [grad_vectors[i, :lot] for i in range(4)]
+    grad_embed = (grad_hidden + gelu_grad(embed) * grad_act).astype(BF16)
     grad_table, grad_conv = reduce_rows([gram(onehot, grad_embed), gram(grad_conv_all, taps)])
     grad_conv = grad_conv.reshape(-1, 3, quarter).transpose(1, 2, 0)
     return (

time: 698 us -> 645 us (0.924)
  matrix products: 130 us -> 59.5 us
  Pallas kernels: 64.3 us -> 92.1 us
  starting transfers between devices: 84 us -> 98.8 us
  local copies, waits for them, and re-layouts: 41.4 us -> 29.2 us
  waiting for transfers between devices: 311 us -> 303 us
    dot_general x59 -> x43, matrix products: 130 us -> 59.1 us  [dot(): return lax.dot_general(a, b, (dims, ((), ())), preferred_element_type=F32)]
    ppermute x10 -> x7, waiting for transfers between devices: 87.9 us -> 25.2 us  [hop(): return lax.ppermute(x, 'seq', [(i, i ^ k) for i in range(8)])]
    pallas_call x4, Pallas kernels: 24.6 us -> 58.6 us  [the longest x1 32.4 us: mlp(): pl.pallas_call(mlp_body, out_shape=[shape((rows, hidden), BF16), shape((r...]
    ppermute x60 -> x59, waiting for transfers between devices: 171 us -> 200 us  [swap(): return lax.ppermute(x, 'cond', [(i, i ^ j) for i in range(4)])]
    all_gather x1 -> x2, waiting for transfers between devices: 0.01 us -> 26.6 us  [the longest x1 26.6 us: on_device(): attn_w = lax.all_gather(attn_shard, 'seq', axis=0, tiled=True)]
    ppermute x10 -> x7, starting transfers between devices: 12.9 us -> 33.3 us  [hop(): return lax.ppermute(x, 'seq', [(i, i ^ k) for i in range(8)])]
    convert_element_type x4 -> x1, other arithmetic: 7.86 us -> 0.02 us  [reduce_rows(): grads = [g.astype(BF16) for g in grads]]
    unnamed x281 -> x196, local copies, waits for them, and re-layouts: 21.2 us -> 13.5 us
  transfers between devices with their start and end apart: 82 -> 78, of which waited for: 29 -> 36; matrix products, arithmetic and copies ran while one was open for 23% -> 18% of each run, Pallas kernels for 9% -> 9%
where the time goes in v4:
time: 645 us; the launch traced here: 637 us
  waiting for transfers between devices  303 us (47%)
  starting transfers between devices  98.8 us (15%)
  Pallas kernels  92.1 us (14%)
  matrix products  59.5 us (9%)
  other arithmetic  37.6 us (6%)
  local copies, waits for them, and re-layouts  29.2 us (5%)
  between operations  15.9 us (2%)
    ppermute x59, waiting for transfers between devices, swap(): return lax.ppermute(x, 'cond', [(i, i ^ j) for i in range(4)])  200 us
    dot_general x43, matrix products, dot(): return lax.dot_general(a, b, (dims, ((), ())), preferred_element_type=F32)  59.1 us
    all_to_all x4, waiting for transfers between devices, along_z(): return lax.all_to_all(x, 'seq', 0, 0, axis_index_groups=ALONG_Z, tiled=True)  46.4 us
    ppermute x7, starting transfers between devices, hop(): return lax.ppermute(x, 'seq', [(i, i ^ k) for i in range(8)])  33.3 us
    pallas_call x1, Pallas kernels, mlp(): pl.pallas_call(mlp_body, out_shape=[shape((rows, hidden), BF16), shape((r...  32.4 us
    ppermute x59, starting transfers between devices, swap(): return lax.ppermute(x, 'cond', [(i, i ^ j) for i in range(4)])  30.6 us
    all_gather x1, waiting for transfers between devices, on_device(): attn_w = lax.all_gather(attn_shard, 'seq', axis=0, tiled=True)  26.6 us
    ppermute x7, waiting for transfers between devices, hop(): return lax.ppermute(x, 'seq', [(i, i ^ k) for i in range(8)])  25.2 us
  transfers between devices with their start and end apart: 78, of which 36 were waited for; matrix products, arithmetic and copies ran while one was open for 18% of the time, Pallas kernels for 9%

profile of v4, /device:TPU:0, one launch (start us, length us, event | category | flops | bytes accessed | tf_op | source)
XLA Modules:
  0.0 636.6 jit_solution(11210592253469349855)
XLA Ops:
  11.3 6.3 all-to-all-start
  19.9 7.1 %collective-permute-done.1.q2 = bf16[512,256]{1,0:T(8,128)(2,1)S(1)} collective-permute-done((bf16[512,256]{1,0:T(8,128)(2,1)S(1)}, bf16[512,256]{1,0:T(8,128)(2,1)S(1)}, u32[]{:S(2)}, u32[]{:S(2)}) %collective-permute-start.1) | collective-permute-done | bytes 262176 | tf_op jit(solution)/shard_map/ppermute | solution.py:25
  27.0 3.2 collective-permute-done.2.q3
  30.2 19.5 %all-to-all-done.refs_0_ = bf16[4,656,256]{2,1,0:T(8,128)(2,1)S(1)} async-done(((bf16[4,656,256]{2,1,0:T(8,128)(2,1)}), bf16[4,656,256]{2,1,0:T(8,128)(2,1)S(1)}, u32[]{:S(2)}, u32[]{:S(2)}) %all-to-all-start) | async-done | bytes 1343520 | tf_op jit(solution)/shard_map/all_to_all | solution.py:88
  56.6 3.5 all-to-all-start.1
  60.3 17.4 %collective-permute-done.8.refs_6_ = bf16[2048,256]{1,0:T(8,128)(2,1)} collective-permute-done((bf16[2048,256]{1,0:T(8,128)(2,1)}, bf16[2048,256]{1,0:T(8,128)(2,1)}, u32[]{:S(2)}, u32[]{:S(2)}) %collective-permute-start.8) | collective-permute-done | bytes 1048608 | tf_op jit(solution)/shard_map/ppermute | solution.py:25
  77.7 2.5 collective-permute-done.3.refs_1_
  80.2 3.2 unpack.2
  85.0 3.4 collective-permute-start.4
  90.9 3.7 collective-permute-done.5
  94.8 2.4 fusion.150
  104.8 5.9 collective-permute-done.10
  111.5 1.9 multiply_convert_fusion
  114.9 5.3 collective-permute-done.12
  124.1 5.1 collective-permute-done.16.refs_1_
  129.6 2.4 fusion.18
  133.6 2.6 collective-permute-done.18
  142.5 2.0 collective-permute-done.20
  146.0 26.6 %all-gather.4.cloned.1.call-done.in_ref = bf16[1024,1024]{1,0:T(8,128)(2,1)} async-done(((bf16[128,1024]{1,0:T(8,128)(2,1)}), bf16[1024,1024]{1,0:T(8,128)(2,1)}) %all-gather.4.cloned.1.call-update) | async-done | bytes 2097168 | tf_op jit(solution)/shard_map/all_gather | solution.py:703
  172.6 6.3 split_columns.1
  181.8 2.5 fusion.10.up_ref
  186.2 28.0 %collective-permute-done.23 = bf16[1024,768]{1,0:T(8,128)(2,1)} collective-permute-done((bf16[1024,768]{1,0:T(8,128)(2,1)}, bf16[1024,768]{1,0:T(8,128)(2,1)}, u32[]{:S(2)}, u32[]{:S(2)}) %collective-permute-start.23) | collective-permute-done | bytes 1572896 | tf_op jit(solution)/shard_map/ppermute | solution.py:25
  219.1 2.4 convolution_convert_fusion.3.refs_2_
  222.8 9.2 %collective-permute-done.26 = bf16[1024,256]{1,0:T(8,128)(2,1)S(1)} collective-permute-done((bf16[1024,256]{1,0:T(8,128)(2,1)S(1)}, bf16[1024,256]{1,0:T(8,128)(2,1)S(1)}, u32[]{:S(2)}, u32[]{:S(2)}) %collective-permute-start.26) | collective-permute-done | bytes 524320 | tf_op jit(solution)/shard_map/ppermute | solution.py:25
  233.2 7.2 %attend.1 = (bf16[512,256]{1,0:T(8,128)(2,1)S(1)}, bf16[512,256]{1,0:T(8,128)(2,1)S(1)}, bf16[512,256]{1,0:T(8,128)(2,1)S(1)}, bf16[512,256]{1,0:T(8,128)(2,1)S(1)}) custom-call(s32[512,1]{1,0:T(8,128)S(1)} %copy.105.column_ref, s32[4,1,128]{2,1,0:T(1,128)S(1)} %get-tuple-element.254.row_ref, bf16[512,768]{1,0:T(8,128)(2,1)S(1)} %convolution_convert_fusion.5.refs_0_, ...), custom_call_target="tpu_custom_call" | custom-call | tf_op jit(solution)/shard_map/attend/pallas_call | solution.py:402
  246.2 24.2 %collective-permute-done.29.refs_2_ = bf16[512,1024]{1,0:T(8,128)(2,1)} collective-permute-done((bf16[512,1024]{1,0:T(8,128)(2,1)}, bf16[512,1024]{1,0:T(8,128)(2,1)}, u32[]{:S(2)}, u32[]{:S(2)}) %collective-permute-start.29) | collective-permute-done | bytes 1048608 | tf_op jit(solution)/shard_map/ppermute | solution.py:25
  270.5 2.8 collective-permute-done.30.refs_3_
  273.4 32.4 %mlp.1 = (bf16[2048,1024]{1,0:T(8,128)(2,1)}, bf16[2048,1024]{1,0:T(8,128)(2,1)}, bf16[2048,1024]{1,0:T(8,128)(2,1)}, bf16[2048,1024]{1,0:T(8,128)(2,1)}, bf16[2...) custom-call(s32[24]{0:T(128)S(1)} %pad_add_fusion.1.index, ...), custom_call_target="tpu_custom_call" | custom-call | tf_op jit(solution)/shard_map/mlp/pallas_call | solution.py:570
  306.3 5.4 collective-permute-done.32
  317.4 13.6 %mlp_grads.1 = bf16[8,2,128,1024]{3,2,1,0:T(8,128)(2,1)S(1)} custom-call(bf16[2048,1024]{1,0:T(8,128)(2,1)} %get-tuple-element.110.norm_ref, bf16[2048,1024]{1,0:T(8,128)(2,1)} %get-tuple-element.111.cot_ref, bf16[2048,1024]{1,0:T(8,128)(2,1)} %get-tuple-element.112.act_ref, bf16[2048,1024]{1,0:T(8,128)(2,1)} %get-tuple-element.113.grad_ref), custom_call_target="tpu_custom_call" | custom-call | tf_op jit(solution)/shard_map/mlp_grads/pallas_call | solution.py:617
  331.1 2.1 copy-done
  333.4 6.7 %collective-permute-done.33 = bf16[512,1024]{1,0:T(8,128)(2,1)} collective-permute-done((bf16[512,1024]{1,0:T(8,128)(2,1)}, bf16[512,1024]{1,0:T(8,128)(2,1)}, u32[]{:S(2)}, u32[]{:S(2)}) %collective-permute-start.33) | collective-permute-done | bytes 1048608 | tf_op jit(solution)/shard_map/ppermute | solution.py:25
  340.1 4.3 multiply_reduce_fusion
  344.5 2.2 fusion.136
  352.1 2.0 convolution_convert_fusion.15.refs_7_
  356.4 2.3 add_convert_fusion.9
  358.8 13.1 %attend_back.1 = (bf16[512,768]{1,0:T(8,128)(2,1)S(1)}, bf16[512,768]{1,0:T(8,128)(2,1)S(1)}, bf16[512,768]{1,0:T(8,128)(2,1)S(1)}, bf16[512,768]{1,0:T(8,128)(2,1)S(1)}) custom-call(s32[512,1]{1,0:T(8,128)S(1)} %copy.105.column_ref, s32[4,1,128]{2,1,0:T(1,128)S(1)} %get-tuple-element.254.row_ref, bf16[512,768]{1,0:T(8,128)(2,1)S(1)} %convolution_convert_fusion.5.refs_0_, ...), custom_call_target="tpu_custom_call" | custom-call | tf_op jit(solution)/shard_map/attend_back/pallas_call | solution.py:402
  380.4 2.4 fusion.159
  386.8 3.0 multiply_reduce_fusion.1
  390.1 7.6 %collective-permute-done.39 = bf16[1024,256]{1,0:T(8,128)(2,1)} collective-permute-done((bf16[1024,256]{1,0:T(8,128)(2,1)}, bf16[1024,256]{1,0:T(8,128)(2,1)}, u32[]{:S(2)}, u32[]{:S(2)}) %collective-permute-start.39) | collective-permute-done | bytes 524320 | tf_op jit(solution)/shard_map/ppermute | solution.py:25
  398.3 3.3 multiply_add_fusion.in_ref
  403.2 7.8 %collective-permute-done.40 = bf16[1024,256]{1,0:T(8,128)(2,1)S(1)} collective-permute-done((bf16[1024,256]{1,0:T(8,128)(2,1)}, bf16[1024,256]{1,0:T(8,128)(2,1)S(1)}, u32[]{:S(2)}, u32[]{:S(2)}) %collective-permute-start.40) | collective-permute-done | bytes 524320 | tf_op jit(solution)/shard_map/ppermute | solution.py:25
  413.6 23.0 %collective-permute-done.41 = bf16[128,4096]{1,0:T(8,128)(2,1)S(1)} collective-permute-done((bf16[128,4096]{1,0:T(8,128)(2,1)S(1)}, bf16[128,4096]{1,0:T(8,128)(2,1)S(1)}, u32[]{:S(2)}, u32[]{:S(2)}) %collective-permute-start.41) | collective-permute-done | bytes 1048608 | tf_op jit(solution)/shard_map/ppermute | solution.py:25
  443.9 8.8 %collective-permute-done.46 = bf16[1024,256]{1,0:T(8,128)(2,1)S(1)} collective-permute-done((bf16[1024,256]{1,0:T(8,128)(2,1)S(1)}, bf16[1024,256]{1,0:T(8,128)(2,1)S(1)}, u32[]{:S(2)}, u32[]{:S(2)}) %collective-permute-start.46) | collective-permute-done | bytes 524320 | tf_op jit(solution)/shard_map/ppermute | solution.py:25
  453.3 2.5 add_convert_fusion.2.b_ref
  455.7 5.6 collective-permute-done.47
  463.6 2.1 fusion.24
  465.7 10.0 %collective-permute-done.49 = bf16[1024,256]{1,0:T(8,128)(2,1)S(1)} collective-permute-done((bf16[1024,256]{1,0:T(8,128)(2,1)S(1)}, bf16[1024,256]{1,0:T(8,128)(2,1)S(1)}, u32[]{:S(2)}, u32[]{:S(2)}) %collective-permute-start.49) | collective-permute-done | bytes 524320 | tf_op jit(solution)/shard_map/ppermute | solution.py:25
  479.1 4.8 collective-permute-done.50
  487.4 5.7 collective-permute-done.52
  494.6 2.1 collective-permute-start.54
  497.9 3.1 collective-permute-done.64
  502.9 6.3 join_columns.1
  509.6 3.6 pack.3
  513.2 4.3 all-to-all-start.3
  517.5 2.2 fusion.69
  521.2 4.5 collective-permute-start.57
  525.9 2.2 convolution_convert_fusion.1.refs_2_
  528.2 2.3 collective-permute-start.59
  532.4 26.8 %collective-permute-start.58 = (bf16[1024,256]{1,0:T(8,128)(2,1)S(1)}, bf16[1024,256]{1,0:T(8,128)(2,1)S(1)}, u32[]{:S(2)}, u32[]{:S(2)}) collective-permute-start(bf16[1024,256]{1,0:T(8,128)(2,1)S(1)} %slice.444), channel_id=1, source_target_pairs={{0,1},{1,0},{2,3},{3,2},{4,5},{5,4},{6,7},{7,6},{8,9},{9,8},{10,11... | collective-permute-start | bytes 1572872 | tf_op jit(solution)/shard_map/ppermute | solution.py:29
  559.2 17.3 %collective-permute-done.58.refs_1_ = bf16[1024,256]{1,0:T(8,128)(2,1)S(1)} collective-permute-done((bf16[1024,256]{1,0:T(8,128)(2,1)S(1)}, bf16[1024,256]{1,0:T(8,128)(2,1)S(1)}, u32[]{:S(2)}, u32[]{:S(2)}) %collective-permute-start.58) | collective-permute-done | bytes 524320 | tf_op jit(solution)/shard_map/ppermute | solution.py:29
  578.2 9.2 %all-to-all-start.2 = ((bf16[4,640,256]{2,1,0:T(8,128)(2,1)}), bf16[4,640,256]{2,1,0:T(8,128)(2,1)S(1)}, u32[]{:S(2)}, u32[]{:S(2)}) async-start(bf16[4,640,256]{2,1,0:T(8,128)(2,1)} %pack.2), calls=%async_computation.2 | async-start | bytes 2621440 | tf_op jit(solution)/shard_map/all_to_all | solution.py:88
  593.1 1.9 convert_bitcast_fusion
  598.3 26.9 %all-to-all-done.2.refs_0_ = bf16[4,640,256]{2,1,0:T(8,128)(2,1)S(1)} async-done(((bf16[4,640,256]{2,1,0:T(8,128)(2,1)}), bf16[4,640,256]{2,1,0:T(8,128)(2,1)S(1)}, u32[]{:S(2)}, u32[]{:S(2)}) %all-to-all-start.2) | async-done | bytes 1310752 | tf_op jit(solution)/shard_map/all_to_all | solution.py:88
  (471 shorter events, 130.4 us)
Async XLA Ops:
  11.3 38.4 %all-to-all-start = ((bf16[4,656,256]{2,1,0:T(8,128)(2,1)}), bf16[4,656,256]{2,1,0:T(8,128)(2,1)S(1)}, u32[]{:S(2)}, u32[]{:S(2)}) async-start(bf16[4,656,256]{2,1,0:T(8,128)(2,1)} %broadcast_in_dim.4), calls=%async_computation | async-start | bytes 2686976 | tf_op jit(solution)/shard_map/all_to_all | solution.py:88
  17.7 9.3 %collective-permute-start.1 = (bf16[512,256]{1,0:T(8,128)(2,1)S(1)}, bf16[512,256]{1,0:T(8,128)(2,1)S(1)}, u32[]{:S(2)}, u32[]{:S(2)}) collective-permute-start(bf16[512,256]{1,0:T(8,128)(2,1)S(1)} %get-tuple-element.229), channel_id=1, source_target_pairs={{0,16},{8,24},{16,0},{24,8},{1,17},{9,25},{17,1},{25,9},{2,18},{10... | collective-permute-start | bytes 786440 | tf_op jit(solution)/shard_map/ppermute | solution.py:25
  19.3 10.9 %collective-permute-start.2 = (bf16[512,256]{1,0:T(8,128)(2,1)S(1)}, bf16[512,256]{1,0:T(8,128)(2,1)S(1)}, u32[]{:S(2)}, u32[]{:S(2)}) collective-permute-start(bf16[512,256]{1,0:T(8,128)(2,1)S(1)} %get-tuple-element.227), channel_id=1, source_target_pairs={{0,24},{8,16},{16,8},{24,0},{1,25},{9,17},{17,9},{25,1},{2,26},{10... | collective-permute-start | bytes 786440 | tf_op jit(solution)/shard_map/ppermute | solution.py:25
  19.3 10.9 %collective-permute-start = (bf16[512,256]{1,0:T(8,128)(2,1)S(1)}, bf16[512,256]{1,0:T(8,128)(2,1)S(1)}, u32[]{:S(2)}, u32[]{:S(2)}) collective-permute-start(bf16[512,256]{1,0:T(8,128)(2,1)S(1)} %get-tuple-element.228), channel_id=1, source_target_pairs={{0,8},{8,0},{16,24},{24,16},{1,9},{9,1},{17,25},{25,17},{2,10},{10... | collective-permute-start | bytes 786440 | tf_op jit(solution)/shard_map/ppermute | solution.py:25
  49.7 30.6 %collective-permute-start.3 = (bf16[4,656,256]{2,1,0:T(8,128)(2,1)S(1)}, bf16[4,656,256]{2,1,0:T(8,128)(2,1)}, u32[]{:S(2)}, u32[]{:S(2)}) collective-permute-start(bf16[4,656,256]{2,1,0:T(8,128)(2,1)S(1)} %all-to-all-done.refs_0_), channel_id=1, source_target_pairs={{0,1},{1,0},{2,3},{3,2},{4,5},{5,4},{6,7},{7,6},{8,9},{9,8},{10,11... | collective-permute-start | bytes 4030472 | tf_op jit(solution)/shard_map/ppermute | solution.py:29
  53.5 24.2 %collective-permute-start.8 = (bf16[2048,256]{1,0:T(8,128)(2,1)}, bf16[2048,256]{1,0:T(8,128)(2,1)}, u32[]{:S(2)}, u32[]{:S(2)}) collective-permute-start(bf16[2048,256]{1,0:T(8,128)(2,1)} %pad_maximum_fusion.1.refs_4_), channel_id=1, source_target_pairs={{0,16},{8,24},{16,0},{24,8},{1,17},{9,25},{17,1},{25,9},{2,18},{10... | collective-permute-start | bytes 3145736 | tf_op jit(solution)/shard_map/ppermute | solution.py:25
  56.6 41.4 %all-to-all-start.1 = ((bf16[4,640,256]{2,1,0:T(8,128)(2,1)}), bf16[4,640,256]{2,1,0:T(8,128)(2,1)S(1)}, u32[]{:S(2)}, u32[]{:S(2)}) async-start(bf16[4,640,256]{2,1,0:T(8,128)(2,1)} %broadcast_in_dim.5), calls=%async_computation.1 | async-start | bytes 2621440 | tf_op jit(solution)/shard_map/all_to_all | solution.py:88
  60.1 112.5 %all-gather.4.cloned.1.call-start = ((), (), s32[]{:S(2)}) async-start(), calls=%async_computation.6 | async-start | bytes 2359296 | tf_op jit(solution)/shard_map/all_gather | solution.py:703
  60.2 37.8 %collective-permute-start.14 = (bf16[2048,256]{1,0:T(8,128)(2,1)}, bf16[2048,256]{1,0:T(8,128)(2,1)}, u32[]{:S(2)}, u32[]{:S(2)}) collective-permute-start(bf16[2048,256]{1,0:T(8,128)(2,1)} %pad_maximum_fusion.1.refs_4_), channel_id=1, source_target_pairs={{0,8},{8,0},{16,24},{24,16},{1,9},{9,1},{17,25},{25,17},{2,10},{10... | collective-permute-start | bytes 3145736 | tf_op jit(solution)/shard_map/ppermute | solution.py:25
  77.7 20.2 %collective-permute-start.15 = (bf16[2048,256]{1,0:T(8,128)(2,1)}, bf16[2048,256]{1,0:T(8,128)(2,1)}, u32[]{:S(2)}, u32[]{:S(2)}) collective-permute-start(bf16[2048,256]{1,0:T(8,128)(2,1)} %collective-permute-done.8.refs_6_), channel_id=1, source_target_pairs={{0,8},{8,0},{16,24},{24,16},{1,9},{9,1},{17,25},{25,17},{2,10},{10... | collective-permute-start | bytes 3145736 | tf_op jit(solution)/shard_map/ppermute | solution.py:25
  88.4 6.2 collective-permute-start.5
  98.0 31.2 %collective-permute-start.16 = (bf16[4,640,256]{2,1,0:T(8,128)(2,1)S(1)}, bf16[4,640,256]{2,1,0:T(8,128)(2,1)S(1)}, u32[]{:S(2)}, u32[]{:S(2)}) collective-permute-start(bf16[4,640,256]{2,1,0:T(8,128)(2,1)S(1)} %all-to-all-done.1.refs_0_), channel_id=1, source_target_pairs={{0,1},{1,0},{2,3},{3,2},{4,5},{5,4},{6,7},{7,6},{8,9},{9,8},{10,11... | collective-permute-start | bytes 3932168 | tf_op jit(solution)/shard_map/ppermute | solution.py:29
  103.3 7.5 %collective-permute-start.10 = (bf16[128,1024]{1,0:T(8,128)(2,1)S(1)}, bf16[128,1024]{1,0:T(8,128)(2,1)S(1)}, u32[]{:S(2)}, u32[]{:S(2)}) collective-permute-start(bf16[128,1024]{1,0:T(8,128)(2,1)S(1)} %fusion.35), channel_id=1, source_target_pairs={{0,16},{8,24},{16,0},{24,8},{1,17},{9,25},{17,1},{25,9},{2,18},{10... | collective-permute-start | bytes 786440 | tf_op jit(solution)/shard_map/ppermute | solution.py:25
  113.4 6.9 %collective-permute-start.12 = (bf16[128,1024]{1,0:T(8,128)(2,1)}, bf16[128,1024]{1,0:T(8,128)(2,1)}, u32[]{:S(2)}, u32[]{:S(2)}) collective-permute-start(bf16[128,1024]{1,0:T(8,128)(2,1)} %multiply_convert_fusion), channel_id=1, source_target_pairs={{0,16},{8,24},{16,0},{24,8},{1,17},{9,25},{17,1},{25,9},{2,18},{10... | collective-permute-start | bytes 786440 | tf_op jit(solution)/shard_map/ppermute | solution.py:25
  114.9 14.6 %collective-permute-start.11 = (bf16[128,1024]{1,0:T(8,128)(2,1)}, bf16[128,1024]{1,0:T(8,128)(2,1)}, u32[]{:S(2)}, u32[]{:S(2)}) collective-permute-start(bf16[128,1024]{1,0:T(8,128)(2,1)} %multiply_convert_fusion), channel_id=1, source_target_pairs={{0,8},{8,0},{16,24},{24,16},{1,9},{9,1},{17,25},{25,17},{2,10},{10... | collective-permute-start | bytes 786440 | tf_op jit(solution)/shard_map/ppermute | solution.py:25
  120.3 9.3 %collective-permute-start.13 = (bf16[128,1024]{1,0:T(8,128)(2,1)}, bf16[128,1024]{1,0:T(8,128)(2,1)}, u32[]{:S(2)}, u32[]{:S(2)}) collective-permute-start(bf16[128,1024]{1,0:T(8,128)(2,1)} %collective-permute-done.12), channel_id=1, source_target_pairs={{0,8},{8,0},{16,24},{24,16},{1,9},{9,1},{17,25},{25,17},{2,10},{10... | collective-permute-start | bytes 786440 | tf_op jit(solution)/shard_map/ppermute | solution.py:25
  124.0 149.4 %all-gather.6.cloned.1.call-start = ((), (), s32[]{:S(2)}) async-start(), calls=%async_computation.9 | async-start | bytes 4718592 | tf_op jit(solution)/shard_map/all_gather | solution.py:704
  138.0 40.9 %collective-permute-start.19 = (bf16[128,4096]{1,0:T(8,128)(2,1)}, bf16[128,4096]{1,0:T(8,128)(2,1)}, u32[]{:S(2)}, u32[]{:S(2)}) collective-permute-start(bf16[128,4096]{1,0:T(8,128)(2,1)} %fusion.9), channel_id=1, source_target_pairs={{0,16},{8,24},{16,0},{24,8},{1,17},{9,25},{17,1},{25,9},{2,18},{10... | collective-permute-start | bytes 3145736 | tf_op jit(solution)/shard_map/ppermute | solution.py:25
  141.7 40.1 %collective-permute-start.17 = (bf16[128,4096]{1,0:T(8,128)(2,1)S(1)}, bf16[128,4096]{1,0:T(8,128)(2,1)}, u32[]{:S(2)}, u32[]{:S(2)}) collective-permute-start(bf16[128,4096]{1,0:T(8,128)(2,1)S(1)} %get-tuple-element.199), channel_id=1, source_target_pairs={{0,8},{8,0},{16,24},{24,16},{1,9},{9,1},{17,25},{25,17},{2,10},{10... | collective-permute-start | bytes 3145736 | tf_op jit(solution)/shard_map/ppermute | solution.py:25
  178.9 35.3 %collective-permute-start.23 = (bf16[1024,768]{1,0:T(8,128)(2,1)}, bf16[1024,768]{1,0:T(8,128)(2,1)}, u32[]{:S(2)}, u32[]{:S(2)}) collective-permute-start(bf16[1024,768]{1,0:T(8,128)(2,1)} %get-tuple-element.95), channel_id=1, source_target_pairs={{0,16},{8,24},{16,0},{24,8},{1,17},{9,25},{17,1},{25,9},{2,18},{10... | collective-permute-start | bytes 4718600 | tf_op jit(solution)/shard_map/ppermute | solution.py:25
  181.3 411.8 %reduce-scatter.5.cloned.1.call-start = ((), (), s32[]{:S(2)}) async-start(), calls=%async_computation.8 | async-start | bytes 4718592 | tf_op jit(solution)/shard_map/reduce_scatter | solution.py:768
  186.1 35.4 %collective-permute-start.22 = (bf16[1024,768]{1,0:T(8,128)(2,1)}, bf16[1024,768]{1,0:T(8,128)(2,1)S(1)}, u32[]{:S(2)}, u32[]{:S(2)}) collective-permute-start(bf16[1024,768]{1,0:T(8,128)(2,1)} %get-tuple-element.95), channel_id=1, source_target_pairs={{0,8},{8,0},{16,24},{24,16},{1,9},{9,1},{17,25},{25,17},{2,10},{10... | collective-permute-start | bytes 4718600 | tf_op jit(solution)/shard_map/ppermute | solution.py:25
  214.2 17.7 %collective-permute-start.24 = (bf16[1024,768]{1,0:T(8,128)(2,1)}, bf16[1024,768]{1,0:T(8,128)(2,1)S(1)}, u32[]{:S(2)}, u32[]{:S(2)}) collective-permute-start(bf16[1024,768]{1,0:T(8,128)(2,1)} %collective-permute-done.23), channel_id=1, source_target_pairs={{0,8},{8,0},{16,24},{24,16},{1,9},{9,1},{17,25},{25,17},{2,10},{10... | collective-permute-start | bytes 4718600 | tf_op jit(solution)/shard_map/ppermute | solution.py:25
  215.6 25.8 %collective-permute-start.25 = (bf16[1024,256]{1,0:T(8,128)(2,1)S(1)}, bf16[1024,256]{1,0:T(8,128)(2,1)S(1)}, u32[]{:S(2)}, u32[]{:S(2)}) collective-permute-start(bf16[1024,256]{1,0:T(8,128)(2,1)S(1)} %copy-done.62), channel_id=1, source_target_pairs={{0,8},{8,0},{16,24},{24,16},{1,9},{9,1},{17,25},{25,17},{2,10},{10... | collective-permute-start | bytes 1572872 | tf_op jit(solution)/shard_map/ppermute | solution.py:25
  217.5 14.4 %collective-permute-start.26 = (bf16[1024,256]{1,0:T(8,128)(2,1)S(1)}, bf16[1024,256]{1,0:T(8,128)(2,1)S(1)}, u32[]{:S(2)}, u32[]{:S(2)}) collective-permute-start(bf16[1024,256]{1,0:T(8,128)(2,1)S(1)} %copy-done.62), channel_id=1, source_target_pairs={{0,16},{8,24},{16,0},{24,8},{1,17},{9,25},{17,1},{25,9},{2,18},{10... | collective-permute-start | bytes 1572872 | tf_op jit(solution)/shard_map/ppermute | solution.py:25
  231.9 10.0 %collective-permute-start.27 = (bf16[1024,256]{1,0:T(8,128)(2,1)S(1)}, bf16[1024,256]{1,0:T(8,128)(2,1)S(1)}, u32[]{:S(2)}, u32[]{:S(2)}) collective-permute-start(bf16[1024,256]{1,0:T(8,128)(2,1)S(1)} %collective-permute-done.26), channel_id=1, source_target_pairs={{0,8},{8,0},{16,24},{24,16},{1,9},{9,1},{17,25},{25,17},{2,10},{10... | collective-permute-start | bytes 1572872 | tf_op jit(solution)/shard_map/ppermute | solution.py:25
  244.5 25.8 %collective-permute-start.29 = (bf16[512,1024]{1,0:T(8,128)(2,1)}, bf16[512,1024]{1,0:T(8,128)(2,1)}, u32[]{:S(2)}, u32[]{:S(2)}) collective-permute-start(bf16[512,1024]{1,0:T(8,128)(2,1)} %add_convert_fusion.refs_0_), channel_id=1, source_target_pairs={{0,16},{8,24},{16,0},{24,8},{1,17},{9,25},{17,1},{25,9},{2,18},{10... | collective-permute-start | bytes 3145736 | tf_op jit(solution)/shard_map/ppermute | solution.py:25
  246.0 24.6 %collective-permute-start.28 = (bf16[512,1024]{1,0:T(8,128)(2,1)}, bf16[512,1024]{1,0:T(8,128)(2,1)}, u32[]{:S(2)}, u32[]{:S(2)}) collective-permute-start(bf16[512,1024]{1,0:T(8,128)(2,1)} %add_convert_fusion.refs_0_), channel_id=1, source_target_pairs={{0,8},{8,0},{16,24},{24,16},{1,9},{9,1},{17,25},{25,17},{2,10},{10... | collective-permute-start | bytes 3145736 | tf_op jit(solution)/shard_map/ppermute | solution.py:25
  305.8 5.9 collective-permute-start.32
  306.0 10.2 %collective-permute-start.34 = (bf16[4,512,256]{2,1,0:T(8,128)(2,1)S(1)}, bf16[4,512,256]{2,1,0:T(8,128)(2,1)S(1)}, u32[]{:S(2)}, u32[]{:S(2)}) collective-permute-start(bf16[4,512,256]{2,1,0:T(8,128)(2,1)S(1)} %bitcast.205), channel_id=1, source_target_pairs={{0,8},{8,0},{16,24},{24,16},{1,9},{9,1},{17,25},{25,17},{2,10},{10... | collective-permute-start | bytes 3145736 | tf_op jit(solution)/shard_map/ppermute | solution.py:25
  314.6 25.5 %collective-permute-start.33 = (bf16[512,1024]{1,0:T(8,128)(2,1)}, bf16[512,1024]{1,0:T(8,128)(2,1)}, u32[]{:S(2)}, u32[]{:S(2)}) collective-permute-start(bf16[512,1024]{1,0:T(8,128)(2,1)} %fusion.8), channel_id=1, source_target_pairs={{0,16},{8,24},{16,0},{24,8},{1,17},{9,25},{17,1},{25,9},{2,18},{10... | collective-permute-start | bytes 3145736 | tf_op jit(solution)/shard_map/ppermute | solution.py:25
  333.1 293.7 %reduce-scatter.3.cloned.1.call-start = ((), (), s32[]{:S(2)}) async-start(), calls=%async_computation.7 | async-start | bytes 2359296 | tf_op jit(solution)/shard_map/reduce_scatter | solution.py:812
  349.7 102.9 %collective-permute-start.69 = (bf16[1024,256]{1,0:T(8,128)(2,1)}, bf16[1024,256]{1,0:T(8,128)(2,1)}, u32[]{:S(2)}, u32[]{:S(2)}) collective-permute-start(bf16[1024,256]{1,0:T(8,128)(2,1)} %convolution_convert_fusion.6), channel_id=1, source_target_pairs={{0,8},{8,0},{16,24},{24,16},{1,9},{9,1},{17,25},{25,17},{2,10},{10... | collective-permute-start | bytes 1572872 | tf_op jit(solution)/shard_map/ppermute | solution.py:25
  349.8 6.6 %collective-permute-start.36 = (bf16[1024,256]{1,0:T(8,128)(2,1)}, bf16[1024,256]{1,0:T(8,128)(2,1)}, u32[]{:S(2)}, u32[]{:S(2)}) collective-permute-start(bf16[1024,256]{1,0:T(8,128)(2,1)} %convolution_convert_fusion.14), channel_id=1, source_target_pairs={{0,8},{8,0},{16,24},{24,16},{1,9},{9,1},{17,25},{25,17},{2,10},{10... | collective-permute-start | bytes 1572872 | tf_op jit(solution)/shard_map/ppermute | solution.py:25
  350.3 32.6 %collective-permute-start.35 = (bf16[4,512,256]{2,1,0:T(8,128)(2,1)}, bf16[4,512,256]{2,1,0:T(8,128)(2,1)}, u32[]{:S(2)}, u32[]{:S(2)}) collective-permute-start(bf16[4,512,256]{2,1,0:T(8,128)(2,1)} %fusion.11), channel_id=1, source_target_pairs={{0,16},{8,24},{16,0},{24,8},{1,17},{9,25},{17,1},{25,9},{2,18},{10... | collective-permute-start | bytes 3145736 | tf_op jit(solution)/shard_map/ppermute | solution.py:25
  377.6 83.8 %collective-permute-start.66 = (bf16[1024,256]{1,0:T(8,128)(2,1)}, bf16[1024,256]{1,0:T(8,128)(2,1)}, u32[]{:S(2)}, u32[]{:S(2)}) collective-permute-start(bf16[1024,256]{1,0:T(8,128)(2,1)} %convolution_convert_fusion.9), channel_id=1, source_target_pairs={{0,8},{8,0},{16,24},{24,16},{1,9},{9,1},{17,25},{25,17},{2,10},{10... | collective-permute-start | bytes 1572872 | tf_op jit(solution)/shard_map/ppermute | solution.py:25
  378.1 32.9 %collective-permute-start.45 = (bf16[1024,256]{1,0:T(8,128)(2,1)}, bf16[1024,256]{1,0:T(8,128)(2,1)}, u32[]{:S(2)}, u32[]{:S(2)}) collective-permute-start(bf16[1024,256]{1,0:T(8,128)(2,1)} %convolution_convert_fusion.12), channel_id=1, source_target_pairs={{0,8},{8,0},{16,24},{24,16},{1,9},{9,1},{17,25},{25,17},{2,10},{10... | collective-permute-start | bytes 1572872 | tf_op jit(solution)/shard_map/ppermute | solution.py:25
  382.9 30.4 %collective-permute-start.48 = (bf16[1024,256]{1,0:T(8,128)(2,1)}, bf16[1024,256]{1,0:T(8,128)(2,1)}, u32[]{:S(2)}, u32[]{:S(2)}) collective-permute-start(bf16[1024,256]{1,0:T(8,128)(2,1)} %convolution_convert_fusion.11), channel_id=1, source_target_pairs={{0,8},{8,0},{16,24},{24,16},{1,9},{9,1},{17,25},{25,17},{2,10},{10... | collective-permute-start | bytes 1572872 | tf_op jit(solution)/shard_map/ppermute | solution.py:25
  383.5 14.2 %collective-permute-start.39 = (bf16[1024,256]{1,0:T(8,128)(2,1)}, bf16[1024,256]{1,0:T(8,128)(2,1)}, u32[]{:S(2)}, u32[]{:S(2)}) collective-permute-start(bf16[1024,256]{1,0:T(8,128)(2,1)} %add_convert_fusion.9), channel_id=1, source_target_pairs={{0,16},{8,24},{16,0},{24,8},{1,17},{9,25},{17,1},{25,9},{2,18},{10... | collective-permute-start | bytes 1572872 | tf_op jit(solution)/shard_map/ppermute | solution.py:25
  397.7 13.3 %collective-permute-start.40 = (bf16[1024,256]{1,0:T(8,128)(2,1)}, bf16[1024,256]{1,0:T(8,128)(2,1)S(1)}, u32[]{:S(2)}, u32[]{:S(2)}) collective-permute-start(bf16[1024,256]{1,0:T(8,128)(2,1)} %add_convert_fusion.8), channel_id=1, source_target_pairs={{0,16},{8,24},{16,0},{24,8},{1,17},{9,25},{17,1},{25,9},{2,18},{10... | collective-permute-start | bytes 1572872 | tf_op jit(solution)/shard_map/ppermute | solution.py:25
  411.0 27.1 %collective-permute-start.38 = (bf16[128,4096]{1,0:T(8,128)(2,1)S(1)}, bf16[128,4096]{1,0:T(8,128)(2,1)S(1)}, u32[]{:S(2)}, u32[]{:S(2)}) collective-permute-start(bf16[128,4096]{1,0:T(8,128)(2,1)S(1)} %get-tuple-element.130), channel_id=1, source_target_pairs={{0,8},{8,0},{16,24},{24,16},{1,9},{9,1},{17,25},{25,17},{2,10},{10... | collective-permute-start | bytes 3145736 | tf_op jit(solution)/shard_map/ppermute | solution.py:25
  411.0 25.6 %collective-permute-start.41 = (bf16[128,4096]{1,0:T(8,128)(2,1)S(1)}, bf16[128,4096]{1,0:T(8,128)(2,1)S(1)}, u32[]{:S(2)}, u32[]{:S(2)}) collective-permute-start(bf16[128,4096]{1,0:T(8,128)(2,1)S(1)} %get-tuple-element.130), channel_id=1, source_target_pairs={{0,16},{8,24},{16,0},{24,8},{1,17},{9,25},{17,1},{25,9},{2,18},{10... | collective-permute-start | bytes 3145736 | tf_op jit(solution)/shard_map/ppermute | solution.py:25
  413.3 29.3 %collective-permute-start.63 = (bf16[128,256]{1,0:T(8,128)(2,1)S(1)}, bf16[128,256]{1,0:T(8,128)(2,1)S(1)}, u32[]{:S(2)}, u32[]{:S(2)}) collective-permute-start(bf16[128,256]{1,0:T(8,128)(2,1)S(1)} %bitcast.226), channel_id=1, source_target_pairs={{0,8},{8,0},{16,24},{24,16},{1,9},{9,1},{17,25},{25,17},{2,10},{10... | collective-permute-start | bytes 196616 | tf_op jit(solution)/shard_map/ppermute | solution.py:25
  438.2 14.4 %collective-permute-start.46 = (bf16[1024,256]{1,0:T(8,128)(2,1)S(1)}, bf16[1024,256]{1,0:T(8,128)(2,1)S(1)}, u32[]{:S(2)}, u32[]{:S(2)}) collective-permute-start(bf16[1024,256]{1,0:T(8,128)(2,1)S(1)} %add_convert_fusion.7), channel_id=1, source_target_pairs={{0,16},{8,24},{16,0},{24,8},{1,17},{9,25},{17,1},{25,9},{2,18},{10... | collective-permute-start | bytes 1572872 | tf_op jit(solution)/shard_map/ppermute | solution.py:25
  442.6 41.9 %collective-permute-start.67 = (bf16[1024,256]{1,0:T(8,128)(2,1)S(1)}, bf16[1024,256]{1,0:T(8,128)(2,1)S(1)}, u32[]{:S(2)}, u32[]{:S(2)}) collective-permute-start(bf16[1024,256]{1,0:T(8,128)(2,1)S(1)} %copy-done.88), channel_id=1, source_target_pairs={{0,8},{8,0},{16,24},{24,16},{1,9},{9,1},{17,25},{25,17},{2,10},{10... | collective-permute-start | bytes 1572872 | tf_op jit(solution)/shard_map/ppermute | solution.py:25
  443.4 53.3 %collective-permute-start.68 = (bf16[1024,256]{1,0:T(8,128)(2,1)S(1)}, bf16[1024,256]{1,0:T(8,128)(2,1)S(1)}, u32[]{:S(2)}, u32[]{:S(2)}) collective-permute-start(bf16[1024,256]{1,0:T(8,128)(2,1)S(1)} %copy-done.87), channel_id=1, source_target_pairs={{0,8},{8,0},{16,24},{24,16},{1,9},{9,1},{17,25},{25,17},{2,10},{10... | collective-permute-start | bytes 1572872 | tf_op jit(solution)/shard_map/ppermute | solution.py:25
  452.6 45.2 %collective-permute-start.62 = (bf16[128,256]{1,0:T(8,128)(2,1)S(1)}, bf16[128,256]{1,0:T(8,128)(2,1)S(1)}, u32[]{:S(2)}, u32[]{:S(2)}) collective-permute-start(bf16[128,256]{1,0:T(8,128)(2,1)S(1)} %bitcast.225), channel_id=1, source_target_pairs={{0,8},{8,0},{16,24},{24,16},{1,9},{9,1},{17,25},{25,17},{2,10},{10... | collective-permute-start | bytes 196616 | tf_op jit(solution)/shard_map/ppermute | solution.py:25
  452.7 8.7 %collective-permute-start.47 = (bf16[128,1024]{1,0:T(8,128)(2,1)S(1)}, bf16[128,1024]{1,0:T(8,128)(2,1)S(1)}, u32[]{:S(2)}, u32[]{:S(2)}) collective-permute-start(bf16[128,1024]{1,0:T(8,128)(2,1)S(1)} %fusion.33), channel_id=1, source_target_pairs={{0,16},{8,24},{16,0},{24,8},{1,17},{9,25},{17,1},{25,9},{2,18},{10... | collective-permute-start | bytes 786440 | tf_op jit(solution)/shard_map/ppermute | solution.py:25
  461.4 14.3 %collective-permute-start.49 = (bf16[1024,256]{1,0:T(8,128)(2,1)S(1)}, bf16[1024,256]{1,0:T(8,128)(2,1)S(1)}, u32[]{:S(2)}, u32[]{:S(2)}) collective-permute-start(bf16[1024,256]{1,0:T(8,128)(2,1)S(1)} %add_convert_fusion.6), channel_id=1, source_target_pairs={{0,16},{8,24},{16,0},{24,8},{1,17},{9,25},{17,1},{25,9},{2,18},{10... | collective-permute-start | bytes 1572872 | tf_op jit(solution)/shard_map/ppermute | solution.py:25
  475.7 8.2 %collective-permute-start.50 = (bf16[128,1024]{1,0:T(8,128)(2,1)}, bf16[128,1024]{1,0:T(8,128)(2,1)}, u32[]{:S(2)}, u32[]{:S(2)}) collective-permute-start(bf16[128,1024]{1,0:T(8,128)(2,1)} %fusion.24), channel_id=1, source_target_pairs={{0,16},{8,24},{16,0},{24,8},{1,17},{9,25},{17,1},{25,9},{2,18},{10... | collective-permute-start | bytes 786440 | tf_op jit(solution)/shard_map/ppermute | solution.py:25
  478.7 30.7 %collective-permute-start.61 = (bf16[2048,256]{1,0:T(8,128)(2,1)}, bf16[2048,256]{1,0:T(8,128)(2,1)}, u32[]{:S(2)}, u32[]{:S(2)}) collective-permute-start(bf16[2048,256]{1,0:T(8,128)(2,1)} %slice.447), channel_id=1, source_target_pairs={{0,1},{1,0},{2,3},{3,2},{4,5},{5,4},{6,7},{7,6},{8,9},{9,8},{10,11... | collective-permute-start | bytes 3145736 | tf_op jit(solution)/shard_map/ppermute | solution.py:29
  483.9 9.2 %collective-permute-start.52 = (bf16[512,256]{1,0:T(8,128)(2,1)S(1)}, bf16[512,256]{1,0:T(8,128)(2,1)S(1)}, u32[]{:S(2)}, u32[]{:S(2)}) collective-permute-start(bf16[512,256]{1,0:T(8,128)(2,1)S(1)} %get-tuple-element.137), channel_id=1, source_target_pairs={{0,16},{8,24},{16,0},{24,8},{1,17},{9,25},{17,1},{25,9},{2,18},{10... | collective-permute-start | bytes 786440 | tf_op jit(solution)/shard_map/ppermute | solution.py:25
  484.5 10.1 %collective-permute-start.51 = (bf16[512,256]{1,0:T(8,128)(2,1)S(1)}, bf16[512,256]{1,0:T(8,128)(2,1)S(1)}, u32[]{:S(2)}, u32[]{:S(2)}) collective-permute-start(bf16[512,256]{1,0:T(8,128)(2,1)S(1)} %get-tuple-element.135), channel_id=1, source_target_pairs={{0,24},{8,16},{16,8},{24,0},{1,25},{9,17},{17,9},{25,1},{2,26},{10... | collective-permute-start | bytes 786440 | tf_op jit(solution)/shard_map/ppermute | solution.py:25
  493.1 16.2 %collective-permute-start.60 = (bf16[512,256]{1,0:T(8,128)(2,1)}, bf16[512,256]{1,0:T(8,128)(2,1)S(1)}, u32[]{:S(2)}, u32[]{:S(2)}) collective-permute-start(bf16[512,256]{1,0:T(8,128)(2,1)} %slice.446), channel_id=1, source_target_pairs={{0,1},{1,0},{2,3},{3,2},{4,5},{5,4},{6,7},{7,6},{8,9},{9,8},{10,11... | collective-permute-start | bytes 786440 | tf_op jit(solution)/shard_map/ppermute | solution.py:29
  494.6 22.9 %collective-permute-start.54 = (bf16[128,1024]{1,0:T(8,128)(2,1)}, bf16[128,1024]{1,0:T(8,128)(2,1)}, u32[]{:S(2)}, u32[]{:S(2)}) collective-permute-start(bf16[128,1024]{1,0:T(8,128)(2,1)} %fusion.24), channel_id=1, source_target_pairs={{0,8},{8,0},{16,24},{24,16},{1,9},{9,1},{17,25},{25,17},{2,10},{10... | collective-permute-start | bytes 786440 | tf_op jit(solution)/shard_map/ppermute | solution.py:25
  497.8 19.7 %collective-permute-start.55 = (bf16[128,1024]{1,0:T(8,128)(2,1)}, bf16[128,1024]{1,0:T(8,128)(2,1)}, u32[]{:S(2)}, u32[]{:S(2)}) collective-permute-start(bf16[128,1024]{1,0:T(8,128)(2,1)} %collective-permute-done.50), channel_id=1, source_target_pairs={{0,8},{8,0},{16,24},{24,16},{1,9},{9,1},{17,25},{25,17},{2,10},{10... | collective-permute-start | bytes 786440 | tf_op jit(solution)/shard_map/ppermute | solution.py:25
  501.0 8.6 %collective-permute-start.65 = (bf16[64,256]{1,0:T(8,128)(2,1)S(1)}, bf16[64,256]{1,0:T(8,128)(2,1)S(1)}, u32[]{:S(2)}, u32[]{:S(2)}) collective-permute-start(bf16[64,256]{1,0:T(8,128)(2,1)S(1)} %slice.450), channel_id=1, source_target_pairs={{0,1},{1,0},{2,3},{3,2},{4,5},{5,4},{6,7},{7,6},{8,9},{9,8},{10,11... | collective-permute-start | bytes 98312 | tf_op jit(solution)/shard_map/ppermute | solution.py:29
  509.3 78.1 %collective-permute-start.31 = (bf16[4,512,256]{2,1,0:T(8,128)(2,1)}, bf16[4,512,256]{2,1,0:T(8,128)(2,1)}, u32[]{:S(2)}, u32[]{:S(2)}) collective-permute-start(bf16[4,512,256]{2,1,0:T(8,128)(2,1)} %bitcast.204), channel_id=1, source_target_pairs={{0,8},{8,0},{16,24},{24,16},{1,9},{9,1},{17,25},{25,17},{2,10},{10... | collective-permute-start | bytes 3145736 | tf_op jit(solution)/shard_map/ppermute | solution.py:25
  513.2 65.0 %all-to-all-start.3 = ((bf16[4,656,256]{2,1,0:T(8,128)(2,1)}), bf16[4,656,256]{2,1,0:T(8,128)(2,1)S(1)}, u32[]{:S(2)}, u32[]{:S(2)}) async-start(bf16[4,656,256]{2,1,0:T(8,128)(2,1)} %pack.3), calls=%async_computation.3 | async-start | bytes 2686976 | tf_op jit(solution)/shard_map/all_to_all | solution.py:88
  519.8 10.7 %collective-permute-start.56 = (bf16[4,27,256]{2,1,0:T(8,128)(2,1)S(1)}, bf16[4,27,256]{2,1,0:T(8,128)(2,1)S(1)}, u32[]{:S(2)}, u32[]{:S(2)}) collective-permute-start(bf16[4,27,256]{2,1,0:T(8,128)(2,1)S(1)} %get-tuple-element.232), channel_id=1, source_target_pairs={{1,0},{2,1},{3,2},{4,3},{5,4},{6,5},{7,6},{9,8},{10,9},{11,10},{12... | collective-permute-start | bytes 165896 | tf_op jit(solution)/shard_map/ppermute | solution.py:648
  521.2 9.3 %collective-permute-start.57 = (bf16[4,27,256]{2,1,0:T(8,128)(2,1)S(1)}, bf16[4,27,256]{2,1,0:T(8,128)(2,1)S(1)}, u32[]{:S(2)}, u32[]{:S(2)}) collective-permute-start(bf16[4,27,256]{2,1,0:T(8,128)(2,1)S(1)} %get-tuple-element.231), channel_id=1, source_target_pairs={{0,1},{1,2},{2,3},{3,4},{4,5},{5,6},{6,7},{8,9},{9,10},{10,11},{11... | collective-permute-start | bytes 165896 | tf_op jit(solution)/shard_map/ppermute | solution.py:647
  528.2 48.2 %collective-permute-start.59 = (bf16[512,768]{1,0:T(8,128)(2,1)S(1)}, bf16[512,768]{1,0:T(8,128)(2,1)S(1)}, u32[]{:S(2)}, u32[]{:S(2)}) collective-permute-start(bf16[512,768]{1,0:T(8,128)(2,1)S(1)} %slice.445), channel_id=1, source_target_pairs={{0,1},{1,0},{2,3},{3,2},{4,5},{5,4},{6,7},{7,6},{8,9},{9,8},{10,11... | collective-permute-start | bytes 2359304 | tf_op jit(solution)/shard_map/ppermute | solution.py:29
  532.4 44.1 %collective-permute-start.58 = (bf16[1024,256]{1,0:T(8,128)(2,1)S(1)}, bf16[1024,256]{1,0:T(8,128)(2,1)S(1)}, u32[]{:S(2)}, u32[]{:S(2)}) collective-permute-start(bf16[1024,256]{1,0:T(8,128)(2,1)S(1)} %slice.444), channel_id=1, source_target_pairs={{0,1},{1,0},{2,3},{3,2},{4,5},{5,4},{6,7},{7,6},{8,9},{9,8},{10,11... | collective-permute-start | bytes 1572872 | tf_op jit(solution)/shard_map/ppermute | solution.py:29
  578.2 47.0 %all-to-all-start.2 = ((bf16[4,640,256]{2,1,0:T(8,128)(2,1)}), bf16[4,640,256]{2,1,0:T(8,128)(2,1)S(1)}, u32[]{:S(2)}, u32[]{:S(2)}) async-start(bf16[4,640,256]{2,1,0:T(8,128)(2,1)} %pack.2), calls=%async_computation.2 | async-start | bytes 2621440 | tf_op jit(solution)/shard_map/all_to_all | solution.py:88
  (103 other events, 715.9 us)
Sparse Core Ops, SparseCore 0:
  124.1 48.4 all-gather.3
  181.3 70.9 all-gather.5
  333.3 86.5 reduce-scatter.4
  509.4 99.1 reduce-scatter.2

commit v5 on v4

--- a/solution.py
+++ b/solution.py
@@ -71,6 +71,10 @@
     shape = x.shape
     x = x.reshape(shape[:dim] + (outer, inner, n) + shape[dim + 1 :])
     return jnp.swapaxes(x, dim, dim + 1).reshape(shape)
+
+
+def cost(us):
+    return pl.CostEstimate(flops=int(us * 1.1e9), transcendentals=0, bytes_accessed=0)
 
 
 CELL = 256
@@ -115,6 +119,7 @@
         out_specs=[pl.BlockSpec((r, w), lambda p: (p, 0)) for r, w in shapes],
         compiler_params=pltpu.CompilerParams(vmem_limit_bytes=VMEM_ROOM),
         name="unpack",
+        cost_estimate=cost(3),
     )(near, far)
 
 
@@ -122,29 +127,37 @@
     return [regroup(lax.all_gather(s, "seq", axis=0, tiled=True), 0, 4, 2) for s in shards]
 
 
-def pack_body(shapes, *refs):
-    out = refs[-1]
-    at = 0
-    for (r, w), near, far in zip(shapes, refs[0::2], refs[1::2]):
-        total = (near[...].astype(F32) + far[...].astype(F32)).astype(BF16)
+def pack_body(count, *refs):
+    half, at = pl.program_id(0), 0
+    for ref in refs[:count]:
+        r, w = ref.shape
         for i in range(0, w, CELL):
-            out[0, at : at + r] = total[:, i : i + CELL]
+            for k, out in enumerate(refs[count:]):
+
+                @pl.when(half == k)
+                def _(out=out, ref=ref, at=at, r=r, i=i):
+                    out[0, at : at + r] = ref[:, i : i + CELL]
+
             at += r
 
 
-def pack(nears, fars):
-    shapes = [(f.shape[0] // 4, f.shape[1]) for f in fars]
+def pack(grads):
+    shapes = [(g.shape[0] // 8, g.shape[1]) for g in grads]
     rows = sum(r * w for r, w in shapes) // CELL
-    specs = [pl.BlockSpec((r, w), lambda p: (p, 0)) for r, w in shapes for _ in range(2)]
+    shape = jax.ShapeDtypeStruct((4, rows, CELL), BF16)
     return pl.pallas_call(
-        lambda *refs: pack_body(shapes, *refs),
-        out_shape=jax.ShapeDtypeStruct((4, rows, CELL), BF16),
-        grid=(4,),
-        in_specs=specs,
-        out_specs=pl.BlockSpec((1, rows, CELL), lambda p: (p, 0, 0)),
+        lambda *refs: pack_body(len(grads), *refs),
+        out_shape=(shape, shape),
+        grid=(2, 4),
+        in_specs=[pl.BlockSpec((r, w), lambda h, p: (4 * h + p, 0)) for r, w in shapes],
+        out_specs=(
+            pl.BlockSpec((1, rows, CELL), lambda h, p: (jnp.where(h == 0, p, 3), 0, 0)),
+            pl.BlockSpec((1, rows, CELL), lambda h, p: (jnp.where(h == 1, p, 0), 0, 0)),
+        ),
         compiler_params=pltpu.CompilerParams(vmem_limit_bytes=VMEM_ROOM),
         name="pack",
-    )(*[x for pair in zip(nears, fars) for x in pair])
+        cost_estimate=cost(2),
+    )(*grads)
 
 
 def total_body(shapes, in_ref, *outs):
@@ -162,20 +175,27 @@
         out_shape=[jax.ShapeDtypeStruct(shape, F32) for shape in shapes],
         compiler_params=pltpu.CompilerParams(vmem_limit_bytes=VMEM_ROOM),
         name="total",
+        cost_estimate=cost(1),
     )(parts)
 
 
-def reduce_rows(grads):
+def cross_x(grads):
+    grads = [g.astype(BF16) for g in grads]
     if tuned():
-        grads = [g.astype(BF16) for g in grads]
-        fars = [hop(g[g.shape[0] // 2 :], 1) for g in grads]
-        shapes = [(g.shape[0] // 8, g.shape[1]) for g in grads]
-        return total(along_z(pack(grads, fars)), shapes)
+        near, far = pack(grads)
+        return near, hop(far, 1)
+    return grads
+
+
+def cross_z(started, shapes):
+    if tuned():
+        near, far = started
+        return total(along_z((near.astype(F32) + far.astype(F32)).astype(BF16)), shapes)
     return [
         lax.psum_scatter(
-            regroup(g.astype(BF16), 0, 2, 4), "seq", scatter_dimension=0, tiled=True
+            regroup(g, 0, 2, 4), "seq", scatter_dimension=0, tiled=True
         ).astype(F32)
-        for g in grads
+        for g in started
     ]
 
 
@@ -214,48 +234,6 @@
 
 def lane_block(i):
     return pl.ds(pl.multiple_of(i * LANES, LANES), LANES)
-
-
-def split_body(index_ref, in_ref, a_ref, b_ref):
-    a_ref[...] = in_ref[:, : a_ref.shape[1]]
-    b_ref[...] = in_ref[:, a_ref.shape[1] :]
-
-
-def join_body(index_ref, a_ref, b_ref, out_ref):
-    out_ref[:, : a_ref.shape[1]] = a_ref[...]
-    out_ref[:, a_ref.shape[1] :] = b_ref[...]
-
-
-def split_columns(x, index, first):
-    n, w = x.shape[0] // 8, x.shape[1]
-    widths = (first, w - first)
-    return pl.pallas_call(
-        split_body,
-        out_shape=[jax.ShapeDtypeStruct((8 * n, v), x.dtype) for v in widths],
-        grid_spec=pltpu.PrefetchScalarGridSpec(
-            num_scalar_prefetch=1,
-            grid=(8,),
-            in_specs=[pl.BlockSpec((n, w), lambda i, index: (index[i], 0))],
-            out_specs=[pl.BlockSpec((n, v), lambda i, index: (i, 0)) for v in widths],
-        ),
-        name="split_columns",
-    )(index, x)
-
-
-def join_columns(a, b, index):
-    n = a.shape[0] // 8
-    widths = (a.shape[1], b.shape[1])
-    return pl.pallas_call(
-        join_body,
-        out_shape=jax.ShapeDtypeStruct((8 * n, sum(widths)), a.dtype),
-        grid_spec=pltpu.PrefetchScalarGridSpec(
-            num_scalar_prefetch=1,
-            grid=(8,),
-            in_specs=[pl.BlockSpec((n, v), lambda i, index: (index[i], 0)) for v in widths],
-            out_specs=pl.BlockSpec((n, sum(widths)), lambda i, index: (i, 0)),
-        ),
-        name="join_columns",
-    )(index, a, b)
 
 
 def enter_body(from_up, to_layer, up_ref, q0, q1, q2, q3, out_ref, held, spaced):
@@ -291,6 +269,7 @@
         ),
         compiler_params=pltpu.CompilerParams(vmem_limit_bytes=VMEM_ROOM),
         name="enter",
+        cost_estimate=cost(2),
     )(from_up, to_layer, up_terms, *quarters)
 
 
@@ -326,6 +305,7 @@
         ),
         compiler_params=pltpu.CompilerParams(vmem_limit_bytes=VMEM_ROOM),
         name="leave",
+        cost_estimate=cost(2),
     )(to_up, to_quarters, grad)
 
 
@@ -366,83 +346,219 @@
     return probs
 
 
-def attend_body(column_ref, row_ref, *refs):
-    allowed = visible(column_ref[...], row_ref[0])
-    for qkv_ref, out_ref in zip(refs[:4], refs[4:]):
-        n = out_ref.shape[1]
-        probs = soft(qkv_ref[:, :n], by_head(qkv_ref[:, n : 2 * n]), allowed)
-        low = jnp.concatenate([p.astype(BF16) for p in probs], axis=1)
-        out_ref[...] = dot(low, by_head(qkv_ref[:, 2 * n :])).astype(BF16)
-
-
-def attend_back_body(column_ref, row_ref, *refs):
-    allowed = visible(column_ref[...], row_ref[0])
-    for qkv_ref, grad_ref, out_ref in zip(refs[:4], refs[4:8], refs[8:]):
-        n = grad_ref.shape[1]
-        query, grad = qkv_ref[:, :n], grad_ref[...]
-        keys = by_head(qkv_ref[:, n : 2 * n])
-        probs = soft(query, keys, allowed)
-        grad_probs = dot_t(grad, by_head(qkv_ref[:, 2 * n :]))
-        grads = []
-        for h, p in enumerate(probs):
-            part = grad_probs[:, h * TILE : (h + 1) * TILE]
-            inner = jnp.sum(p * part, axis=1, keepdims=True)
-            grads.append((p * (part - inner)).astype(BF16))
-        grads = jnp.concatenate(grads, axis=1)
-        low = jnp.concatenate([p.astype(BF16) for p in probs], axis=1)
-        out_ref[:, :n] = (dot(grads, keys) * SCALE).astype(BF16)
-        out_ref[:, n : 2 * n] = (of_heads(gram(grads, query)) * SCALE).astype(BF16)
-        out_ref[:, 2 * n :] = of_heads(gram(low, grad)).astype(BF16)
-
-
-def tiled_call(body, segments, arrays, widths, name):
-    tokens = arrays[0].shape[0]
-    tiles = tokens // TILE
-    wide = lambda w: pl.BlockSpec((TILE, w), lambda i: (i, 0))
-    return pl.pallas_call(
-        body,
-        out_shape=[jax.ShapeDtypeStruct((tokens, w), BF16) for w in widths],
-        grid=(tiles,),
-        in_specs=[wide(1), pl.BlockSpec((1, 1, TILE), lambda i: (i, 0, 0))]
-        + [wide(a.shape[1]) for a in arrays],
-        out_specs=[wide(w) for w in widths],
-        compiler_params=pltpu.CompilerParams(vmem_limit_bytes=VMEM_ROOM),
-        name=name,
-    )(segments.reshape(tokens, 1), segments.reshape(tiles, 1, TILE), *arrays)
-
-
-def attend(qkv, segments):
-    return tiled_call(attend_body, segments, qkv, [q.shape[1] // 3 for q in qkv], "attend")
-
-
-def attend_back(qkv, grads, segments):
-    return tiled_call(
-        attend_back_body, segments, (*qkv, *grads), [q.shape[1] for q in qkv], "attend_back"
-    )
-
-
-def normalize(stream):
+def attend_tile(qkv, allowed):
+    n = qkv.shape[1] // 3
+    probs = soft(qkv[:, :n], by_head(qkv[:, n : 2 * n]), allowed)
+    low = jnp.concatenate([p.astype(BF16) for p in probs], axis=1)
+    return dot(low, by_head(qkv[:, 2 * n :])).astype(BF16)
+
+
+def attend_back_tile(qkv, grad, allowed):
+    n = grad.shape[1]
+    query = qkv[:, :n]
+    keys = by_head(qkv[:, n : 2 * n])
+    probs = soft(query, keys, allowed)
+    grad_probs = dot_t(grad, by_head(qkv[:, 2 * n :]))
+    grads = []
+    for h, p in enumerate(probs):
+        part = grad_probs[:, h * TILE : (h + 1) * TILE]
+        inner = jnp.sum(p * part, axis=1, keepdims=True)
+        grads.append((p * (part - inner)).astype(BF16))
+    grads = jnp.concatenate(grads, axis=1)
+    low = jnp.concatenate([p.astype(BF16) for p in probs], axis=1)
+    return jnp.concatenate(
+        [
+            (dot(grads, keys) * SCALE).astype(BF16),
+            (of_heads(gram(grads, query)) * SCALE).astype(BF16),
+            of_heads(gram(low, grad)).astype(BF16),
+        ],
+        axis=1,
+    )
+
+
+def standard(stream):
     mean = jnp.mean(stream, axis=1, keepdims=True)
     centred = stream - mean
     rstd = lax.rsqrt(jnp.mean(centred * centred, axis=1, keepdims=True) + EPSILON)
     return centred * rstd, rstd
 
 
-def normalize_back(normed, rstd, gain, grad):
+def standard_back(normed, rstd, gain, grad):
     scaled = grad * gain
-    back = rstd * (
+    return rstd * (
         scaled
         - jnp.mean(scaled, axis=1, keepdims=True)
         - normed * jnp.mean(scaled * normed, axis=1, keepdims=True)
     )
-    return back, jnp.sum(grad * normed, axis=0), jnp.sum(grad, axis=0)
+
+
+LAYER_TILE = 256
+SUBS = LAYER_TILE // TILE
+
+
+def joined(ref, start, stop):
+    return ref[:, :, :, start:stop].reshape(-1, stop - start)
+
+
+def masks(column_ref, row_ref):
+    return [
+        visible(column_ref[i * TILE : (i + 1) * TILE], row_ref[i]) for i in range(SUBS)
+    ]
+
+
+def forward_body(*refs):
+    column_ref, row_ref, stream_ref, vec_ref = refs[:4]
+    weights = refs[4:8]
+    norm_ref, out_ref, norm_two_ref = refs[8:11]
+    qkvs, contexts = refs[11:15], refs[15:19]
+    allowed = masks(column_ref, row_ref)
+    stream = stream_ref[...]
+    normed, _ = standard(stream)
+    norm_ref[...] = (normed * vec_ref[0:1] + vec_ref[1:2]).astype(BF16)
+    for weight, qkv_ref, context_ref in zip(weights, qkvs, contexts):
+        n = context_ref.shape[1]
+        qkv_ref[...] = dot(norm_ref[...], joined(weight, 0, 3 * n)).astype(BF16)
+        for i in range(SUBS):
+            at = slice(i * TILE, (i + 1) * TILE)
+            context_ref[at] = attend_tile(qkv_ref[at], allowed[i])
+        stream = stream + dot_t(context_ref[...], joined(weight, 3 * n, 4 * n))
+    out_ref[...] = stream
+    normed, _ = standard(stream)
+    norm_two_ref[...] = (normed * vec_ref[2:3] + vec_ref[3:4]).astype(BF16)
+
+
+def backward_body(*refs):
+    column_ref, row_ref, zero_ref, one_ref, vec_ref, keep_ref, core_ref, y_ref, cot_ref = refs[:9]
+    weights, qkvs = refs[9:13], refs[13:17]
+    att_ref, input_ref, vec_grad_ref = refs[17:20]
+    rows = refs[20:24]
+    allowed = masks(column_ref, row_ref)
+    grad = keep_ref[...] + core_ref[...].astype(F32) + y_ref[...].astype(F32)
+    normed, rstd = standard(one_ref[...])
+    sums = [jnp.sum(grad * normed, axis=0, keepdims=True), jnp.sum(grad, axis=0, keepdims=True)]
+    stream = cot_ref[...].astype(F32) + standard_back(normed, rstd, vec_ref[2:3], grad)
+    att_ref[...] = stream.astype(BF16)
+    grad = None
+    for weight, qkv_ref, row_grad_ref in zip(weights, qkvs, rows):
+        n = qkv_ref.shape[1] // 3
+        context = dot(att_ref[...], joined(weight, 3 * n, 4 * n)).astype(BF16)
+        for i in range(SUBS):
+            at = slice(i * TILE, (i + 1) * TILE)
+            row_grad_ref[at] = attend_back_tile(qkv_ref[at], context[at], allowed[i])
+        part = dot_t(row_grad_ref[...], joined(weight, 0, 3 * n))
+        grad = part if grad is None else grad + part
+    normed, rstd = standard(zero_ref[...])
+    sums = [
+        jnp.sum(grad * normed, axis=0, keepdims=True),
+        jnp.sum(grad, axis=0, keepdims=True),
+    ] + sums
+    input_ref[...] = stream + standard_back(normed, rstd, vec_ref[0:1], grad)
+
+    @pl.when(pl.program_id(0) == 0)
+    def _():
+        vec_grad_ref[...] = jnp.zeros_like(vec_grad_ref)
+
+    for i, v in enumerate(sums):
+        vec_grad_ref[i : i + 1] += v
+
+
+def layer_call(body, segments, arrays, fixed, weights, more, outs, name, us):
+    tokens = segments.shape[0]
+    wide = lambda w: pl.BlockSpec((LAYER_TILE, w), lambda i: (i, 0))
+    still = lambda shape: pl.BlockSpec(shape, lambda i: (0,) * len(shape))
+    _, _, n, w = weights[0].shape
+    tiles = tokens // TILE
+    return pl.pallas_call(
+        body,
+        out_shape=[jax.ShapeDtypeStruct(shape, dtype) for shape, dtype in outs],
+        grid=(tokens // LAYER_TILE,),
+        in_specs=[wide(1), pl.BlockSpec((SUBS, 1, TILE), lambda i: (i, 0, 0))]
+        + [wide(a.shape[1]) for a in arrays]
+        + [still(fixed.shape)]
+        + [wide(a.shape[1]) for a in more[0]]
+        + [pl.BlockSpec((8, 1, n, w), lambda i, k=k: (0, k, 0, 0)) for k in (0, 0, 1, 1)]
+        + [wide(a.shape[1]) for a in more[1]],
+        out_specs=[
+            wide(shape[1]) if shape[0] == tokens else still(shape) for shape, _ in outs
+        ],
+        compiler_params=pltpu.CompilerParams(vmem_limit_bytes=VMEM_ROOM),
+        name=name,
+        cost_estimate=cost(us),
+    )(
+        segments.reshape(tokens, 1),
+        segments.reshape(tiles, 1, TILE),
+        *arrays,
+        fixed,
+        *more[0],
+        weights[0],
+        weights[1],
+        weights[0],
+        weights[1],
+        *more[1],
+    )
+
+
+def layer_forward(segments, stream, vectors, weights):
+    tokens, width = stream.shape
+    quarter = width // 4
+    outs = (
+        [((tokens, width), BF16), ((tokens, width), F32), ((tokens, width), BF16)]
+        + [((tokens, 3 * quarter), BF16)] * 4
+        + [((tokens, quarter), BF16)] * 4
+    )
+    norm_one, stream_one, norm_two, *rest = layer_call(
+        forward_body, segments, [stream], vectors, weights, ([], []), outs, "layer_forward", 18
+    )
+    return norm_one, stream_one, norm_two, rest[:4], rest[4:]
+
+
+def layer_backward(segments, streams, vectors, grads, cot, weights, qkv):
+    tokens, width = cot.shape
+    outs = [((tokens, width), BF16), ((tokens, width), F32), (vectors.shape, F32)]
+    outs += [(q.shape, BF16) for q in qkv]
+    return layer_call(
+        backward_body, segments, streams, vectors, weights, ([*grads, cot], qkv), outs,
+        "layer_backward",
+        24,
+    )
+
+
+def layer_grads_body(norm_ref, att_ref, *refs):
+    rows, contexts, outs = refs[:4], refs[4:8], refs[8:]
+    blocks, _, n, _ = outs[0].shape
+    for j in range(4):
+        out, k = outs[j & 1], j >> 1
+        w = rows[j].shape[1]
+        left = gram(norm_ref[...], rows[j][...]).astype(BF16)
+        right = gram(att_ref[...], contexts[j][...]).astype(BF16)
+        for i in range(blocks):
+            out[i, k, :, :w] = left[i * n : (i + 1) * n]
+            out[i, k, :, w:] = right[i * n : (i + 1) * n]
+
+
+def layer_grads(norm, att, rows, contexts):
+    tokens, width = norm.shape
+    n = width // 8
+    part = pl.BlockSpec((tokens, 2 * n), lambda i: (0, i))
+    whole = lambda a: pl.BlockSpec(a.shape, lambda i: (0, 0))
+    shape = jax.ShapeDtypeStruct((8, 2, n, width), BF16)
+    out = pl.BlockSpec((2, 2, n, width), lambda i: (i, 0, 0, 0))
+    return pl.pallas_call(
+        layer_grads_body,
+        out_shape=(shape, shape),
+        grid=(4,),
+        in_specs=[part, part] + [whole(a) for a in (*rows, *contexts)],
+        out_specs=(out, out),
+        compiler_params=pltpu.CompilerParams(vmem_limit_bytes=VMEM_ROOM),
+        name="layer_grads",
+        cost_estimate=cost(8),
+    )(norm, att, *rows, *contexts)
 
 
 def vector_owner(c, x):
     i = jnp.arange(32)
-    kx, kz, part = i >> 4, (i >> 2) & 3, i & 3
-    source = ((kx ^ x) << 2) | part
-    piece = (kz ^ c) * 8 + ((((source & 1) ^ x) << 2) | (source >> 1))
+    source = i & 7
+    piece = ((i >> 3) ^ c) * 8 + ((((source & 1) ^ x) << 2) | (source >> 1))
     return piece[:, None] == jnp.arange(32)[None, :]
 
 
@@ -488,20 +604,16 @@
 def mlp_body(index, *refs):
     (n0, n1, n2, n3, q0, q1, q2, q3, in_ref, down_ref, stream_ref) = refs[:11]
     (act_ref, grad_ref, norm_ref, cot_ref, d0, d1, d2, d3, keep_ref, send_ref, mine_ref) = refs[11:22]
-    wide, other = refs[22:]
+    (wide,) = refs[22:]
     tile = pl.program_id(0)
     k = tile // 2
-    layer_of_natural, natural_of_layer, quarter_at = (
-        [index[row * 8 + i] for i in range(8)] for row in range(3)
-    )
     for at, ref in enumerate((n0, n2, n1, n3)):
 
         @pl.when(k == at)
         def _(ref=ref):
-            for b in range(8):
-                norm_ref[:, b * LANES : (b + 1) * LANES] = ref[:, lane_block(layer_of_natural[b])]
-
-    quarters = [pl.ds(pl.multiple_of(quarter_at[j] * 256, 256), 256) for j in range(4)]
+            norm_ref[...] = ref[...]
+
+    quarters = [pl.ds(pl.multiple_of(index[j] * 256, 256), 256) for j in range(4)]
     for j, ref in enumerate((q0, q1, q2, q3)):
         cot_ref[:, quarters[j]] = ref[...]
     weight_in = in_ref[...].reshape(-1, in_ref.shape[-1])
@@ -517,27 +629,20 @@
 
     @pl.when(tile < 2)
     def _():
-        for b in range(8):
-            at = slice(b * LANES, (b + 1) * LANES)
-            wide[:, at] = wide[:, at] + stream_ref[:, lane_block(layer_of_natural[b])]
-        for p in range(8):
-            mine_ref[:, p * LANES : (p + 1) * LANES] = cot_ref[:, lane_block(natural_of_layer[p])]
+        wide[...] = wide[...] + stream_ref[...]
+        mine_ref[...] = cot_ref[...]
 
     for j, ref in enumerate((d0, d1, d2, d3)):
         ref[...] = wide[:, quarters[j]].astype(BF16)
-    other[...] = dot_t(grad, weight_in)
+    other = dot_t(grad, weight_in)
 
     @pl.when(tile < 4)
     def _():
-        for p in range(8):
-            keep_ref[:, p * LANES : (p + 1) * LANES] = other[:, lane_block(natural_of_layer[p])]
+        keep_ref[...] = other
 
     @pl.when(tile >= 4)
     def _():
-        for p in range(8):
-            send_ref[:, p * LANES : (p + 1) * LANES] = other[
-                :, lane_block(natural_of_layer[p])
-            ].astype(BF16)
+        send_ref[...] = other.astype(BF16)
 
 
 def mlp(norms, cots, weights, stream, index):
@@ -593,10 +698,11 @@
                 pl.BlockSpec((tile, width), held(4, 4)),
                 pl.BlockSpec((tile, width), held(0, 2)),
             ],
-            scratch_shapes=[pltpu.VMEM((tile, width), F32), pltpu.VMEM((tile, width), F32)],
+            scratch_shapes=[pltpu.VMEM((tile, width), F32)],
         ),
         compiler_params=pltpu.CompilerParams(vmem_limit_bytes=VMEM_ROOM),
         name="mlp",
+        cost_estimate=cost(30),
     )(index, *norms, *cots, weights, weights, stream)
 
 
@@ -622,6 +728,7 @@
         out_specs=pl.BlockSpec((2, 2, n, hidden), lambda i: (i, 0, 0, 0)),
         compiler_params=pltpu.CompilerParams(vmem_limit_bytes=VMEM_ROOM),
         name="mlp_grads",
+        cost_estimate=cost(14),
     )(norm, cot, act, grad)
 
 
@@ -673,37 +780,34 @@
     coarse = coarse_ids.shape[1]
     step = CONV_DILATION
     slot = jnp.arange(8, dtype=jnp.int32)
-    to_layer = (((slot & 3) ^ c) << 1) | ((slot >> 2) ^ x)
-    to_quarters = (((slot & 1) ^ x) << 2) | ((slot >> 1) ^ c)
-    natural_of_layer = ((slot & 3) << 1) | ((slot >> 2) ^ x)
-    layer_of_natural = (((slot & 1) ^ x) << 2) | (slot >> 1)
+    quarters = (((slot >> 1) ^ c) << 1) | (slot & 1)
 
     line = Line()
     stream_in = line.exchange(pick([inputs[i] for i in range(4)], c))
+    attn_shard = jnp.concatenate([qkv_weight.reshape(-1, 3 * quarter), out_weight.T], axis=1)
+    attn_shard = jnp.stack([attn_shard, *line.send((attn_shard, 2))])
+    mlp_shard = jnp.stack([in_weight, down_weight.T])
     cots = line.spread(jnp.concatenate(pick([cotangent[i] for i in range(4)], c), axis=0))
 
     lot = gain_one.shape[0]
     vectors = vector_rows(jnp.stack([gain_one, shift_one, gain_two, shift_two]))
     conv_shard = conv_weight.transpose(2, 0, 1).reshape(-1, 3 * quarter)
     groups = ((embed_table, conv_shard, vectors), (res_weight, up_weight.T))
-    attn_shard = jnp.concatenate([qkv_weight.reshape(-1, 3 * quarter), out_weight.T], axis=1)
-    mlp_shard = jnp.stack([in_weight, down_weight.T])
     if tuned():
         first, second = (bundle(group) for group in groups)
         first = along_z(jnp.broadcast_to(first, (4,) + first.shape))
-        second = after(second, first)
+        second = after(second, first, *stream_in, attn_shard)
         second = along_z(jnp.broadcast_to(second, (4,) + second.shape))
-        attn_shard = after(attn_shard, second)
-        first_far = hop(after(first, *stream_in), 1)
-        second_far = hop(after(second, first_far, *cots), 1)
-        table, conv, vectors = unpack(first, first_far, [w.shape for w in groups[0]])
+        first_far = hop(first, 1)
+        second_far = hop(after(second, first_far), 1)
+        table, conv, vectors = unpack(first, after(first_far, *cots), [w.shape for w in groups[0]])
+        attn_shard = after(attn_shard, second, table)
         res, up = unpack(second, second_far, [w.shape for w in groups[1]])
     else:
         (table, conv, vectors), (res, up) = (gather_plain(group) for group in groups)
-    attn_w = lax.all_gather(attn_shard, "seq", axis=0, tiled=True)
+    attn_w = lax.all_gather(attn_shard, "seq", axis=0)
     mlp_w = lax.all_gather(after(mlp_shard, attn_w), "seq", axis=0)
-    vectors = join_vectors(line.spread(vectors), lot, c, x)
-    gain1, shift1, gain2, shift2 = (vectors[i][None, :] for i in range(4))
+    vectors = jnp.pad(join_vectors(line.spread(vectors), lot, c, x), ((0, 4), (0, 0)))
 
     ids = jnp.concatenate(pick([coarse_ids[i] for i in range(4)], c))
     vocab = table.shape[0]
@@ -721,114 +825,88 @@
     ).reshape(micros * coarse, 3 * quarter)
     conv_terms = dot_t(taps, conv).reshape(micros, coarse, width)
     conv_out = fold(line, [conv_terms[j] for j in range(4)])
-    mixed = gelu(conv_out).astype(BF16)
+    mixed = after(gelu(conv_out).astype(BF16), res, up)
     mixed_all = jnp.concatenate(line.spread(mixed), axis=0)
     hidden = (embed + dot(mixed_all, res)).astype(BF16)
     up_terms = dot_t(hidden, up).reshape(micros, coarse, 4 * width)
     up_terms = fold(line, [up_terms[j] for j in range(4)])
-    qkv_w, out_w = split_columns(attn_w, natural_of_layer, 3 * quarter)
-    qkv_w = line.spread(qkv_w)
-    out_w = line.spread(out_w)
-
     i = jnp.arange(32, dtype=jnp.int32)
-    r, bz, bx = i >> 3, i & 3, ((i >> 2) & 1) ^ x
-    from_up = ((bz >> 1) ^ x) * 16 + r * 4 + ((bz & 1) << 1 | bx)
-    h, r, w = (i >> 4) ^ x, (i >> 2) & 3, i & 3
-    to_up = r * 8 + (((w & 1) ^ x) << 2 | h << 1 | w >> 1)
-    stream_zero = enter(up_terms, stream_in, from_up, to_layer)
-    normed_one, rstd_one = normalize(stream_zero)
-    norm_one = (normed_one * gain1 + shift1).astype(BF16)
+    from_up = (((i >> 2) & 1) ^ x) * 16 + (i >> 3) * 4 + (i & 3)
+    to_up = ((i >> 2) & 3) * 8 + ((i >> 4) ^ x) * 4 + (i & 3)
+    stream_zero = enter(up_terms, stream_in, from_up, quarters)
     segments = lax.dynamic_index_in_dim(segment_ids, c, 0, keepdims=False)
-    qkv = [dot(norm_one, qkv_w[j]).astype(BF16) for j in range(4)]
-    context = attend(qkv, segments)
-    stream_one = stream_zero
-    for j in range(4):
-        stream_one = stream_one + dot_t(context[j], out_w[j])
-    normed_two, rstd_two = normalize(stream_one)
-    norm_two = (normed_two * gain2 + shift2).astype(BF16)
+    attn_w = join_rows(attn_w)
+    attn_w = (attn_w, swap(attn_w, 1))
+    norm_one, stream_one, norm_two, qkv, context = layer_forward(
+        segments, stream_zero, vectors, attn_w
+    )
 
     norm_all = line.spread(norm_two)
-    index = jnp.concatenate([layer_of_natural, natural_of_layer, jnp.tile(jnp.arange(4) ^ c, 2)])
     mlp_act, grad_pre, norm_rows, cot_rows, *outs, keep, send, cot_mine = mlp(
-        norm_all, cots, join_rows(mlp_w), stream_one, index.astype(jnp.int32)
-    )
-    from_core = swap(send, 1).astype(F32)
-    over_y = (keep[tokens:] + from_core[tokens:]).astype(BF16)
+        norm_all, cots, join_rows(mlp_w), stream_one, jnp.arange(4, dtype=jnp.int32) ^ c
+    )
+    from_core = swap(send, 1)
+    over_y = (keep[tokens:] + from_core[tokens:].astype(F32)).astype(BF16)
     (from_y,) = line.send((over_y, 2))
     grad_mlp = mlp_grads(after(norm_rows, over_y), cot_rows, mlp_act, grad_pre)
     turned = lambda v, j: jnp.stack([v[m ^ order_of(j)] for m in range(4)])
     result, over_y = fold_core(
         [d.reshape(micros, tokens, quarter) for d in outs], fix=turned
     )
-    from_y, _, over_y = lax.optimization_barrier((from_y, grad_mlp, over_y))
-    grad_norm_two = keep[:tokens] + from_core[:tokens] + from_y.astype(F32)
+    terms = lax.optimization_barrier((keep, from_core, from_y, grad_mlp, over_y))
+    grads, over_y = terms[:3], terms[4]
     (from_y,) = line.send((over_y, 2))
     result = (result + turned(from_y, 2).astype(F32)).astype(BF16)
+    act_done = from_y
     result = jnp.stack(pick([result[order_of(m)] for m in range(4)], c))
-    grad_mlp = lax.psum_scatter(split_rows(grad_mlp), "seq", scatter_dimension=0, tiled=False)
+    grad_mlp = lax.psum_scatter(split_rows(terms[3]), "seq", scatter_dimension=0, tiled=False)
     grad_in, grad_down = grad_mlp[0].astype(F32), grad_mlp[1].astype(F32).T
 
-    back_two, grad_gain2, grad_shift2 = normalize_back(normed_two, rstd_two, gain2, grad_norm_two)
-    grad_stream_one = cot_mine.astype(F32) + back_two
-    grad_att = grad_stream_one.astype(BF16)
-    grad_out, over_y = fold_core([gram(grad_att, context[j]) for j in range(4)])
-    grad_context = [dot(grad_att, out_w[j]).astype(BF16) for j in range(4)]
-    grad_context[0] = after(grad_context[0], over_y)
-    (from_y,) = line.send((over_y, 2))
-    grad_out = (grad_out + from_y.astype(F32)).astype(BF16)
-    grad_rows = list(attend_back(qkv, grad_context, segments))
-    grad_qkv = [
-        fold_core([gram(norm_one, g[:, k * quarter : (k + 1) * quarter]) for g in grad_rows])
-        for k in range(3)
-    ]
-    grad_rows[0] = after(grad_rows[0], grad_qkv[0][1])
-
-    def finish(part):
-        zero, two = grad_qkv[part]
-        (from_y,) = line.send((two, 2))
-        grad_qkv[part] = (zero + from_y.astype(F32)).astype(BF16)
-
-    finish(0)
-    grad_norm_one = dot_t(grad_rows[0], qkv_w[0])
-    for j in (1, 2, 3):
-        grad_norm_one = grad_norm_one + dot_t(grad_rows[j], qkv_w[j])
-    back_one, grad_gain1, grad_shift1 = normalize_back(normed_one, rstd_one, gain1, grad_norm_one)
-    input_grad = grad_stream_one + back_one
-    grad_vectors = split_vectors(
-        jnp.stack([grad_gain1, grad_shift1, grad_gain2, grad_shift2]), lot, c, x
-    )
-    grad_up_rows, *grad_in_q = leave(input_grad, to_up, to_quarters)
-    grad_up_rows = jnp.concatenate(line.spread(grad_up_rows), axis=0)
-    finish(1)
+    att, input_grad, grad_vectors, *grad_rows = layer_backward(
+        segments, [stream_zero, stream_one], vectors, grads, cot_mine, attn_w, qkv
+    )
+    grad_vectors = split_vectors(grad_vectors[:4], lot, c, x)
+    leave_rows, *grad_in_q = leave(input_grad, to_up, quarters)
+    grad_rows[0] = after(grad_rows[0], leave_rows, act_done)
+    grad_attn, send = layer_grads(norm_one, att, grad_rows, context)
+    grad_up_rows = line.spread(leave_rows)
+    grad_attn = grad_attn.astype(F32) + swap(send, 1).astype(F32)
+    grad_attn = split_rows(grad_attn.astype(BF16))
+    grad_up_rows = jnp.concatenate(grad_up_rows, axis=0)
     grad_hidden = dot(grad_up_rows, up)
-    grad_hidden_low = grad_hidden.astype(BF16)
-    grad_mixed = dot_t(grad_hidden_low, res).reshape(micros, coarse, width)
-    grad_mixed = fold(line, [grad_mixed[j] for j in range(4)])
-    finish(2)
-    grad_conv_low = (gelu_grad(conv_out) * grad_mixed).astype(BF16)
-    grad_up = gram(grad_up_rows, hidden)
-    grad_res = gram(mixed_all, grad_hidden_low)
-    grad_attn = join_columns(jnp.concatenate(grad_qkv, axis=1), grad_out, layer_of_natural)
-    grad_attn = lax.psum_scatter(grad_attn, "seq", scatter_dimension=0, tiled=True).astype(F32)
-    grad_qkv, grad_out = grad_attn[:, : 3 * quarter], grad_attn[:, 3 * quarter :]
+    grad_low = grad_hidden.astype(BF16)
+    grad_up = gram(grad_up_rows, hidden).astype(BF16)
+    grad_res = gram(mixed_all, grad_low).astype(BF16)
+    up_started = cross_x([grad_res, grad_up])
+    grad_mixed = dot_t(after(grad_low, grad_up, grad_res), res).reshape(micros, coarse, width)
+    grad_mixed, over_y = fold_core([grad_mixed[j] for j in range(4)])
+    grad_attn = after(grad_attn, grad_mlp, over_y)
+    grad_attn = lax.psum_scatter(grad_attn, "seq", scatter_dimension=0, tiled=False)
+    grad_mixed = grad_mixed + line.send((over_y, 2))[0].astype(F32)
+    grad_conv_low = after((gelu_grad(conv_out) * grad_mixed).astype(BF16), grad_mlp, up_started[1])
 
     grad_conv_all = jnp.concatenate(line.spread(grad_conv_low), axis=0)
-    input_grads = jnp.stack(pick(line.exchange(grad_in_q), c))
     grad_taps = dot(grad_conv_all, conv).reshape(micros, coarse, 3 * quarter)
     tap = [grad_taps[:, :, k * quarter : (k + 1) * quarter] for k in range(3)]
-    prior, later = edges((tap[0][:, :step].astype(BF16), tap[2][:, coarse - step :].astype(BF16)))
+    rims = tap[0][:, :step].astype(BF16), tap[2][:, coarse - step :].astype(BF16)
+    prior, later = edges(rims)
+    grad_conv = gram(grad_conv_all, taps).astype(BF16)
+    grad_vectors = fold(line, grad_vectors)
     grad_act = (
         tap[1]
         + jnp.concatenate([tap[0][:, step:], later.astype(F32)], axis=1)
         + jnp.concatenate([prior.astype(F32), tap[2][:, : coarse - step]], axis=1)
     ).reshape(micros * coarse, quarter)
-    grad_res, grad_up, grad_vectors = reduce_rows(
-        [grad_res, grad_up, fold(line, grad_vectors)]
-    )
+    grad_embed = (grad_hidden + gelu_grad(embed) * grad_act).astype(BF16)
+    started = cross_x([gram(onehot, grad_embed), grad_conv, grad_vectors])
+    up_started = after(up_started, started[0])
+    grad_res, grad_up = cross_z(up_started, [w.shape for w in groups[1]])
+    grad_table, grad_conv, grad_vectors = cross_z(started, [w.shape for w in groups[0]])
+    grad_conv = grad_conv.reshape(-1, 3, quarter).transpose(1, 2, 0)
+    input_grads = jnp.stack(pick(line.exchange(grad_in_q), c))
+    grad_attn = grad_attn[0].astype(F32) + line.send((grad_attn[1], 2))[0].astype(F32)
+    grad_qkv, grad_out = grad_attn[:, : 3 * quarter], grad_attn[:, 3 * quarter :]
     grad_vectors = [grad_vectors[i, :lot] for i in range(4)]
-    grad_embed = (grad_hidden + gelu_grad(embed) * grad_act).astype(BF16)
-    grad_table, grad_conv = reduce_rows([gram(onehot, grad_embed), gram(grad_conv_all, taps)])
-    grad_conv = grad_conv.reshape(-1, 3, quarter).transpose(1, 2, 0)
     return (
         result,
         input_grads,

time: 645 us -> 571 us (0.89)
  matrix products: 59.5 us -> 17.9 us
  starting transfers between devices: 98.8 us -> 67.9 us
  waiting for transfers between devices: 303 us -> 279 us
  local copies, waits for them, and re-layouts: 29.2 us -> 47.1 us
  Pallas kernels: 92.1 us -> 101 us
    ppermute x7 -> x4, waiting for transfers between devices: 25.2 us -> 81.1 us  [hop(): return lax.ppermute(x, 'seq', [(i, i ^ k) for i in range(8)])]
    ppermute x59 -> x45, waiting for transfers between devices: 200 us -> 146 us  [swap(): return lax.ppermute(x, 'cond', [(i, i ^ j) for i in range(4)])]
    dot_general x43 -> x11, matrix products: 59.1 us -> 16 us  [dot(): return lax.dot_general(a, b, (dims, ((), ())), preferred_element_type=F32)]
    all_to_all x4, waiting for transfers between devices: 46.4 us -> 13.7 us  [along_z(): return lax.all_to_all(x, 'seq', 0, 0, axis_index_groups=ALONG_Z, tiled=True)]
    ppermute x7 -> x4, starting transfers between devices: 33.3 us -> 6.95 us  [hop(): return lax.ppermute(x, 'seq', [(i, i ^ k) for i in range(8)])]
    reduce_scatter x2, waiting for transfers between devices: 0.01 us -> 18.7 us  [the longest x1 18.7 us: on_device(): lax.psum_scatter(split_rows(terms[3]), 'seq', scatter_dimension=0, tiled=...]
    unnamed x196 -> x165, local copies, waits for them, and re-layouts: 13.5 us -> 29.9 us
    pallas_call x6 -> x5, Pallas kernels: 38.2 us -> 51.4 us  [the longest x2 42.8 us: layer_call(): pl.pallas_call(body, out_shape=[jax.ShapeDtypeStruct(shape, dtype) for sh...]
  transfers between devices with their start and end apart: 78 -> 61, of which waited for: 36 -> 35; matrix products, arithmetic and copies ran while one was open for 18% -> 12% of each run, Pallas kernels for 9% -> 13%
where the time goes in v5:
time: 571 us; the launch traced here: 563 us
  waiting for transfers between devices  279 us (49%)
  Pallas kernels  101 us (18%)
  starting transfers between devices  67.9 us (12%)
  local copies, waits for them, and re-layouts  47.1 us (8%)
  other arithmetic  34.4 us (6%)
  matrix products  17.9 us (3%)
  between operations  15.3 us (3%)
    ppermute x45, waiting for transfers between devices, swap(): return lax.ppermute(x, 'cond', [(i, i ^ j) for i in range(4)])  146 us
    ppermute x4, waiting for transfers between devices, hop(): return lax.ppermute(x, 'seq', [(i, i ^ k) for i in range(8)])  81.1 us
    pallas_call x2, Pallas kernels, layer_call(): pl.pallas_call(body, out_shape=[jax.ShapeDtypeStruct(shape, dtype) for sh...  42.8 us
    pallas_call x1, Pallas kernels, mlp(): pl.pallas_call(mlp_body, out_shape=[shape((rows, hidden), BF16), shape((r...  30.1 us
    unnamed x165, local copies, waits for them, and re-layouts  29.9 us
    ppermute x45, starting transfers between devices, swap(): return lax.ppermute(x, 'cond', [(i, i ^ j) for i in range(4)])  26.3 us
    all_to_all x4, starting transfers between devices, along_z(): return lax.all_to_all(x, 'seq', 0, 0, axis_index_groups=ALONG_Z, tiled=True)  23.9 us
    reduce_scatter x1, waiting for transfers between devices, on_device(): lax.psum_scatter(split_rows(terms[3]), 'seq', scatter_dimension=0, tiled=...  18.7 us
  transfers between devices with their start and end apart: 61, of which 35 were waited for; matrix products, arithmetic and copies ran while one was open for 12% of the time, Pallas kernels for 13%

profile of v5, /device:TPU:0, one launch (start us, length us, event | category | flops | bytes accessed | tf_op | source)
XLA Modules:
  0.0 562.7 jit_solution(4147488975223360510)
XLA Ops:
  11.3 6.4 %all-to-all-start = ((bf16[4,656,256]{2,1,0:T(8,128)(2,1)}), bf16[4,656,256]{2,1,0:T(8,128)(2,1)S(1)}, u32[]{:S(2)}, u32[]{:S(2)}) async-start(bf16[4,656,256]{2,1,0:T(8,128)(2,1)} %broadcast_in_dim.4), calls=%async_computation | async-start | bytes 2686976 | tf_op jit(solution)/shard_map/all_to_all | solution.py:92
  20.4 7.7 %collective-permute-done.2.q2 = bf16[512,256]{1,0:T(8,128)(2,1)S(1)} collective-permute-done((bf16[512,256]{1,0:T(8,128)(2,1)}, bf16[512,256]{1,0:T(8,128)(2,1)S(1)}, u32[]{:S(2)}, u32[]{:S(2)}) %collective-permute-start.2) | collective-permute-done | bytes 262176 | tf_op jit(solution)/shard_map/ppermute | solution.py:25
  28.1 3.2 collective-permute-done.3.q3
  34.6 5.7 %collective-permute-done.4 = bf16[128,1024]{0,1:T(8,128)(2,1)S(1)} collective-permute-done((bf16[128,1024]{0,1:T(8,128)(2,1)S(1)}, bf16[128,1024]{0,1:T(8,128)(2,1)S(1)}, u32[]{:S(2)}, u32[]{:S(2)}) %collective-permute-start.4) | collective-permute-done | bytes 262176 | tf_op jit(solution)/shard_map/ppermute | solution.py:25
  42.3 1.8 pad_maximum_fusion.4
  44.1 5.7 %all-to-all-done.refs_0_ = bf16[4,656,256]{2,1,0:T(8,128)(2,1)S(1)} async-done(((bf16[4,656,256]{2,1,0:T(8,128)(2,1)}), bf16[4,656,256]{2,1,0:T(8,128)(2,1)S(1)}, u32[]{:S(2)}, u32[]{:S(2)}) %all-to-all-start) | async-done | bytes 1343520 | tf_op jit(solution)/shard_map/all_to_all | solution.py:92
  51.1 3.5 all-to-all-start.1
  56.3 9.5 %collective-permute-done.5.refs_6_ = bf16[2048,256]{1,0:T(8,128)(2,1)} collective-permute-done((bf16[2048,256]{1,0:T(8,128)(2,1)}, bf16[2048,256]{1,0:T(8,128)(2,1)}, u32[]{:S(2)}, u32[]{:S(2)}) %collective-permute-start.5) | collective-permute-done | bytes 1048608 | tf_op jit(solution)/shard_map/ppermute | solution.py:25
  65.9 2.9 collective-permute-done.6.refs_7_
  68.7 16.5 %collective-permute-done.refs_1_ = bf16[4,656,256]{2,1,0:T(8,128)(2,1)S(1)} collective-permute-done((bf16[4,656,256]{2,1,0:T(8,128)(2,1)S(1)}, bf16[4,656,256]{2,1,0:T(8,128)(2,1)S(1)}, u32[]{:S(2)}, u32[]{:S(2)}) %collective-permute-start) | collective-permute-done | bytes 1343520 | tf_op jit(solution)/shard_map/ppermute | solution.py:29
  87.7 2.4 copy.90
  90.3 2.1 multiply_convert_fusion.1
  92.5 3.4 collective-permute-start.7
  97.8 4.4 collective-permute-done.8
  102.3 4.4 collective-permute-start.14
  107.9 1.7 collective-permute-start.11
  109.8 2.6 collective-permute-done.11
  112.4 1.6 collective-permute-start.12
  114.0 6.3 %collective-permute-done.12 = bf16[128,1024]{1,0:T(8,128)(2,1)S(1)} collective-permute-done((bf16[128,1024]{1,0:T(8,128)(2,1)S(1)}, bf16[128,1024]{1,0:T(8,128)(2,1)S(1)}, u32[]{:S(2)}, u32[]{:S(2)}) %collective-permute-start.12) | collective-permute-done | bytes 262176 | tf_op jit(solution)/shard_map/ppermute | solution.py:25
  120.5 24.3 %collective-permute-done.14.refs_1_ = bf16[4,640,256]{2,1,0:T(8,128)(2,1)S(1)} collective-permute-done((bf16[4,640,256]{2,1,0:T(8,128)(2,1)S(1)}, bf16[4,640,256]{2,1,0:T(8,128)(2,1)S(1)}, u32[]{:S(2)}, u32[]{:S(2)}) %collective-permute-start.14) | collective-permute-done | bytes 1310752 | tf_op jit(solution)/shard_map/ppermute | solution.py:29
  145.1 1.6 collective-permute-start.16
  146.7 4.8 collective-permute-done.16
  153.6 4.7 fusion.101
  159.8 14.0 %all-gather.5.cloned.1.call-done = bf16[16,128,1024]{2,1,0:T(8,128)(2,1)} async-done(((bf16[2,128,1024]{2,1,0:T(8,128)(2,1)}), bf16[16,128,1024]{2,1,0:T(8,128)(2,1)}) %all-gather.5.cloned.1.call-update) | async-done | bytes 4194320 | tf_op jit(solution)/shard_map/all_gather | solution.py:808
  174.9 1.8 pad_maximum_fusion.5
  177.3 3.0 fusion.7
  187.5 18.3 %collective-permute-done.20 = bf16[128,4096]{1,0:T(8,128)(2,1)} collective-permute-done((bf16[128,4096]{1,0:T(8,128)(2,1)}, bf16[128,4096]{1,0:T(8,128)(2,1)}, u32[]{:S(2)}, u32[]{:S(2)}) %collective-permute-start.20) | collective-permute-done | bytes 1048608 | tf_op jit(solution)/shard_map/ppermute | solution.py:25
  205.7 2.5 fusion.8.up_ref
  211.1 18.2 %layer_forward.1 = (bf16[512,1024]{1,0:T(8,128)(2,1)S(1)}, f32[512,1024]{1,0:T(8,128)}, bf16[512,1024]{1,0:T(8,128)(2,1)}, bf16[512,768]{1,0:T(8,128)(2,1)S(1)},...) custom-call(s32[512,1]{1,0:T(8,128)S(1)} %copy.91.refs_0_, ...), custom_call_target="tpu_custom_call" | custom-call | flops 19800000512 | tf_op jit(solution)/shard_map/layer_forward/pallas_call | solution.py:471
  237.6 23.0 %collective-permute-done.25.refs_2_ = bf16[512,1024]{1,0:T(8,128)(2,1)S(1)} collective-permute-done((bf16[512,1024]{1,0:T(8,128)(2,1)}, bf16[512,1024]{1,0:T(8,128)(2,1)S(1)}, u32[]{:S(2)}, u32[]{:S(2)}) %collective-permute-start.25) | collective-permute-done | bytes 1048608 | tf_op jit(solution)/shard_map/ppermute | solution.py:25
  261.5 2.8 collective-permute-done.26.refs_3_
  264.3 30.1 %mlp.1 = (bf16[2048,1024]{1,0:T(8,128)(2,1)}, bf16[2048,1024]{1,0:T(8,128)(2,1)}, bf16[2048,1024]{1,0:T(8,128)(2,1)}, bf16[2048,1024]{1,0:T(8,128)(2,1)}, bf16[2...) custom-call(s32[4]{0:T(128)S(1)} %iota_xor_fusion.index, ...), custom_call_target="tpu_custom_call" | custom-call | flops 32999999488 | tf_op jit(solution)/shard_map/mlp/pallas_call | solution.py:675
  295.0 4.9 collective-permute-done.30
  301.2 2.0 copy-done.46
  304.6 1.6 collective-permute-start.29
  306.1 13.6 %mlp_grads.1 = bf16[8,2,128,1024]{3,2,1,0:T(8,128)(2,1)S(1)} custom-call(bf16[2048,1024]{1,0:T(8,128)(2,1)} %get-tuple-element.124.norm_ref, bf16[2048,1024]{1,0:T(8,128)(2,1)} %get-tuple-element.125.cot_ref, bf16[2048,1024]{1,0:T(8,128)(2,1)} %get-tuple-element.126.act_ref, bf16[2048,1024]{1,0:T(8,128)(2,1)} %get-tuple-element.127.grad_ref), custom_call_target="tpu_custom_call" | custom-call | flops 15399999488 | tf_op jit(solution)/shard_map/mlp_grads/pallas_call | solution.py:723
  319.7 2.1 copy-done
  321.8 8.5 %collective-permute-done.29.refs_7_ = bf16[512,1024]{1,0:T(8,128)(2,1)} collective-permute-done((bf16[512,1024]{1,0:T(8,128)(2,1)}, bf16[512,1024]{1,0:T(8,128)(2,1)}, u32[]{:S(2)}, u32[]{:S(2)}) %collective-permute-start.29) | collective-permute-done | bytes 1048608 | tf_op jit(solution)/shard_map/ppermute | solution.py:25
  335.3 24.5 %layer_backward.1 = (bf16[512,1024]{1,0:T(8,128)(2,1)}, f32[512,1024]{1,0:T(8,128)}, f32[8,1024]{1,0:T(8,128)S(1)}, bf16[512,768]{1,0:T(8,128)(2,1)S(1)}, bf16[5...) custom-call(s32[512,1]{1,0:T(8,128)S(1)} %copy.91.refs_0_, ...), custom_call_target="tpu_custom_call" | custom-call | flops 26400000000 | tf_op jit(solution)/shard_map/layer_backward/pallas_call | solution.py:471
  359.9 1.6 copy-done.16
  361.5 2.0 leave.1
  364.0 7.5 %layer_grads.1 = (bf16[8,2,128,1024]{3,2,1,0:T(8,128)(2,1)}, bf16[8,2,128,1024]{3,2,1,0:T(8,128)(2,1)}) custom-call(bf16[512,1024]{1,0:T(8,128)(2,1)S(1)} %copy-done.18, bf16[512,1024]{1,0:T(8,128)(2,1)} %get-tuple-element.168.att_ref, bf16[512,768]{1,0:T(8,128)(2,1)S(1)} %get-tuple-element.170.refs_0_, bf16[512,768]{1,0:T(8,128)(2,1)S(1)} %get-tuple-element.171.refs_1_, ...), custom_call_target="tpu_custom_call" | custom-call | flops 8800000000 | tf_op jit(solution)/shard_map/layer_grads/pallas_call | solution.py:546
  372.1 15.8 %collective-permute-done.34 = bf16[128,4096]{1,0:T(8,128)(2,1)S(1)} collective-permute-done((bf16[128,4096]{1,0:T(8,128)(2,1)S(1)}, bf16[128,4096]{1,0:T(8,128)(2,1)S(1)}, u32[]{:S(2)}, u32[]{:S(2)}) %collective-permute-start.34) | collective-permute-done | bytes 1048608 | tf_op jit(solution)/shard_map/ppermute | solution.py:25
  388.1 2.4 collective-permute-done.35
  390.6 2.1 fusion.102
  398.2 1.7 fusion.31
  399.9 4.3 add_convert_fusion
  404.2 18.7 %reduce-scatter.3.cloned.1.call-done = bf16[1,2,128,1024]{3,2,1,0:T(8,128)(2,1)} async-done(((bf16[8,2,128,1024]{3,2,1,0:T(8,128)(2,1)}), bf16[1,2,128,1024]{3,2,1,0:T(8,128)(2,1)}) %reduce-scatter.3.cloned.1.call-update) | async-done | bytes 524304 | tf_op jit(solution)/shard_map/reduce_scatter | solution.py:862
  424.9 1.6 collective-permute-start.38
  427.4 6.5 %collective-permute-done.38 = bf16[128,1024]{1,0:T(8,128)(2,1)S(1)} collective-permute-done((bf16[128,1024]{1,0:T(8,128)(2,1)}, bf16[128,1024]{1,0:T(8,128)(2,1)S(1)}, u32[]{:S(2)}, u32[]{:S(2)}) %collective-permute-start.38) | collective-permute-done | bytes 262176 | tf_op jit(solution)/shard_map/ppermute | solution.py:25
  433.9 1.7 fusion.22
  435.7 1.6 collective-permute-start.40
  437.4 7.0 %collective-permute-done.40 = bf16[128,1024]{1,0:T(8,128)(2,1)S(1)} collective-permute-done((bf16[128,1024]{1,0:T(8,128)(2,1)S(1)}, bf16[128,1024]{1,0:T(8,128)(2,1)S(1)}, u32[]{:S(2)}, u32[]{:S(2)}) %collective-permute-start.40) | collective-permute-done | bytes 262176 | tf_op jit(solution)/shard_map/ppermute | solution.py:25
  444.4 1.6 collective-permute-start.41
  446.1 2.6 collective-permute-done.41
  451.3 4.5 collective-permute-start.48
  461.6 2.7 add_convert_fusion.2
  464.3 9.1 %all-to-all-start.3 = ((bf16[4,640,256]{2,1,0:T(8,128)(2,1)}), bf16[4,640,256]{2,1,0:T(8,128)(2,1)S(1)}, u32[]{:S(2)}, u32[]{:S(2)}) async-start(bf16[4,640,256]{2,1,0:T(8,128)(2,1)} %add_convert_fusion.2), calls=%async_computation.4 | async-start | bytes 2621440 | tf_op jit(solution)/shard_map/all_to_all | solution.py:92
  473.3 40.3 %collective-permute-done.50 = bf16[4,656,256]{2,1,0:T(8,128)(2,1)S(1)} collective-permute-done((bf16[4,656,256]{2,1,0:T(8,128)(2,1)}, bf16[4,656,256]{2,1,0:T(8,128)(2,1)S(1)}, u32[]{:S(2)}, u32[]{:S(2)}) %collective-permute-start.50) | collective-permute-done | bytes 1343520 | tf_op jit(solution)/shard_map/ppermute | solution.py:29
  515.0 4.8 all-to-all-start.2
  527.2 2.0 copy.104
  529.2 3.1 collective-permute-done.43
  532.4 4.8 collective-permute-done.42
  543.8 8.0 %all-to-all-done.2.refs_0_ = bf16[4,656,256]{2,1,0:T(8,128)(2,1)S(1)} async-done(((bf16[4,656,256]{2,1,0:T(8,128)(2,1)}), bf16[4,656,256]{2,1,0:T(8,128)(2,1)S(1)}, u32[]{:S(2)}, u32[]{:S(2)}) %all-to-all-start.2) | async-done | bytes 1343520 | tf_op jit(solution)/shard_map/all_to_all | solution.py:92
  (340 shorter events, 91.2 us)
Async XLA Ops:
  11.3 38.5 %all-to-all-start = ((bf16[4,656,256]{2,1,0:T(8,128)(2,1)}), bf16[4,656,256]{2,1,0:T(8,128)(2,1)S(1)}, u32[]{:S(2)}, u32[]{:S(2)}) async-start(bf16[4,656,256]{2,1,0:T(8,128)(2,1)} %broadcast_in_dim.4), calls=%async_computation | async-start | bytes 2686976 | tf_op jit(solution)/shard_map/all_to_all | solution.py:92
  18.6 9.4 %collective-permute-start.2 = (bf16[512,256]{1,0:T(8,128)(2,1)}, bf16[512,256]{1,0:T(8,128)(2,1)S(1)}, u32[]{:S(2)}, u32[]{:S(2)}) collective-permute-start(bf16[512,256]{1,0:T(8,128)(2,1)} %get-tuple-element.247), channel_id=1, source_target_pairs={{0,16},{8,24},{16,0},{24,8},{1,17},{9,25},{17,1},{25,9},{2,18},{10... | collective-permute-start | bytes 786440 | tf_op jit(solution)/shard_map/ppermute | solution.py:25
  20.2 11.1 %collective-permute-start.3 = (bf16[512,256]{1,0:T(8,128)(2,1)S(1)}, bf16[512,256]{1,0:T(8,128)(2,1)S(1)}, u32[]{:S(2)}, u32[]{:S(2)}) collective-permute-start(bf16[512,256]{1,0:T(8,128)(2,1)S(1)} %get-tuple-element.248), channel_id=1, source_target_pairs={{0,24},{8,16},{16,8},{24,0},{1,25},{9,17},{17,9},{25,1},{2,26},{10... | collective-permute-start | bytes 786440 | tf_op jit(solution)/shard_map/ppermute | solution.py:25
  31.3 9.1 %collective-permute-start.4 = (bf16[128,1024]{0,1:T(8,128)(2,1)S(1)}, bf16[128,1024]{0,1:T(8,128)(2,1)S(1)}, u32[]{:S(2)}, u32[]{:S(2)}) collective-permute-start(bf16[128,1024]{0,1:T(8,128)(2,1)S(1)} %get-tuple-element.98), channel_id=1, source_target_pairs={{0,16},{8,24},{16,0},{24,8},{1,17},{9,25},{17,1},{25,9},{2,18},{10... | collective-permute-start | bytes 786440 | tf_op jit(solution)/shard_map/ppermute | solution.py:25
  40.3 25.5 %collective-permute-start.5 = (bf16[2048,256]{1,0:T(8,128)(2,1)}, bf16[2048,256]{1,0:T(8,128)(2,1)}, u32[]{:S(2)}, u32[]{:S(2)}) collective-permute-start(bf16[2048,256]{1,0:T(8,128)(2,1)} %pad_maximum_fusion.refs_4_), channel_id=1, source_target_pairs={{0,16},{8,24},{16,0},{24,8},{1,17},{9,25},{17,1},{25,9},{2,18},{10... | collective-permute-start | bytes 3145736 | tf_op jit(solution)/shard_map/ppermute | solution.py:25
  41.0 3.0 collective-permute-start.13
  51.1 36.6 %all-to-all-start.1 = ((bf16[4,640,256]{2,1,0:T(8,128)(2,1)}), bf16[4,640,256]{2,1,0:T(8,128)(2,1)S(1)}, u32[]{:S(2)}, u32[]{:S(2)}) async-start(bf16[4,640,256]{2,1,0:T(8,128)(2,1)} %broadcast_in_dim.5), calls=%async_computation.1 | async-start | bytes 2621440 | tf_op jit(solution)/shard_map/all_to_all | solution.py:92
  54.7 119.1 %all-gather.5.cloned.1.call-start = ((), (), s32[]{:S(2)}) async-start(), calls=%async_computation.8 | async-start | bytes 4718592 | tf_op jit(solution)/shard_map/all_gather | solution.py:808
  54.7 30.5 %collective-permute-start = (bf16[4,656,256]{2,1,0:T(8,128)(2,1)S(1)}, bf16[4,656,256]{2,1,0:T(8,128)(2,1)S(1)}, u32[]{:S(2)}, u32[]{:S(2)}) collective-permute-start(bf16[4,656,256]{2,1,0:T(8,128)(2,1)S(1)} %all-to-all-done.refs_0_), channel_id=1, source_target_pairs={{0,1},{1,0},{2,3},{3,2},{4,5},{5,4},{6,7},{7,6},{8,9},{9,8},{10,11... | collective-permute-start | bytes 4030472 | tf_op jit(solution)/shard_map/ppermute | solution.py:29
  56.3 9.5 %collective-permute-start.1 = (bf16[2048,256]{1,0:T(8,128)(2,1)}, bf16[2048,256]{1,0:T(8,128)(2,1)S(1)}, u32[]{:S(2)}, u32[]{:S(2)}) collective-permute-start(bf16[2048,256]{1,0:T(8,128)(2,1)} %pad_maximum_fusion.refs_4_), channel_id=1, source_target_pairs={{0,8},{8,0},{16,24},{24,16},{1,9},{9,1},{17,25},{25,17},{2,10},{10... | collective-permute-start | bytes 3145736 | tf_op jit(solution)/shard_map/ppermute | solution.py:25
  65.8 2.9 collective-permute-start.6
  90.1 174.2 %all-gather.7.cloned.1.call-start = ((), (), s32[]{:S(2)}) async-start(), calls=%async_computation.9 | async-start | bytes 4718592 | tf_op jit(solution)/shard_map/all_gather | solution.py:809
  92.4 60.7 %copy-start.37 = (f32[512,256]{1,0:T(8,128)}, f32[512,256]{1,0:T(8,128)S(1)}, u32[]{:S(2)}) copy-start(f32[512,256]{1,0:T(8,128)S(1)} %get-tuple-element.284) | copy-start | bytes 1572868
  92.5 5.3 collective-permute-start.7
  95.9 6.3 %collective-permute-start.8 = (bf16[4,27,256]{2,1,0:T(8,128)(2,1)S(1)}, bf16[4,27,256]{2,1,0:T(8,128)(2,1)S(1)}, u32[]{:S(2)}, u32[]{:S(2)}) collective-permute-start(bf16[4,27,256]{2,1,0:T(8,128)(2,1)S(1)} %get-tuple-element.267), channel_id=1, source_target_pairs={{1,0},{2,1},{3,2},{4,3},{5,4},{6,5},{7,6},{9,8},{10,9},{11,10},{12... | collective-permute-start | bytes 165896 | tf_op jit(solution)/shard_map/ppermute | solution.py:755
  102.3 42.4 %collective-permute-start.14 = (bf16[4,640,256]{2,1,0:T(8,128)(2,1)S(1)}, bf16[4,640,256]{2,1,0:T(8,128)(2,1)S(1)}, u32[]{:S(2)}, u32[]{:S(2)}) collective-permute-start(bf16[4,640,256]{2,1,0:T(8,128)(2,1)S(1)} %all-to-all-done.1.refs_0_), channel_id=1, source_target_pairs={{0,1},{1,0},{2,3},{3,2},{4,5},{5,4},{6,7},{7,6},{8,9},{9,8},{10,11... | collective-permute-start | bytes 3932168 | tf_op jit(solution)/shard_map/ppermute | solution.py:29
  107.8 37.3 %copy-start.43 = (f32[512,1024]{1,0:T(8,128)}, f32[512,1024]{1,0:T(8,128)S(1)}, u32[]{:S(2)}) copy-start(f32[512,1024]{1,0:T(8,128)S(1)} %get-tuple-element.286) | copy-start | bytes 6291460
  107.8 1.9 collective-permute-start.10
  107.9 4.5 collective-permute-start.11
  109.6 4.4 collective-permute-start.9
  112.4 7.9 %collective-permute-start.12 = (bf16[128,1024]{1,0:T(8,128)(2,1)S(1)}, bf16[128,1024]{1,0:T(8,128)(2,1)S(1)}, u32[]{:S(2)}, u32[]{:S(2)}) collective-permute-start(bf16[128,1024]{1,0:T(8,128)(2,1)S(1)} %fusion.33), channel_id=1, source_target_pairs={{0,16},{8,24},{16,0},{24,8},{1,17},{9,25},{17,1},{25,9},{2,18},{10... | collective-permute-start | bytes 786440 | tf_op jit(solution)/shard_map/ppermute | solution.py:25
  145.1 6.4 %collective-permute-start.16 = (bf16[128,1024]{1,0:T(8,128)(2,1)S(1)}, bf16[128,1024]{1,0:T(8,128)(2,1)S(1)}, u32[]{:S(2)}, u32[]{:S(2)}) collective-permute-start(bf16[128,1024]{1,0:T(8,128)(2,1)S(1)} %multiply_convert_fusion), channel_id=1, source_target_pairs={{0,16},{8,24},{16,0},{24,8},{1,17},{9,25},{17,1},{25,9},{2,18},{10... | collective-permute-start | bytes 786440 | tf_op jit(solution)/shard_map/ppermute | solution.py:25
  146.7 4.8 collective-permute-start.15
  151.5 1.5 collective-permute-start.17
  159.7 17.6 %collective-permute-start.19 = (bf16[128,4096]{1,0:T(8,128)(2,1)}, bf16[128,4096]{1,0:T(8,128)(2,1)}, u32[]{:S(2)}, u32[]{:S(2)}) collective-permute-start(bf16[128,4096]{1,0:T(8,128)(2,1)} %get-tuple-element.225), channel_id=1, source_target_pairs={{0,8},{8,0},{16,24},{24,16},{1,9},{9,1},{17,25},{25,17},{2,10},{10... | collective-permute-start | bytes 3145736 | tf_op jit(solution)/shard_map/ppermute | solution.py:25
  173.8 37.3 %collective-permute-start.23 = (bf16[8,2,128,1024]{3,2,1,0:T(8,128)(2,1)}, bf16[8,2,128,1024]{3,2,1,0:T(8,128)(2,1)}, u32[]{:S(2)}, u32[]{:S(2)}) collective-permute-start(bf16[8,2,128,1024]{3,2,1,0:T(8,128)(2,1)} %bitcast.199), channel_id=1, source_target_pairs={{0,8},{8,0},{16,24},{24,16},{1,9},{9,1},{17,25},{25,17},{2,10},{10... | collective-permute-start | bytes 12582920 | tf_op jit(solution)/shard_map/ppermute | solution.py:25
  176.7 10.7 %collective-permute-start.18 = (bf16[128,4096]{1,0:T(8,128)(2,1)}, bf16[128,4096]{1,0:T(8,128)(2,1)}, u32[]{:S(2)}, u32[]{:S(2)}) collective-permute-start(bf16[128,4096]{1,0:T(8,128)(2,1)} %get-tuple-element.224), channel_id=1, source_target_pairs={{0,8},{8,0},{16,24},{24,16},{1,9},{9,1},{17,25},{25,17},{2,10},{10... | collective-permute-start | bytes 3145736 | tf_op jit(solution)/shard_map/ppermute | solution.py:25
  177.3 245.6 %reduce-scatter.3.cloned.1.call-start = ((), (), s32[]{:S(2)}) async-start(), calls=%async_computation.6 | async-start | bytes 4718592 | tf_op jit(solution)/shard_map/reduce_scatter | solution.py:862
  180.4 25.4 %collective-permute-start.20 = (bf16[128,4096]{1,0:T(8,128)(2,1)}, bf16[128,4096]{1,0:T(8,128)(2,1)}, u32[]{:S(2)}, u32[]{:S(2)}) collective-permute-start(bf16[128,4096]{1,0:T(8,128)(2,1)} %fusion.7), channel_id=1, source_target_pairs={{0,16},{8,24},{16,0},{24,8},{1,17},{9,25},{17,1},{25,9},{2,18},{10... | collective-permute-start | bytes 3145736 | tf_op jit(solution)/shard_map/ppermute | solution.py:25
  182.8 1.3 collective-permute-start.21
  184.1 1.5 collective-permute-start.22
  236.1 58.3 %copy-start.21 = (bf16[512,256]{1,0:T(8,128)(2,1)}, bf16[512,256]{1,0:T(8,128)(2,1)S(1)}, u32[]{:S(2)}) copy-start(bf16[512,256]{1,0:T(8,128)(2,1)S(1)} %get-tuple-element.175.refs_5_) | copy-start | bytes 786436
  236.1 24.5 %collective-permute-start.25 = (bf16[512,1024]{1,0:T(8,128)(2,1)}, bf16[512,1024]{1,0:T(8,128)(2,1)S(1)}, u32[]{:S(2)}, u32[]{:S(2)}) collective-permute-start(bf16[512,1024]{1,0:T(8,128)(2,1)} %get-tuple-element.115.refs_0_), channel_id=1, source_target_pairs={{0,16},{8,24},{16,0},{24,8},{1,17},{9,25},{17,1},{25,9},{2,18},{10... | collective-permute-start | bytes 3145736 | tf_op jit(solution)/shard_map/ppermute | solution.py:25
  237.6 23.9 %collective-permute-start.24 = (bf16[512,1024]{1,0:T(8,128)(2,1)}, bf16[512,1024]{1,0:T(8,128)(2,1)}, u32[]{:S(2)}, u32[]{:S(2)}) collective-permute-start(bf16[512,1024]{1,0:T(8,128)(2,1)} %get-tuple-element.115.refs_0_), channel_id=1, source_target_pairs={{0,8},{8,0},{16,24},{24,16},{1,9},{9,1},{17,25},{25,17},{2,10},{10... | collective-permute-start | bytes 3145736 | tf_op jit(solution)/shard_map/ppermute | solution.py:25
  261.5 2.8 collective-permute-start.26
  294.4 6.8 %collective-permute-start.28 = (bf16[1024,1024]{1,0:T(8,128)(2,1)}, bf16[1024,1024]{1,0:T(8,128)(2,1)S(1)}, u32[]{:S(2)}, u32[]{:S(2)}) collective-permute-start(bf16[1024,1024]{1,0:T(8,128)(2,1)} %get-tuple-element.121), channel_id=1, source_target_pairs={{0,8},{8,0},{16,24},{24,16},{1,9},{9,1},{17,25},{25,17},{2,10},{10... | collective-permute-start | bytes 6291464 | tf_op jit(solution)/shard_map/ppermute | solution.py:25
  294.6 5.3 collective-permute-start.30
  304.6 25.8 %collective-permute-start.29 = (bf16[512,1024]{1,0:T(8,128)(2,1)}, bf16[512,1024]{1,0:T(8,128)(2,1)}, u32[]{:S(2)}, u32[]{:S(2)}) collective-permute-start(bf16[512,1024]{1,0:T(8,128)(2,1)} %add_convert_fusion.3), channel_id=1, source_target_pairs={{0,16},{8,24},{16,0},{24,8},{1,17},{9,25},{17,1},{25,9},{2,18},{10... | collective-permute-start | bytes 3145736 | tf_op jit(solution)/shard_map/ppermute | solution.py:25
  330.3 33.2 %collective-permute-start.31 = (bf16[4,512,256]{2,1,0:T(8,128)(2,1)}, bf16[4,512,256]{2,1,0:T(8,128)(2,1)}, u32[]{:S(2)}, u32[]{:S(2)}) collective-permute-start(bf16[4,512,256]{2,1,0:T(8,128)(2,1)} %fusion.9), channel_id=1, source_target_pairs={{0,16},{8,24},{16,0},{24,8},{1,17},{9,25},{17,1},{25,9},{2,18},{10... | collective-permute-start | bytes 3145736 | tf_op jit(solution)/shard_map/ppermute | solution.py:25
  331.9 209.3 %reduce-scatter.5.cloned.1.call-start = ((), (), s32[]{:S(2)}) async-start(), calls=%async_computation.7 | async-start | bytes 4718592 | tf_op jit(solution)/shard_map/reduce_scatter | solution.py:884
  363.5 24.3 %collective-permute-start.34 = (bf16[128,4096]{1,0:T(8,128)(2,1)S(1)}, bf16[128,4096]{1,0:T(8,128)(2,1)S(1)}, u32[]{:S(2)}, u32[]{:S(2)}) collective-permute-start(bf16[128,4096]{1,0:T(8,128)(2,1)S(1)} %get-tuple-element.144), channel_id=1, source_target_pairs={{0,16},{8,24},{16,0},{24,8},{1,17},{9,25},{17,1},{25,9},{2,18},{10... | collective-permute-start | bytes 3145736 | tf_op jit(solution)/shard_map/ppermute | solution.py:25
  364.0 23.9 %collective-permute-start.33 = (bf16[128,4096]{1,0:T(8,128)(2,1)S(1)}, bf16[128,4096]{1,0:T(8,128)(2,1)S(1)}, u32[]{:S(2)}, u32[]{:S(2)}) collective-permute-start(bf16[128,4096]{1,0:T(8,128)(2,1)S(1)} %get-tuple-element.144), channel_id=1, source_target_pairs={{0,8},{8,0},{16,24},{24,16},{1,9},{9,1},{17,25},{25,17},{2,10},{10... | collective-permute-start | bytes 3145736 | tf_op jit(solution)/shard_map/ppermute | solution.py:25
  371.5 28.4 %collective-permute-start.51 = (bf16[8,2,128,1024]{3,2,1,0:T(8,128)(2,1)}, bf16[8,2,128,1024]{3,2,1,0:T(8,128)(2,1)S(1)}, u32[]{:S(2)}, u32[]{:S(2)}) collective-permute-start(bf16[8,2,128,1024]{3,2,1,0:T(8,128)(2,1)} %get-tuple-element.179), channel_id=1, source_target_pairs={{0,8},{8,0},{16,24},{24,16},{1,9},{9,1},{17,25},{25,17},{2,10},{10... | collective-permute-start | bytes 12582920 | tf_op jit(solution)/shard_map/ppermute | solution.py:25
  387.8 2.7 collective-permute-start.35
  396.3 1.9 collective-permute-start.37
  396.8 38.8 %collective-permute-start.39 = (bf16[4,640,256]{2,1,0:T(8,128)(2,1)S(1)}, bf16[4,640,256]{2,1,0:T(8,128)(2,1)}, u32[]{:S(2)}, u32[]{:S(2)}) collective-permute-start(bf16[4,640,256]{2,1,0:T(8,128)(2,1)S(1)} %get-tuple-element.148), channel_id=1, source_target_pairs={{0,1},{1,0},{2,3},{3,2},{4,5},{5,4},{6,7},{7,6},{8,9},{9,8},{10,11... | collective-permute-start | bytes 3932168 | tf_op jit(solution)/shard_map/ppermute | solution.py:29
  424.9 2.6 collective-permute-start.36
  424.9 8.9 %collective-permute-start.38 = (bf16[128,1024]{1,0:T(8,128)(2,1)}, bf16[128,1024]{1,0:T(8,128)(2,1)S(1)}, u32[]{:S(2)}, u32[]{:S(2)}) collective-permute-start(bf16[128,1024]{1,0:T(8,128)(2,1)} %fusion.31), channel_id=1, source_target_pairs={{0,16},{8,24},{16,0},{24,8},{1,17},{9,25},{17,1},{25,9},{2,18},{10... | collective-permute-start | bytes 786440 | tf_op jit(solution)/shard_map/ppermute | solution.py:25
  426.6 10.7 %collective-permute-start.32 = (bf16[128,256]{1,0:T(8,128)(2,1)S(1)}, bf16[128,256]{1,0:T(8,128)(2,1)S(1)}, u32[]{:S(2)}, u32[]{:S(2)}) collective-permute-start(bf16[128,256]{1,0:T(8,128)(2,1)S(1)} %bitcast.191), channel_id=1, source_target_pairs={{0,8},{8,0},{16,24},{24,16},{1,9},{9,1},{17,25},{25,17},{2,10},{10... | collective-permute-start | bytes 196616 | tf_op jit(solution)/shard_map/ppermute | solution.py:25
  427.0 19.1 %collective-permute-start.49 = (bf16[128,256]{1,0:T(8,128)(2,1)S(1)}, bf16[128,256]{1,0:T(8,128)(2,1)S(1)}, u32[]{:S(2)}, u32[]{:S(2)}) collective-permute-start(bf16[128,256]{1,0:T(8,128)(2,1)S(1)} %bitcast.190), channel_id=1, source_target_pairs={{0,8},{8,0},{16,24},{24,16},{1,9},{9,1},{17,25},{25,17},{2,10},{10... | collective-permute-start | bytes 196616 | tf_op jit(solution)/shard_map/ppermute | solution.py:25
  435.6 10.4 %collective-permute-start.45 = (bf16[128,1024]{1,0:T(8,128)(2,1)S(1)}, bf16[128,1024]{1,0:T(8,128)(2,1)S(1)}, u32[]{:S(2)}, u32[]{:S(2)}) collective-permute-start(bf16[128,1024]{1,0:T(8,128)(2,1)S(1)} %fusion.22), channel_id=1, source_target_pairs={{0,8},{8,0},{16,24},{24,16},{1,9},{9,1},{17,25},{25,17},{2,10},{10... | collective-permute-start | bytes 786440 | tf_op jit(solution)/shard_map/ppermute | solution.py:25
  435.7 8.7 %collective-permute-start.40 = (bf16[128,1024]{1,0:T(8,128)(2,1)S(1)}, bf16[128,1024]{1,0:T(8,128)(2,1)S(1)}, u32[]{:S(2)}, u32[]{:S(2)}) collective-permute-start(bf16[128,1024]{1,0:T(8,128)(2,1)S(1)} %fusion.22), channel_id=1, source_target_pairs={{0,16},{8,24},{16,0},{24,8},{1,17},{9,25},{17,1},{25,9},{2,18},{10... | collective-permute-start | bytes 786440 | tf_op jit(solution)/shard_map/ppermute | solution.py:25
  444.4 4.3 collective-permute-start.41
  446.0 2.7 collective-permute-start.46
  449.9 7.5 %collective-permute-start.47 = (bf16[4,27,256]{2,1,0:T(8,128)(2,1)S(1)}, bf16[4,27,256]{2,1,0:T(8,128)(2,1)S(1)}, u32[]{:S(2)}, u32[]{:S(2)}) collective-permute-start(bf16[4,27,256]{2,1,0:T(8,128)(2,1)S(1)} %get-tuple-element.257), channel_id=1, source_target_pairs={{1,0},{2,1},{3,2},{4,3},{5,4},{6,5},{7,6},{9,8},{10,9},{11,10},{12... | collective-permute-start | bytes 165896 | tf_op jit(solution)/shard_map/ppermute | solution.py:755
  451.3 6.4 %collective-permute-start.48 = (bf16[4,27,256]{2,1,0:T(8,128)(2,1)S(1)}, bf16[4,27,256]{2,1,0:T(8,128)(2,1)S(1)}, u32[]{:S(2)}, u32[]{:S(2)}) collective-permute-start(bf16[4,27,256]{2,1,0:T(8,128)(2,1)S(1)} %get-tuple-element.256), channel_id=1, source_target_pairs={{0,1},{1,2},{2,3},{3,4},{4,5},{5,6},{6,7},{8,9},{9,10},{10,11},{11... | collective-permute-start | bytes 165896 | tf_op jit(solution)/shard_map/ppermute | solution.py:754
  464.3 50.8 %all-to-all-start.3 = ((bf16[4,640,256]{2,1,0:T(8,128)(2,1)}), bf16[4,640,256]{2,1,0:T(8,128)(2,1)S(1)}, u32[]{:S(2)}, u32[]{:S(2)}) async-start(bf16[4,640,256]{2,1,0:T(8,128)(2,1)} %add_convert_fusion.2), calls=%async_computation.4 | async-start | bytes 2621440 | tf_op jit(solution)/shard_map/all_to_all | solution.py:92
  473.3 40.3 %collective-permute-start.50 = (bf16[4,656,256]{2,1,0:T(8,128)(2,1)}, bf16[4,656,256]{2,1,0:T(8,128)(2,1)S(1)}, u32[]{:S(2)}, u32[]{:S(2)}) collective-permute-start(bf16[4,656,256]{2,1,0:T(8,128)(2,1)} %copy-done.5), channel_id=1, source_target_pairs={{0,1},{1,0},{2,3},{3,2},{4,5},{5,4},{6,7},{7,6},{8,9},{9,8},{10,11... | collective-permute-start | bytes 4030472 | tf_op jit(solution)/shard_map/ppermute | solution.py:29
  473.3 46.5 %collective-permute-start.27 = (bf16[4,512,256]{2,1,0:T(8,128)(2,1)}, bf16[4,512,256]{2,1,0:T(8,128)(2,1)}, u32[]{:S(2)}, u32[]{:S(2)}) collective-permute-start(bf16[4,512,256]{2,1,0:T(8,128)(2,1)} %bitcast.170), channel_id=1, source_target_pairs={{0,8},{8,0},{16,24},{24,16},{1,9},{9,1},{17,25},{25,17},{2,10},{10... | collective-permute-start | bytes 3145736 | tf_op jit(solution)/shard_map/ppermute | solution.py:25
  515.0 36.7 %all-to-all-start.2 = ((bf16[4,656,256]{2,1,0:T(8,128)(2,1)}), bf16[4,656,256]{2,1,0:T(8,128)(2,1)S(1)}, u32[]{:S(2)}, u32[]{:S(2)}) async-start(bf16[4,656,256]{2,1,0:T(8,128)(2,1)} %add_convert_fusion.1), calls=%async_computation.3 | async-start | bytes 2686976 | tf_op jit(solution)/shard_map/all_to_all | solution.py:92
  521.2 8.0 %collective-permute-start.44 = (bf16[512,256]{1,0:T(8,128)(2,1)}, bf16[512,256]{1,0:T(8,128)(2,1)}, u32[]{:S(2)}, u32[]{:S(2)}) collective-permute-start(bf16[512,256]{1,0:T(8,128)(2,1)} %get-tuple-element.155), channel_id=1, source_target_pairs={{0,8},{8,0},{16,24},{24,16},{1,9},{9,1},{17,25},{25,17},{2,10},{10... | collective-permute-start | bytes 786440 | tf_op jit(solution)/shard_map/ppermute | solution.py:25
  523.1 9.3 %collective-permute-start.43 = (bf16[512,256]{1,0:T(8,128)(2,1)S(1)}, bf16[512,256]{1,0:T(8,128)(2,1)}, u32[]{:S(2)}, u32[]{:S(2)}) collective-permute-start(bf16[512,256]{1,0:T(8,128)(2,1)S(1)} %get-tuple-element.154), channel_id=1, source_target_pairs={{0,16},{8,24},{16,0},{24,8},{1,17},{9,25},{17,1},{25,9},{2,18},{10... | collective-permute-start | bytes 786440 | tf_op jit(solution)/shard_map/ppermute | solution.py:25
  524.7 12.5 %collective-permute-start.42 = (bf16[512,256]{1,0:T(8,128)(2,1)S(1)}, bf16[512,256]{1,0:T(8,128)(2,1)}, u32[]{:S(2)}, u32[]{:S(2)}) collective-permute-start(bf16[512,256]{1,0:T(8,128)(2,1)S(1)} %get-tuple-element.152), channel_id=1, source_target_pairs={{0,24},{8,16},{16,8},{24,0},{1,25},{9,17},{17,9},{25,1},{2,26},{10... | collective-permute-start | bytes 786440 | tf_op jit(solution)/shard_map/ppermute | solution.py:25
  542.2 11.7 %collective-permute-start.52 = (bf16[128,1024]{1,0:T(8,128)(2,1)S(1)}, bf16[128,1024]{1,0:T(8,128)(2,1)S(1)}, u32[]{:S(2)}, u32[]{:S(2)}) collective-permute-start(bf16[128,1024]{1,0:T(8,128)(2,1)S(1)} %slice_bitcast_fusion.2), channel_id=1, source_target_pairs={{0,16},{8,24},{16,0},{24,8},{1,17},{9,25},{17,1},{25,9},{2,18},{10... | collective-permute-start | bytes 786440 | tf_op jit(solution)/shard_map/ppermute | solution.py:25
  (68 other events, 474.5 us)
Sparse Core Ops, SparseCore 0:
  90.3 83.5 all-gather.4
  177.4 72.2 all-gather.6
  332.0 90.8 reduce-scatter.2
  426.8 99.7 reduce-scatter.4

commit v6 on v5

--- a/solution.py
+++ b/solution.py
@@ -392,6 +392,7 @@
     )
 
 
+ANYWHERE = jax.ShapeDtypeStruct
 LAYER_TILE = 256
 SUBS = LAYER_TILE // TILE
 
@@ -470,7 +471,7 @@
     tiles = tokens // TILE
     return pl.pallas_call(
         body,
-        out_shape=[jax.ShapeDtypeStruct(shape, dtype) for shape, dtype in outs],
+        out_shape=[space(shape, dtype) for space, shape, dtype in outs],
         grid=(tokens // LAYER_TILE,),
         in_specs=[wide(1), pl.BlockSpec((SUBS, 1, TILE), lambda i: (i, 0, 0))]
         + [wide(a.shape[1]) for a in arrays]
@@ -479,7 +480,7 @@
         + [pl.BlockSpec((8, 1, n, w), lambda i, k=k: (0, k, 0, 0)) for k in (0, 0, 1, 1)]
         + [wide(a.shape[1]) for a in more[1]],
         out_specs=[
-            wide(shape[1]) if shape[0] == tokens else still(shape) for shape, _ in outs
+            wide(shape[1]) if shape[0] == tokens else still(shape) for _, shape, _ in outs
         ],
         compiler_params=pltpu.CompilerParams(vmem_limit_bytes=VMEM_ROOM),
         name=name,
@@ -502,9 +503,13 @@
     tokens, width = stream.shape
     quarter = width // 4
     outs = (
-        [((tokens, width), BF16), ((tokens, width), F32), ((tokens, width), BF16)]
-        + [((tokens, 3 * quarter), BF16)] * 4
-        + [((tokens, quarter), BF16)] * 4
+        [
+            (pltpu.HBM, (tokens, width), BF16),
+            (ANYWHERE, (tokens, width), F32),
+            (ANYWHERE, (tokens, width), BF16),
+        ]
+        + [(pltpu.HBM, (tokens, 3 * quarter), BF16)] * 4
+        + [(pltpu.HBM, (tokens, quarter), BF16)] * 4
     )
     norm_one, stream_one, norm_two, *rest = layer_call(
         forward_body, segments, [stream], vectors, weights, ([], []), outs, "layer_forward", 18
@@ -514,8 +519,12 @@
 
 def layer_backward(segments, streams, vectors, grads, cot, weights, qkv):
     tokens, width = cot.shape
-    outs = [((tokens, width), BF16), ((tokens, width), F32), (vectors.shape, F32)]
-    outs += [(q.shape, BF16) for q in qkv]
+    outs = [
+        (ANYWHERE, (tokens, width), BF16),
+        (ANYWHERE, (tokens, width), F32),
+        (ANYWHERE, vectors.shape, F32),
+    ]
+    outs += [(ANYWHERE, q.shape, BF16) for q in qkv]
     return layer_call(
         backward_body, segments, streams, vectors, weights, ([*grads, cot], qkv), outs,
         "layer_backward",
@@ -722,7 +731,7 @@
     part = pl.BlockSpec((rows, 2 * n), lambda i: (0, i))
     return pl.pallas_call(
         mlp_grads_body,
-        out_shape=jax.ShapeDtypeStruct((8, 2, n, hidden), BF16),
+        out_shape=pltpu.HBM((8, 2, n, hidden), BF16),
         grid=(4,),
         in_specs=[part, part, whole, whole],
         out_specs=pl.BlockSpec((2, 2, n, hidden), lambda i: (i, 0, 0, 0)),
@@ -869,9 +878,14 @@
     leave_rows, *grad_in_q = leave(input_grad, to_up, quarters)
     grad_rows[0] = after(grad_rows[0], leave_rows, act_done)
     grad_attn, send = layer_grads(norm_one, att, grad_rows, context)
-    grad_up_rows = line.spread(leave_rows)
+    leave_rows, from_y, send = lax.optimization_barrier(
+        (leave_rows, *line.send((leave_rows, 2)), send)
+    )
+    grad_up_rows = [leave_rows, swap(leave_rows, 1), from_y, swap(from_y, 1)]
     grad_attn = grad_attn.astype(F32) + swap(send, 1).astype(F32)
     grad_attn = split_rows(grad_attn.astype(BF16))
+    grad_attn = after(grad_attn, grad_up_rows[2])
+    grad_attn = lax.psum_scatter(grad_attn, "seq", scatter_dimension=0, tiled=False)
     grad_up_rows = jnp.concatenate(grad_up_rows, axis=0)
     grad_hidden = dot(grad_up_rows, up)
     grad_low = grad_hidden.astype(BF16)
@@ -880,8 +894,6 @@
     up_started = cross_x([grad_res, grad_up])
     grad_mixed = dot_t(after(grad_low, grad_up, grad_res), res).reshape(micros, coarse, width)
     grad_mixed, over_y = fold_core([grad_mixed[j] for j in range(4)])
-    grad_attn = after(grad_attn, grad_mlp, over_y)
-    grad_attn = lax.psum_scatter(grad_attn, "seq", scatter_dimension=0, tiled=False)
     grad_mixed = grad_mixed + line.send((over_y, 2))[0].astype(F32)
     grad_conv_low = after((gelu_grad(conv_out) * grad_mixed).astype(BF16), grad_mlp, up_started[1])
 

time: 571 us -> 564 us (0.988)
  waiting for transfers between devices: 279 us -> 272 us
    reduce_scatter x1, waiting for transfers between devices: 18.7 us -> 0.01 us  [on_device(): lax.psum_scatter(split_rows(terms[3]), 'seq', scatter_dimension=0, tiled=...]
    ppermute x4, waiting for transfers between devices: 81.1 us -> 93.7 us  [hop(): return lax.ppermute(x, 'seq', [(i, i ^ k) for i in range(8)])]
    unnamed x165 -> x159, local copies, waits for them, and re-layouts: 29.9 us -> 26.7 us
  transfers between devices with their start and end apart: 61 -> 61, of which waited for: 35 -> 34; matrix products, arithmetic and copies ran while one was open for 12% -> 13% of each run, Pallas kernels for 13% -> 13%
where the time goes in v6:
time: 564 us; the launch traced here: 555 us
  waiting for transfers between devices  272 us (48%)
  Pallas kernels  104 us (18%)
  starting transfers between devices  66.2 us (12%)
  local copies, waits for them, and re-layouts  43.1 us (8%)
  other arithmetic  35.7 us (6%)
  matrix products  18.3 us (3%)
  between operations  15.3 us (3%)
    ppermute x45, waiting for transfers between devices, swap(): return lax.ppermute(x, 'cond', [(i, i ^ j) for i in range(4)])  147 us
    ppermute x4, waiting for transfers between devices, hop(): return lax.ppermute(x, 'seq', [(i, i ^ k) for i in range(8)])  93.7 us
    pallas_call x2, Pallas kernels, layer_call(): pl.pallas_call(body, out_shape=[space(shape, dtype) for space, shape, dty...  43.4 us
    pallas_call x1, Pallas kernels, mlp(): pl.pallas_call(mlp_body, out_shape=[shape((rows, hidden), BF16), shape((r...  30.2 us
    unnamed x159, local copies, waits for them, and re-layouts  26.7 us
    ppermute x45, starting transfers between devices, swap(): return lax.ppermute(x, 'cond', [(i, i ^ j) for i in range(4)])  25 us
    all_to_all x4, starting transfers between devices, along_z(): return lax.all_to_all(x, 'seq', 0, 0, axis_index_groups=ALONG_Z, tiled=True)  23.9 us
    dot_general x11, matrix products, dot(): return lax.dot_general(a, b, (dims, ((), ())), preferred_element_type=F32)  17.2 us
  transfers between devices with their start and end apart: 61, of which 34 were waited for; matrix products, arithmetic and copies ran while one was open for 13% of the time, Pallas kernels for 13%

profile of v6, /device:TPU:0, one launch (start us, length us, event | category | flops | bytes accessed | tf_op | source)
XLA Modules:
  0.0 555.3 jit_solution(17412366041905911186)
XLA Ops:
  11.3 6.4 %all-to-all-start = ((bf16[4,656,256]{2,1,0:T(8,128)(2,1)}), bf16[4,656,256]{2,1,0:T(8,128)(2,1)S(1)}, u32[]{:S(2)}, u32[]{:S(2)}) async-start(bf16[4,656,256]{2,1,0:T(8,128)(2,1)} %broadcast_in_dim.4), calls=%async_computation | async-start | bytes 2686976 | tf_op jit(solution)/shard_map/all_to_all | solution.py:92
  18.6 1.5 collective-permute-start.2
  20.4 7.7 %collective-permute-done.2.q2 = bf16[512,256]{1,0:T(8,128)(2,1)S(1)} collective-permute-done((bf16[512,256]{1,0:T(8,128)(2,1)}, bf16[512,256]{1,0:T(8,128)(2,1)S(1)}, u32[]{:S(2)}, u32[]{:S(2)}) %collective-permute-start.2) | collective-permute-done | bytes 262176 | tf_op jit(solution)/shard_map/ppermute | solution.py:25
  28.1 3.2 collective-permute-done.3.q3
  34.6 5.7 %collective-permute-done.4 = bf16[128,1024]{0,1:T(8,128)(2,1)S(1)} collective-permute-done((bf16[128,1024]{0,1:T(8,128)(2,1)S(1)}, bf16[128,1024]{0,1:T(8,128)(2,1)S(1)}, u32[]{:S(2)}, u32[]{:S(2)}) %collective-permute-start.4) | collective-permute-done | bytes 262176 | tf_op jit(solution)/shard_map/ppermute | solution.py:25
  42.3 1.8 pad_maximum_fusion.4
  44.1 5.7 %all-to-all-done.refs_0_ = bf16[4,656,256]{2,1,0:T(8,128)(2,1)S(1)} async-done(((bf16[4,656,256]{2,1,0:T(8,128)(2,1)}), bf16[4,656,256]{2,1,0:T(8,128)(2,1)S(1)}, u32[]{:S(2)}, u32[]{:S(2)}) %all-to-all-start) | async-done | bytes 1343520 | tf_op jit(solution)/shard_map/all_to_all | solution.py:92
  51.1 3.5 all-to-all-start.1
  54.7 1.6 collective-permute-start
  56.3 9.5 %collective-permute-done.5.refs_6_ = bf16[2048,256]{1,0:T(8,128)(2,1)} collective-permute-done((bf16[2048,256]{1,0:T(8,128)(2,1)}, bf16[2048,256]{1,0:T(8,128)(2,1)}, u32[]{:S(2)}, u32[]{:S(2)}) %collective-permute-start.5) | collective-permute-done | bytes 1048608 | tf_op jit(solution)/shard_map/ppermute | solution.py:25
  65.8 2.9 collective-permute-done.6.refs_7_
  68.7 16.5 %collective-permute-done.refs_1_ = bf16[4,656,256]{2,1,0:T(8,128)(2,1)S(1)} collective-permute-done((bf16[4,656,256]{2,1,0:T(8,128)(2,1)S(1)}, bf16[4,656,256]{2,1,0:T(8,128)(2,1)S(1)}, u32[]{:S(2)}, u32[]{:S(2)}) %collective-permute-start) | collective-permute-done | bytes 1343520 | tf_op jit(solution)/shard_map/ppermute | solution.py:29
  87.7 2.4 copy.90
  90.3 2.1 multiply_convert_fusion.1
  92.5 3.4 collective-permute-start.7
  97.8 4.4 collective-permute-done.8
  102.3 4.4 collective-permute-start.14
  107.9 1.7 collective-permute-start.11
  109.8 2.6 collective-permute-done.11
  112.4 1.6 collective-permute-start.12
  114.0 6.3 %collective-permute-done.12 = bf16[128,1024]{1,0:T(8,128)(2,1)S(1)} collective-permute-done((bf16[128,1024]{1,0:T(8,128)(2,1)S(1)}, bf16[128,1024]{1,0:T(8,128)(2,1)S(1)}, u32[]{:S(2)}, u32[]{:S(2)}) %collective-permute-start.12) | collective-permute-done | bytes 262176 | tf_op jit(solution)/shard_map/ppermute | solution.py:25
  120.4 24.3 %collective-permute-done.14.refs_1_ = bf16[4,640,256]{2,1,0:T(8,128)(2,1)S(1)} collective-permute-done((bf16[4,640,256]{2,1,0:T(8,128)(2,1)S(1)}, bf16[4,640,256]{2,1,0:T(8,128)(2,1)S(1)}, u32[]{:S(2)}, u32[]{:S(2)}) %collective-permute-start.14) | collective-permute-done | bytes 1310752 | tf_op jit(solution)/shard_map/ppermute | solution.py:29
  145.1 1.6 collective-permute-start.16
  146.7 4.8 collective-permute-done.16
  153.5 4.7 fusion.101
  159.8 14.0 %all-gather.5.cloned.1.call-done = bf16[16,128,1024]{2,1,0:T(8,128)(2,1)} async-done(((bf16[2,128,1024]{2,1,0:T(8,128)(2,1)}), bf16[16,128,1024]{2,1,0:T(8,128)(2,1)}) %all-gather.5.cloned.1.call-update) | async-done | bytes 4194320 | tf_op jit(solution)/shard_map/all_gather | solution.py:817
  174.9 1.8 pad_maximum_fusion.5
  177.3 3.0 fusion.7
  187.5 18.3 %collective-permute-done.20 = bf16[128,4096]{1,0:T(8,128)(2,1)} collective-permute-done((bf16[128,4096]{1,0:T(8,128)(2,1)}, bf16[128,4096]{1,0:T(8,128)(2,1)}, u32[]{:S(2)}, u32[]{:S(2)}) %collective-permute-start.20) | collective-permute-done | bytes 1048608 | tf_op jit(solution)/shard_map/ppermute | solution.py:25
  205.7 2.5 fusion.8.up_ref
  208.3 1.5 enter.1.refs_2_
  209.8 18.8 %layer_forward.1 = (bf16[512,1024]{1,0:T(8,128)(2,1)}, f32[512,1024]{1,0:T(8,128)S(1)}, bf16[512,1024]{1,0:T(8,128)(2,1)S(1)}, bf16[512,768]{1,0:T(8,128)(2,1)},...) custom-call(s32[512,1]{1,0:T(8,128)S(1)} %copy.91.refs_0_, ...), custom_call_target="tpu_custom_call" | custom-call | flops 19800000512 | tf_op jit(solution)/shard_map/layer_forward/pallas_call | solution.py:472
  230.0 1.6 collective-permute-start.25
  231.6 22.8 %collective-permute-done.25.refs_2_ = bf16[512,1024]{1,0:T(8,128)(2,1)S(1)} collective-permute-done((bf16[512,1024]{1,0:T(8,128)(2,1)S(1)}, bf16[512,1024]{1,0:T(8,128)(2,1)S(1)}, u32[]{:S(2)}, u32[]{:S(2)}) %collective-permute-start.25) | collective-permute-done | bytes 1048608 | tf_op jit(solution)/shard_map/ppermute | solution.py:25
  257.3 30.2 %mlp.1 = (bf16[2048,1024]{1,0:T(8,128)(2,1)}, bf16[2048,1024]{1,0:T(8,128)(2,1)}, bf16[2048,1024]{1,0:T(8,128)(2,1)}, bf16[2048,1024]{1,0:T(8,128)(2,1)}, bf16[2...) custom-call(s32[4]{0:T(128)S(1)} %iota_xor_fusion.index, ...), custom_call_target="tpu_custom_call" | custom-call | flops 32999999488 | tf_op jit(solution)/shard_map/mlp/pallas_call | solution.py:684
  288.0 4.9 collective-permute-done.30
  294.3 1.8 copy-done.42
  297.5 1.7 collective-permute-start.29
  299.1 14.7 %mlp_grads.1 = bf16[8,2,128,1024]{3,2,1,0:T(8,128)(2,1)} custom-call(bf16[2048,1024]{1,0:T(8,128)(2,1)S(1)} %copy-done.19, bf16[2048,1024]{1,0:T(8,128)(2,1)} %get-tuple-element.128.cot_ref, bf16[2048,1024]{1,0:T(8,128)(2,1)} %get-tuple-element.129.act_ref, bf16[2048,1024]{1,0:T(8,128)(2,1)} %get-tuple-element.130.grad_ref), custom_call_target="tpu_custom_call" | custom-call | flops 15399999488 | tf_op jit(solution)/shard_map/mlp_grads/pallas_call | solution.py:732
  313.8 9.4 %collective-permute-done.29.refs_7_ = bf16[512,1024]{1,0:T(8,128)(2,1)} collective-permute-done((bf16[512,1024]{1,0:T(8,128)(2,1)}, bf16[512,1024]{1,0:T(8,128)(2,1)}, u32[]{:S(2)}, u32[]{:S(2)}) %collective-permute-start.29) | collective-permute-done | bytes 1048608 | tf_op jit(solution)/shard_map/ppermute | solution.py:25
  323.2 1.6 collective-permute-start.31
  328.3 24.6 %layer_backward.1 = (bf16[512,1024]{1,0:T(8,128)(2,1)}, f32[512,1024]{1,0:T(8,128)}, f32[8,1024]{1,0:T(8,128)S(1)}, bf16[512,768]{1,0:T(8,128)(2,1)S(1)}, bf16[5...) custom-call(s32[512,1]{1,0:T(8,128)S(1)} %copy.91.refs_0_, ...), custom_call_target="tpu_custom_call" | custom-call | flops 26400000000 | tf_op jit(solution)/shard_map/layer_backward/pallas_call | solution.py:472
  352.9 1.6 copy-done.18
  354.5 2.2 leave.1
  358.0 7.5 %layer_grads.1 = (bf16[8,2,128,1024]{3,2,1,0:T(8,128)(2,1)}, bf16[8,2,128,1024]{3,2,1,0:T(8,128)(2,1)}) custom-call(bf16[512,1024]{1,0:T(8,128)(2,1)S(1)} %copy-done.20, bf16[512,1024]{1,0:T(8,128)(2,1)} %get-tuple-element.149.att_ref, bf16[512,768]{1,0:T(8,128)(2,1)S(1)} %get-tuple-element.151.refs_0_, bf16[512,768]{1,0:T(8,128)(2,1)S(1)} %get-tuple-element.152.refs_1_, ...), custom_call_target="tpu_custom_call" | custom-call | flops 8800000000 | tf_op jit(solution)/shard_map/layer_grads/pallas_call | solution.py:555
  365.5 16.6 %collective-permute-done.33 = bf16[128,4096]{1,0:T(8,128)(2,1)} collective-permute-done((bf16[128,4096]{1,0:T(8,128)(2,1)}, bf16[128,4096]{1,0:T(8,128)(2,1)}, u32[]{:S(2)}, u32[]{:S(2)}) %collective-permute-start.33) | collective-permute-done | bytes 1048608 | tf_op jit(solution)/shard_map/ppermute | solution.py:25
  388.1 2.0 fusion.102
  392.4 1.9 pack.2
  394.9 1.8 fusion.103
  397.2 6.4 %add_convert_fusion = bf16[8,2,128,1024]{3,2,1,0:T(8,128)(2,1)} fusion(bf16[8,2,128,1024]{3,2,1,0:T(8,128)(2,1)} %collective-permute-done.51, bf16[8,2,128,1024]{3,2,1,0:T(8,128)(2,1)S(1)} %copy-done.30), kind=kLoop, calls=%fused_computation | loop fusion | flops 8388608 | bytes 12582912 | tf_op jit(solution)/shard_map/convert_element_type | solution.py:886
  407.5 7.2 %collective-permute-done.38 = bf16[128,1024]{1,0:T(8,128)(2,1)S(1)} collective-permute-done((bf16[128,1024]{1,0:T(8,128)(2,1)S(1)}, bf16[128,1024]{1,0:T(8,128)(2,1)S(1)}, u32[]{:S(2)}, u32[]{:S(2)}) %collective-permute-start.38) | collective-permute-done | bytes 262176 | tf_op jit(solution)/shard_map/ppermute | solution.py:25
  414.7 1.6 fusion.22
  416.3 11.8 %collective-permute-done.39 = bf16[4,640,256]{2,1,0:T(8,128)(2,1)} collective-permute-done((bf16[4,640,256]{2,1,0:T(8,128)(2,1)}, bf16[4,640,256]{2,1,0:T(8,128)(2,1)}, u32[]{:S(2)}, u32[]{:S(2)}) %collective-permute-start.39) | collective-permute-done | bytes 1310752 | tf_op jit(solution)/shard_map/ppermute | solution.py:29
  429.6 7.2 %collective-permute-done.40 = bf16[128,1024]{1,0:T(8,128)(2,1)S(1)} collective-permute-done((bf16[128,1024]{1,0:T(8,128)(2,1)S(1)}, bf16[128,1024]{1,0:T(8,128)(2,1)S(1)}, u32[]{:S(2)}, u32[]{:S(2)}) %collective-permute-start.40) | collective-permute-done | bytes 262176 | tf_op jit(solution)/shard_map/ppermute | solution.py:25
  438.3 2.7 collective-permute-done.41
  443.7 4.5 collective-permute-start.48
  454.0 2.7 add_convert_fusion.2
  456.7 9.1 %all-to-all-start.3 = ((bf16[4,640,256]{2,1,0:T(8,128)(2,1)}), bf16[4,640,256]{2,1,0:T(8,128)(2,1)S(1)}, u32[]{:S(2)}, u32[]{:S(2)}) async-start(bf16[4,640,256]{2,1,0:T(8,128)(2,1)} %add_convert_fusion.2), calls=%async_computation.3 | async-start | bytes 2621440 | tf_op jit(solution)/shard_map/all_to_all | solution.py:92
  465.9 41.1 %collective-permute-done.50 = bf16[4,656,256]{2,1,0:T(8,128)(2,1)S(1)} collective-permute-done((bf16[4,656,256]{2,1,0:T(8,128)(2,1)}, bf16[4,656,256]{2,1,0:T(8,128)(2,1)S(1)}, u32[]{:S(2)}, u32[]{:S(2)}) %collective-permute-start.50) | collective-permute-done | bytes 1343520 | tf_op jit(solution)/shard_map/ppermute | solution.py:29
  508.4 4.8 all-to-all-start.2
  519.5 6.1 %collective-permute-done.43 = bf16[512,256]{1,0:T(8,128)(2,1)S(1)} collective-permute-done((bf16[512,256]{1,0:T(8,128)(2,1)S(1)}, bf16[512,256]{1,0:T(8,128)(2,1)S(1)}, u32[]{:S(2)}, u32[]{:S(2)}) %collective-permute-start.43) | collective-permute-done | bytes 262176 | tf_op jit(solution)/shard_map/ppermute | solution.py:25
  525.6 4.8 collective-permute-done.42
  533.3 1.9 convert_bitcast_fusion
  538.6 5.7 %all-to-all-done.2.refs_0_ = bf16[4,656,256]{2,1,0:T(8,128)(2,1)S(1)} async-done(((bf16[4,656,256]{2,1,0:T(8,128)(2,1)}), bf16[4,656,256]{2,1,0:T(8,128)(2,1)S(1)}, u32[]{:S(2)}, u32[]{:S(2)}) %all-to-all-start.2) | async-done | bytes 1343520 | tf_op jit(solution)/shard_map/all_to_all | solution.py:92
  (334 shorter events, 85.0 us)
Async XLA Ops:
  11.3 38.5 %all-to-all-start = ((bf16[4,656,256]{2,1,0:T(8,128)(2,1)}), bf16[4,656,256]{2,1,0:T(8,128)(2,1)S(1)}, u32[]{:S(2)}, u32[]{:S(2)}) async-start(bf16[4,656,256]{2,1,0:T(8,128)(2,1)} %broadcast_in_dim.4), calls=%async_computation | async-start | bytes 2686976 | tf_op jit(solution)/shard_map/all_to_all | solution.py:92
  18.6 9.4 %collective-permute-start.2 = (bf16[512,256]{1,0:T(8,128)(2,1)}, bf16[512,256]{1,0:T(8,128)(2,1)S(1)}, u32[]{:S(2)}, u32[]{:S(2)}) collective-permute-start(bf16[512,256]{1,0:T(8,128)(2,1)} %get-tuple-element.253), channel_id=1, source_target_pairs={{0,16},{8,24},{16,0},{24,8},{1,17},{9,25},{17,1},{25,9},{2,18},{10... | collective-permute-start | bytes 786440 | tf_op jit(solution)/shard_map/ppermute | solution.py:25
  20.1 11.1 %collective-permute-start.3 = (bf16[512,256]{1,0:T(8,128)(2,1)S(1)}, bf16[512,256]{1,0:T(8,128)(2,1)S(1)}, u32[]{:S(2)}, u32[]{:S(2)}) collective-permute-start(bf16[512,256]{1,0:T(8,128)(2,1)S(1)} %get-tuple-element.254), channel_id=1, source_target_pairs={{0,24},{8,16},{16,8},{24,0},{1,25},{9,17},{17,9},{25,1},{2,26},{10... | collective-permute-start | bytes 786440 | tf_op jit(solution)/shard_map/ppermute | solution.py:25
  31.3 9.1 %collective-permute-start.4 = (bf16[128,1024]{0,1:T(8,128)(2,1)S(1)}, bf16[128,1024]{0,1:T(8,128)(2,1)S(1)}, u32[]{:S(2)}, u32[]{:S(2)}) collective-permute-start(bf16[128,1024]{0,1:T(8,128)(2,1)S(1)} %get-tuple-element.101), channel_id=1, source_target_pairs={{0,16},{8,24},{16,0},{24,8},{1,17},{9,25},{17,1},{25,9},{2,18},{10... | collective-permute-start | bytes 786440 | tf_op jit(solution)/shard_map/ppermute | solution.py:25
  40.3 25.5 %collective-permute-start.5 = (bf16[2048,256]{1,0:T(8,128)(2,1)}, bf16[2048,256]{1,0:T(8,128)(2,1)}, u32[]{:S(2)}, u32[]{:S(2)}) collective-permute-start(bf16[2048,256]{1,0:T(8,128)(2,1)} %pad_maximum_fusion.refs_4_), channel_id=1, source_target_pairs={{0,16},{8,24},{16,0},{24,8},{1,17},{9,25},{17,1},{25,9},{2,18},{10... | collective-permute-start | bytes 3145736 | tf_op jit(solution)/shard_map/ppermute | solution.py:25
  41.0 3.0 collective-permute-start.13
  51.1 36.6 %all-to-all-start.1 = ((bf16[4,640,256]{2,1,0:T(8,128)(2,1)}), bf16[4,640,256]{2,1,0:T(8,128)(2,1)S(1)}, u32[]{:S(2)}, u32[]{:S(2)}) async-start(bf16[4,640,256]{2,1,0:T(8,128)(2,1)} %broadcast_in_dim.5), calls=%async_computation.1 | async-start | bytes 2621440 | tf_op jit(solution)/shard_map/all_to_all | solution.py:92
  54.7 119.1 %all-gather.5.cloned.1.call-start = ((), (), s32[]{:S(2)}) async-start(), calls=%async_computation.8 | async-start | bytes 4718592 | tf_op jit(solution)/shard_map/all_gather | solution.py:817
  54.7 30.5 %collective-permute-start = (bf16[4,656,256]{2,1,0:T(8,128)(2,1)S(1)}, bf16[4,656,256]{2,1,0:T(8,128)(2,1)S(1)}, u32[]{:S(2)}, u32[]{:S(2)}) collective-permute-start(bf16[4,656,256]{2,1,0:T(8,128)(2,1)S(1)} %all-to-all-done.refs_0_), channel_id=1, source_target_pairs={{0,1},{1,0},{2,3},{3,2},{4,5},{5,4},{6,7},{7,6},{8,9},{9,8},{10,11... | collective-permute-start | bytes 4030472 | tf_op jit(solution)/shard_map/ppermute | solution.py:29
  56.3 9.6 %collective-permute-start.1 = (bf16[2048,256]{1,0:T(8,128)(2,1)}, bf16[2048,256]{1,0:T(8,128)(2,1)S(1)}, u32[]{:S(2)}, u32[]{:S(2)}) collective-permute-start(bf16[2048,256]{1,0:T(8,128)(2,1)} %pad_maximum_fusion.refs_4_), channel_id=1, source_target_pairs={{0,8},{8,0},{16,24},{24,16},{1,9},{9,1},{17,25},{25,17},{2,10},{10... | collective-permute-start | bytes 3145736 | tf_op jit(solution)/shard_map/ppermute | solution.py:25
  65.8 2.9 collective-permute-start.6
  90.1 167.1 %all-gather.7.cloned.1.call-start = ((), (), s32[]{:S(2)}) async-start(), calls=%async_computation.9 | async-start | bytes 4718592 | tf_op jit(solution)/shard_map/all_gather | solution.py:818
  92.4 60.7 %copy-start.31 = (f32[512,256]{1,0:T(8,128)}, f32[512,256]{1,0:T(8,128)S(1)}, u32[]{:S(2)}) copy-start(f32[512,256]{1,0:T(8,128)S(1)} %get-tuple-element.290) | copy-start | bytes 1572868
  92.5 5.3 collective-permute-start.7
  95.9 6.3 %collective-permute-start.8 = (bf16[4,27,256]{2,1,0:T(8,128)(2,1)S(1)}, bf16[4,27,256]{2,1,0:T(8,128)(2,1)S(1)}, u32[]{:S(2)}, u32[]{:S(2)}) collective-permute-start(bf16[4,27,256]{2,1,0:T(8,128)(2,1)S(1)} %get-tuple-element.273), channel_id=1, source_target_pairs={{1,0},{2,1},{3,2},{4,3},{5,4},{6,5},{7,6},{9,8},{10,9},{11,10},{12... | collective-permute-start | bytes 165896 | tf_op jit(solution)/shard_map/ppermute | solution.py:764
  102.3 42.4 %collective-permute-start.14 = (bf16[4,640,256]{2,1,0:T(8,128)(2,1)S(1)}, bf16[4,640,256]{2,1,0:T(8,128)(2,1)S(1)}, u32[]{:S(2)}, u32[]{:S(2)}) collective-permute-start(bf16[4,640,256]{2,1,0:T(8,128)(2,1)S(1)} %all-to-all-done.1.refs_0_), channel_id=1, source_target_pairs={{0,1},{1,0},{2,3},{3,2},{4,5},{5,4},{6,7},{7,6},{8,9},{9,8},{10,11... | collective-permute-start | bytes 3932168 | tf_op jit(solution)/shard_map/ppermute | solution.py:29
  107.7 37.3 %copy-start.37 = (f32[512,1024]{1,0:T(8,128)}, f32[512,1024]{1,0:T(8,128)S(1)}, u32[]{:S(2)}) copy-start(f32[512,1024]{1,0:T(8,128)S(1)} %get-tuple-element.292) | copy-start | bytes 6291460
  107.7 37.0 %copy-start.1 = (bf16[4,640,256]{2,1,0:T(8,128)(2,1)S(1)}, bf16[4,640,256]{2,1,0:T(8,128)(2,1)}, u32[]{:S(2)}) copy-start(bf16[4,640,256]{2,1,0:T(8,128)(2,1)} %copy-done) | copy-start | bytes 3932164
  107.8 1.9 collective-permute-start.10
  107.9 4.5 collective-permute-start.11
  109.5 4.4 collective-permute-start.9
  112.4 7.9 %collective-permute-start.12 = (bf16[128,1024]{1,0:T(8,128)(2,1)S(1)}, bf16[128,1024]{1,0:T(8,128)(2,1)S(1)}, u32[]{:S(2)}, u32[]{:S(2)}) collective-permute-start(bf16[128,1024]{1,0:T(8,128)(2,1)S(1)} %fusion.33), channel_id=1, source_target_pairs={{0,16},{8,24},{16,0},{24,8},{1,17},{9,25},{17,1},{25,9},{2,18},{10... | collective-permute-start | bytes 786440 | tf_op jit(solution)/shard_map/ppermute | solution.py:25
  145.1 6.4 %collective-permute-start.16 = (bf16[128,1024]{1,0:T(8,128)(2,1)S(1)}, bf16[128,1024]{1,0:T(8,128)(2,1)S(1)}, u32[]{:S(2)}, u32[]{:S(2)}) collective-permute-start(bf16[128,1024]{1,0:T(8,128)(2,1)S(1)} %multiply_convert_fusion), channel_id=1, source_target_pairs={{0,16},{8,24},{16,0},{24,8},{1,17},{9,25},{17,1},{25,9},{2,18},{10... | collective-permute-start | bytes 786440 | tf_op jit(solution)/shard_map/ppermute | solution.py:25
  146.7 4.8 collective-permute-start.15
  151.5 1.5 collective-permute-start.17
  159.7 17.6 %collective-permute-start.19 = (bf16[128,4096]{1,0:T(8,128)(2,1)}, bf16[128,4096]{1,0:T(8,128)(2,1)}, u32[]{:S(2)}, u32[]{:S(2)}) collective-permute-start(bf16[128,4096]{1,0:T(8,128)(2,1)} %get-tuple-element.231), channel_id=1, source_target_pairs={{0,8},{8,0},{16,24},{24,16},{1,9},{9,1},{17,25},{25,17},{2,10},{10... | collective-permute-start | bytes 3145736 | tf_op jit(solution)/shard_map/ppermute | solution.py:25
  173.8 36.0 %collective-permute-start.23 = (bf16[8,2,128,1024]{3,2,1,0:T(8,128)(2,1)}, bf16[8,2,128,1024]{3,2,1,0:T(8,128)(2,1)}, u32[]{:S(2)}, u32[]{:S(2)}) collective-permute-start(bf16[8,2,128,1024]{3,2,1,0:T(8,128)(2,1)} %bitcast.198), channel_id=1, source_target_pairs={{0,8},{8,0},{16,24},{24,16},{1,9},{9,1},{17,25},{25,17},{2,10},{10... | collective-permute-start | bytes 12582920 | tf_op jit(solution)/shard_map/ppermute | solution.py:25
  176.7 10.7 %collective-permute-start.18 = (bf16[128,4096]{1,0:T(8,128)(2,1)}, bf16[128,4096]{1,0:T(8,128)(2,1)}, u32[]{:S(2)}, u32[]{:S(2)}) collective-permute-start(bf16[128,4096]{1,0:T(8,128)(2,1)} %get-tuple-element.230), channel_id=1, source_target_pairs={{0,8},{8,0},{16,24},{24,16},{1,9},{9,1},{17,25},{25,17},{2,10},{10... | collective-permute-start | bytes 3145736 | tf_op jit(solution)/shard_map/ppermute | solution.py:25
  177.3 356.1 %reduce-scatter.5.cloned.1.call-start = ((), (), s32[]{:S(2)}) async-start(), calls=%async_computation.7 | async-start | bytes 4718592 | tf_op jit(solution)/shard_map/reduce_scatter | solution.py:871
  180.4 25.4 %collective-permute-start.20 = (bf16[128,4096]{1,0:T(8,128)(2,1)}, bf16[128,4096]{1,0:T(8,128)(2,1)}, u32[]{:S(2)}, u32[]{:S(2)}) collective-permute-start(bf16[128,4096]{1,0:T(8,128)(2,1)} %fusion.7), channel_id=1, source_target_pairs={{0,16},{8,24},{16,0},{24,8},{1,17},{9,25},{17,1},{25,9},{2,18},{10... | collective-permute-start | bytes 3145736 | tf_op jit(solution)/shard_map/ppermute | solution.py:25
  182.8 1.3 collective-permute-start.21
  184.1 1.5 collective-permute-start.22
  230.0 24.5 %collective-permute-start.25 = (bf16[512,1024]{1,0:T(8,128)(2,1)S(1)}, bf16[512,1024]{1,0:T(8,128)(2,1)S(1)}, u32[]{:S(2)}, u32[]{:S(2)}) collective-permute-start(bf16[512,1024]{1,0:T(8,128)(2,1)S(1)} %get-tuple-element.118.refs_0_), channel_id=1, source_target_pairs={{0,16},{8,24},{16,0},{24,8},{1,17},{9,25},{17,1},{25,9},{2,18},{10... | collective-permute-start | bytes 3145736 | tf_op jit(solution)/shard_map/ppermute | solution.py:25
  231.6 22.9 %collective-permute-start.24 = (bf16[512,1024]{1,0:T(8,128)(2,1)S(1)}, bf16[512,1024]{1,0:T(8,128)(2,1)S(1)}, u32[]{:S(2)}, u32[]{:S(2)}) collective-permute-start(bf16[512,1024]{1,0:T(8,128)(2,1)S(1)} %get-tuple-element.118.refs_0_), channel_id=1, source_target_pairs={{0,8},{8,0},{16,24},{24,16},{1,9},{9,1},{17,25},{25,17},{2,10},{10... | collective-permute-start | bytes 3145736 | tf_op jit(solution)/shard_map/ppermute | solution.py:25
  254.5 2.8 collective-permute-start.26
  287.4 6.8 %collective-permute-start.28 = (bf16[1024,1024]{1,0:T(8,128)(2,1)}, bf16[1024,1024]{1,0:T(8,128)(2,1)S(1)}, u32[]{:S(2)}, u32[]{:S(2)}) collective-permute-start(bf16[1024,1024]{1,0:T(8,128)(2,1)} %get-tuple-element.124), channel_id=1, source_target_pairs={{0,8},{8,0},{16,24},{24,16},{1,9},{9,1},{17,25},{25,17},{2,10},{10... | collective-permute-start | bytes 6291464 | tf_op jit(solution)/shard_map/ppermute | solution.py:25
  287.6 5.3 collective-permute-start.30
  297.5 25.8 %collective-permute-start.29 = (bf16[512,1024]{1,0:T(8,128)(2,1)}, bf16[512,1024]{1,0:T(8,128)(2,1)}, u32[]{:S(2)}, u32[]{:S(2)}) collective-permute-start(bf16[512,1024]{1,0:T(8,128)(2,1)} %add_convert_fusion.3), channel_id=1, source_target_pairs={{0,16},{8,24},{16,0},{24,8},{1,17},{9,25},{17,1},{25,9},{2,18},{10... | collective-permute-start | bytes 3145736 | tf_op jit(solution)/shard_map/ppermute | solution.py:25
  323.2 34.2 %collective-permute-start.31 = (bf16[4,512,256]{2,1,0:T(8,128)(2,1)}, bf16[4,512,256]{2,1,0:T(8,128)(2,1)}, u32[]{:S(2)}, u32[]{:S(2)}) collective-permute-start(bf16[4,512,256]{2,1,0:T(8,128)(2,1)} %fusion.9), channel_id=1, source_target_pairs={{0,16},{8,24},{16,0},{24,8},{1,17},{9,25},{17,1},{25,9},{2,18},{10... | collective-permute-start | bytes 3145736 | tf_op jit(solution)/shard_map/ppermute | solution.py:25
  324.8 211.4 %reduce-scatter.3.cloned.1.call-start = ((), (), s32[]{:S(2)}) async-start(), calls=%async_computation.6 | async-start | bytes 4718592 | tf_op jit(solution)/shard_map/reduce_scatter | solution.py:888
  357.5 24.6 %collective-permute-start.33 = (bf16[128,4096]{1,0:T(8,128)(2,1)}, bf16[128,4096]{1,0:T(8,128)(2,1)}, u32[]{:S(2)}, u32[]{:S(2)}) collective-permute-start(bf16[128,4096]{1,0:T(8,128)(2,1)} %get-tuple-element.160), channel_id=1, source_target_pairs={{0,16},{8,24},{16,0},{24,8},{1,17},{9,25},{17,1},{25,9},{2,18},{10... | collective-permute-start | bytes 3145736 | tf_op jit(solution)/shard_map/ppermute | solution.py:25
  382.1 3.0 collective-permute-start.34
  382.1 14.7 %collective-permute-start.51 = (bf16[8,2,128,1024]{3,2,1,0:T(8,128)(2,1)}, bf16[8,2,128,1024]{3,2,1,0:T(8,128)(2,1)}, u32[]{:S(2)}, u32[]{:S(2)}) collective-permute-start(bf16[8,2,128,1024]{3,2,1,0:T(8,128)(2,1)} %get-tuple-element.184), channel_id=1, source_target_pairs={{0,8},{8,0},{16,24},{24,16},{1,9},{9,1},{17,25},{25,17},{2,10},{10... | collective-permute-start | bytes 12582920 | tf_op jit(solution)/shard_map/ppermute | solution.py:25
  383.4 4.5 collective-permute-start.35
  394.4 33.7 %collective-permute-start.39 = (bf16[4,640,256]{2,1,0:T(8,128)(2,1)}, bf16[4,640,256]{2,1,0:T(8,128)(2,1)}, u32[]{:S(2)}, u32[]{:S(2)}) collective-permute-start(bf16[4,640,256]{2,1,0:T(8,128)(2,1)} %get-tuple-element.164), channel_id=1, source_target_pairs={{0,1},{1,0},{2,3},{3,2},{4,5},{5,4},{6,7},{7,6},{8,9},{9,8},{10,11... | collective-permute-start | bytes 3932168 | tf_op jit(solution)/shard_map/ppermute | solution.py:29
  396.7 8.3 %collective-permute-start.37 = (bf16[128,1024]{1,0:T(8,128)(2,1)S(1)}, bf16[128,1024]{1,0:T(8,128)(2,1)S(1)}, u32[]{:S(2)}, u32[]{:S(2)}) collective-permute-start(bf16[128,1024]{1,0:T(8,128)(2,1)S(1)} %get-tuple-element.239), channel_id=1, source_target_pairs={{0,8},{8,0},{16,24},{24,16},{1,9},{9,1},{17,25},{25,17},{2,10},{10... | collective-permute-start | bytes 786440 | tf_op jit(solution)/shard_map/ppermute | solution.py:25
  404.7 2.7 collective-permute-start.36
  406.2 8.5 %collective-permute-start.38 = (bf16[128,1024]{1,0:T(8,128)(2,1)S(1)}, bf16[128,1024]{1,0:T(8,128)(2,1)S(1)}, u32[]{:S(2)}, u32[]{:S(2)}) collective-permute-start(bf16[128,1024]{1,0:T(8,128)(2,1)S(1)} %fusion.31), channel_id=1, source_target_pairs={{0,16},{8,24},{16,0},{24,8},{1,17},{9,25},{17,1},{25,9},{2,18},{10... | collective-permute-start | bytes 786440 | tf_op jit(solution)/shard_map/ppermute | solution.py:25
  406.7 22.9 %collective-permute-start.32 = (bf16[128,256]{1,0:T(8,128)(2,1)S(1)}, bf16[128,256]{1,0:T(8,128)(2,1)S(1)}, u32[]{:S(2)}, u32[]{:S(2)}) collective-permute-start(bf16[128,256]{1,0:T(8,128)(2,1)S(1)} %bitcast.190), channel_id=1, source_target_pairs={{0,8},{8,0},{16,24},{24,16},{1,9},{9,1},{17,25},{25,17},{2,10},{10... | collective-permute-start | bytes 196616 | tf_op jit(solution)/shard_map/ppermute | solution.py:25
  406.9 31.5 %collective-permute-start.49 = (bf16[128,256]{1,0:T(8,128)(2,1)S(1)}, bf16[128,256]{1,0:T(8,128)(2,1)S(1)}, u32[]{:S(2)}, u32[]{:S(2)}) collective-permute-start(bf16[128,256]{1,0:T(8,128)(2,1)S(1)} %bitcast.189), channel_id=1, source_target_pairs={{0,8},{8,0},{16,24},{24,16},{1,9},{9,1},{17,25},{25,17},{2,10},{10... | collective-permute-start | bytes 196616 | tf_op jit(solution)/shard_map/ppermute | solution.py:25
  428.1 10.2 %collective-permute-start.45 = (bf16[128,1024]{1,0:T(8,128)(2,1)S(1)}, bf16[128,1024]{1,0:T(8,128)(2,1)S(1)}, u32[]{:S(2)}, u32[]{:S(2)}) collective-permute-start(bf16[128,1024]{1,0:T(8,128)(2,1)S(1)} %fusion.22), channel_id=1, source_target_pairs={{0,8},{8,0},{16,24},{24,16},{1,9},{9,1},{17,25},{25,17},{2,10},{10... | collective-permute-start | bytes 786440 | tf_op jit(solution)/shard_map/ppermute | solution.py:25
  428.1 8.7 %collective-permute-start.40 = (bf16[128,1024]{1,0:T(8,128)(2,1)S(1)}, bf16[128,1024]{1,0:T(8,128)(2,1)S(1)}, u32[]{:S(2)}, u32[]{:S(2)}) collective-permute-start(bf16[128,1024]{1,0:T(8,128)(2,1)S(1)} %fusion.22), channel_id=1, source_target_pairs={{0,16},{8,24},{16,0},{24,8},{1,17},{9,25},{17,1},{25,9},{2,18},{10... | collective-permute-start | bytes 786440 | tf_op jit(solution)/shard_map/ppermute | solution.py:25
  436.8 4.3 collective-permute-start.41
  438.3 2.8 collective-permute-start.46
  442.3 7.1 %collective-permute-start.47 = (bf16[4,27,256]{2,1,0:T(8,128)(2,1)S(1)}, bf16[4,27,256]{2,1,0:T(8,128)(2,1)S(1)}, u32[]{:S(2)}, u32[]{:S(2)}) collective-permute-start(bf16[4,27,256]{2,1,0:T(8,128)(2,1)S(1)} %get-tuple-element.263), channel_id=1, source_target_pairs={{1,0},{2,1},{3,2},{4,3},{5,4},{6,5},{7,6},{9,8},{10,9},{11,10},{12... | collective-permute-start | bytes 165896 | tf_op jit(solution)/shard_map/ppermute | solution.py:764
  443.7 6.4 %collective-permute-start.48 = (bf16[4,27,256]{2,1,0:T(8,128)(2,1)S(1)}, bf16[4,27,256]{2,1,0:T(8,128)(2,1)S(1)}, u32[]{:S(2)}, u32[]{:S(2)}) collective-permute-start(bf16[4,27,256]{2,1,0:T(8,128)(2,1)S(1)} %get-tuple-element.262), channel_id=1, source_target_pairs={{0,1},{1,2},{2,3},{3,4},{4,5},{5,6},{6,7},{8,9},{9,10},{10,11},{11... | collective-permute-start | bytes 165896 | tf_op jit(solution)/shard_map/ppermute | solution.py:763
  456.7 51.7 %all-to-all-start.3 = ((bf16[4,640,256]{2,1,0:T(8,128)(2,1)}), bf16[4,640,256]{2,1,0:T(8,128)(2,1)S(1)}, u32[]{:S(2)}, u32[]{:S(2)}) async-start(bf16[4,640,256]{2,1,0:T(8,128)(2,1)} %add_convert_fusion.2), calls=%async_computation.3 | async-start | bytes 2621440 | tf_op jit(solution)/shard_map/all_to_all | solution.py:92
  465.8 41.1 %collective-permute-start.50 = (bf16[4,656,256]{2,1,0:T(8,128)(2,1)}, bf16[4,656,256]{2,1,0:T(8,128)(2,1)S(1)}, u32[]{:S(2)}, u32[]{:S(2)}) collective-permute-start(bf16[4,656,256]{2,1,0:T(8,128)(2,1)} %copy-done.4), channel_id=1, source_target_pairs={{0,1},{1,0},{2,3},{3,2},{4,5},{5,4},{6,7},{7,6},{8,9},{9,8},{10,11... | collective-permute-start | bytes 4030472 | tf_op jit(solution)/shard_map/ppermute | solution.py:29
  465.8 47.4 %collective-permute-start.27 = (bf16[4,512,256]{2,1,0:T(8,128)(2,1)}, bf16[4,512,256]{2,1,0:T(8,128)(2,1)}, u32[]{:S(2)}, u32[]{:S(2)}) collective-permute-start(bf16[4,512,256]{2,1,0:T(8,128)(2,1)} %bitcast.169), channel_id=1, source_target_pairs={{0,8},{8,0},{16,24},{24,16},{1,9},{9,1},{17,25},{25,17},{2,10},{10... | collective-permute-start | bytes 3145736 | tf_op jit(solution)/shard_map/ppermute | solution.py:25
  508.4 35.9 %all-to-all-start.2 = ((bf16[4,656,256]{2,1,0:T(8,128)(2,1)}), bf16[4,656,256]{2,1,0:T(8,128)(2,1)S(1)}, u32[]{:S(2)}, u32[]{:S(2)}) async-start(bf16[4,656,256]{2,1,0:T(8,128)(2,1)} %add_convert_fusion.1), calls=%async_computation.2 | async-start | bytes 2686976 | tf_op jit(solution)/shard_map/all_to_all | solution.py:92
  514.6 4.9 collective-permute-start.44
  516.4 9.2 %collective-permute-start.43 = (bf16[512,256]{1,0:T(8,128)(2,1)S(1)}, bf16[512,256]{1,0:T(8,128)(2,1)S(1)}, u32[]{:S(2)}, u32[]{:S(2)}) collective-permute-start(bf16[512,256]{1,0:T(8,128)(2,1)S(1)} %get-tuple-element.170), channel_id=1, source_target_pairs={{0,16},{8,24},{16,0},{24,8},{1,17},{9,25},{17,1},{25,9},{2,18},{10... | collective-permute-start | bytes 786440 | tf_op jit(solution)/shard_map/ppermute | solution.py:25
  517.8 12.6 %collective-permute-start.42 = (bf16[512,256]{1,0:T(8,128)(2,1)S(1)}, bf16[512,256]{1,0:T(8,128)(2,1)S(1)}, u32[]{:S(2)}, u32[]{:S(2)}) collective-permute-start(bf16[512,256]{1,0:T(8,128)(2,1)S(1)} %get-tuple-element.168), channel_id=1, source_target_pairs={{0,24},{8,16},{16,8},{24,0},{1,25},{9,17},{17,9},{25,1},{2,26},{10... | collective-permute-start | bytes 786440 | tf_op jit(solution)/shard_map/ppermute | solution.py:25
  537.2 9.3 %collective-permute-start.52 = (bf16[128,1024]{1,0:T(8,128)(2,1)S(1)}, bf16[128,1024]{1,0:T(8,128)(2,1)S(1)}, u32[]{:S(2)}, u32[]{:S(2)}) collective-permute-start(bf16[128,1024]{1,0:T(8,128)(2,1)S(1)} %slice_bitcast_fusion.2), channel_id=1, source_target_pairs={{0,16},{8,24},{16,0},{24,8},{1,17},{9,25},{17,1},{25,9},{2,18},{10... | collective-permute-start | bytes 786440 | tf_op jit(solution)/shard_map/ppermute | solution.py:25
  (65 other events, 480.8 us)
Sparse Core Ops, SparseCore 0:
  90.3 83.5 all-gather.4
  177.4 72.2 all-gather.6
  325.0 86.7 reduce-scatter.4
  415.6 100.1 reduce-scatter.2

commit v7 on v6

--- a/solution.py
+++ b/solution.py
@@ -74,7 +74,7 @@
 
 
 def cost(us):
-    return pl.CostEstimate(flops=int(us * 1.1e9), transcendentals=0, bytes_accessed=0)
+    return pl.CostEstimate(flops=int(us * 1.76e9), transcendentals=0, bytes_accessed=0)
 
 
 CELL = 256
@@ -869,7 +869,6 @@
     act_done = from_y
     result = jnp.stack(pick([result[order_of(m)] for m in range(4)], c))
     grad_mlp = lax.psum_scatter(split_rows(terms[3]), "seq", scatter_dimension=0, tiled=False)
-    grad_in, grad_down = grad_mlp[0].astype(F32), grad_mlp[1].astype(F32).T
 
     att, input_grad, grad_vectors, *grad_rows = layer_backward(
         segments, [stream_zero, stream_one], vectors, grads, cot_mine, attn_w, qkv
@@ -882,10 +881,6 @@
         (leave_rows, *line.send((leave_rows, 2)), send)
     )
     grad_up_rows = [leave_rows, swap(leave_rows, 1), from_y, swap(from_y, 1)]
-    grad_attn = grad_attn.astype(F32) + swap(send, 1).astype(F32)
-    grad_attn = split_rows(grad_attn.astype(BF16))
-    grad_attn = after(grad_attn, grad_up_rows[2])
-    grad_attn = lax.psum_scatter(grad_attn, "seq", scatter_dimension=0, tiled=False)
     grad_up_rows = jnp.concatenate(grad_up_rows, axis=0)
     grad_hidden = dot(grad_up_rows, up)
     grad_low = grad_hidden.astype(BF16)
@@ -894,8 +889,14 @@
     up_started = cross_x([grad_res, grad_up])
     grad_mixed = dot_t(after(grad_low, grad_up, grad_res), res).reshape(micros, coarse, width)
     grad_mixed, over_y = fold_core([grad_mixed[j] for j in range(4)])
+    over_y, send = lax.optimization_barrier((over_y, swap(send, 1)))
+    grad_attn = grad_attn.astype(F32) + send.astype(F32)
+    grad_attn = split_rows(grad_attn.astype(BF16))
+    grad_attn = lax.psum_scatter(grad_attn, "seq", scatter_dimension=0, tiled=False)
     grad_mixed = grad_mixed + line.send((over_y, 2))[0].astype(F32)
-    grad_conv_low = after((gelu_grad(conv_out) * grad_mixed).astype(BF16), grad_mlp, up_started[1])
+    grad_conv_low = (gelu_grad(conv_out) * grad_mixed).astype(BF16)
+    grad_conv_low, grad_mlp, up_started = lax.optimization_barrier((grad_conv_low, grad_mlp, tuple(up_started)))
+    grad_in, grad_down = grad_mlp[0].astype(F32), grad_mlp[1].astype(F32).T
 
     grad_conv_all = jnp.concatenate(line.spread(grad_conv_low), axis=0)
     grad_taps = dot(grad_conv_all, conv).reshape(micros, coarse, 3 * quarter)
@@ -910,12 +911,15 @@
         + jnp.concatenate([prior.astype(F32), tap[2][:, : coarse - step]], axis=1)
     ).reshape(micros * coarse, quarter)
     grad_embed = (grad_hidden + gelu_grad(embed) * grad_act).astype(BF16)
+    pieces = line.exchange(grad_in_q)
     started = cross_x([gram(onehot, grad_embed), grad_conv, grad_vectors])
-    up_started = after(up_started, started[0])
+    up_started, near = lax.optimization_barrier((tuple(up_started), started[0]))
+    pieces, near = lax.optimization_barrier((pieces, near))
+    started = (near, *started[1:])
     grad_res, grad_up = cross_z(up_started, [w.shape for w in groups[1]])
     grad_table, grad_conv, grad_vectors = cross_z(started, [w.shape for w in groups[0]])
     grad_conv = grad_conv.reshape(-1, 3, quarter).transpose(1, 2, 0)
-    input_grads = jnp.stack(pick(line.exchange(grad_in_q), c))
+    input_grads = jnp.stack(pick(pieces, c))
     grad_attn = grad_attn[0].astype(F32) + line.send((grad_attn[1], 2))[0].astype(F32)
     grad_qkv, grad_out = grad_attn[:, : 3 * quarter], grad_attn[:, 3 * quarter :]
     grad_vectors = [grad_vectors[i, :lot] for i in range(4)]

time: 564 us -> 561 us (level)
  waiting for transfers between devices: 272 us -> 280 us
    all_to_all x4, waiting for transfers between devices: 11.5 us -> 22.4 us  [along_z(): return lax.all_to_all(x, 'seq', 0, 0, axis_index_groups=ALONG_Z, tiled=True)]
    ppermute x4, waiting for transfers between devices: 93.7 us -> 82.9 us  [hop(): return lax.ppermute(x, 'seq', [(i, i ^ k) for i in range(8)])]
    unnamed x159 -> x169, local copies, waits for them, and re-layouts: 26.7 us -> 23.1 us
  transfers between devices with their start and end apart: 61 -> 61, of which waited for: 34 -> 38; matrix products, arithmetic and copies ran while one was open for 13% -> 12% of each run, Pallas kernels for 13% -> 13%
where the time goes in v7:
time: 561 us; the launch traced here: 553 us
  waiting for transfers between devices  280 us (50%)
  Pallas kernels  102 us (18%)
  starting transfers between devices  63.7 us (11%)
  local copies, waits for them, and re-layouts  39.2 us (7%)
  other arithmetic  36.6 us (7%)
  matrix products  16.4 us (3%)
  between operations  15.3 us (3%)
    ppermute x45, waiting for transfers between devices, swap(): return lax.ppermute(x, 'cond', [(i, i ^ j) for i in range(4)])  151 us
    ppermute x4, waiting for transfers between devices, hop(): return lax.ppermute(x, 'seq', [(i, i ^ k) for i in range(8)])  82.9 us
    pallas_call x2, Pallas kernels, layer_call(): pl.pallas_call(body, out_shape=[space(shape, dtype) for space, shape, dty...  43.2 us
    pallas_call x1, Pallas kernels, mlp(): pl.pallas_call(mlp_body, out_shape=[shape((rows, hidden), BF16), shape((r...  30.1 us
    ppermute x45, starting transfers between devices, swap(): return lax.ppermute(x, 'cond', [(i, i ^ j) for i in range(4)])  24.2 us
    unnamed x169, local copies, waits for them, and re-layouts  23.1 us
    all_to_all x4, waiting for transfers between devices, along_z(): return lax.all_to_all(x, 'seq', 0, 0, axis_index_groups=ALONG_Z, tiled=True)  22.4 us
    all_to_all x4, starting transfers between devices, along_z(): return lax.all_to_all(x, 'seq', 0, 0, axis_index_groups=ALONG_Z, tiled=True)  22.2 us
  transfers between devices with their start and end apart: 61, of which 38 were waited for; matrix products, arithmetic and copies ran while one was open for 12% of the time, Pallas kernels for 13%

profile of v7, /device:TPU:0, one launch (start us, length us, event | category | flops | bytes accessed | tf_op | source)
XLA Modules:
  0.0 552.9 jit_solution(16085891042390293080)
XLA Ops:
  11.3 6.4 %all-to-all-start = ((bf16[4,656,256]{2,1,0:T(8,128)(2,1)}), bf16[4,656,256]{2,1,0:T(8,128)(2,1)S(1)}, u32[]{:S(2)}, u32[]{:S(2)}) async-start(bf16[4,656,256]{2,1,0:T(8,128)(2,1)} %broadcast_in_dim.4), calls=%async_computation | async-start | bytes 2686976 | tf_op jit(solution)/shard_map/all_to_all | solution.py:92
  18.6 1.5 collective-permute-start.2
  21.3 6.8 %collective-permute-done.2.q2 = bf16[512,256]{1,0:T(8,128)(2,1)S(1)} collective-permute-done((bf16[512,256]{1,0:T(8,128)(2,1)}, bf16[512,256]{1,0:T(8,128)(2,1)S(1)}, u32[]{:S(2)}, u32[]{:S(2)}) %collective-permute-start.2) | collective-permute-done | bytes 262176 | tf_op jit(solution)/shard_map/ppermute | solution.py:25
  28.1 3.2 collective-permute-done.3.q3
  34.6 5.7 %collective-permute-done.4 = bf16[128,1024]{0,1:T(8,128)(2,1)S(1)} collective-permute-done((bf16[128,1024]{0,1:T(8,128)(2,1)S(1)}, bf16[128,1024]{0,1:T(8,128)(2,1)S(1)}, u32[]{:S(2)}, u32[]{:S(2)}) %collective-permute-start.4) | collective-permute-done | bytes 262176 | tf_op jit(solution)/shard_map/ppermute | solution.py:25
  42.3 1.8 pad_maximum_fusion.4
  44.1 5.7 %all-to-all-done.refs_0_ = bf16[4,656,256]{2,1,0:T(8,128)(2,1)S(1)} async-done(((bf16[4,656,256]{2,1,0:T(8,128)(2,1)}), bf16[4,656,256]{2,1,0:T(8,128)(2,1)S(1)}, u32[]{:S(2)}, u32[]{:S(2)}) %all-to-all-start) | async-done | bytes 1343520 | tf_op jit(solution)/shard_map/all_to_all | solution.py:92
  51.1 3.5 all-to-all-start.1
  54.7 1.6 collective-permute-start
  56.3 9.5 %collective-permute-done.5.refs_6_ = bf16[2048,256]{1,0:T(8,128)(2,1)} collective-permute-done((bf16[2048,256]{1,0:T(8,128)(2,1)}, bf16[2048,256]{1,0:T(8,128)(2,1)}, u32[]{:S(2)}, u32[]{:S(2)}) %collective-permute-start.5) | collective-permute-done | bytes 1048608 | tf_op jit(solution)/shard_map/ppermute | solution.py:25
  65.9 2.9 collective-permute-done.6.refs_7_
  69.7 15.6 %collective-permute-done.refs_1_ = bf16[4,656,256]{2,1,0:T(8,128)(2,1)S(1)} collective-permute-done((bf16[4,656,256]{2,1,0:T(8,128)(2,1)S(1)}, bf16[4,656,256]{2,1,0:T(8,128)(2,1)S(1)}, u32[]{:S(2)}, u32[]{:S(2)}) %collective-permute-start) | collective-permute-done | bytes 1343520 | tf_op jit(solution)/shard_map/ppermute | solution.py:29
  87.7 2.0 copy.90
  89.9 2.1 multiply_convert_fusion.1
  92.2 3.4 collective-permute-start.7
  97.4 4.4 collective-permute-done.8
  102.0 4.3 collective-permute-start.14
  107.5 1.7 collective-permute-start.11
  109.4 2.6 collective-permute-done.11
  112.0 1.6 collective-permute-start.12
  113.6 6.3 %collective-permute-done.12 = bf16[128,1024]{1,0:T(8,128)(2,1)S(1)} collective-permute-done((bf16[128,1024]{1,0:T(8,128)(2,1)S(1)}, bf16[128,1024]{1,0:T(8,128)(2,1)S(1)}, u32[]{:S(2)}, u32[]{:S(2)}) %collective-permute-start.12) | collective-permute-done | bytes 262176 | tf_op jit(solution)/shard_map/ppermute | solution.py:25
  120.6 23.7 %collective-permute-done.14.refs_1_ = bf16[4,640,256]{2,1,0:T(8,128)(2,1)S(1)} collective-permute-done((bf16[4,640,256]{2,1,0:T(8,128)(2,1)S(1)}, bf16[4,640,256]{2,1,0:T(8,128)(2,1)S(1)}, u32[]{:S(2)}, u32[]{:S(2)}) %collective-permute-start.14) | collective-permute-done | bytes 1310752 | tf_op jit(solution)/shard_map/ppermute | solution.py:29
  144.7 1.6 collective-permute-start.16
  146.3 4.8 collective-permute-done.16
  154.1 4.7 fusion.100
  160.1 13.4 %all-gather.5.cloned.1.call-done = bf16[16,128,1024]{2,1,0:T(8,128)(2,1)} async-done(((bf16[2,128,1024]{2,1,0:T(8,128)(2,1)}), bf16[16,128,1024]{2,1,0:T(8,128)(2,1)}) %all-gather.5.cloned.1.call-update) | async-done | bytes 4194320 | tf_op jit(solution)/shard_map/all_gather | solution.py:817
  174.7 3.0 fusion.7
  177.8 1.5 collective-permute-start.20
  180.5 1.8 pad_maximum_fusion.5
  185.5 17.7 %collective-permute-done.20 = bf16[128,4096]{1,0:T(8,128)(2,1)} collective-permute-done((bf16[128,4096]{1,0:T(8,128)(2,1)}, bf16[128,4096]{1,0:T(8,128)(2,1)}, u32[]{:S(2)}, u32[]{:S(2)}) %collective-permute-start.20) | collective-permute-done | bytes 1048608 | tf_op jit(solution)/shard_map/ppermute | solution.py:25
  203.1 2.2 fusion.8.up_ref
  205.4 1.5 enter.1.refs_2_
  207.0 18.7 %layer_forward.1 = (bf16[512,1024]{1,0:T(8,128)(2,1)}, f32[512,1024]{1,0:T(8,128)S(1)}, bf16[512,1024]{1,0:T(8,128)(2,1)S(1)}, bf16[512,768]{1,0:T(8,128)(2,1)},...) custom-call(s32[512,1]{1,0:T(8,128)S(1)} %copy.91.refs_0_, ...), custom_call_target="tpu_custom_call" | custom-call | flops 31680000000 | tf_op jit(solution)/shard_map/layer_forward/pallas_call | solution.py:472
  228.5 22.7 %collective-permute-done.25.refs_2_ = bf16[512,1024]{1,0:T(8,128)(2,1)S(1)} collective-permute-done((bf16[512,1024]{1,0:T(8,128)(2,1)S(1)}, bf16[512,1024]{1,0:T(8,128)(2,1)S(1)}, u32[]{:S(2)}, u32[]{:S(2)}) %collective-permute-start.25) | collective-permute-done | bytes 1048608 | tf_op jit(solution)/shard_map/ppermute | solution.py:25
  252.3 1.7 collective-permute-done.26.refs_3_
  254.0 30.1 %mlp.1 = (bf16[2048,1024]{1,0:T(8,128)(2,1)}, bf16[2048,1024]{1,0:T(8,128)(2,1)}, bf16[2048,1024]{1,0:T(8,128)(2,1)}, bf16[2048,1024]{1,0:T(8,128)(2,1)}, bf16[2...) custom-call(s32[4]{0:T(128)S(1)} %iota_xor_fusion.index, ...), custom_call_target="tpu_custom_call" | custom-call | flops 52800000000 | tf_op jit(solution)/shard_map/mlp/pallas_call | solution.py:684
  284.8 4.9 collective-permute-done.30
  291.0 2.0 copy-done.44
  295.8 14.7 %mlp_grads.1 = bf16[8,2,128,1024]{3,2,1,0:T(8,128)(2,1)} custom-call(bf16[2048,1024]{1,0:T(8,128)(2,1)S(1)} %copy-done.20, bf16[2048,1024]{1,0:T(8,128)(2,1)} %get-tuple-element.138.cot_ref, bf16[2048,1024]{1,0:T(8,128)(2,1)} %get-tuple-element.139.act_ref, bf16[2048,1024]{1,0:T(8,128)(2,1)} %get-tuple-element.140.grad_ref), custom_call_target="tpu_custom_call" | custom-call | flops 24640000000 | tf_op jit(solution)/shard_map/mlp_grads/pallas_call | solution.py:732
  310.5 9.6 %collective-permute-done.29.refs_7_ = bf16[512,1024]{1,0:T(8,128)(2,1)} collective-permute-done((bf16[512,1024]{1,0:T(8,128)(2,1)}, bf16[512,1024]{1,0:T(8,128)(2,1)}, u32[]{:S(2)}, u32[]{:S(2)}) %collective-permute-start.29) | collective-permute-done | bytes 1048608 | tf_op jit(solution)/shard_map/ppermute | solution.py:25
  321.7 24.5 %layer_backward.1 = (bf16[512,1024]{1,0:T(8,128)(2,1)}, f32[512,1024]{1,0:T(8,128)}, f32[8,1024]{1,0:T(8,128)S(1)}, bf16[512,768]{1,0:T(8,128)(2,1)S(1)}, bf16[5...) custom-call(s32[512,1]{1,0:T(8,128)S(1)} %copy.91.refs_0_, ...), custom_call_target="tpu_custom_call" | custom-call | flops 42240000000 | tf_op jit(solution)/shard_map/layer_backward/pallas_call | solution.py:472
  346.2 1.6 copy-done.19
  350.1 7.5 %layer_grads.1 = (bf16[8,2,128,1024]{3,2,1,0:T(8,128)(2,1)}, bf16[8,2,128,1024]{3,2,1,0:T(8,128)(2,1)}) custom-call(bf16[512,1024]{1,0:T(8,128)(2,1)S(1)} %copy-done.21, bf16[512,1024]{1,0:T(8,128)(2,1)} %get-tuple-element.161.att_ref, bf16[512,768]{1,0:T(8,128)(2,1)S(1)} %get-tuple-element.163.refs_0_, bf16[512,768]{1,0:T(8,128)(2,1)S(1)} %get-tuple-element.164.refs_1_, ...), custom_call_target="tpu_custom_call" | custom-call | flops 14080000000 | tf_op jit(solution)/shard_map/layer_grads/pallas_call | solution.py:555
  357.6 16.3 %collective-permute-done.34 = bf16[128,4096]{1,0:T(8,128)(2,1)S(1)} collective-permute-done((bf16[128,4096]{1,0:T(8,128)(2,1)S(1)}, bf16[128,4096]{1,0:T(8,128)(2,1)S(1)}, u32[]{:S(2)}, u32[]{:S(2)}) %collective-permute-start.34) | collective-permute-done | bytes 1048608 | tf_op jit(solution)/shard_map/ppermute | solution.py:25
  374.5 2.1 collective-permute-done.35
  376.7 2.8 collective-permute-done.36
  379.7 2.1 fusion.101
  387.3 1.7 fusion.31
  389.0 4.3 add_convert_fusion
  397.6 5.6 %collective-permute-done.40 = bf16[128,1024]{1,0:T(8,128)(2,1)S(1)} collective-permute-done((bf16[128,1024]{1,0:T(8,128)(2,1)}, bf16[128,1024]{1,0:T(8,128)(2,1)S(1)}, u32[]{:S(2)}, u32[]{:S(2)}) %collective-permute-start.40) | collective-permute-done | bytes 262176 | tf_op jit(solution)/shard_map/ppermute | solution.py:25
  403.2 2.4 fusion.22
  405.7 17.1 %collective-permute-done.41 = bf16[4,640,256]{2,1,0:T(8,128)(2,1)} collective-permute-done((bf16[4,640,256]{2,1,0:T(8,128)(2,1)S(1)}, bf16[4,640,256]{2,1,0:T(8,128)(2,1)}, u32[]{:S(2)}, u32[]{:S(2)}) %collective-permute-start.41) | collective-permute-done | bytes 1310752 | tf_op jit(solution)/shard_map/ppermute | solution.py:29
  425.2 6.5 %collective-permute-done.42 = bf16[128,1024]{1,0:T(8,128)(2,1)S(1)} collective-permute-done((bf16[128,1024]{1,0:T(8,128)(2,1)}, bf16[128,1024]{1,0:T(8,128)(2,1)S(1)}, u32[]{:S(2)}, u32[]{:S(2)}) %collective-permute-start.42) | collective-permute-done | bytes 262176 | tf_op jit(solution)/shard_map/ppermute | solution.py:25
  432.2 3.7 collective-permute-done.43
  439.5 4.5 collective-permute-start.49
  450.4 2.7 add_convert_fusion.2
  453.1 7.3 %all-to-all-start.3 = ((bf16[4,640,256]{2,1,0:T(8,128)(2,1)}), bf16[4,640,256]{2,1,0:T(8,128)(2,1)S(1)}, u32[]{:S(2)}, u32[]{:S(2)}) async-start(bf16[4,640,256]{2,1,0:T(8,128)(2,1)} %add_convert_fusion.2), calls=%async_computation.4 | async-start | bytes 2621440 | tf_op jit(solution)/shard_map/all_to_all | solution.py:92
  464.3 5.0 collective-permute-done.45
  469.2 5.9 %collective-permute-done.44 = bf16[512,256]{1,0:T(8,128)(2,1)S(1)} collective-permute-done((bf16[512,256]{1,0:T(8,128)(2,1)S(1)}, bf16[512,256]{1,0:T(8,128)(2,1)S(1)}, u32[]{:S(2)}, u32[]{:S(2)}) %collective-permute-start.44) | collective-permute-done | bytes 262176 | tf_op jit(solution)/shard_map/ppermute | solution.py:25
  475.8 26.5 %collective-permute-done.51 = bf16[4,656,256]{2,1,0:T(8,128)(2,1)S(1)} collective-permute-done((bf16[4,656,256]{2,1,0:T(8,128)(2,1)}, bf16[4,656,256]{2,1,0:T(8,128)(2,1)S(1)}, u32[]{:S(2)}, u32[]{:S(2)}) %collective-permute-start.51) | collective-permute-done | bytes 1343520 | tf_op jit(solution)/shard_map/ppermute | solution.py:29
  503.7 5.0 all-to-all-start.2
  518.0 3.3 reduce-scatter.5.cloned.1.call-done
  522.3 3.0 collective-permute-start.52
  525.2 16.7 %all-to-all-done.2.refs_0_ = bf16[4,656,256]{2,1,0:T(8,128)(2,1)S(1)} async-done(((bf16[4,656,256]{2,1,0:T(8,128)(2,1)}), bf16[4,656,256]{2,1,0:T(8,128)(2,1)S(1)}, u32[]{:S(2)}, u32[]{:S(2)}) %all-to-all-start.2) | async-done | bytes 1343520 | tf_op jit(solution)/shard_map/all_to_all | solution.py:92
  (344 shorter events, 86.5 us)
Async XLA Ops:
  11.3 38.5 %all-to-all-start = ((bf16[4,656,256]{2,1,0:T(8,128)(2,1)}), bf16[4,656,256]{2,1,0:T(8,128)(2,1)S(1)}, u32[]{:S(2)}, u32[]{:S(2)}) async-start(bf16[4,656,256]{2,1,0:T(8,128)(2,1)} %broadcast_in_dim.4), calls=%async_computation | async-start | bytes 2686976 | tf_op jit(solution)/shard_map/all_to_all | solution.py:92
  18.6 9.4 %collective-permute-start.2 = (bf16[512,256]{1,0:T(8,128)(2,1)}, bf16[512,256]{1,0:T(8,128)(2,1)S(1)}, u32[]{:S(2)}, u32[]{:S(2)}) collective-permute-start(bf16[512,256]{1,0:T(8,128)(2,1)} %get-tuple-element.273), channel_id=1, source_target_pairs={{0,16},{8,24},{16,0},{24,8},{1,17},{9,25},{17,1},{25,9},{2,18},{10... | collective-permute-start | bytes 786440 | tf_op jit(solution)/shard_map/ppermute | solution.py:25
  20.2 11.1 %collective-permute-start.3 = (bf16[512,256]{1,0:T(8,128)(2,1)S(1)}, bf16[512,256]{1,0:T(8,128)(2,1)S(1)}, u32[]{:S(2)}, u32[]{:S(2)}) collective-permute-start(bf16[512,256]{1,0:T(8,128)(2,1)S(1)} %get-tuple-element.274), channel_id=1, source_target_pairs={{0,24},{8,16},{16,8},{24,0},{1,25},{9,17},{17,9},{25,1},{2,26},{10... | collective-permute-start | bytes 786440 | tf_op jit(solution)/shard_map/ppermute | solution.py:25
  31.3 9.1 %collective-permute-start.4 = (bf16[128,1024]{0,1:T(8,128)(2,1)S(1)}, bf16[128,1024]{0,1:T(8,128)(2,1)S(1)}, u32[]{:S(2)}, u32[]{:S(2)}) collective-permute-start(bf16[128,1024]{0,1:T(8,128)(2,1)S(1)} %get-tuple-element.111), channel_id=1, source_target_pairs={{0,16},{8,24},{16,0},{24,8},{1,17},{9,25},{17,1},{25,9},{2,18},{10... | collective-permute-start | bytes 786440 | tf_op jit(solution)/shard_map/ppermute | solution.py:25
  40.3 25.5 %collective-permute-start.5 = (bf16[2048,256]{1,0:T(8,128)(2,1)}, bf16[2048,256]{1,0:T(8,128)(2,1)}, u32[]{:S(2)}, u32[]{:S(2)}) collective-permute-start(bf16[2048,256]{1,0:T(8,128)(2,1)} %pad_maximum_fusion.refs_4_), channel_id=1, source_target_pairs={{0,16},{8,24},{16,0},{24,8},{1,17},{9,25},{17,1},{25,9},{2,18},{10... | collective-permute-start | bytes 3145736 | tf_op jit(solution)/shard_map/ppermute | solution.py:25
  41.0 3.0 collective-permute-start.13
  51.1 36.6 %all-to-all-start.1 = ((bf16[4,640,256]{2,1,0:T(8,128)(2,1)}), bf16[4,640,256]{2,1,0:T(8,128)(2,1)S(1)}, u32[]{:S(2)}, u32[]{:S(2)}) async-start(bf16[4,640,256]{2,1,0:T(8,128)(2,1)} %broadcast_in_dim.5), calls=%async_computation.1 | async-start | bytes 2621440 | tf_op jit(solution)/shard_map/all_to_all | solution.py:92
  54.7 35.2 %copy-start.64 = (s32[4,128]{1,0:T(4,128)S(1)}, s32[4,128]{1,0:T(4,128)}, u32[]{:S(2)}) copy-start(s32[4,128]{1,0:T(4,128)} %param.17) | copy-start | bytes 6148
  54.7 118.8 %all-gather.5.cloned.1.call-start = ((), (), s32[]{:S(2)}) async-start(), calls=%async_computation.8 | async-start | bytes 4718592 | tf_op jit(solution)/shard_map/all_gather | solution.py:817
  54.7 30.5 %collective-permute-start = (bf16[4,656,256]{2,1,0:T(8,128)(2,1)S(1)}, bf16[4,656,256]{2,1,0:T(8,128)(2,1)S(1)}, u32[]{:S(2)}, u32[]{:S(2)}) collective-permute-start(bf16[4,656,256]{2,1,0:T(8,128)(2,1)S(1)} %all-to-all-done.refs_0_), channel_id=1, source_target_pairs={{0,1},{1,0},{2,3},{3,2},{4,5},{5,4},{6,7},{7,6},{8,9},{9,8},{10,11... | collective-permute-start | bytes 4030472 | tf_op jit(solution)/shard_map/ppermute | solution.py:29
  56.3 9.5 %collective-permute-start.1 = (bf16[2048,256]{1,0:T(8,128)(2,1)}, bf16[2048,256]{1,0:T(8,128)(2,1)S(1)}, u32[]{:S(2)}, u32[]{:S(2)}) collective-permute-start(bf16[2048,256]{1,0:T(8,128)(2,1)} %pad_maximum_fusion.refs_4_), channel_id=1, source_target_pairs={{0,8},{8,0},{16,24},{24,16},{1,9},{9,1},{17,25},{25,17},{2,10},{10... | collective-permute-start | bytes 3145736 | tf_op jit(solution)/shard_map/ppermute | solution.py:25
  65.8 2.9 collective-permute-start.6
  89.8 164.2 %all-gather.7.cloned.1.call-start = ((), (), s32[]{:S(2)}) async-start(), calls=%async_computation.9 | async-start | bytes 4718592 | tf_op jit(solution)/shard_map/all_gather | solution.py:818
  92.1 60.6 %copy-start.33 = (f32[512,256]{1,0:T(8,128)}, f32[512,256]{1,0:T(8,128)S(1)}, u32[]{:S(2)}) copy-start(f32[512,256]{1,0:T(8,128)S(1)} %get-tuple-element.310) | copy-start | bytes 1572868
  92.2 5.3 collective-permute-start.7
  95.6 6.3 %collective-permute-start.8 = (bf16[4,27,256]{2,1,0:T(8,128)(2,1)S(1)}, bf16[4,27,256]{2,1,0:T(8,128)(2,1)S(1)}, u32[]{:S(2)}, u32[]{:S(2)}) collective-permute-start(bf16[4,27,256]{2,1,0:T(8,128)(2,1)S(1)} %get-tuple-element.293), channel_id=1, source_target_pairs={{1,0},{2,1},{3,2},{4,3},{5,4},{6,5},{7,6},{9,8},{10,9},{11,10},{12... | collective-permute-start | bytes 165896 | tf_op jit(solution)/shard_map/ppermute | solution.py:764
  102.0 42.3 %collective-permute-start.14 = (bf16[4,640,256]{2,1,0:T(8,128)(2,1)S(1)}, bf16[4,640,256]{2,1,0:T(8,128)(2,1)S(1)}, u32[]{:S(2)}, u32[]{:S(2)}) collective-permute-start(bf16[4,640,256]{2,1,0:T(8,128)(2,1)S(1)} %all-to-all-done.1.refs_0_), channel_id=1, source_target_pairs={{0,1},{1,0},{2,3},{3,2},{4,5},{5,4},{6,7},{7,6},{8,9},{9,8},{10,11... | collective-permute-start | bytes 3932168 | tf_op jit(solution)/shard_map/ppermute | solution.py:29
  107.4 37.3 %copy-start.41 = (f32[512,1024]{1,0:T(8,128)}, f32[512,1024]{1,0:T(8,128)S(1)}, u32[]{:S(2)}) copy-start(f32[512,1024]{1,0:T(8,128)S(1)} %get-tuple-element.312) | copy-start | bytes 6291460
  107.4 1.9 collective-permute-start.10
  107.5 4.5 collective-permute-start.11
  109.2 4.4 collective-permute-start.9
  112.0 7.9 %collective-permute-start.12 = (bf16[128,1024]{1,0:T(8,128)(2,1)S(1)}, bf16[128,1024]{1,0:T(8,128)(2,1)S(1)}, u32[]{:S(2)}, u32[]{:S(2)}) collective-permute-start(bf16[128,1024]{1,0:T(8,128)(2,1)S(1)} %fusion.33), channel_id=1, source_target_pairs={{0,16},{8,24},{16,0},{24,8},{1,17},{9,25},{17,1},{25,9},{2,18},{10... | collective-permute-start | bytes 786440 | tf_op jit(solution)/shard_map/ppermute | solution.py:25
  144.7 6.4 %collective-permute-start.16 = (bf16[128,1024]{1,0:T(8,128)(2,1)S(1)}, bf16[128,1024]{1,0:T(8,128)(2,1)S(1)}, u32[]{:S(2)}, u32[]{:S(2)}) collective-permute-start(bf16[128,1024]{1,0:T(8,128)(2,1)S(1)} %multiply_convert_fusion), channel_id=1, source_target_pairs={{0,16},{8,24},{16,0},{24,8},{1,17},{9,25},{17,1},{25,9},{2,18},{10... | collective-permute-start | bytes 786440 | tf_op jit(solution)/shard_map/ppermute | solution.py:25
  146.3 4.8 collective-permute-start.15
  151.1 1.5 collective-permute-start.17
  160.0 14.8 %collective-permute-start.19 = (bf16[128,4096]{1,0:T(8,128)(2,1)}, bf16[128,4096]{1,0:T(8,128)(2,1)}, u32[]{:S(2)}, u32[]{:S(2)}) collective-permute-start(bf16[128,4096]{1,0:T(8,128)(2,1)} %get-tuple-element.251), channel_id=1, source_target_pairs={{0,8},{8,0},{16,24},{24,16},{1,9},{9,1},{17,25},{25,17},{2,10},{10... | collective-permute-start | bytes 3145736 | tf_op jit(solution)/shard_map/ppermute | solution.py:25
  173.5 33.4 %collective-permute-start.23 = (bf16[8,2,128,1024]{3,2,1,0:T(8,128)(2,1)}, bf16[8,2,128,1024]{3,2,1,0:T(8,128)(2,1)}, u32[]{:S(2)}, u32[]{:S(2)}) collective-permute-start(bf16[8,2,128,1024]{3,2,1,0:T(8,128)(2,1)} %bitcast.195), channel_id=1, source_target_pairs={{0,8},{8,0},{16,24},{24,16},{1,9},{9,1},{17,25},{25,17},{2,10},{10... | collective-permute-start | bytes 12582920 | tf_op jit(solution)/shard_map/ppermute | solution.py:25
  174.2 11.2 %collective-permute-start.18 = (bf16[128,4096]{1,0:T(8,128)(2,1)S(1)}, bf16[128,4096]{1,0:T(8,128)(2,1)S(1)}, u32[]{:S(2)}, u32[]{:S(2)}) collective-permute-start(bf16[128,4096]{1,0:T(8,128)(2,1)S(1)} %get-tuple-element.250), channel_id=1, source_target_pairs={{0,8},{8,0},{16,24},{24,16},{1,9},{9,1},{17,25},{25,17},{2,10},{10... | collective-permute-start | bytes 3145736 | tf_op jit(solution)/shard_map/ppermute | solution.py:25
  177.8 25.4 %collective-permute-start.20 = (bf16[128,4096]{1,0:T(8,128)(2,1)}, bf16[128,4096]{1,0:T(8,128)(2,1)}, u32[]{:S(2)}, u32[]{:S(2)}) collective-permute-start(bf16[128,4096]{1,0:T(8,128)(2,1)} %fusion.7), channel_id=1, source_target_pairs={{0,16},{8,24},{16,0},{24,8},{1,17},{9,25},{17,1},{25,9},{2,18},{10... | collective-permute-start | bytes 3145736 | tf_op jit(solution)/shard_map/ppermute | solution.py:25
  182.4 240.4 %reduce-scatter.3.cloned.1.call-start = ((), (), s32[]{:S(2)}) async-start(), calls=%async_computation.6 | async-start | bytes 4718592 | tf_op jit(solution)/shard_map/reduce_scatter | solution.py:871
  182.4 1.3 collective-permute-start.21
  183.8 1.3 collective-permute-start.22
  227.0 24.2 %collective-permute-start.25 = (bf16[512,1024]{1,0:T(8,128)(2,1)S(1)}, bf16[512,1024]{1,0:T(8,128)(2,1)S(1)}, u32[]{:S(2)}, u32[]{:S(2)}) collective-permute-start(bf16[512,1024]{1,0:T(8,128)(2,1)S(1)} %get-tuple-element.128.refs_0_), channel_id=1, source_target_pairs={{0,16},{8,24},{16,0},{24,8},{1,17},{9,25},{17,1},{25,9},{2,18},{10... | collective-permute-start | bytes 3145736 | tf_op jit(solution)/shard_map/ppermute | solution.py:25
  228.5 22.7 %collective-permute-start.24 = (bf16[512,1024]{1,0:T(8,128)(2,1)S(1)}, bf16[512,1024]{1,0:T(8,128)(2,1)S(1)}, u32[]{:S(2)}, u32[]{:S(2)}) collective-permute-start(bf16[512,1024]{1,0:T(8,128)(2,1)S(1)} %get-tuple-element.128.refs_0_), channel_id=1, source_target_pairs={{0,8},{8,0},{16,24},{24,16},{1,9},{9,1},{17,25},{25,17},{2,10},{10... | collective-permute-start | bytes 3145736 | tf_op jit(solution)/shard_map/ppermute | solution.py:25
  251.2 2.8 collective-permute-start.26
  284.2 6.8 %collective-permute-start.28 = (bf16[1024,1024]{1,0:T(8,128)(2,1)}, bf16[1024,1024]{1,0:T(8,128)(2,1)S(1)}, u32[]{:S(2)}, u32[]{:S(2)}) collective-permute-start(bf16[1024,1024]{1,0:T(8,128)(2,1)} %get-tuple-element.134), channel_id=1, source_target_pairs={{0,8},{8,0},{16,24},{24,16},{1,9},{9,1},{17,25},{25,17},{2,10},{10... | collective-permute-start | bytes 6291464 | tf_op jit(solution)/shard_map/ppermute | solution.py:25
  284.4 5.3 collective-permute-start.30
  294.3 25.8 %collective-permute-start.29 = (bf16[512,1024]{1,0:T(8,128)(2,1)}, bf16[512,1024]{1,0:T(8,128)(2,1)}, u32[]{:S(2)}, u32[]{:S(2)}) collective-permute-start(bf16[512,1024]{1,0:T(8,128)(2,1)} %add_convert_fusion.3), channel_id=1, source_target_pairs={{0,16},{8,24},{16,0},{24,8},{1,17},{9,25},{17,1},{25,9},{2,18},{10... | collective-permute-start | bytes 3145736 | tf_op jit(solution)/shard_map/ppermute | solution.py:25
  320.0 29.8 %collective-permute-start.31 = (bf16[4,512,256]{2,1,0:T(8,128)(2,1)}, bf16[4,512,256]{2,1,0:T(8,128)(2,1)}, u32[]{:S(2)}, u32[]{:S(2)}) collective-permute-start(bf16[4,512,256]{2,1,0:T(8,128)(2,1)} %fusion.9), channel_id=1, source_target_pairs={{0,16},{8,24},{16,0},{24,8},{1,17},{9,25},{17,1},{25,9},{2,18},{10... | collective-permute-start | bytes 3145736 | tf_op jit(solution)/shard_map/ppermute | solution.py:25
  321.6 199.7 %reduce-scatter.5.cloned.1.call-start = ((), (), s32[]{:S(2)}) async-start(), calls=%async_computation.7 | async-start | bytes 4718592 | tf_op jit(solution)/shard_map/reduce_scatter | solution.py:895
  349.8 24.1 %collective-permute-start.34 = (bf16[128,4096]{1,0:T(8,128)(2,1)S(1)}, bf16[128,4096]{1,0:T(8,128)(2,1)S(1)}, u32[]{:S(2)}, u32[]{:S(2)}) collective-permute-start(bf16[128,4096]{1,0:T(8,128)(2,1)S(1)} %get-tuple-element.172), channel_id=1, source_target_pairs={{0,16},{8,24},{16,0},{24,8},{1,17},{9,25},{17,1},{25,9},{2,18},{10... | collective-permute-start | bytes 3145736 | tf_op jit(solution)/shard_map/ppermute | solution.py:25
  373.9 2.7 collective-permute-start.35
  373.9 5.7 %collective-permute-start.36 = (bf16[128,4096]{1,0:T(8,128)(2,1)S(1)}, bf16[128,4096]{1,0:T(8,128)(2,1)S(1)}, u32[]{:S(2)}, u32[]{:S(2)}) collective-permute-start(bf16[128,4096]{1,0:T(8,128)(2,1)S(1)} %collective-permute-done.34), channel_id=1, source_target_pairs={{0,8},{8,0},{16,24},{24,16},{1,9},{9,1},{17,25},{25,17},{2,10},{10... | collective-permute-start | bytes 3145736 | tf_op jit(solution)/shard_map/ppermute | solution.py:25
  374.4 14.6 %collective-permute-start.39 = (bf16[8,2,128,1024]{3,2,1,0:T(8,128)(2,1)}, bf16[8,2,128,1024]{3,2,1,0:T(8,128)(2,1)S(1)}, u32[]{:S(2)}, u32[]{:S(2)}) collective-permute-start(bf16[8,2,128,1024]{3,2,1,0:T(8,128)(2,1)} %get-tuple-element.175), channel_id=1, source_target_pairs={{0,8},{8,0},{16,24},{24,16},{1,9},{9,1},{17,25},{25,17},{2,10},{10... | collective-permute-start | bytes 12582920 | tf_op jit(solution)/shard_map/ppermute | solution.py:25
  385.4 1.9 collective-permute-start.38
  385.9 36.8 %collective-permute-start.41 = (bf16[4,640,256]{2,1,0:T(8,128)(2,1)S(1)}, bf16[4,640,256]{2,1,0:T(8,128)(2,1)}, u32[]{:S(2)}, u32[]{:S(2)}) collective-permute-start(bf16[4,640,256]{2,1,0:T(8,128)(2,1)S(1)} %get-tuple-element.180), channel_id=1, source_target_pairs={{0,1},{1,0},{2,3},{3,2},{4,5},{5,4},{6,7},{7,6},{8,9},{9,8},{10,11... | collective-permute-start | bytes 3932168 | tf_op jit(solution)/shard_map/ppermute | solution.py:29
  394.2 3.4 collective-permute-start.37
  394.5 8.7 %collective-permute-start.40 = (bf16[128,1024]{1,0:T(8,128)(2,1)}, bf16[128,1024]{1,0:T(8,128)(2,1)S(1)}, u32[]{:S(2)}, u32[]{:S(2)}) collective-permute-start(bf16[128,1024]{1,0:T(8,128)(2,1)} %fusion.31), channel_id=1, source_target_pairs={{0,16},{8,24},{16,0},{24,8},{1,17},{9,25},{17,1},{25,9},{2,18},{10... | collective-permute-start | bytes 786440 | tf_op jit(solution)/shard_map/ppermute | solution.py:25
  395.6 27.7 %collective-permute-start.33 = (bf16[128,256]{1,0:T(8,128)(2,1)}, bf16[128,256]{1,0:T(8,128)(2,1)}, u32[]{:S(2)}, u32[]{:S(2)}) collective-permute-start(bf16[128,256]{1,0:T(8,128)(2,1)} %bitcast.56), channel_id=1, source_target_pairs={{0,8},{8,0},{16,24},{24,16},{1,9},{9,1},{17,25},{25,17},{2,10},{10... | collective-permute-start | bytes 196616 | tf_op jit(solution)/shard_map/ppermute | solution.py:25
  396.4 35.8 %collective-permute-start.50 = (bf16[128,256]{1,0:T(8,128)(2,1)S(1)}, bf16[128,256]{1,0:T(8,128)(2,1)S(1)}, u32[]{:S(2)}, u32[]{:S(2)}) collective-permute-start(bf16[128,256]{1,0:T(8,128)(2,1)S(1)} %bitcast.187), channel_id=1, source_target_pairs={{0,8},{8,0},{16,24},{24,16},{1,9},{9,1},{17,25},{25,17},{2,10},{10... | collective-permute-start | bytes 196616 | tf_op jit(solution)/shard_map/ppermute | solution.py:25
  422.8 9.4 %collective-permute-start.46 = (bf16[128,1024]{1,0:T(8,128)(2,1)}, bf16[128,1024]{1,0:T(8,128)(2,1)S(1)}, u32[]{:S(2)}, u32[]{:S(2)}) collective-permute-start(bf16[128,1024]{1,0:T(8,128)(2,1)} %fusion.22), channel_id=1, source_target_pairs={{0,8},{8,0},{16,24},{24,16},{1,9},{9,1},{17,25},{25,17},{2,10},{10... | collective-permute-start | bytes 786440 | tf_op jit(solution)/shard_map/ppermute | solution.py:25
  422.8 8.9 %collective-permute-start.42 = (bf16[128,1024]{1,0:T(8,128)(2,1)}, bf16[128,1024]{1,0:T(8,128)(2,1)S(1)}, u32[]{:S(2)}, u32[]{:S(2)}) collective-permute-start(bf16[128,1024]{1,0:T(8,128)(2,1)} %fusion.22), channel_id=1, source_target_pairs={{0,16},{8,24},{16,0},{24,8},{1,17},{9,25},{17,1},{25,9},{2,18},{10... | collective-permute-start | bytes 786440 | tf_op jit(solution)/shard_map/ppermute | solution.py:25
  431.7 4.3 collective-permute-start.43
  432.2 4.7 collective-permute-start.47
  438.1 7.7 %collective-permute-start.48 = (bf16[4,27,256]{2,1,0:T(8,128)(2,1)S(1)}, bf16[4,27,256]{2,1,0:T(8,128)(2,1)S(1)}, u32[]{:S(2)}, u32[]{:S(2)}) collective-permute-start(bf16[4,27,256]{2,1,0:T(8,128)(2,1)S(1)} %get-tuple-element.283), channel_id=1, source_target_pairs={{1,0},{2,1},{3,2},{4,3},{5,4},{6,5},{7,6},{9,8},{10,9},{11,10},{12... | collective-permute-start | bytes 165896 | tf_op jit(solution)/shard_map/ppermute | solution.py:764
  439.5 7.3 %collective-permute-start.49 = (bf16[4,27,256]{2,1,0:T(8,128)(2,1)S(1)}, bf16[4,27,256]{2,1,0:T(8,128)(2,1)S(1)}, u32[]{:S(2)}, u32[]{:S(2)}) collective-permute-start(bf16[4,27,256]{2,1,0:T(8,128)(2,1)S(1)} %get-tuple-element.282), channel_id=1, source_target_pairs={{0,1},{1,2},{2,3},{3,4},{4,5},{5,6},{6,7},{8,9},{9,10},{10,11},{11... | collective-permute-start | bytes 165896 | tf_op jit(solution)/shard_map/ppermute | solution.py:763
  453.1 50.6 %all-to-all-start.3 = ((bf16[4,640,256]{2,1,0:T(8,128)(2,1)}), bf16[4,640,256]{2,1,0:T(8,128)(2,1)S(1)}, u32[]{:S(2)}, u32[]{:S(2)}) async-start(bf16[4,640,256]{2,1,0:T(8,128)(2,1)} %add_convert_fusion.2), calls=%async_computation.4 | async-start | bytes 2621440 | tf_op jit(solution)/shard_map/all_to_all | solution.py:92
  460.4 42.0 %collective-permute-start.51 = (bf16[4,656,256]{2,1,0:T(8,128)(2,1)}, bf16[4,656,256]{2,1,0:T(8,128)(2,1)S(1)}, u32[]{:S(2)}, u32[]{:S(2)}) collective-permute-start(bf16[4,656,256]{2,1,0:T(8,128)(2,1)} %copy-done.6), channel_id=1, source_target_pairs={{0,1},{1,0},{2,3},{3,2},{4,5},{5,4},{6,7},{7,6},{8,9},{9,8},{10,11... | collective-permute-start | bytes 4030472 | tf_op jit(solution)/shard_map/ppermute | solution.py:29
  460.4 2.9 collective-permute-start.27
  460.4 3.9 collective-permute-start.32
  460.9 8.4 %collective-permute-start.45 = (bf16[512,256]{1,0:T(8,128)(2,1)S(1)}, bf16[512,256]{1,0:T(8,128)(2,1)S(1)}, u32[]{:S(2)}, u32[]{:S(2)}) collective-permute-start(bf16[512,256]{1,0:T(8,128)(2,1)S(1)} %get-tuple-element.186), channel_id=1, source_target_pairs={{0,24},{8,16},{16,8},{24,0},{1,25},{9,17},{17,9},{25,1},{2,26},{10... | collective-permute-start | bytes 786440 | tf_op jit(solution)/shard_map/ppermute | solution.py:25
  461.2 13.9 %collective-permute-start.44 = (bf16[512,256]{1,0:T(8,128)(2,1)S(1)}, bf16[512,256]{1,0:T(8,128)(2,1)S(1)}, u32[]{:S(2)}, u32[]{:S(2)}) collective-permute-start(bf16[512,256]{1,0:T(8,128)(2,1)S(1)} %get-tuple-element.184), channel_id=1, source_target_pairs={{0,16},{8,24},{16,0},{24,8},{1,17},{9,25},{17,1},{25,9},{2,18},{10... | collective-permute-start | bytes 786440 | tf_op jit(solution)/shard_map/ppermute | solution.py:25
  503.7 38.2 %all-to-all-start.2 = ((bf16[4,656,256]{2,1,0:T(8,128)(2,1)}), bf16[4,656,256]{2,1,0:T(8,128)(2,1)S(1)}, u32[]{:S(2)}, u32[]{:S(2)}) async-start(bf16[4,656,256]{2,1,0:T(8,128)(2,1)} %add_convert_fusion.1), calls=%async_computation.3 | async-start | bytes 2686976 | tf_op jit(solution)/shard_map/all_to_all | solution.py:92
  522.3 21.9 %collective-permute-start.52 = (bf16[128,1024]{1,0:T(8,128)(2,1)S(1)}, bf16[128,1024]{1,0:T(8,128)(2,1)S(1)}, u32[]{:S(2)}, u32[]{:S(2)}) collective-permute-start(bf16[128,1024]{1,0:T(8,128)(2,1)S(1)} %slice_bitcast_fusion), channel_id=1, source_target_pairs={{0,16},{8,24},{16,0},{24,8},{1,17},{9,25},{17,1},{25,9},{2,18},{10... | collective-permute-start | bytes 786440 | tf_op jit(solution)/shard_map/ppermute | solution.py:25
  (70 other events, 445.7 us)
Sparse Core Ops, SparseCore 0:
  89.9 83.5 all-gather.4
  182.5 71.2 all-gather.6
  321.7 90.4 reduce-scatter.2
  416.1 105.1 reduce-scatter.4

commit v8 on v7

--- a/solution.py
+++ b/solution.py
@@ -74,7 +74,7 @@
 
 
 def cost(us):
-    return pl.CostEstimate(flops=int(us * 1.76e9), transcendentals=0, bytes_accessed=0)
+    return pl.CostEstimate(flops=int(us * 1.5e9), transcendentals=0, bytes_accessed=0)
 
 
 CELL = 256

time: 561 us -> 560 us (level)
    unnamed x169 -> x165, local copies, waits for them, and re-layouts: 23.1 us -> 23.5 us
where the time goes in v8:
time: 560 us; the launch traced here: 552 us
  waiting for transfers between devices  278 us (50%)
  Pallas kernels  102 us (18%)
  starting transfers between devices  65.7 us (12%)
  local copies, waits for them, and re-layouts  39.9 us (7%)
  other arithmetic  34.6 us (6%)
  matrix products  16.4 us (3%)
  between operations  15.3 us (3%)
    ppermute x45, waiting for transfers between devices, swap(): return lax.ppermute(x, 'cond', [(i, i ^ j) for i in range(4)])  155 us
    ppermute x4, waiting for transfers between devices, hop(): return lax.ppermute(x, 'seq', [(i, i ^ k) for i in range(8)])  78.4 us
    pallas_call x2, Pallas kernels, layer_call(): pl.pallas_call(body, out_shape=[space(shape, dtype) for space, shape, dty...  43.6 us
    pallas_call x1, Pallas kernels, mlp(): pl.pallas_call(mlp_body, out_shape=[shape((rows, hidden), BF16), shape((r...  30.2 us
    ppermute x45, starting transfers between devices, swap(): return lax.ppermute(x, 'cond', [(i, i ^ j) for i in range(4)])  25.1 us
    all_to_all x4, waiting for transfers between devices, along_z(): return lax.all_to_all(x, 'seq', 0, 0, axis_index_groups=ALONG_Z, tiled=True)  25 us
    all_to_all x4, starting transfers between devices, along_z(): return lax.all_to_all(x, 'seq', 0, 0, axis_index_groups=ALONG_Z, tiled=True)  23.9 us
    unnamed x165, local copies, waits for them, and re-layouts  23.5 us
  transfers between devices with their start and end apart: 61, of which 38 were waited for; matrix products, arithmetic and copies ran while one was open for 12% of the time, Pallas kernels for 13%

profile of v8, /device:TPU:0, one launch (start us, length us, event | category | flops | bytes accessed | tf_op | source)
XLA Modules:
  0.0 551.6 jit_solution(4483951296445233548)
XLA Ops:
  11.3 6.4 %all-to-all-start = ((bf16[4,656,256]{2,1,0:T(8,128)(2,1)}), bf16[4,656,256]{2,1,0:T(8,128)(2,1)S(1)}, u32[]{:S(2)}, u32[]{:S(2)}) async-start(bf16[4,656,256]{2,1,0:T(8,128)(2,1)} %broadcast_in_dim.4), calls=%async_computation | async-start | bytes 2686976 | tf_op jit(solution)/shard_map/all_to_all | solution.py:92
  18.6 1.5 collective-permute-start.2
  21.3 6.8 %collective-permute-done.2.q2 = bf16[512,256]{1,0:T(8,128)(2,1)S(1)} collective-permute-done((bf16[512,256]{1,0:T(8,128)(2,1)}, bf16[512,256]{1,0:T(8,128)(2,1)S(1)}, u32[]{:S(2)}, u32[]{:S(2)}) %collective-permute-start.2) | collective-permute-done | bytes 262176 | tf_op jit(solution)/shard_map/ppermute | solution.py:25
  28.1 3.2 collective-permute-done.3.q3
  34.6 5.7 %collective-permute-done.4 = bf16[128,1024]{0,1:T(8,128)(2,1)S(1)} collective-permute-done((bf16[128,1024]{0,1:T(8,128)(2,1)S(1)}, bf16[128,1024]{0,1:T(8,128)(2,1)S(1)}, u32[]{:S(2)}, u32[]{:S(2)}) %collective-permute-start.4) | collective-permute-done | bytes 262176 | tf_op jit(solution)/shard_map/ppermute | solution.py:25
  42.3 1.8 pad_maximum_fusion.4
  44.1 5.7 %all-to-all-done.refs_0_ = bf16[4,656,256]{2,1,0:T(8,128)(2,1)S(1)} async-done(((bf16[4,656,256]{2,1,0:T(8,128)(2,1)}), bf16[4,656,256]{2,1,0:T(8,128)(2,1)S(1)}, u32[]{:S(2)}, u32[]{:S(2)}) %all-to-all-start) | async-done | bytes 1343520 | tf_op jit(solution)/shard_map/all_to_all | solution.py:92
  51.1 3.5 all-to-all-start.1
  54.7 1.6 collective-permute-start
  56.3 9.5 %collective-permute-done.5.refs_6_ = bf16[2048,256]{1,0:T(8,128)(2,1)} collective-permute-done((bf16[2048,256]{1,0:T(8,128)(2,1)}, bf16[2048,256]{1,0:T(8,128)(2,1)}, u32[]{:S(2)}, u32[]{:S(2)}) %collective-permute-start.5) | collective-permute-done | bytes 1048608 | tf_op jit(solution)/shard_map/ppermute | solution.py:25
  65.8 2.9 collective-permute-done.6.refs_7_
  69.7 15.6 %collective-permute-done.refs_1_ = bf16[4,656,256]{2,1,0:T(8,128)(2,1)S(1)} collective-permute-done((bf16[4,656,256]{2,1,0:T(8,128)(2,1)S(1)}, bf16[4,656,256]{2,1,0:T(8,128)(2,1)S(1)}, u32[]{:S(2)}, u32[]{:S(2)}) %collective-permute-start) | collective-permute-done | bytes 1343520 | tf_op jit(solution)/shard_map/ppermute | solution.py:29
  87.8 2.0 copy.90
  90.0 2.1 multiply_convert_fusion.1
  92.2 3.4 collective-permute-start.7
  97.5 4.4 collective-permute-done.8
  102.0 4.3 collective-permute-start.14
  107.5 1.7 collective-permute-start.11
  109.5 2.6 collective-permute-done.11
  112.1 1.6 collective-permute-start.12
  113.7 6.3 %collective-permute-done.12 = bf16[128,1024]{1,0:T(8,128)(2,1)S(1)} collective-permute-done((bf16[128,1024]{1,0:T(8,128)(2,1)S(1)}, bf16[128,1024]{1,0:T(8,128)(2,1)S(1)}, u32[]{:S(2)}, u32[]{:S(2)}) %collective-permute-start.12) | collective-permute-done | bytes 262176 | tf_op jit(solution)/shard_map/ppermute | solution.py:25
  120.7 23.7 %collective-permute-done.14.refs_1_ = bf16[4,640,256]{2,1,0:T(8,128)(2,1)S(1)} collective-permute-done((bf16[4,640,256]{2,1,0:T(8,128)(2,1)S(1)}, bf16[4,640,256]{2,1,0:T(8,128)(2,1)S(1)}, u32[]{:S(2)}, u32[]{:S(2)}) %collective-permute-start.14) | collective-permute-done | bytes 1310752 | tf_op jit(solution)/shard_map/ppermute | solution.py:29
  144.7 1.6 collective-permute-start.16
  146.4 4.8 collective-permute-done.16
  154.2 4.7 fusion.100
  160.1 13.4 %all-gather.5.cloned.1.call-done = bf16[16,128,1024]{2,1,0:T(8,128)(2,1)} async-done(((bf16[2,128,1024]{2,1,0:T(8,128)(2,1)}), bf16[16,128,1024]{2,1,0:T(8,128)(2,1)}) %all-gather.5.cloned.1.call-update) | async-done | bytes 4194320 | tf_op jit(solution)/shard_map/all_gather | solution.py:817
  175.1 3.0 fusion.7
  178.2 1.5 collective-permute-start.20
  180.7 1.6 collective-permute-done.21
  184.0 19.6 %collective-permute-done.20 = bf16[128,4096]{1,0:T(8,128)(2,1)} collective-permute-done((bf16[128,4096]{1,0:T(8,128)(2,1)}, bf16[128,4096]{1,0:T(8,128)(2,1)}, u32[]{:S(2)}, u32[]{:S(2)}) %collective-permute-start.20) | collective-permute-done | bytes 1048608 | tf_op jit(solution)/shard_map/ppermute | solution.py:25
  203.6 2.2 fusion.8.up_ref
  205.8 1.5 enter.1.refs_2_
  207.3 19.1 %layer_forward.1 = (bf16[512,1024]{1,0:T(8,128)(2,1)}, f32[512,1024]{1,0:T(8,128)S(1)}, bf16[512,1024]{1,0:T(8,128)(2,1)S(1)}, bf16[512,768]{1,0:T(8,128)(2,1)},...) custom-call(s32[512,1]{1,0:T(8,128)S(1)} %copy.91.refs_0_, ...), custom_call_target="tpu_custom_call" | custom-call | flops 27000000512 | tf_op jit(solution)/shard_map/layer_forward/pallas_call | solution.py:472
  227.8 1.6 collective-permute-start.25
  229.4 22.7 %collective-permute-done.25.refs_2_ = bf16[512,1024]{1,0:T(8,128)(2,1)S(1)} collective-permute-done((bf16[512,1024]{1,0:T(8,128)(2,1)S(1)}, bf16[512,1024]{1,0:T(8,128)(2,1)S(1)}, u32[]{:S(2)}, u32[]{:S(2)}) %collective-permute-start.25) | collective-permute-done | bytes 1048608 | tf_op jit(solution)/shard_map/ppermute | solution.py:25
  253.2 1.7 collective-permute-done.26.refs_3_
  254.9 30.2 %mlp.1 = (bf16[2048,1024]{1,0:T(8,128)(2,1)}, bf16[2048,1024]{1,0:T(8,128)(2,1)}, bf16[2048,1024]{1,0:T(8,128)(2,1)}, bf16[2048,1024]{1,0:T(8,128)(2,1)}, bf16[2...) custom-call(s32[4]{0:T(128)S(1)} %iota_xor_fusion.index, ...), custom_call_target="tpu_custom_call" | custom-call | flops 44999999488 | tf_op jit(solution)/shard_map/mlp/pallas_call | solution.py:684
  285.7 4.9 collective-permute-done.30
  291.1 2.5 copy-done.40
  296.4 14.7 %mlp_grads.1 = bf16[8,2,128,1024]{3,2,1,0:T(8,128)(2,1)} custom-call(bf16[2048,1024]{1,0:T(8,128)(2,1)S(1)} %copy-done.18, bf16[2048,1024]{1,0:T(8,128)(2,1)} %get-tuple-element.138.cot_ref, bf16[2048,1024]{1,0:T(8,128)(2,1)} %get-tuple-element.139.act_ref, bf16[2048,1024]{1,0:T(8,128)(2,1)} %get-tuple-element.140.grad_ref), custom_call_target="tpu_custom_call" | custom-call | flops 20999999488 | tf_op jit(solution)/shard_map/mlp_grads/pallas_call | solution.py:732
  311.0 9.6 %collective-permute-done.29.refs_7_ = bf16[512,1024]{1,0:T(8,128)(2,1)} collective-permute-done((bf16[512,1024]{1,0:T(8,128)(2,1)}, bf16[512,1024]{1,0:T(8,128)(2,1)}, u32[]{:S(2)}, u32[]{:S(2)}) %collective-permute-start.29) | collective-permute-done | bytes 1048608 | tf_op jit(solution)/shard_map/ppermute | solution.py:25
  323.3 24.6 %layer_backward.1 = (bf16[512,1024]{1,0:T(8,128)(2,1)}, f32[512,1024]{1,0:T(8,128)}, f32[8,1024]{1,0:T(8,128)S(1)}, bf16[512,768]{1,0:T(8,128)(2,1)S(1)}, bf16[5...) custom-call(s32[512,1]{1,0:T(8,128)S(1)} %copy.91.refs_0_, ...), custom_call_target="tpu_custom_call" | custom-call | flops 35999997952 | tf_op jit(solution)/shard_map/layer_backward/pallas_call | solution.py:472
  347.9 1.6 copy-done.17
  352.2 7.5 %layer_grads.1 = (bf16[8,2,128,1024]{3,2,1,0:T(8,128)(2,1)}, bf16[8,2,128,1024]{3,2,1,0:T(8,128)(2,1)}) custom-call(bf16[512,1024]{1,0:T(8,128)(2,1)S(1)} %copy-done.19, bf16[512,1024]{1,0:T(8,128)(2,1)} %get-tuple-element.161.att_ref, bf16[512,768]{1,0:T(8,128)(2,1)S(1)} %get-tuple-element.163.refs_0_, bf16[512,768]{1,0:T(8,128)(2,1)S(1)} %get-tuple-element.164.refs_1_, ...), custom_call_target="tpu_custom_call" | custom-call | flops 12000000000 | tf_op jit(solution)/shard_map/layer_grads/pallas_call | solution.py:555
  359.6 16.2 %collective-permute-done.34 = bf16[128,4096]{1,0:T(8,128)(2,1)S(1)} collective-permute-done((bf16[128,4096]{1,0:T(8,128)(2,1)S(1)}, bf16[128,4096]{1,0:T(8,128)(2,1)S(1)}, u32[]{:S(2)}, u32[]{:S(2)}) %collective-permute-start.34) | collective-permute-done | bytes 1048608 | tf_op jit(solution)/shard_map/ppermute | solution.py:25
  376.4 3.5 collective-permute-done.35
  380.2 2.8 collective-permute-done.36
  383.1 2.1 fusion.101
  390.7 1.7 fusion.31
  392.4 4.3 add_convert_fusion
  400.8 5.8 %collective-permute-done.40 = bf16[128,1024]{1,0:T(8,128)(2,1)S(1)} collective-permute-done((bf16[128,1024]{1,0:T(8,128)(2,1)}, bf16[128,1024]{1,0:T(8,128)(2,1)S(1)}, u32[]{:S(2)}, u32[]{:S(2)}) %collective-permute-start.40) | collective-permute-done | bytes 262176 | tf_op jit(solution)/shard_map/ppermute | solution.py:25
  406.7 2.4 fusion.22
  409.1 14.1 %collective-permute-done.41 = bf16[4,640,256]{2,1,0:T(8,128)(2,1)} collective-permute-done((bf16[4,640,256]{2,1,0:T(8,128)(2,1)S(1)}, bf16[4,640,256]{2,1,0:T(8,128)(2,1)}, u32[]{:S(2)}, u32[]{:S(2)}) %collective-permute-start.41) | collective-permute-done | bytes 1310752 | tf_op jit(solution)/shard_map/ppermute | solution.py:29
  423.2 1.5 collective-permute-start.42
  426.6 5.5 collective-permute-done.42
  433.6 2.7 collective-permute-done.43
  439.9 4.5 collective-permute-start.49
  450.2 2.7 add_convert_fusion.2
  452.9 9.3 %all-to-all-start.3 = ((bf16[4,640,256]{2,1,0:T(8,128)(2,1)}), bf16[4,640,256]{2,1,0:T(8,128)(2,1)S(1)}, u32[]{:S(2)}, u32[]{:S(2)}) async-start(bf16[4,640,256]{2,1,0:T(8,128)(2,1)} %add_convert_fusion.2), calls=%async_computation.4 | async-start | bytes 2621440 | tf_op jit(solution)/shard_map/all_to_all | solution.py:92
  465.1 6.0 %collective-permute-done.45 = bf16[512,256]{1,0:T(8,128)(2,1)S(1)} collective-permute-done((bf16[512,256]{1,0:T(8,128)(2,1)S(1)}, bf16[512,256]{1,0:T(8,128)(2,1)S(1)}, u32[]{:S(2)}, u32[]{:S(2)}) %collective-permute-start.45) | collective-permute-done | bytes 262176 | tf_op jit(solution)/shard_map/ppermute | solution.py:25
  471.0 5.9 %collective-permute-done.44 = bf16[512,256]{1,0:T(8,128)(2,1)S(1)} collective-permute-done((bf16[512,256]{1,0:T(8,128)(2,1)S(1)}, bf16[512,256]{1,0:T(8,128)(2,1)S(1)}, u32[]{:S(2)}, u32[]{:S(2)}) %collective-permute-start.44) | collective-permute-done | bytes 262176 | tf_op jit(solution)/shard_map/ppermute | solution.py:25
  477.6 25.0 %collective-permute-done.51 = bf16[4,656,256]{2,1,0:T(8,128)(2,1)S(1)} collective-permute-done((bf16[4,656,256]{2,1,0:T(8,128)(2,1)}, bf16[4,656,256]{2,1,0:T(8,128)(2,1)S(1)}, u32[]{:S(2)}, u32[]{:S(2)}) %collective-permute-start.51) | collective-permute-done | bytes 1343520 | tf_op jit(solution)/shard_map/ppermute | solution.py:29
  504.1 4.6 all-to-all-start.2
  521.4 19.3 %all-to-all-done.2.refs_0_ = bf16[4,656,256]{2,1,0:T(8,128)(2,1)S(1)} async-done(((bf16[4,656,256]{2,1,0:T(8,128)(2,1)}), bf16[4,656,256]{2,1,0:T(8,128)(2,1)S(1)}, u32[]{:S(2)}, u32[]{:S(2)}) %all-to-all-start.2) | async-done | bytes 1343520 | tf_op jit(solution)/shard_map/all_to_all | solution.py:92
  (340 shorter events, 85.4 us)
Async XLA Ops:
  11.3 38.5 %all-to-all-start = ((bf16[4,656,256]{2,1,0:T(8,128)(2,1)}), bf16[4,656,256]{2,1,0:T(8,128)(2,1)S(1)}, u32[]{:S(2)}, u32[]{:S(2)}) async-start(bf16[4,656,256]{2,1,0:T(8,128)(2,1)} %broadcast_in_dim.4), calls=%async_computation | async-start | bytes 2686976 | tf_op jit(solution)/shard_map/all_to_all | solution.py:92
  18.6 9.4 %collective-permute-start.2 = (bf16[512,256]{1,0:T(8,128)(2,1)}, bf16[512,256]{1,0:T(8,128)(2,1)S(1)}, u32[]{:S(2)}, u32[]{:S(2)}) collective-permute-start(bf16[512,256]{1,0:T(8,128)(2,1)} %get-tuple-element.273), channel_id=1, source_target_pairs={{0,16},{8,24},{16,0},{24,8},{1,17},{9,25},{17,1},{25,9},{2,18},{10... | collective-permute-start | bytes 786440 | tf_op jit(solution)/shard_map/ppermute | solution.py:25
  20.2 11.1 %collective-permute-start.3 = (bf16[512,256]{1,0:T(8,128)(2,1)S(1)}, bf16[512,256]{1,0:T(8,128)(2,1)S(1)}, u32[]{:S(2)}, u32[]{:S(2)}) collective-permute-start(bf16[512,256]{1,0:T(8,128)(2,1)S(1)} %get-tuple-element.274), channel_id=1, source_target_pairs={{0,24},{8,16},{16,8},{24,0},{1,25},{9,17},{17,9},{25,1},{2,26},{10... | collective-permute-start | bytes 786440 | tf_op jit(solution)/shard_map/ppermute | solution.py:25
  31.3 9.1 %collective-permute-start.4 = (bf16[128,1024]{0,1:T(8,128)(2,1)S(1)}, bf16[128,1024]{0,1:T(8,128)(2,1)S(1)}, u32[]{:S(2)}, u32[]{:S(2)}) collective-permute-start(bf16[128,1024]{0,1:T(8,128)(2,1)S(1)} %get-tuple-element.111), channel_id=1, source_target_pairs={{0,16},{8,24},{16,0},{24,8},{1,17},{9,25},{17,1},{25,9},{2,18},{10... | collective-permute-start | bytes 786440 | tf_op jit(solution)/shard_map/ppermute | solution.py:25
  40.3 25.5 %collective-permute-start.5 = (bf16[2048,256]{1,0:T(8,128)(2,1)}, bf16[2048,256]{1,0:T(8,128)(2,1)}, u32[]{:S(2)}, u32[]{:S(2)}) collective-permute-start(bf16[2048,256]{1,0:T(8,128)(2,1)} %pad_maximum_fusion.refs_4_), channel_id=1, source_target_pairs={{0,16},{8,24},{16,0},{24,8},{1,17},{9,25},{17,1},{25,9},{2,18},{10... | collective-permute-start | bytes 3145736 | tf_op jit(solution)/shard_map/ppermute | solution.py:25
  41.0 3.0 collective-permute-start.13
  51.1 36.6 %all-to-all-start.1 = ((bf16[4,640,256]{2,1,0:T(8,128)(2,1)}), bf16[4,640,256]{2,1,0:T(8,128)(2,1)S(1)}, u32[]{:S(2)}, u32[]{:S(2)}) async-start(bf16[4,640,256]{2,1,0:T(8,128)(2,1)} %broadcast_in_dim.5), calls=%async_computation.1 | async-start | bytes 2621440 | tf_op jit(solution)/shard_map/all_to_all | solution.py:92
  54.7 35.2 %copy-start.62 = (s32[4,128]{1,0:T(4,128)S(1)}, s32[4,128]{1,0:T(4,128)}, u32[]{:S(2)}) copy-start(s32[4,128]{1,0:T(4,128)} %param.17) | copy-start | bytes 6148
  54.7 118.8 %all-gather.5.cloned.1.call-start = ((), (), s32[]{:S(2)}) async-start(), calls=%async_computation.8 | async-start | bytes 4718592 | tf_op jit(solution)/shard_map/all_gather | solution.py:817
  54.7 30.5 %collective-permute-start = (bf16[4,656,256]{2,1,0:T(8,128)(2,1)S(1)}, bf16[4,656,256]{2,1,0:T(8,128)(2,1)S(1)}, u32[]{:S(2)}, u32[]{:S(2)}) collective-permute-start(bf16[4,656,256]{2,1,0:T(8,128)(2,1)S(1)} %all-to-all-done.refs_0_), channel_id=1, source_target_pairs={{0,1},{1,0},{2,3},{3,2},{4,5},{5,4},{6,7},{7,6},{8,9},{9,8},{10,11... | collective-permute-start | bytes 4030472 | tf_op jit(solution)/shard_map/ppermute | solution.py:29
  56.3 9.5 %collective-permute-start.1 = (bf16[2048,256]{1,0:T(8,128)(2,1)}, bf16[2048,256]{1,0:T(8,128)(2,1)S(1)}, u32[]{:S(2)}, u32[]{:S(2)}) collective-permute-start(bf16[2048,256]{1,0:T(8,128)(2,1)} %pad_maximum_fusion.refs_4_), channel_id=1, source_target_pairs={{0,8},{8,0},{16,24},{24,16},{1,9},{9,1},{17,25},{25,17},{2,10},{10... | collective-permute-start | bytes 3145736 | tf_op jit(solution)/shard_map/ppermute | solution.py:25
  65.8 2.9 collective-permute-start.6
  89.8 165.1 %all-gather.7.cloned.1.call-start = ((), (), s32[]{:S(2)}) async-start(), calls=%async_computation.9 | async-start | bytes 4718592 | tf_op jit(solution)/shard_map/all_gather | solution.py:818
  92.1 60.6 %copy-start.31 = (f32[512,256]{1,0:T(8,128)}, f32[512,256]{1,0:T(8,128)S(1)}, u32[]{:S(2)}) copy-start(f32[512,256]{1,0:T(8,128)S(1)} %get-tuple-element.310) | copy-start | bytes 1572868
  92.2 5.3 collective-permute-start.7
  95.6 6.3 %collective-permute-start.8 = (bf16[4,27,256]{2,1,0:T(8,128)(2,1)S(1)}, bf16[4,27,256]{2,1,0:T(8,128)(2,1)S(1)}, u32[]{:S(2)}, u32[]{:S(2)}) collective-permute-start(bf16[4,27,256]{2,1,0:T(8,128)(2,1)S(1)} %get-tuple-element.293), channel_id=1, source_target_pairs={{1,0},{2,1},{3,2},{4,3},{5,4},{6,5},{7,6},{9,8},{10,9},{11,10},{12... | collective-permute-start | bytes 165896 | tf_op jit(solution)/shard_map/ppermute | solution.py:764
  102.0 42.3 %collective-permute-start.14 = (bf16[4,640,256]{2,1,0:T(8,128)(2,1)S(1)}, bf16[4,640,256]{2,1,0:T(8,128)(2,1)S(1)}, u32[]{:S(2)}, u32[]{:S(2)}) collective-permute-start(bf16[4,640,256]{2,1,0:T(8,128)(2,1)S(1)} %all-to-all-done.1.refs_0_), channel_id=1, source_target_pairs={{0,1},{1,0},{2,3},{3,2},{4,5},{5,4},{6,7},{7,6},{8,9},{9,8},{10,11... | collective-permute-start | bytes 3932168 | tf_op jit(solution)/shard_map/ppermute | solution.py:29
  107.4 37.3 %copy-start.37 = (f32[512,1024]{1,0:T(8,128)}, f32[512,1024]{1,0:T(8,128)S(1)}, u32[]{:S(2)}) copy-start(f32[512,1024]{1,0:T(8,128)S(1)} %get-tuple-element.312) | copy-start | bytes 6291460
  107.5 1.9 collective-permute-start.10
  107.5 4.5 collective-permute-start.11
  109.2 4.4 collective-permute-start.9
  112.1 7.9 %collective-permute-start.12 = (bf16[128,1024]{1,0:T(8,128)(2,1)S(1)}, bf16[128,1024]{1,0:T(8,128)(2,1)S(1)}, u32[]{:S(2)}, u32[]{:S(2)}) collective-permute-start(bf16[128,1024]{1,0:T(8,128)(2,1)S(1)} %fusion.33), channel_id=1, source_target_pairs={{0,16},{8,24},{16,0},{24,8},{1,17},{9,25},{17,1},{25,9},{2,18},{10... | collective-permute-start | bytes 786440 | tf_op jit(solution)/shard_map/ppermute | solution.py:25
  144.7 6.4 %collective-permute-start.16 = (bf16[128,1024]{1,0:T(8,128)(2,1)S(1)}, bf16[128,1024]{1,0:T(8,128)(2,1)S(1)}, u32[]{:S(2)}, u32[]{:S(2)}) collective-permute-start(bf16[128,1024]{1,0:T(8,128)(2,1)S(1)} %multiply_convert_fusion), channel_id=1, source_target_pairs={{0,16},{8,24},{16,0},{24,8},{1,17},{9,25},{17,1},{25,9},{2,18},{10... | collective-permute-start | bytes 786440 | tf_op jit(solution)/shard_map/ppermute | solution.py:25
  146.4 4.8 collective-permute-start.15
  151.2 1.5 collective-permute-start.17
  160.0 15.1 %collective-permute-start.19 = (bf16[128,4096]{1,0:T(8,128)(2,1)}, bf16[128,4096]{1,0:T(8,128)(2,1)}, u32[]{:S(2)}, u32[]{:S(2)}) collective-permute-start(bf16[128,4096]{1,0:T(8,128)(2,1)} %get-tuple-element.251), channel_id=1, source_target_pairs={{0,8},{8,0},{16,24},{24,16},{1,9},{9,1},{17,25},{25,17},{2,10},{10... | collective-permute-start | bytes 3145736 | tf_op jit(solution)/shard_map/ppermute | solution.py:25
  173.5 33.8 %collective-permute-start.23 = (bf16[8,2,128,1024]{3,2,1,0:T(8,128)(2,1)}, bf16[8,2,128,1024]{3,2,1,0:T(8,128)(2,1)}, u32[]{:S(2)}, u32[]{:S(2)}) collective-permute-start(bf16[8,2,128,1024]{3,2,1,0:T(8,128)(2,1)} %bitcast.195), channel_id=1, source_target_pairs={{0,8},{8,0},{16,24},{24,16},{1,9},{9,1},{17,25},{25,17},{2,10},{10... | collective-permute-start | bytes 12582920 | tf_op jit(solution)/shard_map/ppermute | solution.py:25
  174.5 9.4 %collective-permute-start.18 = (bf16[128,4096]{1,0:T(8,128)(2,1)S(1)}, bf16[128,4096]{1,0:T(8,128)(2,1)S(1)}, u32[]{:S(2)}, u32[]{:S(2)}) collective-permute-start(bf16[128,4096]{1,0:T(8,128)(2,1)S(1)} %get-tuple-element.250), channel_id=1, source_target_pairs={{0,8},{8,0},{16,24},{24,16},{1,9},{9,1},{17,25},{25,17},{2,10},{10... | collective-permute-start | bytes 3145736 | tf_op jit(solution)/shard_map/ppermute | solution.py:25
  175.1 248.1 %reduce-scatter.3.cloned.1.call-start = ((), (), s32[]{:S(2)}) async-start(), calls=%async_computation.6 | async-start | bytes 4718592 | tf_op jit(solution)/shard_map/reduce_scatter | solution.py:871
  178.2 25.4 %collective-permute-start.20 = (bf16[128,4096]{1,0:T(8,128)(2,1)}, bf16[128,4096]{1,0:T(8,128)(2,1)}, u32[]{:S(2)}, u32[]{:S(2)}) collective-permute-start(bf16[128,4096]{1,0:T(8,128)(2,1)} %fusion.7), channel_id=1, source_target_pairs={{0,16},{8,24},{16,0},{24,8},{1,17},{9,25},{17,1},{25,9},{2,18},{10... | collective-permute-start | bytes 3145736 | tf_op jit(solution)/shard_map/ppermute | solution.py:25
  180.6 1.7 collective-permute-start.21
  182.3 1.3 collective-permute-start.22
  227.8 24.3 %collective-permute-start.25 = (bf16[512,1024]{1,0:T(8,128)(2,1)S(1)}, bf16[512,1024]{1,0:T(8,128)(2,1)S(1)}, u32[]{:S(2)}, u32[]{:S(2)}) collective-permute-start(bf16[512,1024]{1,0:T(8,128)(2,1)S(1)} %get-tuple-element.128.refs_0_), channel_id=1, source_target_pairs={{0,16},{8,24},{16,0},{24,8},{1,17},{9,25},{17,1},{25,9},{2,18},{10... | collective-permute-start | bytes 3145736 | tf_op jit(solution)/shard_map/ppermute | solution.py:25
  229.4 22.7 %collective-permute-start.24 = (bf16[512,1024]{1,0:T(8,128)(2,1)S(1)}, bf16[512,1024]{1,0:T(8,128)(2,1)S(1)}, u32[]{:S(2)}, u32[]{:S(2)}) collective-permute-start(bf16[512,1024]{1,0:T(8,128)(2,1)S(1)} %get-tuple-element.128.refs_0_), channel_id=1, source_target_pairs={{0,8},{8,0},{16,24},{24,16},{1,9},{9,1},{17,25},{25,17},{2,10},{10... | collective-permute-start | bytes 3145736 | tf_op jit(solution)/shard_map/ppermute | solution.py:25
  252.1 2.8 collective-permute-start.26
  285.1 5.9 %collective-permute-start.28 = (bf16[1024,1024]{1,0:T(8,128)(2,1)}, bf16[1024,1024]{1,0:T(8,128)(2,1)S(1)}, u32[]{:S(2)}, u32[]{:S(2)}) collective-permute-start(bf16[1024,1024]{1,0:T(8,128)(2,1)} %get-tuple-element.134), channel_id=1, source_target_pairs={{0,8},{8,0},{16,24},{24,16},{1,9},{9,1},{17,25},{25,17},{2,10},{10... | collective-permute-start | bytes 6291464 | tf_op jit(solution)/shard_map/ppermute | solution.py:25
  285.3 5.3 collective-permute-start.30
  294.8 25.8 %collective-permute-start.29 = (bf16[512,1024]{1,0:T(8,128)(2,1)}, bf16[512,1024]{1,0:T(8,128)(2,1)}, u32[]{:S(2)}, u32[]{:S(2)}) collective-permute-start(bf16[512,1024]{1,0:T(8,128)(2,1)} %add_convert_fusion.3), channel_id=1, source_target_pairs={{0,16},{8,24},{16,0},{24,8},{1,17},{9,25},{17,1},{25,9},{2,18},{10... | collective-permute-start | bytes 3145736 | tf_op jit(solution)/shard_map/ppermute | solution.py:25
  320.6 30.9 %collective-permute-start.31 = (bf16[4,512,256]{2,1,0:T(8,128)(2,1)S(1)}, bf16[4,512,256]{2,1,0:T(8,128)(2,1)}, u32[]{:S(2)}, u32[]{:S(2)}) collective-permute-start(bf16[4,512,256]{2,1,0:T(8,128)(2,1)S(1)} %fusion.9), channel_id=1, source_target_pairs={{0,16},{8,24},{16,0},{24,8},{1,17},{9,25},{17,1},{25,9},{2,18},{10... | collective-permute-start | bytes 3145736 | tf_op jit(solution)/shard_map/ppermute | solution.py:25
  322.1 196.8 %reduce-scatter.5.cloned.1.call-start = ((), (), s32[]{:S(2)}) async-start(), calls=%async_computation.7 | async-start | bytes 4718592 | tf_op jit(solution)/shard_map/reduce_scatter | solution.py:895
  351.5 24.3 %collective-permute-start.34 = (bf16[128,4096]{1,0:T(8,128)(2,1)S(1)}, bf16[128,4096]{1,0:T(8,128)(2,1)S(1)}, u32[]{:S(2)}, u32[]{:S(2)}) collective-permute-start(bf16[128,4096]{1,0:T(8,128)(2,1)S(1)} %get-tuple-element.172), channel_id=1, source_target_pairs={{0,16},{8,24},{16,0},{24,8},{1,17},{9,25},{17,1},{25,9},{2,18},{10... | collective-permute-start | bytes 3145736 | tf_op jit(solution)/shard_map/ppermute | solution.py:25
  375.9 4.1 collective-permute-start.35
  375.9 16.5 %collective-permute-start.39 = (bf16[8,2,128,1024]{3,2,1,0:T(8,128)(2,1)}, bf16[8,2,128,1024]{3,2,1,0:T(8,128)(2,1)S(1)}, u32[]{:S(2)}, u32[]{:S(2)}) collective-permute-start(bf16[8,2,128,1024]{3,2,1,0:T(8,128)(2,1)} %get-tuple-element.175), channel_id=1, source_target_pairs={{0,8},{8,0},{16,24},{24,16},{1,9},{9,1},{17,25},{25,17},{2,10},{10... | collective-permute-start | bytes 12582920 | tf_op jit(solution)/shard_map/ppermute | solution.py:25
  376.4 6.6 %collective-permute-start.36 = (bf16[128,4096]{1,0:T(8,128)(2,1)S(1)}, bf16[128,4096]{1,0:T(8,128)(2,1)S(1)}, u32[]{:S(2)}, u32[]{:S(2)}) collective-permute-start(bf16[128,4096]{1,0:T(8,128)(2,1)S(1)} %collective-permute-done.34), channel_id=1, source_target_pairs={{0,8},{8,0},{16,24},{24,16},{1,9},{9,1},{17,25},{25,17},{2,10},{10... | collective-permute-start | bytes 3145736 | tf_op jit(solution)/shard_map/ppermute | solution.py:25
  388.8 1.9 collective-permute-start.38
  389.3 33.8 %collective-permute-start.41 = (bf16[4,640,256]{2,1,0:T(8,128)(2,1)S(1)}, bf16[4,640,256]{2,1,0:T(8,128)(2,1)}, u32[]{:S(2)}, u32[]{:S(2)}) collective-permute-start(bf16[4,640,256]{2,1,0:T(8,128)(2,1)S(1)} %get-tuple-element.180), channel_id=1, source_target_pairs={{0,1},{1,0},{2,3},{3,2},{4,5},{5,4},{6,7},{7,6},{8,9},{9,8},{10,11... | collective-permute-start | bytes 3932168 | tf_op jit(solution)/shard_map/ppermute | solution.py:29
  397.7 3.2 collective-permute-start.37
  397.9 8.8 %collective-permute-start.40 = (bf16[128,1024]{1,0:T(8,128)(2,1)}, bf16[128,1024]{1,0:T(8,128)(2,1)S(1)}, u32[]{:S(2)}, u32[]{:S(2)}) collective-permute-start(bf16[128,1024]{1,0:T(8,128)(2,1)} %fusion.31), channel_id=1, source_target_pairs={{0,16},{8,24},{16,0},{24,8},{1,17},{9,25},{17,1},{25,9},{2,18},{10... | collective-permute-start | bytes 786440 | tf_op jit(solution)/shard_map/ppermute | solution.py:25
  398.8 25.9 %collective-permute-start.33 = (bf16[128,256]{1,0:T(8,128)(2,1)}, bf16[128,256]{1,0:T(8,128)(2,1)}, u32[]{:S(2)}, u32[]{:S(2)}) collective-permute-start(bf16[128,256]{1,0:T(8,128)(2,1)} %bitcast.56), channel_id=1, source_target_pairs={{0,8},{8,0},{16,24},{24,16},{1,9},{9,1},{17,25},{25,17},{2,10},{10... | collective-permute-start | bytes 196616 | tf_op jit(solution)/shard_map/ppermute | solution.py:25
  399.6 34.0 %collective-permute-start.50 = (bf16[128,256]{1,0:T(8,128)(2,1)S(1)}, bf16[128,256]{1,0:T(8,128)(2,1)S(1)}, u32[]{:S(2)}, u32[]{:S(2)}) collective-permute-start(bf16[128,256]{1,0:T(8,128)(2,1)S(1)} %bitcast.187), channel_id=1, source_target_pairs={{0,8},{8,0},{16,24},{24,16},{1,9},{9,1},{17,25},{25,17},{2,10},{10... | collective-permute-start | bytes 196616 | tf_op jit(solution)/shard_map/ppermute | solution.py:25
  423.2 10.4 %collective-permute-start.46 = (bf16[128,1024]{1,0:T(8,128)(2,1)}, bf16[128,1024]{1,0:T(8,128)(2,1)S(1)}, u32[]{:S(2)}, u32[]{:S(2)}) collective-permute-start(bf16[128,1024]{1,0:T(8,128)(2,1)} %fusion.22), channel_id=1, source_target_pairs={{0,8},{8,0},{16,24},{24,16},{1,9},{9,1},{17,25},{25,17},{2,10},{10... | collective-permute-start | bytes 786440 | tf_op jit(solution)/shard_map/ppermute | solution.py:25
  423.2 8.9 %collective-permute-start.42 = (bf16[128,1024]{1,0:T(8,128)(2,1)}, bf16[128,1024]{1,0:T(8,128)(2,1)S(1)}, u32[]{:S(2)}, u32[]{:S(2)}) collective-permute-start(bf16[128,1024]{1,0:T(8,128)(2,1)} %fusion.22), channel_id=1, source_target_pairs={{0,16},{8,24},{16,0},{24,8},{1,17},{9,25},{17,1},{25,9},{2,18},{10... | collective-permute-start | bytes 786440 | tf_op jit(solution)/shard_map/ppermute | solution.py:25
  432.1 4.3 collective-permute-start.43
  433.6 3.7 collective-permute-start.47
  438.5 7.7 %collective-permute-start.48 = (bf16[4,27,256]{2,1,0:T(8,128)(2,1)S(1)}, bf16[4,27,256]{2,1,0:T(8,128)(2,1)S(1)}, u32[]{:S(2)}, u32[]{:S(2)}) collective-permute-start(bf16[4,27,256]{2,1,0:T(8,128)(2,1)S(1)} %get-tuple-element.283), channel_id=1, source_target_pairs={{1,0},{2,1},{3,2},{4,3},{5,4},{6,5},{7,6},{9,8},{10,9},{11,10},{12... | collective-permute-start | bytes 165896 | tf_op jit(solution)/shard_map/ppermute | solution.py:764
  439.9 6.7 %collective-permute-start.49 = (bf16[4,27,256]{2,1,0:T(8,128)(2,1)S(1)}, bf16[4,27,256]{2,1,0:T(8,128)(2,1)S(1)}, u32[]{:S(2)}, u32[]{:S(2)}) collective-permute-start(bf16[4,27,256]{2,1,0:T(8,128)(2,1)S(1)} %get-tuple-element.282), channel_id=1, source_target_pairs={{0,1},{1,2},{2,3},{3,4},{4,5},{5,6},{6,7},{8,9},{9,10},{10,11},{11... | collective-permute-start | bytes 165896 | tf_op jit(solution)/shard_map/ppermute | solution.py:763
  452.9 51.1 %all-to-all-start.3 = ((bf16[4,640,256]{2,1,0:T(8,128)(2,1)}), bf16[4,640,256]{2,1,0:T(8,128)(2,1)S(1)}, u32[]{:S(2)}, u32[]{:S(2)}) async-start(bf16[4,640,256]{2,1,0:T(8,128)(2,1)} %add_convert_fusion.2), calls=%async_computation.4 | async-start | bytes 2621440 | tf_op jit(solution)/shard_map/all_to_all | solution.py:92
  462.2 40.5 %collective-permute-start.51 = (bf16[4,656,256]{2,1,0:T(8,128)(2,1)}, bf16[4,656,256]{2,1,0:T(8,128)(2,1)S(1)}, u32[]{:S(2)}, u32[]{:S(2)}) collective-permute-start(bf16[4,656,256]{2,1,0:T(8,128)(2,1)} %copy-done.6), channel_id=1, source_target_pairs={{0,1},{1,0},{2,3},{3,2},{4,5},{5,4},{6,7},{7,6},{8,9},{9,8},{10,11... | collective-permute-start | bytes 4030472 | tf_op jit(solution)/shard_map/ppermute | solution.py:29
  462.2 46.5 %collective-permute-start.27 = (bf16[4,512,256]{2,1,0:T(8,128)(2,1)}, bf16[4,512,256]{2,1,0:T(8,128)(2,1)}, u32[]{:S(2)}, u32[]{:S(2)}) collective-permute-start(bf16[4,512,256]{2,1,0:T(8,128)(2,1)} %bitcast.166), channel_id=1, source_target_pairs={{0,8},{8,0},{16,24},{24,16},{1,9},{9,1},{17,25},{25,17},{2,10},{10... | collective-permute-start | bytes 3145736 | tf_op jit(solution)/shard_map/ppermute | solution.py:25
  462.2 2.9 collective-permute-start.32
  462.7 8.4 %collective-permute-start.45 = (bf16[512,256]{1,0:T(8,128)(2,1)S(1)}, bf16[512,256]{1,0:T(8,128)(2,1)S(1)}, u32[]{:S(2)}, u32[]{:S(2)}) collective-permute-start(bf16[512,256]{1,0:T(8,128)(2,1)S(1)} %get-tuple-element.186), channel_id=1, source_target_pairs={{0,24},{8,16},{16,8},{24,0},{1,25},{9,17},{17,9},{25,1},{2,26},{10... | collective-permute-start | bytes 786440 | tf_op jit(solution)/shard_map/ppermute | solution.py:25
  463.8 13.1 %collective-permute-start.44 = (bf16[512,256]{1,0:T(8,128)(2,1)S(1)}, bf16[512,256]{1,0:T(8,128)(2,1)S(1)}, u32[]{:S(2)}, u32[]{:S(2)}) collective-permute-start(bf16[512,256]{1,0:T(8,128)(2,1)S(1)} %get-tuple-element.184), channel_id=1, source_target_pairs={{0,16},{8,24},{16,0},{24,8},{1,17},{9,25},{17,1},{25,9},{2,18},{10... | collective-permute-start | bytes 786440 | tf_op jit(solution)/shard_map/ppermute | solution.py:25
  504.1 36.6 %all-to-all-start.2 = ((bf16[4,656,256]{2,1,0:T(8,128)(2,1)}), bf16[4,656,256]{2,1,0:T(8,128)(2,1)S(1)}, u32[]{:S(2)}, u32[]{:S(2)}) async-start(bf16[4,656,256]{2,1,0:T(8,128)(2,1)} %add_convert_fusion.1), calls=%async_computation.3 | async-start | bytes 2686976 | tf_op jit(solution)/shard_map/all_to_all | solution.py:92
  519.9 23.0 %collective-permute-start.52 = (bf16[128,1024]{1,0:T(8,128)(2,1)S(1)}, bf16[128,1024]{1,0:T(8,128)(2,1)S(1)}, u32[]{:S(2)}, u32[]{:S(2)}) collective-permute-start(bf16[128,1024]{1,0:T(8,128)(2,1)S(1)} %slice_bitcast_fusion), channel_id=1, source_target_pairs={{0,16},{8,24},{16,0},{24,8},{1,17},{9,25},{17,1},{25,9},{2,18},{10... | collective-permute-start | bytes 786440 | tf_op jit(solution)/shard_map/ppermute | solution.py:25
  (68 other events, 388.9 us)
Sparse Core Ops, SparseCore 0:
  90.0 83.5 all-gather.4
  176.2 72.1 all-gather.6
  322.2 88.7 reduce-scatter.2
  415.0 100.2 reduce-scatter.4
